TPU v7x, 32 devices: a whole 2x2x4 slice. The times are simulated.
32 devices in a mesh: bucket: 4 (over z), fsdp: 8 (over y, x, core).
Axes of the slice: x: 2, y: 2, z: 4, core: 2. Of those that a mesh axis runs over, the one named last changes fastest.
Arguments:
- tokens: bfloat16 [32, 128, 1536], P(('bucket', 'fsdp')), may hold values from -6 to 6
- cond: bfloat16 [32, 4, 1024], P(('bucket', 'fsdp')), may hold values from -6 to 6
- text: bfloat16 [32, 256, 4096], P(('bucket', 'fsdp')), may hold values from -6 to 6
- segments: int32 [32, 128], P(('bucket', 'fsdp')), may hold values from 0 to 3, never falling along the last dimension, each value on 1 to 64 neighbouring positions
- positions: int32 [32, 2, 128], P(('bucket', 'fsdp')), may hold values from 0 to 63
- counts: int32 [4], replicated, may hold values from 256 to 1024
- ada_weight: bfloat16 [1024, 6144], P('fsdp'), may hold values from -0.1875 to 0.1875
- ada_bias: bfloat16 [6144], P('fsdp'), may hold values from -1.5 to 1.5
- gains: bfloat16 [6, 1536], P(None, 'fsdp'), may hold values from 0.099609375 to 1.8984375
- attn_weight: bfloat16 [3, 1536, 1536], P(None, 'fsdp'), may hold values from -0.15625 to 0.15625
- out_weight: bfloat16 [1536, 1536], P('fsdp'), may hold values from -0.625 to 0.625
- text_weight: bfloat16 [2, 4096, 1536], P(None, 'fsdp'), may hold values from -0.09375 to 0.09375
- ffn_weight: bfloat16 [2, 1536, 4096], P(None, 'fsdp'), may hold values from -0.15625 to 0.15625
- down_weight: bfloat16 [4096, 1536], P('fsdp'), may hold values from -0.09375 to 0.09375
- cotangent: bfloat16 [32, 128, 1536], P(('bucket', 'fsdp')), may hold values from -6 to 6
Outputs:
- block_out: bfloat16 [32, 128, 1536], P(('bucket', 'fsdp'))
- token_grad: float32 [32, 128, 1536], P(('bucket', 'fsdp'))
- ada_weight_grad: float32 [1024, 6144], P(('bucket', 'fsdp'))
- ada_bias_grad: float32 [6144], P(('bucket', 'fsdp'))
- gains_grad: float32 [6, 1536], P(None, ('bucket', 'fsdp'))
- attn_weight_grad: float32 [3, 1536, 1536], P(None, ('bucket', 'fsdp'))
- out_weight_grad: float32 [1536, 1536], P(('bucket', 'fsdp'))
- text_weight_grad: float32 [2, 4096, 1536], P(None, ('bucket', 'fsdp'))
- ffn_weight_grad: float32 [2, 1536, 4096], P(None, ('bucket', 'fsdp'))
- down_weight_grad: float32 [4096, 1536], P(('bucket', 'fsdp'))
Inputs may be any that keep to these rules, and one draw needn't show every extreme that they name: `segments`: in each row image numbers never fall, every image holds one token or more, and one image holds exactly half of the row's 128 tokens.
All inputs are finite; a program needn't handle non-finite values.
Results may differ from a plain program's by a relative error of at most 0.014.
The roundings to bfloat16 on the way count: a program that leaves them out, or rounds other values in their place, can miss the bound.
Values may be sent and summed in bfloat16 or wider, within the bound.
A program may use at most 512 MiB of HBM per device.

v0:
```python
import jax
import jax.numpy as jnp
from jax import lax
from jax.sharding import PartitionSpec as P

D = 1536
HEADS = 24
HDIM = 64
IMGS = 4
TXT = 64


EPS = 1e-06
NEGATIVE = -1e30
HIGH = lax.Precision.HIGHEST


def silu(v):
    return v * jax.nn.sigmoid(v)


def norm_rows(v):
    inverse = lax.rsqrt(jnp.mean(v * v, axis=-1, keepdims=True) + EPS)
    return (v * inverse, inverse)


def norm_back(grad, normed, inverse):
    return inverse * (grad - normed * jnp.mean(grad * normed, axis=-1, keepdims=True))


def rotary_tables(pos):
    quarter = HDIM // 4
    freq = 10000.0 ** (-jnp.arange(quarter, dtype=jnp.float32) / quarter)
    angle = jnp.transpose(pos.astype(jnp.float32), (1, 0))[:, :, None] * freq[None, None, :]
    return (jnp.cos(angle), jnp.sin(angle))


def rotate(v, cosine, sine):
    rows = v.shape[0]
    parts = v.reshape(rows, HEADS, 2, 2, HDIM // 4)
    first = parts[:, :, :, 0]
    second = parts[:, :, :, 1]
    cosine = cosine[:, None]
    sine = sine[:, None]
    turned = jnp.stack([first * cosine - second * sine, first * sine + second * cosine], axis=3)
    return turned.reshape(rows, HEADS * HDIM)


def to_pairs(v):
    return jnp.transpose(v.reshape(v.shape[0], HEADS // 2, 2 * HDIM), (1, 0, 2))


def from_pairs(v):
    return jnp.transpose(v, (1, 0, 2)).reshape(v.shape[1], HEADS * HDIM)


def pair_scores(query, keys):
    q_heads = query.reshape(query.shape[0], 2, HDIM)
    k_heads = keys.reshape(keys.shape[0], 2, HDIM)
    return jnp.einsum(
        "rhd,khd->hrk", q_heads, k_heads, preferred_element_type=jnp.float32
    ) * HDIM ** (-0.5)


def attend_forward(q_b, k_b, v_b, allowed):

    def one_pair(item):
        query, keys, values = item
        scores = jnp.where(allowed[None], pair_scores(query, keys), NEGATIVE)
        top = jnp.max(scores, axis=-1, keepdims=True)
        expo = jnp.exp(scores - top)
        total = jnp.sum(expo, axis=-1, keepdims=True)
        probs = (expo / total).astype(jnp.bfloat16)
        result = jnp.einsum(
            "hrk,khd->rhd",
            probs,
            values.reshape(values.shape[0], 2, HDIM),
            preferred_element_type=jnp.float32,
        )
        return (result.reshape(query.shape[0], 2 * HDIM), (top + jnp.log(total))[..., 0])

    outputs, saved = lax.map(one_pair, (to_pairs(q_b), to_pairs(k_b), to_pairs(v_b)))
    return (from_pairs(outputs), saved)


def attend_back(q_b, k_b, v_b, saved, grad_b, allowed):

    def one_pair(item):
        query, keys, values, lse_pair, grad = item
        rows = query.shape[0]
        count = keys.shape[0]
        scores = jnp.where(allowed[None], pair_scores(query, keys), NEGATIVE)
        probs = jnp.exp(scores - lse_pair[..., None])
        probs_b = probs.astype(jnp.bfloat16)
        grad_heads = grad.reshape(rows, 2, HDIM)
        dprob = jnp.einsum(
            "rhd,khd->hrk",
            grad_heads,
            values.reshape(count, 2, HDIM),
            preferred_element_type=jnp.float32,
        )
        dscore = (probs * (dprob - jnp.sum(probs * dprob, axis=-1, keepdims=True))).astype(
            jnp.bfloat16
        )
        factor = HDIM ** (-0.5)
        dquery = (
            jnp.einsum(
                "hrk,khd->rhd",
                dscore,
                keys.reshape(count, 2, HDIM),
                preferred_element_type=jnp.float32,
            )
            * factor
        )
        dkeys = (
            jnp.einsum(
                "hrk,rhd->khd",
                dscore,
                query.reshape(rows, 2, HDIM),
                preferred_element_type=jnp.float32,
            )
            * factor
        )
        dvalues = jnp.einsum(
            "hrk,rhd->khd", probs_b, grad_heads, preferred_element_type=jnp.float32
        )
        return (
            dquery.reshape(rows, 2 * HDIM),
            dkeys.reshape(count, 2 * HDIM),
            dvalues.reshape(count, 2 * HDIM),
        )

    d_query, d_keys, d_values = lax.map(
        one_pair, (to_pairs(q_b), to_pairs(k_b), to_pairs(v_b), saved, to_pairs(grad_b))
    )
    return (from_pairs(d_query), from_pairs(d_keys), from_pairs(d_values))


def mult(left, right):
    return jnp.dot(left, right, preferred_element_type=jnp.float32)


def per_device(
    tokens,
    cond,
    text,
    segments,
    positions,
    counts,
    ada_weight,
    ada_bias,
    gains,
    attn_weight,
    out_weight,
    text_weight,
    ffn_weight,
    down_weight,
    cotangent,
):
    ada_w, ada_b, gain_rows, attn_w, out_w, text_w = (
        lax.all_gather(ada_weight, "fsdp", axis=0, tiled=True),
        lax.all_gather(ada_bias, "fsdp", axis=0, tiled=True),
        lax.all_gather(gains, "fsdp", axis=1, tiled=True),
        lax.all_gather(attn_weight, "fsdp", axis=1, tiled=True),
        lax.all_gather(out_weight, "fsdp", axis=0, tiled=True),
        lax.all_gather(text_weight, "fsdp", axis=1, tiled=True),
    )
    gain_f = gain_rows.astype(jnp.float32)
    x = tokens[0].astype(jnp.float32)
    seg = segments[0]
    cosine, sine = rotary_tables(positions[0])
    text_b = text[0]
    cond_act = silu(cond[0].astype(jnp.float32)).astype(jnp.bfloat16)
    mod = mult(cond_act, ada_w) + ada_b.astype(jnp.float32)[None, :]
    pick = (seg[:, None] == jnp.arange(IMGS, dtype=jnp.int32)[None, :]).astype(jnp.float32)
    per_token = jnp.dot(pick, mod, precision=HIGH)
    scale1 = per_token[:, :D]
    gate1 = per_token[:, D : 2 * D]
    scale2 = per_token[:, 2 * D : 3 * D]
    gate2 = per_token[:, 3 * D :]
    normed1, inverse1 = norm_rows(x)
    h_one = (normed1 * gain_f[0] * (1.0 + scale1)).astype(jnp.bfloat16)
    query = mult(h_one, attn_w[0])
    keyed = mult(h_one, attn_w[1])
    valued = mult(h_one, attn_w[2]).astype(jnp.bfloat16)
    q_norm, q_inv = norm_rows(query)
    k_norm, k_inv = norm_rows(keyed)
    q_rot = rotate(q_norm * gain_f[2], cosine, sine).astype(jnp.bfloat16)
    k_rot = rotate(k_norm * gain_f[3], cosine, sine).astype(jnp.bfloat16)
    text_keys = mult(text_b, text_w[0])
    text_vals = mult(text_b, text_w[1]).astype(jnp.bfloat16)
    t_norm, t_inv = norm_rows(text_keys)
    text_rot = (t_norm * gain_f[4]).astype(jnp.bfloat16)
    same = seg[:, None] == seg[None, :]
    owner = jnp.arange(IMGS * TXT, dtype=jnp.int32) // TXT
    mine = seg[:, None] == owner[None, :]
    self_out, self_lse = attend_forward(q_rot, k_rot, valued, same)
    cross_out, cross_lse = attend_forward(q_rot, text_rot, text_vals, mine)
    cross_gate = jnp.tanh(gain_f[5])
    comb = (self_out + cross_gate * cross_out).astype(jnp.bfloat16)
    branch = mult(comb, out_w)
    tanh_one = jnp.tanh(gate1)
    x_one = x + tanh_one * branch
    normed2, inverse2 = norm_rows(x_one)
    h_two = (normed2 * gain_f[1] * (1.0 + scale2)).astype(jnp.bfloat16)
    ffn_w, down_w = (
        lax.all_gather(ffn_weight, "fsdp", axis=1, tiled=True),
        lax.all_gather(down_weight, "fsdp", axis=0, tiled=True),
    )
    gate_pre = mult(h_two, ffn_w[0])
    upper = mult(h_two, ffn_w[1])
    sigm = jax.nn.sigmoid(gate_pre)
    silu_pre = gate_pre * sigm
    hidden = (silu_pre * upper).astype(jnp.bfloat16)
    ffn_out = mult(hidden, down_w)
    tanh_two = jnp.tanh(gate2)
    block_out = (x_one + tanh_two * ffn_out).astype(jnp.bfloat16)
    totals = counts.astype(jnp.float32)
    here = jnp.sum(
        jnp.where(
            jnp.arange(totals.shape[0], dtype=jnp.int32) == lax.axis_index("bucket"), totals, 0.0
        )
    )
    weight = lax.axis_size("bucket") * here / jnp.sum(totals)
    grad = cotangent[0].astype(jnp.float32) * weight
    back_ffn, back_down = (
        lax.all_gather(ffn_weight, "fsdp", axis=1, tiled=True),
        lax.all_gather(down_weight, "fsdp", axis=0, tiled=True),
    )
    d_gate2 = grad * ffn_out * (1.0 - tanh_two * tanh_two)
    d_ffn = (grad * tanh_two).astype(jnp.bfloat16)
    d_hidden = mult(d_ffn, back_down.T)
    g_down = mult(hidden.T, d_ffn)
    d_pre = (d_hidden * upper * sigm * (1.0 + gate_pre * (1.0 - sigm))).astype(jnp.bfloat16)
    d_up = (d_hidden * silu_pre).astype(jnp.bfloat16)
    d_h_two = mult(d_pre, back_ffn[0].T) + mult(d_up, back_ffn[1].T)
    g_ffn = jnp.stack([mult(h_two.T, d_pre), mult(h_two.T, d_up)])
    s_ffn, s_down = (
        lax.psum_scatter(g_ffn, ("bucket", "fsdp"), scatter_dimension=1, tiled=True),
        lax.psum_scatter(g_down, ("bucket", "fsdp"), scatter_dimension=0, tiled=True),
    )
    back_attn, back_out = (
        lax.all_gather(attn_weight, "fsdp", axis=1, tiled=True),
        lax.all_gather(out_weight, "fsdp", axis=0, tiled=True),
    )
    g_gain_one = jnp.sum(d_h_two * normed2 * (1.0 + scale2), axis=0)
    d_scale2 = d_h_two * normed2 * gain_f[1]
    d_x_one = grad + norm_back(d_h_two * gain_f[1] * (1.0 + scale2), normed2, inverse2)
    d_gate1 = d_x_one * branch * (1.0 - tanh_one * tanh_one)
    d_branch = (d_x_one * tanh_one).astype(jnp.bfloat16)
    d_comb = mult(d_branch, back_out.T)
    g_out = mult(comb.T, d_branch)
    g_gain_five = jnp.sum(d_comb * cross_out, axis=0) * (1.0 - cross_gate * cross_gate)
    d_self = d_comb.astype(jnp.bfloat16)
    d_cross = (d_comb * cross_gate).astype(jnp.bfloat16)
    dq_self, dk_self, dv_self = attend_back(q_rot, k_rot, valued, self_lse, d_self, same)
    dq_cross, dk_text, dv_text = attend_back(q_rot, text_rot, text_vals, cross_lse, d_cross, mine)
    d_q_norm = rotate(dq_self + dq_cross, cosine, -sine)
    g_gain_two = jnp.sum(d_q_norm * q_norm, axis=0)
    d_query = norm_back(d_q_norm * gain_f[2], q_norm, q_inv).astype(jnp.bfloat16)
    d_k_norm = rotate(dk_self, cosine, -sine)
    g_gain_three = jnp.sum(d_k_norm * k_norm, axis=0)
    d_keyed = norm_back(d_k_norm * gain_f[3], k_norm, k_inv).astype(jnp.bfloat16)
    d_valued = dv_self.astype(jnp.bfloat16)
    g_gain_four = jnp.sum(dk_text * t_norm, axis=0)
    d_text_keys = norm_back(dk_text * gain_f[4], t_norm, t_inv).astype(jnp.bfloat16)
    d_text_vals = dv_text.astype(jnp.bfloat16)
    g_text = jnp.stack([mult(text_b.T, d_text_keys), mult(text_b.T, d_text_vals)])
    d_h_one = (
        mult(d_query, back_attn[0].T)
        + mult(d_keyed, back_attn[1].T)
        + mult(d_valued, back_attn[2].T)
    )
    g_attn = jnp.stack([mult(h_one.T, d_query), mult(h_one.T, d_keyed), mult(h_one.T, d_valued)])
    g_gain_zero = jnp.sum(d_h_one * normed1 * (1.0 + scale1), axis=0)
    d_scale1 = d_h_one * normed1 * gain_f[0]
    token_grad = d_x_one + norm_back(d_h_one * gain_f[0] * (1.0 + scale1), normed1, inverse1)
    d_token_mod = jnp.concatenate([d_scale1, d_gate1, d_scale2, d_gate2], axis=1)
    d_mod = jnp.dot(pick.T, d_token_mod, precision=HIGH)
    g_ada_b = jnp.sum(d_mod, axis=0)
    g_ada_w = mult(cond_act.T, d_mod.astype(jnp.bfloat16))
    g_gains = jnp.stack(
        [g_gain_zero, g_gain_one, g_gain_two, g_gain_three, g_gain_four, g_gain_five]
    )
    s_ada_w, s_ada_b, s_gains, s_attn, s_out, s_text = (
        lax.psum_scatter(g_ada_w, ("bucket", "fsdp"), scatter_dimension=0, tiled=True),
        lax.psum_scatter(g_ada_b, ("bucket", "fsdp"), scatter_dimension=0, tiled=True),
        lax.psum_scatter(g_gains, ("bucket", "fsdp"), scatter_dimension=1, tiled=True),
        lax.psum_scatter(g_attn, ("bucket", "fsdp"), scatter_dimension=1, tiled=True),
        lax.psum_scatter(g_out, ("bucket", "fsdp"), scatter_dimension=0, tiled=True),
        lax.psum_scatter(g_text, ("bucket", "fsdp"), scatter_dimension=1, tiled=True),
    )
    return (
        block_out[None],
        token_grad[None],
        s_ada_w,
        s_ada_b,
        s_gains,
        s_attn,
        s_out,
        s_text,
        s_ffn,
        s_down,
    )


def solution(mesh):
    in_specs = (
        P(("bucket", "fsdp"), None, None),
        P(("bucket", "fsdp"), None, None),
        P(("bucket", "fsdp"), None, None),
        P(("bucket", "fsdp"), None),
        P(("bucket", "fsdp"), None, None),
        P(),
        P("fsdp", None),
        P("fsdp"),
        P(None, "fsdp"),
        P(None, "fsdp", None),
        P("fsdp", None),
        P(None, "fsdp", None),
        P(None, "fsdp", None),
        P("fsdp", None),
        P(("bucket", "fsdp"), None, None),
    )
    out_specs = (
        P(("bucket", "fsdp"), None, None),
        P(("bucket", "fsdp"), None, None),
        P(("bucket", "fsdp"), None),
        P(("bucket", "fsdp")),
        P(None, ("bucket", "fsdp")),
        P(None, ("bucket", "fsdp"), None),
        P(("bucket", "fsdp"), None),
        P(None, ("bucket", "fsdp"), None),
        P(None, ("bucket", "fsdp"), None),
        P(("bucket", "fsdp"), None),
    )
    return jax.shard_map(
        per_device, mesh=mesh, in_specs=in_specs, out_specs=out_specs, check_vma=False
    )
```

profile of v0, /device:TPU:0, one launch (start us, length us, event | category | flops | bytes accessed | tf_op | source)
XLA Modules:
  0.0 2636.6 jit_solution(10611992128861024796)
XLA Ops:
  12.1 10.6 all-gather
  22.7 9.5 all-gather.1
  34.8 50.0 %all-gather.9.cloned.1.call-done = bf16[1024,6144]{1,0:T(8,128)(2,1)} async-done(((bf16[128,6144]{1,0:T(8,128)(2,1)}), bf16[1024,6144]{1,0:T(8,128)(2,1)}) %all-gather.9.cloned.1.call-update) | async-done | bytes 12582928 | tf_op jit(solution)/shard_map/all_gather | solution.py:161
  84.7 6.3 convolution_add_fusion
  94.4 70.9 %all-gather.11.cloned.1.call-done = bf16[3,1536,1536]{2,1,0:T(8,128)(2,1)} async-done(((bf16[3,192,1536]{2,1,0:T(8,128)(2,1)}), bf16[3,1536,1536]{2,1,0:T(8,128)(2,1)}) %all-gather.11.cloned.1.call-update) | async-done | bytes 14155792 | tf_op jit(solution)/shard_map/all_gather | solution.py:164
  165.3 3.1 fusion.50
  169.4 3.2 multiply_reduce_fusion.14
  176.0 3.9 multiply_reduce_fusion.15
  187.6 32.6 %while.56 = (s32[]{:T(128)}, f32[12,128,128]{1,2,0:T(8,128)}, f32[12,2,128]{2,1,0:T(2,128)S(1)}, bf16[12,128,128]{1,2,0:T(8,128)(2,1)}, bf16[12,128,128]{1,2,0:T...) while((s32[]{:T(128)}, f32[12,128,128]{1,2,0:T(8,128)}, ...), condition=%wide.region_6.7_spmd.clone, body=%wide.region_3.6_spmd.clone.sunk | while | flops 8666882 | bytes 926317 | solution.py:82
  220.2 2.6 copy.122
  222.8 69.7 %all-gather.13.cloned.1.call-done = bf16[2,4096,1536]{2,1,0:T(8,128)(2,1)} async-done(((bf16[2,512,1536]{2,1,0:T(8,128)(2,1)}), bf16[2,4096,1536]{2,1,0:T(8,128)(2,1)}) %all-gather.13.cloned.1.call-update) | async-done | bytes 25165840 | tf_op jit(solution)/shard_map/all_gather | solution.py:166
  292.5 8.9 fusion.46
  303.7 6.5 multiply_reduce_fusion.4
  315.7 38.8 %while.57 = (s32[]{:T(128)}, f32[12,128,128]{1,2,0:T(8,128)}, f32[12,2,128]{2,1,0:T(2,128)S(1)}, bf16[12,256,128]{1,2,0:T(8,128)(2,1)}, bf16[12,128,128]{1,2,0:T...) while((s32[]{:T(128)}, f32[12,128,128]{1,2,0:T(8,128)}, ...), condition=%wide.region_11.12_spmd.clone, body=%wide.region_8.11_spmd.clone.sunk | while | flops 17334016 | bytes 1549941 | solution.py:82
  359.1 4.5 multiply_reduce_fusion.13
  365.7 94.4 %all-gather.17.cloned.1.call-done = bf16[2,1536,4096]{2,1,0:T(8,128)(2,1)} async-done(((bf16[2,192,4096]{2,1,0:T(8,128)(2,1)}), bf16[2,1536,4096]{2,1,0:T(8,128)(2,1)}) %all-gather.17.cloned.1.call-update) | async-done | bytes 25165840 | tf_op jit(solution)/shard_map/all_gather | solution.py:207
  460.1 7.9 fusion.29
  468.0 9.4 fusion.31
  477.3 56.5 %all-gather.19.cloned.1.call-done = bf16[4096,1536]{1,0:T(8,128)(2,1)} async-done(((bf16[512,1536]{1,0:T(8,128)(2,1)}), bf16[4096,1536]{1,0:T(8,128)(2,1)}) %all-gather.19.cloned.1.call-update) | async-done | bytes 12582928 | tf_op jit(solution)/shard_map/all_gather | solution.py:208
  533.8 10.2 multiply_convert_fusion.2
  544.1 10.9 fusion.28
  555.0 22.6 multiply_reduce_fusion.8
  577.6 8.9 fusion.69
  593.1 64.3 %while.58 = (s32[]{:T(128)}, f32[12,128,128]{1,2,0:T(8,128)}, f32[12,128,128]{1,2,0:T(8,128)}, bf16[12,128,128]{1,2,0:T(8,128)(2,1)}, bf16[12,128,128]{1,2,0:T(8...) while((s32[]{:T(128)}, f32[12,128,128]{1,2,0:T(8,128)}, ...), condition=%wide.region_18.19_spmd.clone, body=%wide.region_16.18_spmd.clone.sunk | while | flops 21315328 | bytes 2004625 | solution.py:133
  660.3 58.6 %while.59 = (s32[]{:T(128)}, f32[12,128,128]{1,2,0:T(8,128)}, f32[12,256,128]{1,2,0:T(8,128)}, bf16[12,256,128]{1,2,0:T(8,128)(2,1)}, bf16[12,256,128]{1,2,0:T(8...) while((s32[]{:T(128)}, f32[12,128,128]{1,2,0:T(8,128)}, ...), condition=%wide.region_21.22_spmd.clone, body=%wide.region_19.21_spmd.clone.sunk | while | flops 42614528 | bytes 3545749 | solution.py:133
  734.6 4.1 fusion.34
  738.7 4.0 fusion.47
  742.8 6.0 multiply_reduce_fusion.9
  748.8 3.0 copy.129
  755.6 11.5 convolution_bitcast_fusion.2
  767.1 10.5 convolution_bitcast_fusion.3
  777.6 34.6 %pad_maximum_fusion = f32[2,4096,1536]{1,2,0:T(8,128)} fusion(f32[1,4096,1536]{1,2,0:T(8,128)} %convolution_bitcast_fusion.2, f32[1,4096,1536]{1,2,0:T(8,128)} %convolution_bitcast_fusion.3), kind=kLoop, calls=%fused_computation.68 | loop fusion | flops 12582912 | bytes 100663296 | tf_op jit(solution)/shard_map/stack | solution.py:268
  813.3 5.0 fusion.94
  822.2 10.2 fusion.76
  833.8 10.1 fusion.95
  849.2 9.7 pad_maximum_fusion.2
  860.2 15.3 convolution_bitcast_fusion
  875.5 15.4 convolution_bitcast_fusion.1
  890.9 40.6 %pad_maximum_fusion.1 = f32[2,1536,4096]{2,1,0:T(8,128)} fusion(f32[1,1536,4096]{2,1,0:T(8,128)} %convolution_bitcast_fusion, f32[1,1536,4096]{2,1,0:T(8,128)} %convolution_bitcast_fusion.1), kind=kLoop, calls=%fused_computation.69 | loop fusion | flops 12582912 | bytes 100663296 | tf_op jit(solution)/shard_map/stack | solution.py:237
  931.6 42.9 %all-reduce = f32[6144]{0:T(1024)S(1)} all-reduce(f32[6144]{0:T(1024)S(1)} %get-tuple-element.491), channel_id=3, replica_groups=mesh['bucket'=4,'fsdp'=8] {'bucket','fsdp'}, use_global_device_ids=true, to_apply=%region_27.28.clone | all-reduce | flops 6144 | bytes 49152
  975.3 2.6 fusion.66
  979.2 307.1 %reduce-scatter.16.cloned.1.call-done = f32[2,128,1536]{1,2,0:T(8,128)} async-done(((f32[2,4096,1536]{1,2,0:T(8,128)}), f32[2,128,1536]{1,2,0:T(8,128)}) %reduce-scatter.16.cloned.1.call-update) | async-done | bytes 1572880 | tf_op jit(solution)/shard_map/reduce_scatter | solution.py:291
  1286.3 3.0 copy.132
  1289.4 138.8 %reduce-scatter.14.cloned.1.call-done = f32[48,1536]{1,0:T(8,128)} async-done(((f32[1536,1536]{1,0:T(8,128)}), f32[48,1536]{1,0:T(8,128)}) %reduce-scatter.14.cloned.1.call-update) | async-done | bytes 294928 | tf_op jit(solution)/shard_map/reduce_scatter | solution.py:290
  1428.2 248.9 %reduce-scatter.10.cloned.1.call-done = f32[32,6144]{1,0:T(8,128)} async-done(((f32[1024,6144]{1,0:T(8,128)}), f32[32,6144]{1,0:T(8,128)}) %reduce-scatter.10.cloned.1.call-update) | async-done | bytes 786448 | tf_op jit(solution)/shard_map/reduce_scatter | solution.py:286
  1677.0 249.6 %reduce-scatter.20.cloned.1.call-done = f32[128,1536]{1,0:T(8,128)} async-done(((f32[4096,1536]{1,0:T(8,128)}), f32[128,1536]{1,0:T(8,128)}) %reduce-scatter.20.cloned.1.call-update) | async-done | bytes 786448 | tf_op jit(solution)/shard_map/reduce_scatter | solution.py:240
  1926.6 267.4 %reduce-scatter.12.cloned.1.call-done = f32[3,48,1536]{2,1,0:T(8,128)} async-done(((f32[3,1536,1536]{2,1,0:T(8,128)}), f32[3,48,1536]{2,1,0:T(8,128)}) %reduce-scatter.12.cloned.1.call-update) | async-done | bytes 884752 | tf_op jit(solution)/shard_map/reduce_scatter | solution.py:289
  2194.1 435.6 %reduce-scatter.18.cloned.1.call-done = f32[2,48,4096]{2,1,0:T(8,128)} async-done(((f32[2,1536,4096]{2,1,0:T(8,128)}), f32[2,48,4096]{2,1,0:T(8,128)}) %reduce-scatter.18.cloned.1.call-update) | async-done | bytes 1572880 | tf_op jit(solution)/shard_map/reduce_scatter | solution.py:239
  (732 shorter events, 272.1 us)
Async XLA Ops:
  7.2 285.3 %copy-start = (bf16[1,256,4096]{2,1,0:T(8,128)(2,1)S(1)}, bf16[1,256,4096]{2,1,0:T(8,128)(2,1)}, u32[]{:S(2)}) copy-start(bf16[1,256,4096]{2,1,0:T(8,128)(2,1)} %param.25) | copy-start | bytes 6291460
  7.2 77.5 %all-gather.9.cloned.1.call-start = ((), (), s32[]{:S(2)}) async-start(), calls=%async_computation.7 | async-start | bytes 14155776 | tf_op jit(solution)/shard_map/all_gather | solution.py:161
  7.9 157.4 %all-gather.11.cloned.1.call-start = ((), (), s32[]{:S(2)}) async-start(), calls=%async_computation.8 | async-start | bytes 15925248 | tf_op jit(solution)/shard_map/all_gather | solution.py:164
  8.7 14.1 copy-start.47
  8.7 23.8 copy-start.17
  8.7 23.9 copy-start.51
  8.7 24.0 copy-start.52
  8.7 76.0 %copy-start.45 = (bf16[1,4,1024]{2,1,0:T(4,128)(2,1)S(1)}, bf16[1,4,1024]{2,1,0:T(4,128)(2,1)}, u32[]{:S(2)}) copy-start(bf16[1,4,1024]{2,1,0:T(4,128)(2,1)} %param.24) | copy-start | bytes 24580
  8.7 283.8 %all-gather.13.cloned.1.call-start = ((), (), s32[]{:S(2)}) async-start(), calls=%async_computation.9 | async-start | bytes 28311552 | tf_op jit(solution)/shard_map/all_gather | solution.py:166
  9.5 349.6 %all-gather.15.cloned.1.call-start = ((), (), s32[]{:S(2)}) async-start(), calls=%async_computation.10 | async-start | bytes 5308416 | tf_op jit(solution)/shard_map/all_gather | solution.py:165
  10.1 450.0 %all-gather.17.cloned.1.call-start = ((), (), s32[]{:S(2)}) async-start(), calls=%async_computation.11 | async-start | bytes 28311552 | tf_op jit(solution)/shard_map/all_gather | solution.py:207
  10.6 523.2 %all-gather.19.cloned.1.call-start = ((), (), s32[]{:S(2)}) async-start(), calls=%async_computation.12 | async-start | bytes 14155776 | tf_op jit(solution)/shard_map/all_gather | solution.py:208
  11.2 966.6 %reduce-scatter.22.cloned.1.call-start = ((), (), s32[]{:S(2)}) async-start(), calls=%async_computation.19 | async-start | bytes 811008
  32.5 710.3 %copy-start.43 = (f32[1536]{0:T(1024)}, f32[1536]{0:T(1024)S(1)}, u32[]{:S(2)}) copy-start(f32[1536]{0:T(1024)S(1)} %get-tuple-element.355) | copy-start | bytes 18436
  32.7 710.1 %copy-start.48 = (f32[128]{0:T(128)}, f32[128]{0:T(128)S(1)}, u32[]{:S(2)}) copy-start(f32[128]{0:T(128)S(1)} %add_rsqrt_fusion.4) | copy-start | bytes 1540
  84.7 6.3 copy-start.42
  94.4 81.7 %copy-start.8 = (bf16[128,1536]{1,0:T(8,128)(2,1)}, bf16[128,1536]{1,0:T(8,128)(2,1)S(1)}, u32[]{:S(2)}) copy-start(bf16[128,1536]{1,0:T(8,128)(2,1)S(1)} %fusion.61) | copy-start | bytes 1179652
  220.2 81.2 %copy-start.27 = (bf16[12,128,128]{1,2,0:T(8,128)(2,1)}, bf16[12,128,128]{1,2,0:T(8,128)(2,1)S(1)}, u32[]{:S(2)}) copy-start(bf16[12,128,128]{1,2,0:T(8,128)(2,1)S(1)} %get-tuple-element.907) | copy-start | bytes 1179652
  315.7 43.4 %copy-start.18 = (bf16[1,128,1536]{2,1,0:T(8,128)(2,1)S(1)}, bf16[1,128,1536]{2,1,0:T(8,128)(2,1)}, u32[]{:S(2)}) copy-start(bf16[1,128,1536]{2,1,0:T(8,128)(2,1)} %param.23) | copy-start | bytes 1179652
  359.1 5.4 copy-start.3
  359.1 5.4 copy-start.33
  460.1 7.9 copy-start.22
  544.0 10.9 copy-start.36
  544.0 10.9 copy-start.38
  544.0 33.5 %copy-start.20 = (bf16[128,4096]{1,0:T(8,128)(2,1)}, bf16[128,4096]{1,0:T(8,128)(2,1)S(1)}, u32[]{:S(2)}) copy-start(bf16[128,4096]{1,0:T(8,128)(2,1)S(1)} %get-tuple-element.454) | copy-start | bytes 3145732
  544.0 10.9 copy-start.4
  544.1 10.9 copy-start.16
  554.9 22.6 copy-start.34
  555.0 31.7 %slice-start = ((s8[4718592]{0:T(1024)(128)(4,1)}), s8[4194304]{0:T(1024)(128)(4,1)S(1)}, s32[]{:S(2)}) async-start(s8[4718592]{0:T(1024)(128)(4,1)} %bitcast.369), calls=%async_computation.20 | async-start | bytes 8388608
  577.6 9.1 slice-start.1
  577.6 9.1 copy-start.13
  734.6 8.2 copy-start.30
  738.7 4.1 copy-start.32
  755.5 530.8 %reduce-scatter.16.cloned.1.call-start = ((), (), s32[]{:S(2)}) async-start(), calls=%async_computation.16 | async-start | bytes 51904512 | tf_op jit(solution)/shard_map/reduce_scatter | solution.py:291
  755.6 11.5 copy-start.6
  755.6 11.5 copy-start.7
  812.2 615.9 %reduce-scatter.14.cloned.1.call-start = ((), (), s32[]{:S(2)}) async-start(), calls=%async_computation.15 | async-start | bytes 9732096 | tf_op jit(solution)/shard_map/reduce_scatter | solution.py:290
  818.3 858.7 %reduce-scatter.10.cloned.1.call-start = ((), (), s32[]{:S(2)}) async-start(), calls=%async_computation.13 | async-start | bytes 25952256 | tf_op jit(solution)/shard_map/reduce_scatter | solution.py:286
  832.5 1094.1 %reduce-scatter.20.cloned.1.call-start = ((), (), s32[]{:S(2)}) async-start(), calls=%async_computation.18 | async-start | bytes 25952256 | tf_op jit(solution)/shard_map/reduce_scatter | solution.py:240
  843.9 1350.1 %reduce-scatter.12.cloned.1.call-start = ((), (), s32[]{:S(2)}) async-start(), calls=%async_computation.14 | async-start | bytes 29196288 | tf_op jit(solution)/shard_map/reduce_scatter | solution.py:289
  858.9 16.6 copy-start.37
  858.9 1770.7 %reduce-scatter.18.cloned.1.call-start = ((), (), s32[]{:S(2)}) async-start(), calls=%async_computation.17 | async-start | bytes 51904512 | tf_op jit(solution)/shard_map/reduce_scatter | solution.py:239
  931.6 43.7 %copy-start.53 = (f32[128]{0:T(128)S(1)}, f32[128]{0:T(128)}, u32[]{:S(2)}) copy-start(f32[128]{0:T(128)} %get-tuple-element.343) | copy-start | bytes 1540
  931.6 43.7 %copy-start.11 = (f32[128,1536]{1,0:T(8,128)S(1)}, f32[128,1536]{1,0:T(8,128)}, u32[]{:S(2)}) copy-start(f32[128,1536]{1,0:T(8,128)} %copy-done.10) | copy-start | bytes 2359300
  931.6 43.7 %copy-start.19 = (bf16[1,128,1536]{2,1,0:T(8,128)(2,1)S(1)}, bf16[1,128,1536]{2,1,0:T(8,128)(2,1)}, u32[]{:S(2)}) copy-start(bf16[1,128,1536]{2,1,0:T(8,128)(2,1)} %param.23) | copy-start | bytes 1179652
  931.6 43.7 %copy-start.44 = (f32[1536]{0:T(1024)S(1)}, f32[1536]{0:T(1024)}, u32[]{:S(2)}) copy-start(f32[1536]{0:T(1024)} %copy-done.43) | copy-start | bytes 18436
  931.6 43.7 %copy-start.49 = (f32[128]{0:T(128)S(1)}, f32[128]{0:T(128)}, u32[]{:S(2)}) copy-start(f32[128]{0:T(128)} %copy-done.48) | copy-start | bytes 1540
  931.6 1698.0 %copy-start.1 = (bf16[1,256,4096]{2,1,0:T(8,128)(2,1)S(1)}, bf16[1,256,4096]{2,1,0:T(8,128)(2,1)}, u32[]{:S(2)}) copy-start(bf16[1,256,4096]{2,1,0:T(8,128)(2,1)} %param.25) | copy-start | bytes 6291460
  (21 other events, 36.1 us)
Sparse Core Ops, SparseCore 0:
  9.9 74.7 all-gather.8
  86.6 78.6 all-gather.10
  167.2 125.2 all-gather.12
  294.2 38.7 all-gather.14
  334.8 125.2 all-gather.16
  461.8 71.9 all-gather.18
  755.6 96.2 reduce-scatter.21
  858.4 427.9 reduce-scatter.15
  1292.8 135.3 reduce-scatter.13
  1435.0 241.9 reduce-scatter.9
  1684.0 242.5 reduce-scatter.19
  1933.5 260.5 reduce-scatter.11
  2201.1 428.5 reduce-scatter.17
where the time goes:
time: 2650 us; the launch traced here: 2640 us
  waiting for transfers between devices  1990 us (75%)
  matrix products  244 us (9%)
  local copies, waits for them, and re-layouts  198 us (7%)
  other arithmetic  120 us (5%)
  blocking collectives  63 us (2%)
    reduce_scatter x1, waiting for transfers between devices, per_device(): lax.psum_scatter(g_ffn, ('bucket', 'fsdp'), scatter_dimension=1, tiled=True)  436 us
    reduce_scatter x1, waiting for transfers between devices, per_device(): lax.psum_scatter(g_text, ('bucket', 'fsdp'), scatter_dimension=1, tiled=T...  307 us
    reduce_scatter x1, waiting for transfers between devices, per_device(): lax.psum_scatter(g_attn, ('bucket', 'fsdp'), scatter_dimension=1, tiled=T...  267 us
    reduce_scatter x1, waiting for transfers between devices, per_device(): lax.psum_scatter(g_down, ('bucket', 'fsdp'), scatter_dimension=0, tiled=T...  250 us
    reduce_scatter x1, waiting for transfers between devices, per_device(): lax.psum_scatter(g_ada_w, ('bucket', 'fsdp'), scatter_dimension=0, tiled=...  249 us
    dot_general x27, matrix products, mult(): return jnp.dot(left, right, preferred_element_type=jnp.float32)  205 us
    reduce_scatter x1, waiting for transfers between devices, per_device(): lax.psum_scatter(g_out, ('bucket', 'fsdp'), scatter_dimension=0, tiled=True)  139 us
    dynamic_slice x120, local copies, waits for them, and re-layouts, attend_forward(): lax.map(one_pair, (to_pairs(q_b), to_pairs(k_b), to_pairs(v_b)))  95 us
  transfers between devices with their start and end apart: 13, of which 11 were waited for; matrix products, arithmetic and copies ran while one was open for 13% of the time, Pallas kernels for 0%

commit v1 on v0

--- a/solution.py
+++ b/solution.py
@@ -1,6 +1,8 @@
 import jax
 import jax.numpy as jnp
 from jax import lax
+from jax.experimental import pallas as pl
+from jax.experimental.pallas import tpu as pltpu
 from jax.sharding import PartitionSpec as P
 
 D = 1536
@@ -140,7 +142,7 @@
     return jnp.dot(left, right, preferred_element_type=jnp.float32)
 
 
-def per_device(
+def per_device_general(
     tokens,
     cond,
     text,
@@ -304,6 +306,602 @@
     )
 
 
+ROW = 128
+CHIPS = 4
+HW = D // CHIPS
+PAIRS = HW // 128
+
+
+def swap(v, mask):
+    return lax.ppermute(v, "fsdp", [(i, i ^ mask) for i in range(8)])
+
+
+def at_x(v):
+    return swap(v, 2)
+
+
+def at_y(v):
+    return swap(v, 4)
+
+
+def at_core(v):
+    return swap(v, 1)
+
+
+def reorder(parts, index):
+    bit = 1
+    while bit < len(parts):
+        odd = (index // bit) % 2 == 1
+        parts = [jnp.where(odd, parts[j ^ bit], parts[j]) for j in range(len(parts))]
+        bit *= 2
+    return parts
+
+
+def gather4(v):
+    half = v.shape[0] // 2
+    by_x = at_x(v)
+    by_y = at_y(v)
+    far = jnp.concatenate([at_y(by_x[:half]), at_x(by_y[half:])], axis=0)
+    return [v, by_x, by_y, far]
+
+
+def reduce4(parts):
+    half = parts[0].shape[0] // 2
+    low = jnp.bfloat16
+    far_x = at_x(parts[3][:half].astype(low))
+    far_y = at_y(parts[3][half:].astype(low))
+    from_xa = at_x(parts[1][:half].astype(low))
+    from_yb = at_y(parts[2][half:].astype(low))
+    from_ya = at_y((parts[2][:half] + far_x.astype(jnp.float32)).astype(low))
+    from_xb = at_x((parts[1][half:] + far_y.astype(jnp.float32)).astype(low))
+    top = parts[0][:half] + from_xa.astype(jnp.float32) + from_ya.astype(jnp.float32)
+    bottom = parts[0][half:] + from_yb.astype(jnp.float32) + from_xb.astype(jnp.float32)
+    return jnp.concatenate([top, bottom], axis=0)
+
+
+def exchange4(pick):
+    return [pick(0), at_x(pick(1)), at_y(pick(2)), swap(pick(3), 6)]
+
+
+def sum4(v):
+    v = v + at_x(v)
+    return v + at_y(v)
+
+
+def sum4_rows(v):
+    rows = v.reshape(CHIPS, -1)
+    rows = rows + jnp.stack([at_x(rows)[j ^ 1] for j in range(CHIPS)])
+    rows = rows + jnp.stack([at_y(rows)[j ^ 2] for j in range(CHIPS)])
+    return rows.reshape(-1)
+
+
+def both_cores(mine, core, axis):
+    other = at_core(mine)
+    first = jnp.where(core == 0, mine, other)
+    second = jnp.where(core == 0, other, mine)
+    return first, second
+
+
+def column_weights(shard, chip, core, width):
+    count, rows, _ = shard.shape
+    got = exchange4(
+        lambda j: lax.dynamic_slice_in_dim(shard, jnp.bitwise_xor(chip, j) * width, width, axis=2)
+    )
+    mine = jnp.stack(reorder(got, chip), axis=1)
+    first, second = both_cores(mine, core, 0)
+    return jnp.stack([first, second], axis=2).reshape(count, 8 * rows, width)
+
+
+def row_weights(shard, core):
+    first, second = both_cores(shard, core, 0)
+    return jnp.concatenate([first, second], axis=0)
+
+
+def core_half(view, core, axis):
+    low = jnp.bfloat16
+    keep = lax.dynamic_index_in_dim(view, core, axis, keepdims=False)
+    give = lax.dynamic_index_in_dim(view, 1 - core, axis, keepdims=False)
+    return keep + at_core(give.astype(low)).astype(jnp.float32)
+
+
+def reduce_buckets(view, plane):
+    low = jnp.bfloat16
+    size = view.shape[0]
+    up = down = None
+    for step in range(1, size):
+        piece = lax.dynamic_index_in_dim(
+            view, jnp.minimum(plane + size - step, size - 1), 0, keepdims=False
+        )
+        if up is not None:
+            piece = piece + up.astype(jnp.float32)
+        up = lax.ppermute(piece.astype(low), "bucket", [(i, i + 1) for i in range(step)])
+        piece = lax.dynamic_index_in_dim(
+            view, jnp.maximum(plane - size + step, 0), 0, keepdims=False
+        )
+        if down is not None:
+            piece = piece + down.astype(jnp.float32)
+        down = lax.ppermute(
+            piece.astype(low), "bucket", [(size - 1 - i, size - 2 - i) for i in range(step)]
+        )
+    own = lax.dynamic_index_in_dim(view, plane, 0, keepdims=False)
+    return own + up.astype(jnp.float32) + down.astype(jnp.float32)
+
+
+def to_column_owner(block, chip):
+    got = exchange4(
+        lambda j: lax.dynamic_index_in_dim(
+            block, jnp.bitwise_xor(chip, j), 0, keepdims=False
+        ).astype(jnp.bfloat16)
+    )
+    return jnp.concatenate(reorder(got, chip), axis=-1).astype(jnp.float32)
+
+
+def to_row_owner(block):
+    pairs = [
+        (a * 8 + b * 2 + k, b * 8 + a * 2 + k) for a in range(4) for b in range(4) for k in range(2)
+    ]
+    return lax.ppermute(block.astype(jnp.bfloat16), ("bucket", "fsdp"), pairs).astype(jnp.float32)
+
+
+def column_grad(partial, chip, core, plane):
+    count, rows, width = partial.shape
+    view = partial.reshape(count, 4, 4, 2, rows // 32, width)
+    half = core_half(view, core, 3)
+    mine = reduce_buckets(jnp.transpose(half, (1, 0, 2, 3, 4)), plane)
+    return to_column_owner(jnp.transpose(mine, (1, 0, 2, 3)), chip)
+
+
+def row_grad(partial, core, plane):
+    rows, width = partial.shape
+    half = core_half(partial.reshape(4, 2, rows // 8, width), core, 1)
+    return to_row_owner(reduce_buckets(half, plane))
+
+
+def partner(u):
+    lane = lax.broadcasted_iota(jnp.int32, u.shape, 1)
+    ahead = pltpu.roll(u, u.shape[1] - 16, 1)
+    behind = pltpu.roll(u, 16, 1)
+    return jnp.where((lane // 16) % 2 == 0, ahead, behind)
+
+
+def dot_t(a, b):
+    return lax.dot_general(a, b, (((1,), (1,)), ((), ())), preferred_element_type=jnp.float32)
+
+
+def dot_n(a, b):
+    return lax.dot_general(a, b, (((1,), (0,)), ((), ())), preferred_element_type=jnp.float32)
+
+
+def t_dot(a, b):
+    return lax.dot_general(a, b, (((0,), (0,)), ((), ())), preferred_element_type=jnp.float32)
+
+
+def softmax_of(scores, allowed):
+    scores = jnp.where(allowed, scores * HDIM ** (-0.5), NEGATIVE)
+    top = jnp.max(scores, axis=-1, keepdims=True)
+    expo = jnp.exp(scores - top)
+    return expo / jnp.sum(expo, axis=-1, keepdims=True)
+
+
+def head_mask(v, head):
+    lane = lax.broadcasted_iota(jnp.int32, v.shape, 1)
+    return jnp.where((lane // HDIM) == head, v, jnp.zeros_like(v))
+
+
+def masks_of(seg_col, seg_row, captions):
+    same = seg_col == seg_row
+    owner = lax.broadcasted_iota(jnp.int32, (seg_col.shape[0], captions), 1) // TXT
+    return same, seg_col == owner
+
+
+def attend_kernel(
+    q_ref, k_ref, v_ref, iq_ref, ik_ref, cos_ref, sin_ref, tk_ref, it_ref, tv_ref, sc_ref, sr_ref,
+    g_ref, comb_ref, cross_ref, qr_ref, kr_ref, tr_ref,
+):
+    same, mine = masks_of(sc_ref[...], sr_ref[0], tk_ref.shape[0])
+    cosine = cos_ref[...]
+    sine = sin_ref[...]
+    low = jnp.bfloat16
+    for pair in range(PAIRS):
+        at = pl.ds(pair * 128, 128)
+        qn = q_ref[:, at] * iq_ref[...] * g_ref[2:3, at]
+        kn = k_ref[:, at] * ik_ref[...] * g_ref[3:4, at]
+        qr = (qn * cosine + partner(qn) * sine).astype(low)
+        kr = (kn * cosine + partner(kn) * sine).astype(low)
+        tr = (tk_ref[:, at] * it_ref[...] * g_ref[4:5, at]).astype(low)
+        qr_ref[:, at] = qr
+        kr_ref[:, at] = kr
+        tr_ref[:, at] = tr
+        vv = v_ref[:, at]
+        tv = tv_ref[:, at]
+        self_out = jnp.zeros(qn.shape, jnp.float32)
+        cross_out = jnp.zeros(qn.shape, jnp.float32)
+        for head in range(2):
+            qh = head_mask(qr, head)
+            probs = softmax_of(dot_t(qh, kr), same).astype(low)
+            self_out = self_out + head_mask(dot_n(probs, vv), head)
+            probs = softmax_of(dot_t(qh, tr), mine).astype(low)
+            cross_out = cross_out + head_mask(dot_n(probs, tv), head)
+        cross_ref[:, at] = cross_out
+        comb_ref[:, at] = (self_out + jnp.tanh(g_ref[5:6, at]) * cross_out).astype(low)
+
+
+def attend_back_kernel(
+    qr_ref, kr_ref, v_ref, tr_ref, tv_ref, dc_ref, cross_ref, q_ref, k_ref, tk_ref, iq_ref, ik_ref,
+    it_ref, cos_ref, sin_ref, sc_ref, sr_ref, g_ref,
+    dq_ref, dk_ref, dv_ref, dt_ref, dtv_ref, sq_ref, sk_ref, st_ref, gg_ref,
+):
+    same, mine = masks_of(sc_ref[...], sr_ref[0], tk_ref.shape[0])
+    cosine = cos_ref[...]
+    sine = sin_ref[...]
+    low = jnp.bfloat16
+    factor = HDIM ** (-0.5)
+    gg_ref[...] = jnp.zeros(gg_ref.shape, jnp.float32)
+    sum_q = sum_k = sum_t = 0.0
+    for pair in range(PAIRS):
+        at = pl.ds(pair * 128, 128)
+        qr = qr_ref[:, at]
+        kr = kr_ref[:, at]
+        vv = v_ref[:, at]
+        tr = tr_ref[:, at]
+        tv = tv_ref[:, at]
+        dcomb = dc_ref[:, at]
+        d_self = dcomb.astype(low)
+        d_cross = (dcomb * jnp.tanh(g_ref[5:6, at])).astype(low)
+        dq = jnp.zeros(dcomb.shape, jnp.float32)
+        dk = jnp.zeros(dcomb.shape, jnp.float32)
+        dv = jnp.zeros(dcomb.shape, jnp.float32)
+        dt = jnp.zeros((tr.shape[0], 128), jnp.float32)
+        dtv = jnp.zeros((tr.shape[0], 128), jnp.float32)
+        for head in range(2):
+            qh = head_mask(qr, head)
+            probs = softmax_of(dot_t(qh, kr), same)
+            grad = head_mask(d_self, head)
+            dprob = dot_t(grad, vv)
+            dscore = probs * (dprob - jnp.sum(probs * dprob, axis=-1, keepdims=True))
+            dscore = dscore.astype(low)
+            dq = dq + dot_n(dscore, head_mask(kr, head))
+            dk = dk + t_dot(dscore, qh)
+            dv = dv + t_dot(probs.astype(low), grad)
+            probs = softmax_of(dot_t(qh, tr), mine)
+            grad = head_mask(d_cross, head)
+            dprob = dot_t(grad, tv)
+            dscore = probs * (dprob - jnp.sum(probs * dprob, axis=-1, keepdims=True))
+            dscore = dscore.astype(low)
+            dq = dq + dot_n(dscore, head_mask(tr, head))
+            dt = dt + t_dot(dscore, qh)
+            dtv = dtv + t_dot(probs.astype(low), grad)
+        dq = dq * factor
+        dk = dk * factor
+        dt = dt * factor
+        dq = dq * cosine - partner(dq) * sine
+        dk = dk * cosine - partner(dk) * sine
+        q_norm = q_ref[:, at] * iq_ref[...]
+        k_norm = k_ref[:, at] * ik_ref[...]
+        t_norm = tk_ref[:, at] * it_ref[...]
+        gg_ref[0, 0:1, at] = jnp.sum(dq * q_norm, axis=0, keepdims=True)
+        gg_ref[0, 1:2, at] = jnp.sum(dk * k_norm, axis=0, keepdims=True)
+        gg_ref[0, 2:3, at] = jnp.sum(dt * t_norm, axis=0, keepdims=True)
+        gg_ref[0, 3:4, at] = jnp.sum(dcomb * cross_ref[:, at], axis=0, keepdims=True)
+        dq = dq * g_ref[2:3, at]
+        dk = dk * g_ref[3:4, at]
+        dt = dt * g_ref[4:5, at]
+        sum_q = sum_q + jnp.sum(dq * q_norm, axis=-1, keepdims=True)
+        sum_k = sum_k + jnp.sum(dk * k_norm, axis=-1, keepdims=True)
+        sum_t = sum_t + jnp.sum(dt * t_norm, axis=-1, keepdims=True)
+        dq_ref[:, at] = dq
+        dk_ref[:, at] = dk
+        dv_ref[:, at] = dv.astype(low)
+        dt_ref[:, at] = dt
+        dtv_ref[:, at] = dtv.astype(low)
+    sq_ref[...] = sum_q
+    sk_ref[...] = sum_k
+    st_ref[...] = sum_t
+
+
+def row_spec(rows, width):
+    return pl.BlockSpec((rows, width), lambda i: (i, 0))
+
+
+def attend_all(q, k, v, iq, ik, cosine, sine, tk, it, tv, seg_col, seg_row, gains):
+    cap = IMGS * TXT
+    low = jnp.bfloat16
+    big = row_spec(ROW, HW)
+    text = row_spec(cap, HW)
+    one = row_spec(ROW, 1)
+    table = row_spec(ROW, 128)
+    shape = jax.ShapeDtypeStruct
+    return pl.pallas_call(
+        attend_kernel,
+        grid=(CHIPS,),
+        in_specs=[
+            big, big, big, one, one, table, table, text, row_spec(cap, 1), text, one,
+            pl.BlockSpec((1, 1, ROW), lambda i: (i, 0, 0)),
+            pl.BlockSpec((6, HW), lambda i: (0, 0)),
+        ],
+        out_specs=[big, big, big, big, text],
+        out_shape=[
+            shape((CHIPS * ROW, HW), low),
+            shape((CHIPS * ROW, HW), jnp.float32),
+            shape((CHIPS * ROW, HW), low),
+            shape((CHIPS * ROW, HW), low),
+            shape((CHIPS * cap, HW), low),
+        ],
+        cost_estimate=pl.CostEstimate(
+            flops=4 * 24 * 128 * 384 * 128, bytes_accessed=10_000_000, transcendentals=1_200_000
+        ),
+    )(q, k, v, iq, ik, cosine, sine, tk, it, tv, seg_col, seg_row, gains)
+
+
+def attend_all_back(
+    qr, kr, v, tr, tv, dcomb, cross, q, k, tk, iq, ik, it, cosine, sine, seg_col, seg_row, gains
+):
+    cap = IMGS * TXT
+    low = jnp.bfloat16
+    big = row_spec(ROW, HW)
+    text = row_spec(cap, HW)
+    one = row_spec(ROW, 1)
+    table = row_spec(ROW, 128)
+    shape = jax.ShapeDtypeStruct
+    return pl.pallas_call(
+        attend_back_kernel,
+        grid=(CHIPS,),
+        in_specs=[
+            big, big, big, text, text, big, big, big, big, text, one, one, row_spec(cap, 1), table,
+            table, one,
+            pl.BlockSpec((1, 1, ROW), lambda i: (i, 0, 0)),
+            pl.BlockSpec((6, HW), lambda i: (0, 0)),
+        ],
+        out_specs=[
+            big, big, big, text, text, one, one, row_spec(cap, 1),
+            pl.BlockSpec((1, 8, HW), lambda i: (i, 0, 0)),
+        ],
+        out_shape=[
+            shape((CHIPS * ROW, HW), jnp.float32),
+            shape((CHIPS * ROW, HW), jnp.float32),
+            shape((CHIPS * ROW, HW), low),
+            shape((CHIPS * cap, HW), jnp.float32),
+            shape((CHIPS * cap, HW), low),
+            shape((CHIPS * ROW, 1), jnp.float32),
+            shape((CHIPS * ROW, 1), jnp.float32),
+            shape((CHIPS * cap, 1), jnp.float32),
+            shape((CHIPS, 8, HW), jnp.float32),
+        ],
+        cost_estimate=pl.CostEstimate(
+            flops=10 * 24 * 128 * 384 * 128, bytes_accessed=20_000_000, transcendentals=1_200_000
+        ),
+    )(qr, kr, v, tr, tv, dcomb, cross, q, k, tk, iq, ik, it, cosine, sine, seg_col, seg_row, gains)
+
+
+def per_device(
+    tokens,
+    cond,
+    text,
+    segments,
+    positions,
+    counts,
+    ada_weight,
+    ada_bias,
+    gains,
+    attn_weight,
+    out_weight,
+    text_weight,
+    ffn_weight,
+    down_weight,
+    cotangent,
+):
+    low = jnp.bfloat16
+    full = jnp.float32
+    plane = lax.axis_index("bucket")
+    slot = lax.axis_index("fsdp")
+    core = slot % 2
+    chip = slot // 2
+    ff = ffn_weight.shape[2] // CHIPS
+
+    cond_act = silu(cond[0].astype(full)).astype(low)
+    packed = []
+    for j in range(8):
+        piece = lax.dynamic_slice_in_dim(cond_act, jnp.bitwise_xor(slot, j) * 128, 128, axis=1)
+        piece = jnp.concatenate([piece.reshape(4, 128), gains.reshape(9, 128)], axis=0)
+        packed.append(piece if j == 0 else swap(piece, j))
+    conds = jnp.concatenate([p[:4] for p in packed], axis=0)
+    gain_f = jnp.stack(reorder([p[4:].reshape(6, 192) for p in packed], slot), axis=1)
+    gain_f = gain_f.reshape(6, D).astype(full)
+    bias = lax.dynamic_update_slice_in_dim(
+        jnp.zeros((ada_weight.shape[1],), full), ada_bias.astype(full), slot * ada_bias.shape[0], 0
+    )
+    mod_parts = (mult(conds, ada_weight) + bias[None, :]).reshape(8, IMGS, -1)
+    mod = mod_parts[0]
+    for j in range(1, 8):
+        mod = mod + swap(mod_parts[j], j)
+
+    seg = segments[0]
+    index = jnp.concatenate([seg[None, :], positions[0]], axis=0)
+    indices = [index, at_x(index), at_y(index), swap(index, 6)]
+    seg_all = jnp.stack([i[0] for i in indices])
+    pos_all = jnp.stack([i[1:] for i in indices])
+    seg_col = seg_all.reshape(CHIPS * ROW, 1)
+    seg_row = seg_all.reshape(CHIPS, 1, ROW)
+    lane = jnp.arange(128, dtype=jnp.int32)
+    quarter = HDIM // 4
+    freq = (10000.0 ** (-jnp.arange(quarter, dtype=full) / quarter))[lane % quarter]
+    where_row = ((lane // 32) % 2 == 0)[None, None, :]
+    pos_lane = jnp.where(where_row, pos_all[:, 0, :, None], pos_all[:, 1, :, None]).astype(full)
+    angle = (pos_lane * freq[None, None, :]).reshape(CHIPS * ROW, 128)
+    cosine = jnp.cos(angle)
+    sine = jnp.where(((lane // quarter) % 2 == 0)[None, :], -1.0, 1.0) * jnp.sin(angle)
+
+    attn_w = column_weights(attn_weight, chip, core, HW)
+    text_w = column_weights(text_weight, chip, core, HW)
+    ffn_w = column_weights(ffn_weight, chip, core, ff)
+    out_w = row_weights(out_weight, core)
+    down_w = row_weights(down_weight, core)
+    gain_s = lax.dynamic_slice_in_dim(gain_f, chip * HW, HW, axis=1)
+
+    def per_token(part):
+        rows = mod[:, part * D : (part + 1) * D]
+        out = rows[IMGS - 1][None, :]
+        for i in range(IMGS - 2, -1, -1):
+            out = jnp.where(seg[:, None] == i, rows[i][None, :], out)
+        return out
+
+    scale1 = per_token(0)
+    gate1 = per_token(1)
+    scale2 = per_token(2)
+    gate2 = per_token(3)
+    tanh_one = jnp.tanh(gate1)
+    tanh_two = jnp.tanh(gate2)
+
+    x = tokens[0].astype(full)
+    normed1, inverse1 = norm_rows(x)
+    h_one = (normed1 * gain_f[0] * (1.0 + scale1)).astype(low)
+    h_all = jnp.concatenate(gather4(h_one), axis=0)
+    query = mult(h_all, attn_w[0])
+    keyed = mult(h_all, attn_w[1])
+    valued = mult(h_all, attn_w[2]).astype(low)
+    squares = jnp.stack(
+        [jnp.sum(query * query, axis=-1), jnp.sum(keyed * keyed, axis=-1)]
+    ).reshape(2, CHIPS, ROW)
+    squares = sum4_rows(jnp.transpose(squares, (1, 0, 2)))
+    squares = jnp.transpose(squares.reshape(CHIPS, 2, ROW), (1, 0, 2)).reshape(2, CHIPS * ROW)
+    inv_qk = lax.rsqrt(squares / D + EPS)[:, :, None]
+
+    text_parts = gather4(text[0])
+    text_all = jnp.concatenate(text_parts, axis=0)
+    text_keys = mult(text_all, text_w[0])
+    text_vals = mult(text_all, text_w[1]).astype(low)
+    inv_t = lax.rsqrt(sum4_rows(jnp.sum(text_keys * text_keys, axis=-1)) / D + EPS)[:, None]
+
+    comb, cross_out, q_rot, k_rot, text_rot = attend_all(
+        query, keyed, valued, inv_qk[0], inv_qk[1], cosine, sine, text_keys, inv_t, text_vals,
+        seg_col, seg_row, gain_s,
+    )
+    branch = reduce4(list(mult(comb, out_w).reshape(CHIPS, ROW, D)))
+    x_one = x + tanh_one * branch
+    normed2, inverse2 = norm_rows(x_one)
+    h_two = (normed2 * gain_f[1] * (1.0 + scale2)).astype(low)
+    h_two_all = jnp.concatenate(gather4(h_two), axis=0)
+
+    totals = counts.astype(full)
+    here = jnp.sum(jnp.where(jnp.arange(totals.shape[0], dtype=jnp.int32) == plane, totals, 0.0))
+    weight = lax.axis_size("bucket") * here / jnp.sum(totals)
+    grad = cotangent[0].astype(full) * weight
+    d_ffn = (grad * tanh_two).astype(low)
+    d_ffn_all = jnp.concatenate(gather4(d_ffn), axis=0)
+
+    gate_pre = mult(h_two_all, ffn_w[0])
+    upper = mult(h_two_all, ffn_w[1])
+    d_hidden = dot_t(d_ffn_all, down_w)
+    sigm = jax.nn.sigmoid(gate_pre)
+    silu_pre = gate_pre * sigm
+    hidden = (silu_pre * upper).astype(low)
+    d_pre = (d_hidden * upper * sigm * (1.0 + gate_pre * (1.0 - sigm))).astype(low)
+    d_up = (d_hidden * silu_pre).astype(low)
+    d_h_two = reduce4(
+        list((dot_t(d_pre, ffn_w[0]) + dot_t(d_up, ffn_w[1])).reshape(CHIPS, ROW, D))
+    )
+    ffn_out = reduce4(list(mult(hidden, down_w).reshape(CHIPS, ROW, D)))
+    block_out = (x_one + tanh_two * ffn_out).astype(low)
+    d_gate2 = grad * ffn_out * (1.0 - tanh_two * tanh_two)
+
+    g_gain_one = jnp.sum(d_h_two * normed2 * (1.0 + scale2), axis=0)
+    d_scale2 = d_h_two * normed2 * gain_f[1]
+    d_x_one = grad + norm_back(d_h_two * gain_f[1] * (1.0 + scale2), normed2, inverse2)
+    d_gate1 = d_x_one * branch * (1.0 - tanh_one * tanh_one)
+    d_branch = (d_x_one * tanh_one).astype(low)
+    d_branch_all = jnp.concatenate(gather4(d_branch), axis=0)
+
+    s_down = row_grad(t_dot(hidden, d_ffn_all), core, plane)
+    s_ffn = column_grad(
+        jnp.stack([t_dot(h_two_all, d_pre), t_dot(h_two_all, d_up)]), chip, core, plane
+    )
+
+    d_comb = dot_t(d_branch_all, out_w)
+    (
+        dq, dk, d_valued, dt, d_text_vals, sum_q, sum_k, sum_t, gg,
+    ) = attend_all_back(
+        q_rot, k_rot, valued, text_rot, text_vals, d_comb, cross_out, query, keyed, text_keys,
+        inv_qk[0], inv_qk[1], inv_t, cosine, sine, seg_col, seg_row, gain_s,
+    )
+    sums = jnp.concatenate([s.reshape(CHIPS, -1) for s in (sum_q, sum_k, sum_t)], axis=1)
+    sums = sum4_rows(sums).reshape(CHIPS, -1) / D
+    mean_q = sums[:, :ROW].reshape(-1, 1)
+    mean_k = sums[:, ROW : 2 * ROW].reshape(-1, 1)
+    mean_t = sums[:, 2 * ROW :].reshape(-1, 1)
+    d_query = (inv_qk[0] * (dq - query * inv_qk[0] * mean_q)).astype(low)
+    d_keyed = (inv_qk[1] * (dk - keyed * inv_qk[1] * mean_k)).astype(low)
+    d_text_keys = (inv_t * (dt - text_keys * inv_t * mean_t)).astype(low)
+    d_h_one = reduce4(
+        list(
+            (
+                dot_t(d_query, attn_w[0]) + dot_t(d_keyed, attn_w[1]) + dot_t(d_valued, attn_w[2])
+            ).reshape(CHIPS, ROW, D)
+        )
+    )
+    s_text = column_grad(
+        jnp.stack([t_dot(text_all, d_text_keys), t_dot(text_all, d_text_vals)]), chip, core, plane
+    )
+    s_attn = column_grad(
+        jnp.stack([t_dot(h_all, d_query), t_dot(h_all, d_keyed), t_dot(h_all, d_valued)]),
+        chip, core, plane,
+    )
+    s_out = row_grad(t_dot(comb, d_branch_all), core, plane)
+
+    g_gain_zero = jnp.sum(d_h_one * normed1 * (1.0 + scale1), axis=0)
+    d_scale1 = d_h_one * normed1 * gain_f[0]
+    token_grad = d_x_one + norm_back(d_h_one * gain_f[0] * (1.0 + scale1), normed1, inverse1)
+    d_token_mod = jnp.concatenate([d_scale1, d_gate1, d_scale2, d_gate2], axis=1)
+    pick = (seg[:, None] == jnp.arange(IMGS, dtype=jnp.int32)[None, :]).astype(full)
+    d_mod = jnp.dot(pick.T, d_token_mod, precision=HIGH)
+
+    gg = jnp.sum(gg, axis=0)[:4]
+    cross_gate = jnp.tanh(gain_s[5])
+    gg = gg.at[3].multiply(1.0 - cross_gate * cross_gate)
+    spread = lax.dynamic_update_slice_in_dim(jnp.zeros((4, D), full), gg, chip * HW, axis=1)
+    small = jnp.concatenate(
+        [g_gain_zero[None], g_gain_one[None], spread, jnp.sum(d_mod, axis=0).reshape(4, D)], axis=0
+    )
+    small = small + at_core(small)
+    small = sum4(small)
+    small = small + lax.ppermute(small, "bucket", [(i, i ^ 1) for i in range(4)])
+    small = small + lax.ppermute(small, "bucket", [(i, i ^ 2) for i in range(4)])
+    rank = plane * 8 + slot
+    s_gains = lax.dynamic_slice_in_dim(small[:6], rank * 48, 48, axis=1)
+    s_ada_b = lax.dynamic_slice_in_dim(small[6:].reshape(-1), rank * 192, 192, axis=0)
+
+    mod_low = d_mod.astype(low)
+    mods = jnp.concatenate(gather4(mod_low), axis=0)
+    planes_m = [mods]
+    for shift in (1, 2, 3):
+        planes_m.append(
+            lax.ppermute(mods, "bucket", [(i, i ^ shift) for i in range(4)])
+        )
+    mods = jnp.concatenate(planes_m, axis=0)
+    mods = jnp.concatenate([mods, at_core(mods)], axis=0)
+    conds_all = jnp.concatenate(gather4(cond_act), axis=0)
+    planes_c = [conds_all]
+    for shift in (1, 2, 3):
+        planes_c.append(
+            lax.ppermute(conds_all, "bucket", [(i, i ^ shift) for i in range(4)])
+        )
+    conds_all = jnp.concatenate(planes_c, axis=0)
+    conds_all = jnp.concatenate([conds_all, at_core(conds_all)], axis=0)
+    s_ada_w = t_dot(lax.dynamic_slice_in_dim(conds_all, rank * 32, 32, axis=1), mods)
+
+    return (
+        block_out[None],
+        token_grad[None],
+        s_ada_w,
+        s_ada_b,
+        s_gains,
+        s_attn,
+        s_out,
+        s_text,
+        s_ffn,
+        s_down,
+    )
+
+
 def solution(mesh):
     in_specs = (
         P(("bucket", "fsdp"), None, None),
@@ -334,6 +932,7 @@
         P(None, ("bucket", "fsdp"), None),
         P(("bucket", "fsdp"), None),
     )
+    fast = mesh.shape["fsdp"] == 8 and mesh.shape["bucket"] == 4
     return jax.shard_map(
-        per_device, mesh=mesh, in_specs=in_specs, out_specs=out_specs, check_vma=False
-    )
+        per_device if fast else per_device_general, mesh=mesh, in_specs=in_specs, out_specs=out_specs, check_vma=False
+    )

time: 2650 us -> 838 us (0.32)
  waiting for transfers between devices: 1990 us -> 303 us
  starting transfers between devices: 0.98 us -> 207 us
  matrix products: 244 us -> 77.8 us
  local copies, waits for them, and re-layouts: 198 us -> 77.5 us
  blocking collectives: 63 us -> 0 us
  Pallas kernels: 0 us -> 36.5 us
    reduce_scatter x6 -> x0, waiting for transfers between devices: 1650 us -> none  [the longest x1 436 us: per_device(): lax.psum_scatter(g_ffn, ('bucket', 'fsdp'), scatter_dimension=1, tiled=True)]
    all_gather x6 -> x0, waiting for transfers between devices: 341 us -> none  [the longest x1 94.4 us: per_device(): lax.all_gather(ffn_weight, 'fsdp', axis=1, tiled=True)]
    ppermute x0 -> x148, waiting for transfers between devices: none -> 303 us  [the longest x108 209 us: swap(): return lax.ppermute(v, 'fsdp', [(i, i ^ mask) for i in range(8)])]
    ppermute x0 -> x148, starting transfers between devices: none -> 207 us  [the longest x108 114 us: swap(): return lax.ppermute(v, 'fsdp', [(i, i ^ mask) for i in range(8)])]
    dot_general x27 -> x10, matrix products: 205 us -> 29.6 us  [mult(): return jnp.dot(left, right, preferred_element_type=jnp.float32)]
    dynamic_slice x120 -> x7, local copies, waits for them, and re-layouts: 95 us -> 9.23 us  [the longest x3 7.31 us: column_weights(): lax.dynamic_slice_in_dim(shard, jnp.bitwise_xor(chip, j) * width, width,...]
    another operation x10 -> x16, other arithmetic: 90.3 us -> 19.1 us  [the longest x6 9.82 us: column_weights(): mine = jnp.stack(reorder(got, chip), axis=1)]
    dynamic_update_slice x84 -> x1, local copies, waits for them, and re-layouts: 54.1 us -> 0.01 us  [per_device(): lax.dynamic_update_slice_in_dim(jnp.zeros((4, D), full), gg, chip * HW, a...]
  transfers between devices with their start and end apart: 13 -> 148, of which waited for: 11 -> 46; matrix products, arithmetic and copies ran while one was open for 13% -> 30% of each run, Pallas kernels for 0% -> 4%
where the time goes in v1:
time: 838 us; the launch traced here: 826 us
  waiting for transfers between devices  303 us (36%)
  starting transfers between devices  207 us (25%)
  other arithmetic  120 us (14%)
  matrix products  77.8 us (9%)
  local copies, waits for them, and re-layouts  77.5 us (9%)
  Pallas kernels  36.5 us (4%)
    ppermute x108, waiting for transfers between devices, swap(): return lax.ppermute(v, 'fsdp', [(i, i ^ mask) for i in range(8)])  209 us
    ppermute x108, starting transfers between devices, swap(): return lax.ppermute(v, 'fsdp', [(i, i ^ mask) for i in range(8)])  114 us
    ppermute x15, starting transfers between devices, reduce_buckets(): lax.ppermute(piece.astype(low), 'bucket', [(i, i + 1) for i in range(step)])  61.2 us
    ppermute x15, waiting for transfers between devices, reduce_buckets(): lax.ppermute(piece.astype(low), 'bucket', [(i, i + 1) for i in range(step)])  31.9 us
    dot_general x10, matrix products, t_dot(): lax.dot_general(a, b, (((0,), (0,)), ((), ())), preferred_element_type=jn...  30 us
    dot_general x10, matrix products, mult(): return jnp.dot(left, right, preferred_element_type=jnp.float32)  29.6 us
    ppermute x15, waiting for transfers between devices, reduce_buckets(): lax.ppermute(piece.astype(low), 'bucket', [(size - 1 - i, size - 2 - i) f...  29.4 us
    unnamed x303, local copies, waits for them, and re-layouts  22.3 us
  transfers between devices with their start and end apart: 148, of which 46 were waited for; matrix products, arithmetic and copies ran while one was open for 30% of the time, Pallas kernels for 4%

profile of v1, /device:TPU:0, one launch (start us, length us, event | category | flops | bytes accessed | tf_op | source)
XLA Modules:
  0.0 826.2 jit_solution(16867684784856083283)
XLA Ops:
  1.5 3.9 collective-permute-start.26
  22.9 9.9 %bitcast_select_fusion.8 = (f32[128]{0:T(128)S(1)}, f32[128]{0:T(128)S(1)}) fusion(f32[]{:T(128)} %bitcast.63, f32[]{:T(128)} %bitcast.64, f32[]{:T(128)} %bitcast.65, f32[]{:T(128)} %bitcast.66, f32[]{:T(128)} %bitcast.67, f32[]{:T(128)} %bitcast.69, f32[]{:T(128)} %bitcast.68, f32[]{:T(128)} %bitcast.46, f32[]{:T(128)} %bitcast.48, f32[]{:T(128)} %bitcast.50, ...), kind=kLoop, calls=%fused_computation.485 | loop fusion | flops 7680 | bytes 1088 | tf_op jit(solution)/shard_map/gather | solution.py:727
  51.0 4.4 collective-permute-done.83
  65.8 8.0 collective-permute-done.18
  73.9 9.5 %collective-permute-done.19 = bf16[3,192,384]{2,1,0:T(8,128)(2,1)S(1)} collective-permute-done((bf16[3,192,384]{2,1,0:T(8,128)(2,1)}, bf16[3,192,384]{2,1,0:T(8,128)(2,1)S(1)}, u32[]{:S(2)}, u32[]{:S(2)}) %collective-permute-start.19) | collective-permute-done | bytes 442400 | tf_op jit(solution)/shard_map/ppermute | solution.py:316
  87.3 20.4 %collective-permute-done.14 = bf16[128,1536]{1,0:T(8,128)(2,1)S(1)} collective-permute-done((bf16[128,1536]{1,0:T(8,128)(2,1)S(1)}, bf16[128,1536]{1,0:T(8,128)(2,1)S(1)}, u32[]{:S(2)}, u32[]{:S(2)}) %collective-permute-start.14) | collective-permute-done | bytes 393248 | tf_op jit(solution)/shard_map/ppermute | solution.py:316
  108.5 16.5 %collective-permute-done.15 = bf16[128,1536]{1,0:T(8,128)(2,1)S(1)} collective-permute-done((bf16[128,1536]{1,0:T(8,128)(2,1)S(1)}, bf16[128,1536]{1,0:T(8,128)(2,1)S(1)}, u32[]{:S(2)}, u32[]{:S(2)}) %collective-permute-start.15) | collective-permute-done | bytes 393248 | tf_op jit(solution)/shard_map/ppermute | solution.py:316
  126.9 4.8 collective-permute-done.16
  138.4 58.4 %collective-permute-done.48 = bf16[2,192,1024]{2,1,0:T(8,128)(2,1)S(1)} collective-permute-done((bf16[2,192,1024]{2,1,0:T(8,128)(2,1)S(1)}, bf16[2,192,1024]{2,1,0:T(8,128)(2,1)S(1)}, u32[]{:S(2)}, u32[]{:S(2)}) %collective-permute-start.48) | collective-permute-done | bytes 786464 | tf_op jit(solution)/shard_map/ppermute | solution.py:316
  201.4 11.3 %collective-permute-done.49 = bf16[2,192,1024]{2,1,0:T(8,128)(2,1)S(1)} collective-permute-done((bf16[2,192,1024]{2,1,0:T(8,128)(2,1)S(1)}, bf16[2,192,1024]{2,1,0:T(8,128)(2,1)S(1)}, u32[]{:S(2)}, u32[]{:S(2)}) %collective-permute-start.49) | collective-permute-done | bytes 786464 | tf_op jit(solution)/shard_map/ppermute | solution.py:316
  231.0 14.8 %collective-permute-done.22 = f32[4,256]{1,0:T(4,128)S(1)} collective-permute-done((f32[4,256]{1,0:T(4,128)S(1)}, f32[4,256]{1,0:T(4,128)S(1)}, u32[]{:S(2)}, u32[]{:S(2)}) %collective-permute-start.22) | collective-permute-done | bytes 4128 | tf_op jit(solution)/shard_map/ppermute | solution.py:316
  265.8 4.7 multiply_reduce_fusion
  275.2 9.7 %convolution_convert_fusion.tv_ref = bf16[1024,384]{1,0:T(8,128)(2,1)} fusion(bf16[1024,4096]{1,0:T(8,128)(2,1)} %constant_dynamic-update-slice_fusion.13, bf16[4096,384]{1,0:T(8,128)(2,1)} %bitcast.550), kind=kOutput, calls=%fused_computation.97 | convolution fusion | flops 3221618688 | bytes 12320768 | tf_op jit(solution)/shard_map/dot_general | solution.py:142
  291.2 14.4 %shard_map.222 = (bf16[512,384]{1,0:T(8,128)(2,1)}, f32[512,384]{1,0:T(8,128)}, bf16[512,384]{1,0:T(8,128)(2,1)}, bf16[512,384]{1,0:T(8,128)(2,1)}, bf16[1024,384]{1,0:T(8,128)(2,1)}) custom-call(f32[512,384]{1,0:T(8,128)} %copy.97.q_ref, f32[512,384]{1,0:T(8,128)} %copy.98.k_ref, bf16[512,384]{1,0:T(8,128)(2,1)} %convolution_convert_fusion.1.v_ref, ...), custom_call_target="tpu_custom_call" | custom-call | flops 603979776 | bytes 10000000 | tf_op jit(solution)/shard_map/pallas_call | solution.py:614
  305.7 4.0 fusion.181
  322.1 4.6 concatenate.195
  335.6 4.2 collective-permute-done.40
  353.7 7.3 collective-permute-done.44
  363.3 6.1 collective-permute-done.59
  376.5 4.8 multiply_convert_fusion
  393.9 3.6 fusion.183
  408.1 3.8 collective-permute-done.67
  417.6 4.5 collective-permute-done.55
  453.3 22.1 %shard_map.223 = (f32[512,384]{1,0:T(8,128)}, f32[512,384]{1,0:T(8,128)}, bf16[512,384]{1,0:T(8,128)(2,1)}, f32[1024,384]{1,0:T(8,128)}, bf16[1024,384]{1,0:T(8,...) custom-call(bf16[512,384]{1,0:T(8,128)(2,1)} %get-tuple-element.37.qr_ref, ...), custom_call_target="tpu_custom_call" | custom-call | flops 1509949440 | bytes 20000000 | tf_op jit(solution)/shard_map/pallas_call | solution.py:646
  486.3 9.9 %fusion.193 = f32[4096,384]{1,0:T(8,128)} fusion(bf16[1024,4096]{1,0:T(8,128)(2,1)} %constant_dynamic-update-slice_fusion.13, bf16[1024,384]{1,0:T(8,128)(2,1)S(1)} %copy-done.124), kind=kOutput, calls=%fused_computation.564 | convolution fusion | flops 3221225472 | bytes 15466496 | tf_op jit(solution)/shard_map/dot_general | solution.py:476
  511.9 4.8 fusion.55
  530.9 4.7 bitcast_add_fusion
  572.3 11.1 %collective-permute-done.100 = f32[10,1536]{1,0:T(8,128)S(1)} collective-permute-done((f32[10,1536]{1,0:T(8,128)S(1)}, f32[10,1536]{1,0:T(8,128)S(1)}, u32[]{:S(2)}, u32[]{:S(2)}) %collective-permute-start.100) | collective-permute-done | bytes 61472 | tf_op jit(solution)/shard_map/ppermute | solution.py:866
  587.6 5.2 collective-permute-start.94
  593.2 15.3 %collective-permute-done.94 = bf16[16,6144]{1,0:T(8,128)(2,1)S(1)} collective-permute-done((bf16[16,6144]{1,0:T(8,128)(2,1)S(1)}, bf16[16,6144]{1,0:T(8,128)(2,1)S(1)}, u32[]{:S(2)}, u32[]{:S(2)}) %collective-permute-start.94) | collective-permute-done | bytes 196640 | tf_op jit(solution)/shard_map/ppermute | solution.py:877
  608.5 6.7 collective-permute-start.115
  622.2 4.8 collective-permute-start.142
  632.7 5.6 collective-permute-start.103
  638.3 4.1 fusion.4
  645.4 4.5 collective-permute-start.131
  658.9 14.7 %collective-permute-done.104 = bf16[3,4,48,384]{3,2,0,1:T(8,128)(2,1)S(1)} collective-permute-done((bf16[3,4,48,384]{3,2,0,1:T(8,128)(2,1)S(1)}, bf16[3,4,48,384]{3,2,0,1:T(8,128)(2,1)S(1)}, u32[]{:S(2)}, u32[]{:S(2)}) %collective-permute-start.104) | collective-permute-done | bytes 442400 | tf_op jit(solution)/shard_map/ppermute | solution.py:417
  679.0 5.2 collective-permute-start.132
  691.2 4.6 collective-permute-start.121
  700.9 4.1 concatenate.200
  707.8 4.8 collective-permute-start.105
  720.5 6.2 collective-permute-done.143
  727.5 5.0 collective-permute-start.122
  736.8 7.1 collective-permute-start.133
  747.0 6.0 collective-permute-done.122
  754.7 9.2 %collective-permute-start.111 = (bf16[3,48,384]{2,1,0:T(8,128)(2,1)S(1)}, bf16[3,48,384]{2,1,0:T(8,128)(2,1)S(1)}, u32[]{:S(2)}, u32[]{:S(2)}) collective-permute-start(bf16[3,48,384]{2,1,0:T(8,128)(2,1)S(1)} %get-tuple-element.205), channel_id=1, source_target_pairs={{0,2},{1,3},{2,0},{3,1},{4,6},{5,7},{6,4},{7,5},{8,10},{9,11},{10,... | collective-permute-start | bytes 331784 | tf_op jit(solution)/shard_map/ppermute | solution.py:316
  767.8 4.8 collective-permute-start.123
  772.6 4.6 collective-permute-done.136
  790.0 24.3 %collective-permute-done.126 = bf16[2,4,128,384]{3,2,0,1:T(8,128)(2,1)S(1)} collective-permute-done((bf16[2,4,128,384]{3,2,0,1:T(8,128)(2,1)S(1)}, bf16[2,4,128,384]{3,2,0,1:T(8,128)(2,1)S(1)}, u32[]{:S(2)}, u32[]{:S(2)}) %collective-permute-start.126) | collective-permute-done | bytes 786464 | tf_op jit(solution)/shard_map/ppermute | solution.py:423
  (823 shorter events, 387.4 us)
Async XLA Ops:
  1.5 31.5 %collective-permute-start.26 = (s32[3,128]{1,0:T(4,128)S(1)}, s32[3,128]{1,0:T(4,128)S(1)}, u32[]{:S(2)}, u32[]{:S(2)}) collective-permute-start(s32[3,128]{1,0:T(4,128)S(1)} %pad_add_fusion.1), channel_id=1, source_target_pairs={{0,6},{1,7},{2,4},{3,5},{4,2},{5,3},{6,0},{7,1},{8,14},{9,15},{10,... | collective-permute-start | bytes 4616 | tf_op jit(solution)/shard_map/ppermute | solution.py:316
  5.4 27.7 %collective-permute-start.25 = (s32[3,128]{1,0:T(4,128)S(1)}, s32[3,128]{1,0:T(4,128)S(1)}, u32[]{:S(2)}, u32[]{:S(2)}) collective-permute-start(s32[3,128]{1,0:T(4,128)S(1)} %pad_add_fusion.1), channel_id=1, source_target_pairs={{0,4},{1,5},{2,6},{3,7},{4,0},{5,1},{6,2},{7,3},{8,12},{9,13},{10,... | collective-permute-start | bytes 4616 | tf_op jit(solution)/shard_map/ppermute | solution.py:316
  5.9 28.9 %collective-permute-start.24 = (s32[3,128]{1,0:T(4,128)S(1)}, s32[3,128]{1,0:T(4,128)S(1)}, u32[]{:S(2)}, u32[]{:S(2)}) collective-permute-start(s32[3,128]{1,0:T(4,128)S(1)} %pad_add_fusion.1), channel_id=1, source_target_pairs={{0,2},{1,3},{2,0},{3,1},{4,6},{5,7},{6,4},{7,5},{8,10},{9,11},{10,... | collective-permute-start | bytes 4616 | tf_op jit(solution)/shard_map/ppermute | solution.py:316
  7.6 29.2 %collective-permute-start = (bf16[13,128]{1,0:T(8,128)(2,1)S(1)}, bf16[13,128]{1,0:T(8,128)(2,1)S(1)}, u32[]{:S(2)}, u32[]{:S(2)}) collective-permute-start(bf16[13,128]{1,0:T(8,128)(2,1)S(1)} %get-tuple-element.267), channel_id=1, source_target_pairs={{0,1},{1,0},{2,3},{3,2},{4,5},{5,4},{6,7},{7,6},{8,9},{9,8},{10,11... | collective-permute-start | bytes 9992 | tf_op jit(solution)/shard_map/ppermute | solution.py:316
  7.6 31.8 %collective-permute-start.1 = (bf16[13,128]{1,0:T(8,128)(2,1)S(1)}, bf16[13,128]{1,0:T(8,128)(2,1)S(1)}, u32[]{:S(2)}, u32[]{:S(2)}) collective-permute-start(bf16[13,128]{1,0:T(8,128)(2,1)S(1)} %get-tuple-element.262), channel_id=1, source_target_pairs={{0,2},{1,3},{2,0},{3,1},{4,6},{5,7},{6,4},{7,5},{8,10},{9,11},{10,... | collective-permute-start | bytes 9992 | tf_op jit(solution)/shard_map/ppermute | solution.py:316
  63.2 70.5 %collective-permute-start.31 = (bf16[2,512,384]{2,1,0:T(8,128)(2,1)}, bf16[2,512,384]{2,1,0:T(8,128)(2,1)S(1)}, u32[]{:S(2)}, u32[]{:S(2)}) collective-permute-start(bf16[2,512,384]{2,1,0:T(8,128)(2,1)} %get-tuple-element.151), channel_id=1, source_target_pairs={{0,6},{1,7},{2,4},{3,5},{4,2},{5,3},{6,0},{7,1},{8,14},{9,15},{10,... | collective-permute-start | bytes 2359304 | tf_op jit(solution)/shard_map/ppermute | solution.py:316
  64.7 71.7 %collective-permute-start.32 = (bf16[2,512,384]{2,1,0:T(8,128)(2,1)}, bf16[2,512,384]{2,1,0:T(8,128)(2,1)S(1)}, u32[]{:S(2)}, u32[]{:S(2)}) collective-permute-start(bf16[2,512,384]{2,1,0:T(8,128)(2,1)} %get-tuple-element.150), channel_id=1, source_target_pairs={{0,4},{1,5},{2,6},{3,7},{4,0},{5,1},{6,2},{7,3},{8,12},{9,13},{10,... | collective-permute-start | bytes 2359304 | tf_op jit(solution)/shard_map/ppermute | solution.py:316
  73.9 51.7 %collective-permute-start.37 = (bf16[192,1536]{1,0:T(8,128)(2,1)}, bf16[192,1536]{1,0:T(8,128)(2,1)S(1)}, u32[]{:S(2)}, u32[]{:S(2)}) collective-permute-start(bf16[192,1536]{1,0:T(8,128)(2,1)} %param.27), channel_id=1, source_target_pairs={{0,1},{1,0},{2,3},{3,2},{4,5},{5,4},{6,7},{7,6},{8,9},{9,8},{10,11... | collective-permute-start | bytes 1769480 | tf_op jit(solution)/shard_map/ppermute | solution.py:316
  83.8 41.2 %collective-permute-start.15 = (bf16[128,1536]{1,0:T(8,128)(2,1)S(1)}, bf16[128,1536]{1,0:T(8,128)(2,1)S(1)}, u32[]{:S(2)}, u32[]{:S(2)}) collective-permute-start(bf16[128,1536]{1,0:T(8,128)(2,1)S(1)} %get-tuple-element.91), channel_id=1, source_target_pairs={{0,4},{1,5},{2,6},{3,7},{4,0},{5,1},{6,2},{7,3},{8,12},{9,13},{10,... | collective-permute-start | bytes 1179656 | tf_op jit(solution)/shard_map/ppermute | solution.py:316
  107.8 29.4 %collective-permute-start.33 = (bf16[2,512,384]{2,1,0:T(8,128)(2,1)S(1)}, bf16[2,512,384]{2,1,0:T(8,128)(2,1)S(1)}, u32[]{:S(2)}, u32[]{:S(2)}) collective-permute-start(bf16[2,512,384]{2,1,0:T(8,128)(2,1)S(1)} %copy-done.64), channel_id=1, source_target_pairs={{0,2},{1,3},{2,0},{3,1},{4,6},{5,7},{6,4},{7,5},{8,10},{9,11},{10,... | collective-permute-start | bytes 2359304 | tf_op jit(solution)/shard_map/ppermute | solution.py:316
  131.7 85.8 %collective-permute-start.27 = (bf16[256,4096]{1,0:T(8,128)(2,1)S(1)}, bf16[256,4096]{1,0:T(8,128)(2,1)S(1)}, u32[]{:S(2)}, u32[]{:S(2)}) collective-permute-start(bf16[256,4096]{1,0:T(8,128)(2,1)S(1)} %bitcast.552), channel_id=1, source_target_pairs={{0,2},{1,3},{2,0},{3,1},{4,6},{5,7},{6,4},{7,5},{8,10},{9,11},{10,... | collective-permute-start | bytes 6291464 | tf_op jit(solution)/shard_map/ppermute | solution.py:316
  132.5 87.1 %collective-permute-start.28 = (bf16[256,4096]{1,0:T(8,128)(2,1)S(1)}, bf16[256,4096]{1,0:T(8,128)(2,1)S(1)}, u32[]{:S(2)}, u32[]{:S(2)}) collective-permute-start(bf16[256,4096]{1,0:T(8,128)(2,1)S(1)} %bitcast.553), channel_id=1, source_target_pairs={{0,4},{1,5},{2,6},{3,7},{4,0},{5,1},{6,2},{7,3},{8,12},{9,13},{10,... | collective-permute-start | bytes 6291464 | tf_op jit(solution)/shard_map/ppermute | solution.py:316
  133.7 63.2 %collective-permute-start.48 = (bf16[2,192,1024]{2,1,0:T(8,128)(2,1)S(1)}, bf16[2,192,1024]{2,1,0:T(8,128)(2,1)S(1)}, u32[]{:S(2)}, u32[]{:S(2)}) collective-permute-start(bf16[2,192,1024]{2,1,0:T(8,128)(2,1)S(1)} %copy-done.65), channel_id=1, source_target_pairs={{0,6},{1,7},{2,4},{3,5},{4,2},{5,3},{6,0},{7,1},{8,14},{9,15},{10,... | collective-permute-start | bytes 2359304 | tf_op jit(solution)/shard_map/ppermute | solution.py:316
  136.4 76.3 %collective-permute-start.49 = (bf16[2,192,1024]{2,1,0:T(8,128)(2,1)S(1)}, bf16[2,192,1024]{2,1,0:T(8,128)(2,1)S(1)}, u32[]{:S(2)}, u32[]{:S(2)}) collective-permute-start(bf16[2,192,1024]{2,1,0:T(8,128)(2,1)S(1)} %copy-done.63), channel_id=1, source_target_pairs={{0,4},{1,5},{2,6},{3,7},{4,0},{5,1},{6,2},{7,3},{8,12},{9,13},{10,... | collective-permute-start | bytes 2359304 | tf_op jit(solution)/shard_map/ppermute | solution.py:316
  137.1 75.6 %collective-permute-start.50 = (bf16[2,192,1024]{2,1,0:T(8,128)(2,1)S(1)}, bf16[2,192,1024]{2,1,0:T(8,128)(2,1)S(1)}, u32[]{:S(2)}, u32[]{:S(2)}) collective-permute-start(bf16[2,192,1024]{2,1,0:T(8,128)(2,1)S(1)} %copy-done.62), channel_id=1, source_target_pairs={{0,2},{1,3},{2,0},{3,1},{4,6},{5,7},{6,4},{7,5},{8,10},{9,11},{10,... | collective-permute-start | bytes 2359304 | tf_op jit(solution)/shard_map/ppermute | solution.py:316
  196.8 26.3 %collective-permute-start.21 = (bf16[3,4,192,384]{3,2,1,0:T(8,128)(2,1)S(1)}, bf16[3,4,192,384]{3,2,1,0:T(8,128)(2,1)S(1)}, u32[]{:S(2)}, u32[]{:S(2)}) collective-permute-start(bf16[3,4,192,384]{3,2,1,0:T(8,128)(2,1)S(1)} %pad_maximum_fusion.8), channel_id=1, source_target_pairs={{0,1},{1,0},{2,3},{3,2},{4,5},{5,4},{6,7},{7,6},{8,9},{9,8},{10,11... | collective-permute-start | bytes 5308424 | tf_op jit(solution)/shard_map/ppermute | solution.py:316
  212.7 118.4 %collective-permute-start.52 = (bf16[512,1536]{1,0:T(8,128)(2,1)}, bf16[512,1536]{1,0:T(8,128)(2,1)}, u32[]{:S(2)}, u32[]{:S(2)}) collective-permute-start(bf16[512,1536]{1,0:T(8,128)(2,1)} %param.30), channel_id=1, source_target_pairs={{0,1},{1,0},{2,3},{3,2},{4,5},{5,4},{6,7},{7,6},{8,9},{9,8},{10,11... | collective-permute-start | bytes 4718600 | tf_op jit(solution)/shard_map/ppermute | solution.py:316
  212.7 47.1 %collective-permute-start.34 = (bf16[2,4,512,384]{3,2,1,0:T(8,128)(2,1)}, bf16[2,4,512,384]{3,2,1,0:T(8,128)(2,1)}, u32[]{:S(2)}, u32[]{:S(2)}) collective-permute-start(bf16[2,4,512,384]{3,2,1,0:T(8,128)(2,1)} %pad_maximum_fusion.3), channel_id=1, source_target_pairs={{0,1},{1,0},{2,3},{3,2},{4,5},{5,4},{6,7},{7,6},{8,9},{9,8},{10,11... | collective-permute-start | bytes 9437192 | tf_op jit(solution)/shard_map/ppermute | solution.py:316
  218.6 36.3 %collective-permute-start.29 = (bf16[128,4096]{1,0:T(8,128)(2,1)}, bf16[128,4096]{1,0:T(8,128)(2,1)}, u32[]{:S(2)}, u32[]{:S(2)}) collective-permute-start(bf16[128,4096]{1,0:T(8,128)(2,1)} %slice.743), channel_id=1, source_target_pairs={{0,4},{1,5},{2,6},{3,7},{4,0},{5,1},{6,2},{7,3},{8,12},{9,13},{10,... | collective-permute-start | bytes 3145736 | tf_op jit(solution)/shard_map/ppermute | solution.py:316
  220.7 36.7 %collective-permute-start.30 = (bf16[128,4096]{1,0:T(8,128)(2,1)}, bf16[128,4096]{1,0:T(8,128)(2,1)}, u32[]{:S(2)}, u32[]{:S(2)}) collective-permute-start(bf16[128,4096]{1,0:T(8,128)(2,1)} %slice.744), channel_id=1, source_target_pairs={{0,2},{1,3},{2,0},{3,1},{4,6},{5,7},{6,4},{7,5},{8,10},{9,11},{10,... | collective-permute-start | bytes 3145736 | tf_op jit(solution)/shard_map/ppermute | solution.py:316
  253.3 60.7 %collective-permute-start.85 = (bf16[16,1024]{1,0:T(8,128)(2,1)}, bf16[16,1024]{1,0:T(8,128)(2,1)S(1)}, u32[]{:S(2)}, u32[]{:S(2)}) collective-permute-start(bf16[16,1024]{1,0:T(8,128)(2,1)} %concatenate.193), channel_id=1, source_target_pairs={{0,8},{8,0},{16,24},{24,16},{1,9},{9,1},{17,25},{25,17},{2,10},{10... | collective-permute-start | bytes 98312 | tf_op jit(solution)/shard_map/ppermute | solution.py:885
  254.9 87.1 %collective-permute-start.51 = (bf16[2,4,192,1024]{3,2,1,0:T(8,128)(2,1)}, bf16[2,4,192,1024]{3,2,1,0:T(8,128)(2,1)}, u32[]{:S(2)}, u32[]{:S(2)}) collective-permute-start(bf16[2,4,192,1024]{3,2,1,0:T(8,128)(2,1)} %pad_maximum_fusion.4), channel_id=1, source_target_pairs={{0,1},{1,0},{2,3},{3,2},{4,5},{5,4},{6,7},{7,6},{8,9},{9,8},{10,11... | collective-permute-start | bytes 9437192 | tf_op jit(solution)/shard_map/ppermute | solution.py:316
  389.9 27.1 %collective-permute-start.53 = (bf16[64,1536]{1,0:T(8,128)(2,1)S(1)}, bf16[64,1536]{1,0:T(8,128)(2,1)}, u32[]{:S(2)}, u32[]{:S(2)}) collective-permute-start(bf16[64,1536]{1,0:T(8,128)(2,1)S(1)} %get-tuple-element.168), channel_id=1, source_target_pairs={{0,2},{1,3},{2,0},{3,1},{4,6},{5,7},{6,4},{7,5},{8,10},{9,11},{10,... | collective-permute-start | bytes 589832 | tf_op jit(solution)/shard_map/ppermute | solution.py:316
  390.8 26.3 %collective-permute-start.57 = (bf16[64,1536]{1,0:T(8,128)(2,1)S(1)}, bf16[64,1536]{1,0:T(8,128)(2,1)}, u32[]{:S(2)}, u32[]{:S(2)}) collective-permute-start(bf16[64,1536]{1,0:T(8,128)(2,1)S(1)} %get-tuple-element.169), channel_id=1, source_target_pairs={{0,4},{1,5},{2,6},{3,7},{4,0},{5,1},{6,2},{7,3},{8,12},{9,13},{10,... | collective-permute-start | bytes 589832 | tf_op jit(solution)/shard_map/ppermute | solution.py:316
  407.3 26.4 %collective-permute-start.56 = (bf16[64,1536]{1,0:T(8,128)(2,1)S(1)}, bf16[64,1536]{1,0:T(8,128)(2,1)S(1)}, u32[]{:S(2)}, u32[]{:S(2)}) collective-permute-start(bf16[64,1536]{1,0:T(8,128)(2,1)S(1)} %get-tuple-element.170), channel_id=1, source_target_pairs={{0,4},{1,5},{2,6},{3,7},{4,0},{5,1},{6,2},{7,3},{8,12},{9,13},{10,... | collective-permute-start | bytes 589832 | tf_op jit(solution)/shard_map/ppermute | solution.py:316
  417.1 215.7 %collective-permute-start.130 = (bf16[2,4,4,48,1024]{4,3,0,2,1:T(8,128)(2,1)}, bf16[2,4,4,48,1024]{4,3,0,2,1:T(8,128)(2,1)}, u32[]{:S(2)}, u32[]{:S(2)}) collective-permute-start(bf16[2,4,4,48,1024]{4,3,0,2,1:T(8,128)(2,1)} %fusion.8), channel_id=1, source_target_pairs={{0,1},{1,0},{2,3},{3,2},{4,5},{5,4},{6,7},{7,6},{8,9},{9,8},{10,11... | collective-permute-start | bytes 9437192 | tf_op jit(solution)/shard_map/ppermute | solution.py:316
  417.1 112.5 %collective-permute-start.140 = (bf16[4,128,1536]{2,1,0:T(8,128)(2,1)}, bf16[4,128,1536]{2,1,0:T(8,128)(2,1)}, u32[]{:S(2)}, u32[]{:S(2)}) collective-permute-start(bf16[4,128,1536]{2,1,0:T(8,128)(2,1)} %fusion.23), channel_id=1, source_target_pairs={{0,1},{1,0},{2,3},{3,2},{4,5},{5,4},{6,7},{7,6},{8,9},{9,8},{10,11... | collective-permute-start | bytes 4718600 | tf_op jit(solution)/shard_map/ppermute | solution.py:316
  497.0 43.1 %collective-permute-start.112 = (bf16[4,48,1536]{2,1,0:T(8,128)(2,1)}, bf16[4,48,1536]{2,1,0:T(8,128)(2,1)}, u32[]{:S(2)}, u32[]{:S(2)}) collective-permute-start(bf16[4,48,1536]{2,1,0:T(8,128)(2,1)} %fusion.80), channel_id=1, source_target_pairs={{0,1},{1,0},{2,3},{3,2},{4,5},{5,4},{6,7},{7,6},{8,9},{9,8},{10,11... | collective-permute-start | bytes 1769480 | tf_op jit(solution)/shard_map/ppermute | solution.py:316
  511.0 24.6 %collective-permute-start.75 = (bf16[64,1536]{1,0:T(8,128)(2,1)}, bf16[64,1536]{1,0:T(8,128)(2,1)}, u32[]{:S(2)}, u32[]{:S(2)}) collective-permute-start(bf16[64,1536]{1,0:T(8,128)(2,1)} %get-tuple-element.160), channel_id=1, source_target_pairs={{0,2},{1,3},{2,0},{3,1},{4,6},{5,7},{6,4},{7,5},{8,10},{9,11},{10,... | collective-permute-start | bytes 589832 | tf_op jit(solution)/shard_map/ppermute | solution.py:316
  564.7 62.3 %collective-permute-start.102 = (bf16[3,4,4,48,384]{4,3,0,2,1:T(8,128)(2,1)}, bf16[3,4,4,48,384]{4,3,0,2,1:T(8,128)(2,1)}, u32[]{:S(2)}, u32[]{:S(2)}) collective-permute-start(bf16[3,4,4,48,384]{4,3,0,2,1:T(8,128)(2,1)} %fusion.22), channel_id=1, source_target_pairs={{0,1},{1,0},{2,3},{3,2},{4,5},{5,4},{6,7},{7,6},{8,9},{9,8},{10,11... | collective-permute-start | bytes 5308424 | tf_op jit(solution)/shard_map/ppermute | solution.py:316
  568.5 24.4 %collective-permute-start.93 = (bf16[16,6144]{1,0:T(8,128)(2,1)}, bf16[16,6144]{1,0:T(8,128)(2,1)S(1)}, u32[]{:S(2)}, u32[]{:S(2)}) collective-permute-start(bf16[16,6144]{1,0:T(8,128)(2,1)} %concatenate.198), channel_id=1, source_target_pairs={{0,8},{8,0},{16,24},{24,16},{1,9},{9,1},{17,25},{25,17},{2,10},{10... | collective-permute-start | bytes 589832 | tf_op jit(solution)/shard_map/ppermute | solution.py:877
  608.5 70.5 %collective-permute-start.120 = (bf16[2,4,4,128,384]{4,3,0,2,1:T(8,128)(2,1)}, bf16[2,4,4,128,384]{4,3,0,2,1:T(8,128)(2,1)}, u32[]{:S(2)}, u32[]{:S(2)}) collective-permute-start(bf16[2,4,4,128,384]{4,3,0,2,1:T(8,128)(2,1)} %fusion.7), channel_id=1, source_target_pairs={{0,1},{1,0},{2,3},{3,2},{4,5},{5,4},{6,7},{7,6},{8,9},{9,8},{10,11... | collective-permute-start | bytes 9437192 | tf_op jit(solution)/shard_map/ppermute | solution.py:316
  620.3 30.7 %collective-permute-start.144 = (bf16[128,1536]{1,0:T(8,128)(2,1)}, bf16[128,1536]{1,0:T(8,128)(2,1)}, u32[]{:S(2)}, u32[]{:S(2)}) collective-permute-start(bf16[128,1536]{1,0:T(8,128)(2,1)} %get-tuple-element.135), channel_id=1, source_target_pairs={{24,16},{25,17},{26,18},{27,19},{28,20},{29,21},{30,22},{31,23}} | collective-permute-start | bytes 1179656 | tf_op jit(solution)/shard_map/ppermute | solution.py:423
  622.2 29.7 %collective-permute-start.142 = (bf16[128,1536]{1,0:T(8,128)(2,1)}, bf16[128,1536]{1,0:T(8,128)(2,1)}, u32[]{:S(2)}, u32[]{:S(2)}) collective-permute-start(bf16[128,1536]{1,0:T(8,128)(2,1)} %fusion.70), channel_id=1, source_target_pairs={{0,8},{8,16},{1,9},{9,17},{2,10},{10,18},{3,11},{11,19},{4,12},{12... | collective-permute-start | bytes 1179656 | tf_op jit(solution)/shard_map/ppermute | solution.py:417
  627.1 28.8 %collective-permute-start.119 = (bf16[48,1536]{1,0:T(8,128)(2,1)S(1)}, bf16[48,1536]{1,0:T(8,128)(2,1)}, u32[]{:S(2)}, u32[]{:S(2)}) collective-permute-start(bf16[48,1536]{1,0:T(8,128)(2,1)S(1)} %fusion.109), channel_id=1, source_target_pairs={{0,0},{1,1},{2,8},{3,9},{4,16},{5,17},{6,24},{7,25},{8,2},{9,3},{1... | collective-permute-start | bytes 442376 | tf_op jit(solution)/shard_map/ppermute | solution.py:443
  645.4 31.0 %collective-permute-start.131 = (bf16[2,4,48,1024]{3,2,0,1:T(8,128)(2,1)S(1)}, bf16[2,4,48,1024]{3,2,0,1:T(8,128)(2,1)S(1)}, u32[]{:S(2)}, u32[]{:S(2)}) collective-permute-start(bf16[2,4,48,1024]{3,2,0,1:T(8,128)(2,1)S(1)} %get-tuple-element.98), channel_id=1, source_target_pairs={{0,8},{1,9},{2,10},{3,11},{4,12},{5,13},{6,14},{7,15}} | collective-permute-start | bytes 2359304 | tf_op jit(solution)/shard_map/ppermute | solution.py:417
  655.9 41.9 %collective-permute-start.96 = (bf16[64,6144]{1,0:T(8,128)(2,1)S(1)}, bf16[64,6144]{1,0:T(8,128)(2,1)S(1)}, u32[]{:S(2)}, u32[]{:S(2)}) collective-permute-start(bf16[64,6144]{1,0:T(8,128)(2,1)S(1)} %concatenate.199), channel_id=1, source_target_pairs={{0,1},{1,0},{2,3},{3,2},{4,5},{5,4},{6,7},{7,6},{8,9},{9,8},{10,11... | collective-permute-start | bytes 2359304 | tf_op jit(solution)/shard_map/ppermute | solution.py:316
  657.5 33.6 %collective-permute-start.145 = (bf16[128,1536]{1,0:T(8,128)(2,1)}, bf16[128,1536]{1,0:T(8,128)(2,1)}, u32[]{:S(2)}, u32[]{:S(2)}) collective-permute-start(bf16[128,1536]{1,0:T(8,128)(2,1)} %get-tuple-element.133), channel_id=1, source_target_pairs={{24,16},{16,8},{25,17},{17,9},{26,18},{18,10},{27,19},{19,11},{28,... | collective-permute-start | bytes 1179656 | tf_op jit(solution)/shard_map/ppermute | solution.py:423
  673.7 34.1 %collective-permute-start.134 = (bf16[2,4,48,1024]{3,2,0,1:T(8,128)(2,1)}, bf16[2,4,48,1024]{3,2,0,1:T(8,128)(2,1)}, u32[]{:S(2)}, u32[]{:S(2)}) collective-permute-start(bf16[2,4,48,1024]{3,2,0,1:T(8,128)(2,1)} %get-tuple-element.99), channel_id=1, source_target_pairs={{24,16},{25,17},{26,18},{27,19},{28,20},{29,21},{30,22},{31,23}} | collective-permute-start | bytes 2359304 | tf_op jit(solution)/shard_map/ppermute | solution.py:423
  676.4 28.6 %collective-permute-start.107 = (bf16[3,4,48,384]{3,2,0,1:T(8,128)(2,1)}, bf16[3,4,48,384]{3,2,0,1:T(8,128)(2,1)}, u32[]{:S(2)}, u32[]{:S(2)}) collective-permute-start(bf16[3,4,48,384]{3,2,0,1:T(8,128)(2,1)} %get-tuple-element.124), channel_id=1, source_target_pairs={{24,16},{16,8},{25,17},{17,9},{26,18},{18,10},{27,19},{19,11},{28,... | collective-permute-start | bytes 1327112 | tf_op jit(solution)/shard_map/ppermute | solution.py:423
  679.0 33.7 %collective-permute-start.132 = (bf16[2,4,48,1024]{3,2,0,1:T(8,128)(2,1)}, bf16[2,4,48,1024]{3,2,0,1:T(8,128)(2,1)}, u32[]{:S(2)}, u32[]{:S(2)}) collective-permute-start(bf16[2,4,48,1024]{3,2,0,1:T(8,128)(2,1)} %fusion.26), channel_id=1, source_target_pairs={{0,8},{8,16},{1,9},{9,17},{2,10},{10,18},{3,11},{11,19},{4,12},{12... | collective-permute-start | bytes 2359304 | tf_op jit(solution)/shard_map/ppermute | solution.py:417
  691.2 27.1 %collective-permute-start.121 = (bf16[2,4,128,384]{3,2,0,1:T(8,128)(2,1)}, bf16[2,4,128,384]{3,2,0,1:T(8,128)(2,1)}, u32[]{:S(2)}, u32[]{:S(2)}) collective-permute-start(bf16[2,4,128,384]{3,2,0,1:T(8,128)(2,1)} %get-tuple-element.102), channel_id=1, source_target_pairs={{0,8},{1,9},{2,10},{3,11},{4,12},{5,13},{6,14},{7,15}} | collective-permute-start | bytes 2359304 | tf_op jit(solution)/shard_map/ppermute | solution.py:417
  698.7 28.0 %collective-permute-start.143 = (bf16[128,1536]{1,0:T(8,128)(2,1)}, bf16[128,1536]{1,0:T(8,128)(2,1)}, u32[]{:S(2)}, u32[]{:S(2)}) collective-permute-start(bf16[128,1536]{1,0:T(8,128)(2,1)} %get-tuple-element.132), channel_id=1, source_target_pairs={{0,8},{8,16},{16,24},{1,9},{9,17},{17,25},{2,10},{10,18},{18,26},{... | collective-permute-start | bytes 1179656 | tf_op jit(solution)/shard_map/ppermute | solution.py:417
  707.8 28.3 %collective-permute-start.105 = (bf16[3,4,48,384]{3,2,0,1:T(8,128)(2,1)S(1)}, bf16[3,4,48,384]{3,2,0,1:T(8,128)(2,1)S(1)}, u32[]{:S(2)}, u32[]{:S(2)}) collective-permute-start(bf16[3,4,48,384]{3,2,0,1:T(8,128)(2,1)S(1)} %copy-done.74), channel_id=1, source_target_pairs={{0,8},{8,16},{16,24},{1,9},{9,17},{17,25},{2,10},{10,18},{18,26},{... | collective-permute-start | bytes 1327112 | tf_op jit(solution)/shard_map/ppermute | solution.py:417
  718.3 27.5 %collective-permute-start.124 = (bf16[2,4,128,384]{3,2,0,1:T(8,128)(2,1)S(1)}, bf16[2,4,128,384]{3,2,0,1:T(8,128)(2,1)S(1)}, u32[]{:S(2)}, u32[]{:S(2)}) collective-permute-start(bf16[2,4,128,384]{3,2,0,1:T(8,128)(2,1)S(1)} %copy-done.59), channel_id=1, source_target_pairs={{24,16},{25,17},{26,18},{27,19},{28,20},{29,21},{30,22},{31,23}} | collective-permute-start | bytes 2359304 | tf_op jit(solution)/shard_map/ppermute | solution.py:423
  727.5 25.5 %collective-permute-start.122 = (bf16[2,4,128,384]{3,2,0,1:T(8,128)(2,1)S(1)}, bf16[2,4,128,384]{3,2,0,1:T(8,128)(2,1)S(1)}, u32[]{:S(2)}, u32[]{:S(2)}) collective-permute-start(bf16[2,4,128,384]{3,2,0,1:T(8,128)(2,1)S(1)} %fusion.31), channel_id=1, source_target_pairs={{0,8},{8,16},{1,9},{9,17},{2,10},{10,18},{3,11},{11,19},{4,12},{12... | collective-permute-start | bytes 2359304 | tf_op jit(solution)/shard_map/ppermute | solution.py:417
  736.8 35.8 %collective-permute-start.133 = (bf16[2,4,48,1024]{3,2,0,1:T(8,128)(2,1)S(1)}, bf16[2,4,48,1024]{3,2,0,1:T(8,128)(2,1)S(1)}, u32[]{:S(2)}, u32[]{:S(2)}) collective-permute-start(bf16[2,4,48,1024]{3,2,0,1:T(8,128)(2,1)S(1)} %get-tuple-element.96), channel_id=1, source_target_pairs={{0,8},{8,16},{16,24},{1,9},{9,17},{17,25},{2,10},{10,18},{18,26},{... | collective-permute-start | bytes 2359304 | tf_op jit(solution)/shard_map/ppermute | solution.py:417
  777.8 36.6 %collective-permute-start.126 = (bf16[2,4,128,384]{3,2,0,1:T(8,128)(2,1)S(1)}, bf16[2,4,128,384]{3,2,0,1:T(8,128)(2,1)S(1)}, u32[]{:S(2)}, u32[]{:S(2)}) collective-permute-start(bf16[2,4,128,384]{3,2,0,1:T(8,128)(2,1)S(1)} %fusion.30), channel_id=1, source_target_pairs={{24,16},{16,8},{8,0},{25,17},{17,9},{9,1},{26,18},{18,10},{10,2},{... | collective-permute-start | bytes 2359304 | tf_op jit(solution)/shard_map/ppermute | solution.py:423
  (240 other events, 4826.7 us)

commit v2 on v1

--- a/solution.py
+++ b/solution.py
@@ -529,15 +529,13 @@
 def attend_back_kernel(
     qr_ref, kr_ref, v_ref, tr_ref, tv_ref, dc_ref, cross_ref, q_ref, k_ref, tk_ref, iq_ref, ik_ref,
     it_ref, cos_ref, sin_ref, sc_ref, sr_ref, g_ref,
-    dq_ref, dk_ref, dv_ref, dt_ref, dtv_ref, sq_ref, sk_ref, st_ref, gg_ref,
+    dq_ref, dk_ref, dv_ref, dt_ref, dtv_ref, gg_ref,
 ):
-    same, mine = masks_of(sc_ref[...], sr_ref[0], tk_ref.shape[0])
+    same, mine = masks_of(sc_ref[...], sr_ref[...], tk_ref.shape[0])
     cosine = cos_ref[...]
     sine = sin_ref[...]
     low = jnp.bfloat16
     factor = HDIM ** (-0.5)
-    gg_ref[...] = jnp.zeros(gg_ref.shape, jnp.float32)
-    sum_q = sum_k = sum_t = 0.0
     for pair in range(PAIRS):
         at = pl.ds(pair * 128, 128)
         qr = qr_ref[:, at]
@@ -579,24 +577,987 @@
         q_norm = q_ref[:, at] * iq_ref[...]
         k_norm = k_ref[:, at] * ik_ref[...]
         t_norm = tk_ref[:, at] * it_ref[...]
-        gg_ref[0, 0:1, at] = jnp.sum(dq * q_norm, axis=0, keepdims=True)
-        gg_ref[0, 1:2, at] = jnp.sum(dk * k_norm, axis=0, keepdims=True)
-        gg_ref[0, 2:3, at] = jnp.sum(dt * t_norm, axis=0, keepdims=True)
-        gg_ref[0, 3:4, at] = jnp.sum(dcomb * cross_ref[:, at], axis=0, keepdims=True)
+        gg_ref[0:1, at] += jnp.sum(dq * q_norm, axis=0, keepdims=True)
+        gg_ref[1:2, at] += jnp.sum(dk * k_norm, axis=0, keepdims=True)
+        gg_ref[2:3, at] += jnp.sum(dt * t_norm, axis=0, keepdims=True)
+        gg_ref[3:4, at] += jnp.sum(dcomb * cross_ref[:, at], axis=0, keepdims=True)
         dq = dq * g_ref[2:3, at]
         dk = dk * g_ref[3:4, at]
         dt = dt * g_ref[4:5, at]
-        sum_q = sum_q + jnp.sum(dq * q_norm, axis=-1, keepdims=True)
-        sum_k = sum_k + jnp.sum(dk * k_norm, axis=-1, keepdims=True)
-        sum_t = sum_t + jnp.sum(dt * t_norm, axis=-1, keepdims=True)
         dq_ref[:, at] = dq
         dk_ref[:, at] = dk
         dv_ref[:, at] = dv.astype(low)
         dt_ref[:, at] = dt
         dtv_ref[:, at] = dtv.astype(low)
-    sq_ref[...] = sum_q
-    sk_ref[...] = sum_k
-    st_ref[...] = sum_t
+
+
+MESH_IDS = pl.DeviceIdType.MESH
+VMEM_SPEC = pl.BlockSpec(memory_space=pltpu.VMEM)
+ANY_SPEC = pl.BlockSpec(memory_space=pl.ANY)
+
+
+class Net:
+    def __init__(self, send_sems, recv_sems):
+        self.me = lax.axis_index("fsdp")
+        self.send_sems = send_sems
+        self.recv_sems = recv_sems
+        self.count = 0
+        self.all = []
+
+    def peer(self, mask):
+        out = self.me
+        for bit in (1, 2, 4):
+            if mask & bit:
+                out = out + bit * (1 - 2 * ((self.me // bit) % 2))
+        return out
+
+    def meet(self, masks):
+        sem = pltpu.get_barrier_semaphore()
+        for mask in masks:
+            pl.semaphore_signal(
+                sem, inc=1, device_id={"fsdp": self.peer(mask)}, device_id_type=MESH_IDS
+            )
+        pl.semaphore_wait(sem, len(masks))
+
+    def send(self, src, dst, mask):
+        copy = pltpu.make_async_remote_copy(
+            src_ref=src,
+            dst_ref=dst,
+            send_sem=self.send_sems.at[self.count],
+            recv_sem=self.recv_sems.at[self.count],
+            device_id={"fsdp": self.peer(mask)},
+            device_id_type=MESH_IDS,
+        )
+        self.count += 1
+        copy.start()
+        self.all.append(copy)
+        return copy
+
+    def close(self):
+        for copy in self.all:
+            copy.wait_send()
+
+
+def net_scratch(count):
+    return [pltpu.SemaphoreType.DMA((count,)), pltpu.SemaphoreType.DMA((count,))]
+
+
+def share4_start(net, out):
+    return net.send(out.at[0], out.at[1], 2), net.send(out.at[0], out.at[2], 4)
+
+
+def share4_relay(net, out, by_x, by_y):
+    half = out.shape[1] // 2
+    top, bottom = pl.ds(0, half), pl.ds(half, half)
+    by_x.wait_recv()
+    first = net.send(out.at[1, top], out.at[3, top], 4)
+    by_y.wait_recv()
+    second = net.send(out.at[2, bottom], out.at[3, bottom], 2)
+    return first, second
+
+
+def collect4(net, part, buf, far):
+    half = far.shape[1]
+    rows = (pl.ds(0, half), pl.ds(half, half))
+    low = jnp.bfloat16
+    full = jnp.float32
+    for i in (0, 1):
+        buf[2, rows[i]] = part(3, i).astype(low)
+    far_x = net.send(buf.at[2, rows[0]], far.at[0], 2)
+    far_y = net.send(buf.at[2, rows[1]], far.at[1], 4)
+    buf[0, rows[0]] = part(1, 0).astype(low)
+    one_a = net.send(buf.at[0, rows[0]], buf.at[3, rows[0]], 2)
+    buf[1, rows[1]] = part(2, 1).astype(low)
+    two_b = net.send(buf.at[1, rows[1]], buf.at[4, rows[1]], 4)
+    later = []
+
+    def middle():
+        far_x.wait_recv()
+        buf[1, rows[0]] = (part(2, 0) + far[0].astype(full)).astype(low)
+        later.append(net.send(buf.at[1, rows[0]], buf.at[4, rows[0]], 4))
+        far_y.wait_recv()
+        buf[0, rows[1]] = (part(1, 1) + far[1].astype(full)).astype(low)
+        later.append(net.send(buf.at[0, rows[1]], buf.at[3, rows[1]], 2))
+
+    def finish(i):
+        (one_a, two_b)[i].wait_recv()
+        later[i].wait_recv()
+        return part(0, i) + buf[3, rows[i]].astype(full) + buf[4, rows[i]].astype(full)
+
+    return middle, finish
+
+
+def pick_rows(table, seg, first):
+    out = table[first + IMGS - 1 : first + IMGS]
+    for i in range(IMGS - 2, -1, -1):
+        out = jnp.where(seg == i, table[first + i : first + i + 1], out)
+    return out
+
+
+def row_sums(a, b):
+    ones = jnp.ones((8, a.shape[1]), jnp.float32)
+
+    def one(v):
+        return lax.dot_general(
+            ones, v, (((1,), (1,)), ((), ())), precision=HIGH, preferred_element_type=jnp.float32
+        )
+
+    if b is None:
+        return one(a)
+    got = one(a)
+    return jnp.where(lax.broadcasted_iota(jnp.int32, got.shape, 0) < 4, got, one(b))
+
+
+ALL_PEERS = (1, 2, 3, 4, 5, 6, 7)
+
+
+def open_kernel(
+    cond_ref, gain_ref, bias_ref, ada_ref, tok_ref, seg_ref, idx_ref, attn_ref, textw_ref, text_ref,
+    mod_ref, gains_ref, h_ref, idxs_ref, aw_ref, ta_ref, q_ref, k_ref, v_ref, tk_ref, tv_ref,
+    iqk_ref, it_ref,
+    conds, parts, mods, gbuf, tw_ref, sums, tsums, local_sems, send_sems, recv_sems,
+):
+    low = jnp.bfloat16
+    full = jnp.float32
+    net = Net(send_sems, recv_sems)
+    me = net.me
+    chip = me // 2
+    net.meet(ALL_PEERS)
+
+    act = cond_ref[...].astype(full)
+    act = (act * jax.nn.sigmoid(act)).astype(low).astype(full)
+    for j in range(8):
+        gbuf[8, :, 128 * j : 128 * j + 128] = act[:, 128 * j : 128 * j + 128]
+    waits = []
+    for m in ALL_PEERS:
+        at = pl.ds(pl.multiple_of(net.peer(m) * 128, 128), 128)
+        waits.append(net.send(gbuf.at[8, :, at], conds.at[m], m))
+    conds[0] = gbuf[8, :, pl.ds(pl.multiple_of(me * 128, 128), 128)]
+    gwaits = [net.send(gain_ref, gbuf.at[m], m) for m in ALL_PEERS]
+    iwaits = [net.send(idx_ref, idxs_ref.at[i], m) for i, m in ((1, 2), (2, 4), (3, 6))]
+    idxs_ref[0] = idx_ref[...]
+
+    def spread(src, dst, rows, width, sem):
+        def cut(c):
+            return src.at[:, :, pl.ds(pl.multiple_of(c * width, 128), width)]
+
+        def put(f):
+            return dst.at[:, pl.ds(pl.multiple_of(f * rows, rows), rows), :]
+
+        here = pltpu.make_async_copy(cut(chip), put(me), sem)
+        here.start()
+        core = net.send(cut(chip), put(me), 1)
+        away = [net.send(cut(net.peer(m) // 2), put(me), m) for m in (2, 4, 6)]
+        return here, core, away, put
+
+    for w in waits:
+        w.wait_recv()
+    lhs = jnp.concatenate([conds[m] for m in range(8)], axis=0).astype(low)
+    half_cols = 3072
+    step = 512
+
+    def mod_cols(i, _):
+        lo = pl.ds(pl.multiple_of(i * step, step), step)
+        hi = pl.ds(pl.multiple_of(half_cols + i * step, step), step)
+        a = jnp.dot(lhs, ada_ref[:, lo], preferred_element_type=full)
+        b = jnp.dot(lhs, ada_ref[:, hi], preferred_element_type=full)
+        row = lax.broadcasted_iota(jnp.int32, (8, step), 0)
+        for m in range(8):
+            parts[m, :, lo] = (
+                jnp.where(row < 4, a[8 * m : 8 * m + 8], b[8 * m : 8 * m + 8]) + bias_ref[:, lo]
+            )
+        return 0
+
+    lax.fori_loop(0, half_cols // step, mod_cols, 0)
+    waits = [net.send(parts.at[m], mods.at[m], m) for m in ALL_PEERS]
+    attn_io = spread(attn_ref, aw_ref, attn_ref.shape[1], HW, local_sems.at[0])
+    text_io = spread(textw_ref, tw_ref, textw_ref.shape[1], HW, local_sems.at[1])
+    own_text = pltpu.make_async_copy(text_ref, ta_ref.at[0], local_sems.at[2])
+    own_text.start()
+    for w in gwaits:
+        w.wait_recv()
+    gains = gain_ref[...]
+    for m in ALL_PEERS:
+        gains = gains + gbuf[m]
+    gains_ref[...] = gains
+    for w in waits:
+        w.wait_recv()
+
+    def mod_sum(i, _):
+        at = pl.ds(pl.multiple_of(i * step, step), step)
+        total = parts[0, :, at]
+        for m in ALL_PEERS:
+            total = total + mods[m, :, at]
+        mod_ref[:, at] = total
+        return 0
+
+    lax.fori_loop(0, half_cols // step, mod_sum, 0)
+
+    block = 32
+
+    def first_norm(i, _):
+        at = pl.ds(pl.multiple_of(i * block, block), block)
+        x = tok_ref[at, :].astype(full)
+        normed = x * lax.rsqrt(jnp.mean(x * x, axis=-1, keepdims=True) + EPS)
+        scale = pick_rows(mod_ref[:, :D], seg_ref[at, :], 0)
+        h_ref[0, at, :] = (normed * gains_ref[0:1, :] * (1.0 + scale)).astype(low)
+        return 0
+
+    lax.fori_loop(0, ROW // block, first_norm, 0)
+    hx, hy = share4_start(net, h_ref)
+
+    def pass_on(io):
+        here, core, away, put = io
+        here.wait()
+        return [core] + [
+            (c.wait_recv(), net.send(put(net.peer(m)), put(net.peer(m)), 1))[1]
+            for c, m in zip(away, (2, 4, 6))
+        ]
+
+    attn_core = pass_on(attn_io)
+    text_core = pass_on(text_io)
+    h_far = share4_relay(net, h_ref, hx, hy)
+    own_text.wait()
+    chunks = 4
+    size = ta_ref.shape[1] // chunks
+    tx, ty = [None] * chunks, [None] * chunks
+    for s in range(chunks):
+        i, j = s, (s + chunks // 2) % chunks
+        at = pl.ds(i * size, size)
+        tx[i] = net.send(ta_ref.at[0, at], ta_ref.at[1, at], 2)
+        at = pl.ds(j * size, size)
+        ty[j] = net.send(ta_ref.at[0, at], ta_ref.at[2, at], 4)
+
+    for c in attn_core:
+        c.wait_recv()
+    for c in h_far:
+        c.wait_recv()
+
+    for j in range(CHIPS):
+        h = h_ref[j]
+        at = pl.ds(j * ROW, ROW)
+        qv = jnp.dot(h, aw_ref[0], preferred_element_type=full)
+        q_ref[at, :] = qv
+        kv = jnp.dot(h, aw_ref[1], preferred_element_type=full)
+        k_ref[at, :] = kv
+        v_ref[at, :] = jnp.dot(h, aw_ref[2], preferred_element_type=full).astype(low)
+        sums[0, :, at] = row_sums(qv * qv, kv * kv)
+    sum_io = [net.send(sums.at[0], sums.at[i], m) for i, m in ((1, 2), (2, 4), (3, 6))]
+
+    for c in text_core:
+        c.wait_recv()
+
+    def text_rows(j, lo, count):
+        kt = 1024
+
+        def body(i, acc):
+            at = pl.ds(pl.multiple_of(i * kt, kt), kt)
+            rows = ta_ref[j, pl.ds(lo, count), at]
+            return (
+                acc[0] + jnp.dot(rows, tw_ref[0, at, :], preferred_element_type=full),
+                acc[1] + jnp.dot(rows, tw_ref[1, at, :], preferred_element_type=full),
+            )
+
+        zero = jnp.zeros((count, HW), full)
+        keys, vals = lax.fori_loop(0, TXTD_OF(ta_ref) // kt, body, (zero, zero))
+        at = pl.ds(j * ta_ref.shape[1] + lo, count)
+        tk_ref[at, :] = keys
+        tv_ref[at, :] = vals.astype(low)
+        tsums[0, :, at] = row_sums(keys * keys, None)
+
+    cap = ta_ref.shape[1]
+    half = cap // 2
+    for lo in (0, half):
+        text_rows(0, lo, half)
+    relays = []
+    for s in range(chunks // 2):
+        i, j = s, s + chunks // 2
+        tx[i].wait_recv()
+        at = pl.ds(i * size, size)
+        relays.append(net.send(ta_ref.at[1, at], ta_ref.at[3, at], 4))
+        ty[j].wait_recv()
+        at = pl.ds(j * size, size)
+        relays.append(net.send(ta_ref.at[2, at], ta_ref.at[3, at], 2))
+    for i, c in enumerate(sum_io):
+        c.wait_recv()
+    for j in range(CHIPS):
+        total = sums[0, :, pl.ds(j * ROW, ROW)]
+        for i in (1, 2, 3):
+            total = total + sums[i, :, pl.ds((j ^ i) * ROW, ROW)]
+        iqk_ref[:, pl.ds(j * ROW, ROW)] = lax.rsqrt(total / D + EPS)
+    text_rows(1, 0, half)
+    text_rows(2, half, half)
+    for s in range(chunks // 2):
+        tx[s + chunks // 2].wait_recv()
+        ty[s].wait_recv()
+    text_rows(1, half, half)
+    text_rows(2, 0, half)
+    for c in relays:
+        c.wait_recv()
+    for lo in (0, half):
+        text_rows(3, lo, half)
+    sum_io = [net.send(tsums.at[0], tsums.at[i], m) for i, m in ((1, 2), (2, 4), (3, 6))]
+    for c in sum_io:
+        c.wait_recv()
+    for j in range(CHIPS):
+        total = tsums[0, :, pl.ds(j * cap, cap)]
+        for i in (1, 2, 3):
+            total = total + tsums[i, :, pl.ds((j ^ i) * cap, cap)]
+        it_ref[:, pl.ds(j * cap, cap)] = lax.rsqrt(total / D + EPS)
+    for c in iwaits:
+        c.wait_recv()
+    net.close()
+
+
+def TXTD_OF(ref):
+    return ref.shape[2]
+
+
+def open_layer(cond8, gain_pad, bias_pad, ada, tok, seg_col, idx, attn, textw, text):
+    low = jnp.bfloat16
+    full = jnp.float32
+    shape = jax.ShapeDtypeStruct
+    cap, txtd = text.shape
+    V = VMEM_SPEC
+    return pl.pallas_call(
+        open_kernel,
+        in_specs=[V, V, V, V, V, V, V, ANY_SPEC, ANY_SPEC, ANY_SPEC],
+        out_specs=[V] * 13,
+        out_shape=[
+            shape((8, 3072), full),
+            shape((8, D), full),
+            shape((CHIPS, ROW, D), low),
+            shape((CHIPS, 8, ROW), jnp.int32),
+            shape((3, D, HW), low),
+            shape((CHIPS, cap, txtd), low),
+            shape((CHIPS * ROW, HW), full),
+            shape((CHIPS * ROW, HW), full),
+            shape((CHIPS * ROW, HW), low),
+            shape((CHIPS * cap, HW), full),
+            shape((CHIPS * cap, HW), low),
+            shape((8, CHIPS * ROW), full),
+            shape((8, CHIPS * cap), full),
+        ],
+        scratch_shapes=[
+            pltpu.VMEM((8, 8, 128), full),
+            pltpu.VMEM((8, 8, 3072), full),
+            pltpu.VMEM((8, 8, 3072), full),
+            pltpu.VMEM((9, 8, D), full),
+            pltpu.VMEM((2, txtd, HW), low),
+            pltpu.VMEM((CHIPS, 8, CHIPS * ROW), full),
+            pltpu.VMEM((CHIPS, 8, CHIPS * cap), full),
+            pltpu.SemaphoreType.DMA((3,)),
+            *net_scratch(64),
+        ],
+        compiler_params=pltpu.CompilerParams(
+            collective_id=1, has_side_effects=True, vmem_limit_bytes=56 * 1024 * 1024
+        ),
+        cost_estimate=pl.CostEstimate(
+            flops=10_000_000_000, bytes_accessed=400_000_000, transcendentals=0
+        ),
+    )(cond8, gain_pad, bias_pad, ada, tok, seg_col, idx, attn, textw, text)
+
+
+class Chain:
+    def __init__(self, net, grad, mine, arrive, total, sems, columns):
+        self.net = net
+        self.grad = grad
+        self.mine = mine
+        self.arrive = arrive
+        self.total = total
+        self.sems = sems
+        self.columns = columns
+        self.plane = lax.axis_index("bucket")
+        self.core = net.me % 2
+
+    def piece(self, ref, p):
+        return ref.at[:, p] if self.columns else ref.at[p]
+
+    def half(self, core):
+        return self.grad.at[:, :, :, core] if self.columns else self.grad.at[:, core]
+
+    def each(self, ref, body):
+        lead = ref.shape[:-2]
+        if not lead:
+            body(())
+            return
+        total = 1
+        for n in lead:
+            total *= n
+
+        def step(i, _):
+            index = []
+            for n in reversed(lead):
+                index.insert(0, i % n)
+                i = i // n
+            body(tuple(index))
+            return 0
+
+        lax.fori_loop(0, total, step, 0)
+
+    def core_start(self, keep=None, sem=None):
+        self.exchange = self.net.send(self.half(1 - self.core), self.mine, 1)
+        self.keep = self.half(self.core)
+        self.load = None
+        if keep is not None:
+            self.load = pltpu.make_async_copy(self.keep, keep, sem)
+            self.load.start()
+            self.keep = keep
+
+    def add(self, into, other):
+        def body(index):
+            value = into[index].astype(jnp.float32) + other[index].astype(jnp.float32)
+            into[index] = value.astype(into.dtype)
+
+        self.each(into, body)
+
+    def core_finish(self):
+        self.exchange.wait_recv()
+        if self.load is not None:
+            self.load.wait()
+        self.add(self.mine, self.keep)
+
+    def copy(self, up, p, slot):
+        first = 0 if up else 8
+        return pltpu.make_async_remote_copy(
+            src_ref=self.piece(self.mine, p),
+            dst_ref=self.arrive.at[slot],
+            send_sem=self.sems.at[first + p],
+            recv_sem=self.sems.at[first + 4 + p],
+            device_id={"bucket": self.plane + (1 if up else -1)},
+            device_id_type=MESH_IDS,
+        )
+
+    def moves(self, t):
+        up = self.plane + 3 - t
+        down = self.plane - 3 + t
+        return (
+            (True, up, up, self.plane <= t, self.plane >= 1),
+            (False, down, 4 if t == 2 else down, self.plane >= 3 - t, self.plane <= 2),
+        )
+
+    def step(self, t):
+        for up, p, slot, sends, inner in self.moves(t):
+
+            @pl.when(sends)
+            def _(up=up, p=p, slot=slot, inner=inner):
+                @pl.when(inner)
+                def _():
+                    self.copy(up, p, p).wait_recv()
+                    self.add(self.piece(self.mine, p), self.arrive.at[p])
+
+                self.copy(up, p, slot).start()
+
+    def finish(self):
+        own = self.piece(self.mine, self.plane)
+
+        def first(index):
+            self.total[index] = own[index].astype(jnp.float32)
+
+        self.each(self.total, first)
+        for up, slot, inner in ((True, self.plane, self.plane >= 1), (False, 4, self.plane <= 2)):
+
+            @pl.when(inner)
+            def _(up=up, slot=slot):
+                self.copy(up, self.plane, slot).wait_recv()
+                self.add(self.total, self.arrive.at[slot])
+
+    def close(self):
+        for t in range(3):
+            for up, p, slot, sends, inner in self.moves(t):
+
+                @pl.when(sends)
+                def _(up=up, p=p, slot=slot):
+                    self.copy(up, p, slot).wait_send()
+
+
+def chain_scratch(columns, shape, width):
+    low = jnp.bfloat16
+    if columns:
+        n, rows = shape
+        return [
+            pltpu.VMEM((n, 4, 4, rows, width), low),
+            pltpu.VMEM((5, n, 4, rows, width), low),
+            pltpu.VMEM((n, 4, rows, width), jnp.float32),
+            pltpu.SemaphoreType.DMA((16,)),
+        ]
+    return [
+        pltpu.VMEM((4, shape, width), low),
+        pltpu.VMEM((5, shape, width), low),
+        pltpu.VMEM((shape, width), jnp.float32),
+        pltpu.SemaphoreType.DMA((16,)),
+    ]
+
+
+class Columns:
+    def __init__(self, net, total, stage, wide, out):
+        self.net, self.total, self.stage, self.wide, self.out = net, total, stage, wide, out
+
+    def start(self):
+        net = self.net
+        chip = net.me // 2
+        n, _, rows, width = self.total.shape
+        at = pl.ds(pl.multiple_of(chip * width, width), width)
+
+        def cast(i, _):
+            self.stage[i // 4, i % 4] = self.total[i // 4, i % 4].astype(jnp.bfloat16)
+            return 0
+
+        lax.fori_loop(0, n * 4, cast, 0)
+        self.copies = [
+            net.send(self.stage.at[:, net.peer(m) // 2], self.wide.at[:, :, at], m)
+            for m in (2, 4, 6)
+        ]
+        for i in range(n):
+            self.wide[i, :, at] = self.stage[i, chip]
+
+    def finish(self):
+        for c in self.copies:
+            c.wait_recv()
+        for i in range(self.out.shape[0]):
+            self.out[i] = self.wide[i].astype(jnp.float32)
+
+
+def meet_all(net):
+    plane = lax.axis_index("bucket")
+    chip = net.me // 2
+    sem = pltpu.get_barrier_semaphore()
+    for mask in ALL_PEERS:
+        pl.semaphore_signal(
+            sem, inc=1, device_id={"fsdp": net.peer(mask)}, device_id_type=MESH_IDS
+        )
+    for inner, step in ((plane >= 1, -1), (plane <= 2, 1)):
+
+        @pl.when(inner)
+        def _(step=step):
+            pl.semaphore_signal(
+                sem, inc=1, device_id={"bucket": plane + step}, device_id_type=MESH_IDS
+            )
+
+    @pl.when(chip != plane)
+    def _():
+        pl.semaphore_signal(
+            sem,
+            inc=1,
+            device_id={"bucket": chip, "fsdp": plane * 2 + net.me % 2},
+            device_id_type=MESH_IDS,
+        )
+
+    one = jnp.int32(1)
+    zero = jnp.int32(0)
+    count = (
+        7
+        + jnp.where(plane >= 1, one, zero)
+        + jnp.where(plane <= 2, one, zero)
+        + jnp.where(chip != plane, one, zero)
+    )
+    pl.semaphore_wait(sem, count)
+
+
+def transposed(net, src, dst, sems):
+    plane = lax.axis_index("bucket")
+    return pltpu.make_async_remote_copy(
+        src_ref=src,
+        dst_ref=dst,
+        send_sem=sems.at[0],
+        recv_sem=sems.at[1],
+        device_id={"bucket": net.me // 2, "fsdp": plane * 2 + net.me % 2},
+        device_id_type=MESH_IDS,
+    )
+
+
+def close_kernel(
+    text_g, attn_g, out_g,
+    text_o, attn_o, out_o,
+    tm, ta, tt, ts, am, aa, at_, as_, om, oa, ot, os_,
+    t_wide, a_wide, t_stage, a_stage, o_stage, o_got, o_sem, send_sems, recv_sems,
+):
+    net = Net(send_sems, recv_sems)
+    meet_all(net)
+    plane = lax.axis_index("bucket")
+    chip = net.me // 2
+    out = Chain(net, out_g, om, oa, ot, os_, False)
+    attn = Chain(net, attn_g, am, aa, at_, as_, True)
+    text = Chain(net, text_g, tm, ta, tt, ts, True)
+    chains = [out, attn, text]
+    for c in chains:
+        c.core_start()
+    for c in chains:
+        c.core_finish()
+        c.step(0)
+    for t in (1, 2):
+        for c in chains:
+            c.step(t)
+    out.finish()
+    o_stage[...] = ot[...].astype(jnp.bfloat16)
+
+    @pl.when(chip != plane)
+    def _():
+        transposed(net, o_stage, o_got, o_sem).start()
+
+    attn.finish()
+    attn_cols = Columns(net, at_, a_stage, a_wide, attn_o)
+    attn_cols.start()
+
+    @pl.when(chip != plane)
+    def _():
+        transposed(net, o_stage, o_got, o_sem).wait()
+        out_o[...] = o_got[...].astype(jnp.float32)
+
+    @pl.when(chip == plane)
+    def _():
+        out_o[...] = ot[...]
+
+    attn_cols.finish()
+    text.finish()
+    text_cols = Columns(net, tt, t_stage, t_wide, text_o)
+    text_cols.start()
+    text_cols.finish()
+    for c in chains:
+        c.close()
+    net.close()
+
+
+def close_layer(text_g, attn_g, out_g):
+    low = jnp.bfloat16
+    full = jnp.float32
+    shape = jax.ShapeDtypeStruct
+    V = VMEM_SPEC
+    tr, tw = text_g.shape[-2:]
+    ar, aw = attn_g.shape[-2:]
+    orow, ow = out_g.shape[-2:]
+    return pl.pallas_call(
+        close_kernel,
+        in_specs=[V] * 3,
+        out_specs=[V] * 3,
+        out_shape=[
+            shape((2, tr, 4 * tw), full),
+            shape((3, ar, 4 * aw), full),
+            shape((orow, ow), full),
+        ],
+        scratch_shapes=[
+            *chain_scratch(True, (2, tr), tw),
+            *chain_scratch(True, (3, ar), aw),
+            *chain_scratch(False, orow, ow),
+            pltpu.VMEM((2, tr, 4 * tw), low),
+            pltpu.VMEM((3, ar, 4 * aw), low),
+            pltpu.VMEM((2, 4, tr, tw), low),
+            pltpu.VMEM((3, 4, ar, aw), low),
+            pltpu.VMEM((orow, ow), low),
+            pltpu.VMEM((orow, ow), low),
+            pltpu.SemaphoreType.DMA((2,)),
+            *net_scratch(16),
+        ],
+        compiler_params=pltpu.CompilerParams(
+            collective_id=2, has_side_effects=True, vmem_limit_bytes=63 * 1024 * 1024
+        ),
+        cost_estimate=pl.CostEstimate(
+            flops=1_000_000, bytes_accessed=400_000_000, transcendentals=0
+        ),
+    )(text_g, attn_g, out_g)
+
+
+def column_of(v):
+    return jnp.transpose(v)[:, 0:1]
+
+
+def back_kernel(
+    dh2_ref, fo_ref, x1_ref, branch_ref, cot_ref, w_ref, mod_ref, seg_ref, gain_ref, tok_ref,
+    sr_ref, gs_ref, *rest,
+):
+    late, rest = rest[:LATE], rest[LATE:]
+    places, rest = rest[-LATE - 1 : -1], rest[: -LATE - 1] + rest[-1:]
+    loads = [
+        pltpu.make_async_copy(src, dst, rest[-1].at[i])
+        for i, (src, dst) in enumerate(zip(late, places))
+    ]
+    back_body(
+        dh2_ref, fo_ref, x1_ref, branch_ref, cot_ref, w_ref, mod_ref, seg_ref, gain_ref, tok_ref,
+        *places, sr_ref, gs_ref, *rest[:-1], loads,
+    )
+
+
+LATE = 17
+
+
+def back_body(
+    dh2_ref, fo_ref, x1_ref, branch_ref, cot_ref, w_ref, mod_ref, seg_ref, gain_ref, tok_ref,
+    ow_ref, aw_ref, qr_ref, kr_ref, v_ref, tr_ref, tv_ref, cross_ref, q_ref, k_ref, tk_ref,
+    iq_ref, ik_ref, it_ref, cos_ref, sin_ref, sc_ref, sr_ref, gs_ref, ffn_g, down_g,
+    block_o, token_o, db_ref, dq_o, dk_o, dv_o, dt_o, dtv_o, dmod_o, gg_o, gs_o, ffn_o, down_o,
+    dx_s, dc_s, dqf, dkf, dtf, part_s, sums, tsums, buf_a, far_a, buf_b, far_b, buf_c, far_c,
+    fm, fa, ft, fs, dm, da, dt_c, ds_, f_wide, f_stage, d_stage, d_got, d_sem,
+    f_keep, d_keep, keep_sem, send_sems, recv_sems, loads,
+):
+    low = jnp.bfloat16
+    full = jnp.float32
+    net = Net(send_sems, recv_sems)
+    meet_all(net)
+    plane = lax.axis_index("bucket")
+    chip = net.me // 2
+    ffn = Chain(net, ffn_g, fm, fa, ft, fs, True)
+    down = Chain(net, down_g, dm, da, dt_c, ds_, False)
+    ffn.core_start(f_keep, keep_sem.at[0])
+    down.core_start(d_keep, keep_sem.at[1])
+    for c in loads:
+        c.start()
+
+    def rows_of(ref):
+        half = ROW // 2
+        return lambda j, i: ref[pl.ds(j * ROW + i * half, half), :].astype(full)
+
+    middle, finish = collect4(net, rows_of(dh2_ref), buf_a, far_a)
+    middle()
+    ffn.core_finish()
+    ffn.step(0)
+    down.core_finish()
+    down.step(0)
+    half = ROW // 2
+    for i in (0, 1):
+        dx_s[pl.ds(i * half, half), :] = finish(i)
+    part_s[pl.ds(0, ROW), :] = dx_s[...]
+    block = 32
+    weight = w_ref[0:1, 0:1]
+
+    def second_norm(at):
+        x1 = x1_ref[at, :]
+        inverse = lax.rsqrt(jnp.mean(x1 * x1, axis=-1, keepdims=True) + EPS)
+        scale = pick_rows(mod_ref[:, :D], seg_ref[at, :], 4)
+        return x1 * inverse, inverse, scale
+
+    def to_branch(b, _):
+        at = pl.ds(pl.multiple_of(b * block, block), block)
+        normed, inverse, scale = second_norm(at)
+        dn = dx_s[at, :] * gain_ref[1:2, :] * (1.0 + scale)
+        back = inverse * (dn - normed * jnp.mean(dn * normed, axis=-1, keepdims=True))
+        dx = cot_ref[at, :].astype(full) * weight + back
+        dx_s[at, :] = dx
+        gate = jnp.tanh(pick_rows(mod_ref[:, D:], seg_ref[at, :], 0))
+        db_ref[0, at, :] = (dx * gate).astype(low)
+        return 0
+
+    lax.fori_loop(0, ROW // block, to_branch, 0)
+    bx, by = share4_start(net, db_ref)
+
+    def by_image(value, seg, row, lo):
+        for i in range(IMGS):
+            dmod_o[row + i : row + i + 1, lo : lo + D] += jnp.sum(
+                jnp.where(seg == i, value, 0.0), axis=0, keepdims=True
+            )
+
+    dmod_o[...] = jnp.zeros(dmod_o.shape, full)
+    gg_o[...] = jnp.zeros(gg_o.shape, full)
+
+    def second_sums(b, _):
+        at = pl.ds(pl.multiple_of(b * block, block), block)
+        normed, inverse, scale = second_norm(at)
+        seg = seg_ref[at, :]
+        dh = part_s[at, :] * normed
+        gg_o[1:2, :] += jnp.sum(dh * (1.0 + scale), axis=0, keepdims=True)
+        by_image(dh * gain_ref[1:2, :], seg, 4, 0)
+        gate = jnp.tanh(pick_rows(mod_ref[:, D:], seg, 0))
+        by_image(dx_s[at, :] * branch_ref[at, :] * (1.0 - gate * gate), seg, 0, D)
+        return 0
+
+    lax.fori_loop(0, ROW // block, second_sums, 0)
+    far = share4_relay(net, db_ref, bx, by)
+    middle_b, finish_b = collect4(net, rows_of(fo_ref), buf_b, far_b)
+    gs_o[...] = jnp.zeros(gs_o.shape, full)
+    for c in loads:
+        c.wait()
+    cap = IMGS * TXT
+
+    def attention_row(j, _):
+        @pl.when(j == 3)
+        def _():
+            for c in far:
+                c.wait_recv()
+
+        @pl.when(j == 1)
+        def _():
+            ffn.step(1)
+            down.step(1)
+
+        @pl.when(j == 3)
+        def _():
+            ffn.step(2)
+            down.step(2)
+
+        rows = pl.ds(pl.multiple_of(j * ROW, ROW), ROW)
+        text = pl.ds(pl.multiple_of(j * cap, cap), cap)
+        dc_s[...] = dot_t(db_ref[j], ow_ref[...])
+        dqv, dkv, dtv = dqf.at[rows], dkf.at[rows], dtf.at[text]
+        attend_back_kernel(
+            qr_ref.at[rows], kr_ref.at[rows], v_ref.at[rows], tr_ref.at[text], tv_ref.at[text],
+            dc_s, cross_ref.at[rows], q_ref.at[rows], k_ref.at[rows], tk_ref.at[text],
+            iq_ref.at[rows], ik_ref.at[rows], it_ref.at[text], cos_ref.at[rows], sin_ref.at[rows],
+            sc_ref.at[rows], sr_ref.at[j], gs_ref,
+            dqv, dkv, dv_o.at[rows], dtv, dtv_o.at[text], gs_o,
+        )
+        sums[0, :, rows] = row_sums(
+            dqv[...] * (q_ref[rows, :] * iq_ref[rows, :]),
+            dkv[...] * (k_ref[rows, :] * ik_ref[rows, :]),
+        )
+        tsums[0, :, text] = row_sums(dtv[...] * (tk_ref[text, :] * it_ref[text, :]), None)
+        return 0
+
+    lax.fori_loop(0, CHIPS, attention_row, 0)
+    sum_io = []
+    for i, m in ((1, 2), (2, 4), (3, 6)):
+        sum_io.append(net.send(sums.at[0], sums.at[i], m))
+        sum_io.append(net.send(tsums.at[0], tsums.at[i], m))
+    middle_b()
+    for i in (0, 1):
+        part_s[pl.ds(i * half, half), :] = finish_b(i)
+
+    def block_rows(b, _):
+        at = pl.ds(pl.multiple_of(b * block, block), block)
+        seg = seg_ref[at, :]
+        gate = jnp.tanh(pick_rows(mod_ref[:, D:], seg, 4))
+        out = part_s[at, :]
+        block_o[at, :] = (x1_ref[at, :] + gate * out).astype(low)
+        grad = cot_ref[at, :].astype(full) * weight
+        by_image(grad * out * (1.0 - gate * gate), seg, 4, D)
+        return 0
+
+    for c in sum_io:
+        c.wait_recv()
+    for j in range(CHIPS):
+        rows = pl.ds(j * ROW, ROW)
+        text = pl.ds(j * cap, cap)
+        total = sums[0, :, rows]
+        words = tsums[0, :, text]
+        for i in (1, 2, 3):
+            total = total + sums[i, :, pl.ds((j ^ i) * ROW, ROW)]
+            words = words + tsums[i, :, pl.ds((j ^ i) * cap, cap)]
+        mean = jnp.transpose(total / D)
+        iq, ik, it = iq_ref[rows, :], ik_ref[rows, :], it_ref[text, :]
+        dq_o[rows, :] = (iq * (dqf[rows, :] - q_ref[rows, :] * iq * mean[:, 0:1])).astype(low)
+        dk_o[rows, :] = (ik * (dkf[rows, :] - k_ref[rows, :] * ik * mean[:, 4:5])).astype(low)
+        mean = jnp.transpose(words / D)
+        dt_o[text, :] = (it * (dtf[text, :] - tk_ref[text, :] * it * mean[:, 0:1])).astype(low)
+
+    lax.fori_loop(0, ROW // block, block_rows, 0)
+    wide = 256
+
+    def first_grad(n, _):
+        at = pl.ds(pl.multiple_of(n * wide, wide), wide)
+        part_s[:, at] = (
+            dot_t(dq_o[...], aw_ref[0, at, :])
+            + dot_t(dk_o[...], aw_ref[1, at, :])
+            + dot_t(dv_o[...], aw_ref[2, at, :])
+        )
+        return 0
+
+    lax.fori_loop(0, D // wide, first_grad, 0)
+    middle_c, finish_c = collect4(net, rows_of(part_s), buf_c, far_c)
+    ffn.finish()
+    f_cols = Columns(net, ft, f_stage, f_wide, ffn_o)
+    middle_c()
+    f_cols.start()
+    down.finish()
+    d_stage[...] = dt_c[...].astype(low)
+
+    @pl.when(chip != plane)
+    def _():
+        transposed(net, d_stage, d_got, d_sem).start()
+
+    for i in (0, 1):
+        part_s[pl.ds(i * half, half), :] = finish_c(i)
+
+    def first_rows(b, _):
+        at = pl.ds(pl.multiple_of(b * block, block), block)
+        x = tok_ref[at, :].astype(full)
+        inverse = lax.rsqrt(jnp.mean(x * x, axis=-1, keepdims=True) + EPS)
+        normed = x * inverse
+        seg = seg_ref[at, :]
+        scale = pick_rows(mod_ref[:, :D], seg, 0)
+        dh = part_s[at, :]
+        gg_o[0:1, :] += jnp.sum(dh * normed * (1.0 + scale), axis=0, keepdims=True)
+        by_image(dh * normed * gain_ref[0:1, :], seg, 0, 0)
+        dn = dh * gain_ref[0:1, :] * (1.0 + scale)
+        token_o[at, :] = dx_s[at, :] + inverse * (
+            dn - normed * jnp.mean(dn * normed, axis=-1, keepdims=True)
+        )
+        return 0
+
+    lax.fori_loop(0, ROW // block, first_rows, 0)
+    f_cols.finish()
+
+    @pl.when(chip != plane)
+    def _():
+        transposed(net, d_stage, d_got, d_sem).wait()
+        down_o[...] = d_got[...].astype(full)
+
+    @pl.when(chip == plane)
+    def _():
+        down_o[...] = dt_c[...]
+
+    ffn.close()
+    down.close()
+    net.close()
+
+
+def back_layer(early, late, ffn_g, down_g):
+    low = jnp.bfloat16
+    full = jnp.float32
+    shape = jax.ShapeDtypeStruct
+    V = VMEM_SPEC
+    cap = IMGS * TXT
+    fr, fw = ffn_g.shape[-2:]
+    dr, dw = down_g.shape[-2:]
+    tok = CHIPS * ROW
+    reduce_scratch = [pltpu.VMEM((5, ROW, D), low), pltpu.VMEM((2, ROW // 2, D), low)]
+    return pl.pallas_call(
+        back_kernel,
+        in_specs=[V] * len(early) + [ANY_SPEC] * (LATE + 2),
+        out_specs=[V] * 13,
+        out_shape=[
+            shape((ROW, D), low),
+            shape((ROW, D), full),
+            shape((CHIPS, ROW, D), low),
+            shape((tok, HW), low),
+            shape((tok, HW), low),
+            shape((tok, HW), low),
+            shape((CHIPS * cap, HW), low),
+            shape((CHIPS * cap, HW), low),
+            shape((8, 2 * D), full),
+            shape((8, D), full),
+            shape((8, HW), full),
+            shape((2, fr, 4 * fw), full),
+            shape((dr, dw), full),
+        ],
+        scratch_shapes=[
+            pltpu.VMEM((ROW, D), full),
+            pltpu.VMEM((ROW, HW), full),
+            pltpu.VMEM((tok, HW), full),
+            pltpu.VMEM((tok, HW), full),
+            pltpu.VMEM((CHIPS * cap, HW), full),
+            pltpu.VMEM((tok, D), full),
+            pltpu.VMEM((CHIPS, 8, tok), full),
+            pltpu.VMEM((CHIPS, 8, CHIPS * cap), full),
+            *reduce_scratch, *reduce_scratch, *reduce_scratch,
+            *chain_scratch(True, (2, fr), fw),
+            *chain_scratch(False, dr, dw),
+            pltpu.VMEM((2, fr, 4 * fw), low),
+            pltpu.VMEM((2, 4, fr, fw), low),
+            pltpu.VMEM((dr, dw), low),
+            pltpu.VMEM((dr, dw), low),
+            pltpu.SemaphoreType.DMA((2,)),
+            pltpu.VMEM((2, 4, 4, fr, fw), low),
+            pltpu.VMEM((4, dr, dw), low),
+            pltpu.SemaphoreType.DMA((2,)),
+            *net_scratch(48),
+            *[pltpu.VMEM(v.shape, v.dtype) for v in late],
+            pltpu.SemaphoreType.DMA((LATE,)),
+        ],
+        compiler_params=pltpu.CompilerParams(
+            collective_id=3, has_side_effects=True, vmem_limit_bytes=63 * 1024 * 1024
+        ),
+        cost_estimate=pl.CostEstimate(
+            flops=10_000_000_000, bytes_accessed=400_000_000, transcendentals=0
+        ),
+    )(*early, *late, ffn_g, down_g)
 
 
 def row_spec(rows, width):
@@ -633,46 +1594,6 @@
     )(q, k, v, iq, ik, cosine, sine, tk, it, tv, seg_col, seg_row, gains)
 
 
-def attend_all_back(
-    qr, kr, v, tr, tv, dcomb, cross, q, k, tk, iq, ik, it, cosine, sine, seg_col, seg_row, gains
-):
-    cap = IMGS * TXT
-    low = jnp.bfloat16
-    big = row_spec(ROW, HW)
-    text = row_spec(cap, HW)
-    one = row_spec(ROW, 1)
-    table = row_spec(ROW, 128)
-    shape = jax.ShapeDtypeStruct
-    return pl.pallas_call(
-        attend_back_kernel,
-        grid=(CHIPS,),
-        in_specs=[
-            big, big, big, text, text, big, big, big, big, text, one, one, row_spec(cap, 1), table,
-            table, one,
-            pl.BlockSpec((1, 1, ROW), lambda i: (i, 0, 0)),
-            pl.BlockSpec((6, HW), lambda i: (0, 0)),
-        ],
-        out_specs=[
-            big, big, big, text, text, one, one, row_spec(cap, 1),
-            pl.BlockSpec((1, 8, HW), lambda i: (i, 0, 0)),
-        ],
-        out_shape=[
-            shape((CHIPS * ROW, HW), jnp.float32),
-            shape((CHIPS * ROW, HW), jnp.float32),
-            shape((CHIPS * ROW, HW), low),
-            shape((CHIPS * cap, HW), jnp.float32),
-            shape((CHIPS * cap, HW), low),
-            shape((CHIPS * ROW, 1), jnp.float32),
-            shape((CHIPS * ROW, 1), jnp.float32),
-            shape((CHIPS * cap, 1), jnp.float32),
-            shape((CHIPS, 8, HW), jnp.float32),
-        ],
-        cost_estimate=pl.CostEstimate(
-            flops=10 * 24 * 128 * 384 * 128, bytes_accessed=20_000_000, transcendentals=1_200_000
-        ),
-    )(qr, kr, v, tr, tv, dcomb, cross, q, k, tk, iq, ik, it, cosine, sine, seg_col, seg_row, gains)
-
-
 def per_device(
     tokens,
     cond,
@@ -698,28 +1619,29 @@
     chip = slot // 2
     ff = ffn_weight.shape[2] // CHIPS
 
-    cond_act = silu(cond[0].astype(full)).astype(low)
-    packed = []
-    for j in range(8):
-        piece = lax.dynamic_slice_in_dim(cond_act, jnp.bitwise_xor(slot, j) * 128, 128, axis=1)
-        piece = jnp.concatenate([piece.reshape(4, 128), gains.reshape(9, 128)], axis=0)
-        packed.append(piece if j == 0 else swap(piece, j))
-    conds = jnp.concatenate([p[:4] for p in packed], axis=0)
-    gain_f = jnp.stack(reorder([p[4:].reshape(6, 192) for p in packed], slot), axis=1)
-    gain_f = gain_f.reshape(6, D).astype(full)
+    gain_pad = lax.dynamic_update_slice_in_dim(
+        jnp.zeros((8, D), full), jnp.pad(gains.astype(full), ((0, 2), (0, 0))), slot * 192, axis=1
+    )
     bias = lax.dynamic_update_slice_in_dim(
         jnp.zeros((ada_weight.shape[1],), full), ada_bias.astype(full), slot * ada_bias.shape[0], 0
     )
-    mod_parts = (mult(conds, ada_weight) + bias[None, :]).reshape(8, IMGS, -1)
-    mod = mod_parts[0]
-    for j in range(1, 8):
-        mod = mod + swap(mod_parts[j], j)
-
+    bias_pad = jnp.repeat(bias.reshape(2, 3072), 4, axis=0)
     seg = segments[0]
-    index = jnp.concatenate([seg[None, :], positions[0]], axis=0)
-    indices = [index, at_x(index), at_y(index), swap(index, 6)]
-    seg_all = jnp.stack([i[0] for i in indices])
-    pos_all = jnp.stack([i[1:] for i in indices])
+    idx = jnp.concatenate([seg[None, :], positions[0], jnp.zeros((5, ROW), jnp.int32)], axis=0)
+    (
+        mod, gain_f, h_rows, idx_all, attn_w, text_rows, query, keyed, valued, text_keys, text_vals,
+        inv_qk, inv_t,
+    ) = open_layer(
+        jnp.concatenate([cond[0], cond[0]], axis=0), gain_pad, bias_pad, ada_weight, tokens[0],
+        seg[:, None], idx, attn_weight, text_weight, text[0],
+    )
+    cond_act = silu(cond[0].astype(full)).astype(low)
+    h_all = h_rows.reshape(CHIPS * ROW, D)
+    text_all = text_rows.reshape(CHIPS * IMGS * TXT, -1)
+    inv_qk = jnp.stack([inv_qk[0], inv_qk[4]])[:, :, None]
+    inv_t = inv_t[0][:, None]
+    seg_all = idx_all[:, 0]
+    pos_all = idx_all[:, 1:3]
     seg_col = seg_all.reshape(CHIPS * ROW, 1)
     seg_row = seg_all.reshape(CHIPS, 1, ROW)
     lane = jnp.arange(128, dtype=jnp.int32)
@@ -731,15 +1653,13 @@
     cosine = jnp.cos(angle)
     sine = jnp.where(((lane // quarter) % 2 == 0)[None, :], -1.0, 1.0) * jnp.sin(angle)
 
-    attn_w = column_weights(attn_weight, chip, core, HW)
-    text_w = column_weights(text_weight, chip, core, HW)
     ffn_w = column_weights(ffn_weight, chip, core, ff)
     out_w = row_weights(out_weight, core)
     down_w = row_weights(down_weight, core)
-    gain_s = lax.dynamic_slice_in_dim(gain_f, chip * HW, HW, axis=1)
+    gain_s = lax.dynamic_slice_in_dim(gain_f, chip * HW, HW, axis=1)[:6]
 
     def per_token(part):
-        rows = mod[:, part * D : (part + 1) * D]
+        rows = mod[4 * (part // 2) :, (part % 2) * D : (part % 2 + 1) * D]
         out = rows[IMGS - 1][None, :]
         for i in range(IMGS - 2, -1, -1):
             out = jnp.where(seg[:, None] == i, rows[i][None, :], out)
@@ -754,24 +1674,6 @@
 
     x = tokens[0].astype(full)
     normed1, inverse1 = norm_rows(x)
-    h_one = (normed1 * gain_f[0] * (1.0 + scale1)).astype(low)
-    h_all = jnp.concatenate(gather4(h_one), axis=0)
-    query = mult(h_all, attn_w[0])
-    keyed = mult(h_all, attn_w[1])
-    valued = mult(h_all, attn_w[2]).astype(low)
-    squares = jnp.stack(
-        [jnp.sum(query * query, axis=-1), jnp.sum(keyed * keyed, axis=-1)]
-    ).reshape(2, CHIPS, ROW)
-    squares = sum4_rows(jnp.transpose(squares, (1, 0, 2)))
-    squares = jnp.transpose(squares.reshape(CHIPS, 2, ROW), (1, 0, 2)).reshape(2, CHIPS * ROW)
-    inv_qk = lax.rsqrt(squares / D + EPS)[:, :, None]
-
-    text_parts = gather4(text[0])
-    text_all = jnp.concatenate(text_parts, axis=0)
-    text_keys = mult(text_all, text_w[0])
-    text_vals = mult(text_all, text_w[1]).astype(low)
-    inv_t = lax.rsqrt(sum4_rows(jnp.sum(text_keys * text_keys, axis=-1)) / D + EPS)[:, None]
-
     comb, cross_out, q_rot, k_rot, text_rot = attend_all(
         query, keyed, valued, inv_qk[0], inv_qk[1], cosine, sine, text_keys, inv_t, text_vals,
         seg_col, seg_row, gain_s,
@@ -797,69 +1699,46 @@
     hidden = (silu_pre * upper).astype(low)
     d_pre = (d_hidden * upper * sigm * (1.0 + gate_pre * (1.0 - sigm))).astype(low)
     d_up = (d_hidden * silu_pre).astype(low)
-    d_h_two = reduce4(
-        list((dot_t(d_pre, ffn_w[0]) + dot_t(d_up, ffn_w[1])).reshape(CHIPS, ROW, D))
-    )
-    ffn_out = reduce4(list(mult(hidden, down_w).reshape(CHIPS, ROW, D)))
-    block_out = (x_one + tanh_two * ffn_out).astype(low)
-    d_gate2 = grad * ffn_out * (1.0 - tanh_two * tanh_two)
-
-    g_gain_one = jnp.sum(d_h_two * normed2 * (1.0 + scale2), axis=0)
-    d_scale2 = d_h_two * normed2 * gain_f[1]
-    d_x_one = grad + norm_back(d_h_two * gain_f[1] * (1.0 + scale2), normed2, inverse2)
-    d_gate1 = d_x_one * branch * (1.0 - tanh_one * tanh_one)
-    d_branch = (d_x_one * tanh_one).astype(low)
-    d_branch_all = jnp.concatenate(gather4(d_branch), axis=0)
-
-    s_down = row_grad(t_dot(hidden, d_ffn_all), core, plane)
-    s_ffn = column_grad(
-        jnp.stack([t_dot(h_two_all, d_pre), t_dot(h_two_all, d_up)]), chip, core, plane
-    )
-
-    d_comb = dot_t(d_branch_all, out_w)
+    d_h_two = (dot_t(d_pre, ffn_w[0]) + dot_t(d_up, ffn_w[1])).astype(low)
+    ffn_out = mult(hidden, down_w).astype(low)
+    g_down = t_dot(hidden, d_ffn_all).astype(low)
+    g_ffn = jnp.stack([t_dot(h_two_all, d_pre).astype(low), t_dot(h_two_all, d_up).astype(low)])
+
     (
-        dq, dk, d_valued, dt, d_text_vals, sum_q, sum_k, sum_t, gg,
-    ) = attend_all_back(
-        q_rot, k_rot, valued, text_rot, text_vals, d_comb, cross_out, query, keyed, text_keys,
-        inv_qk[0], inv_qk[1], inv_t, cosine, sine, seg_col, seg_row, gain_s,
-    )
-    sums = jnp.concatenate([s.reshape(CHIPS, -1) for s in (sum_q, sum_k, sum_t)], axis=1)
-    sums = sum4_rows(sums).reshape(CHIPS, -1) / D
-    mean_q = sums[:, :ROW].reshape(-1, 1)
-    mean_k = sums[:, ROW : 2 * ROW].reshape(-1, 1)
-    mean_t = sums[:, 2 * ROW :].reshape(-1, 1)
-    d_query = (inv_qk[0] * (dq - query * inv_qk[0] * mean_q)).astype(low)
-    d_keyed = (inv_qk[1] * (dk - keyed * inv_qk[1] * mean_k)).astype(low)
-    d_text_keys = (inv_t * (dt - text_keys * inv_t * mean_t)).astype(low)
-    d_h_one = reduce4(
-        list(
-            (
-                dot_t(d_query, attn_w[0]) + dot_t(d_keyed, attn_w[1]) + dot_t(d_valued, attn_w[2])
-            ).reshape(CHIPS, ROW, D)
-        )
-    )
-    s_text = column_grad(
-        jnp.stack([t_dot(text_all, d_text_keys), t_dot(text_all, d_text_vals)]), chip, core, plane
-    )
-    s_attn = column_grad(
-        jnp.stack([t_dot(h_all, d_query), t_dot(h_all, d_keyed), t_dot(h_all, d_valued)]),
-        chip, core, plane,
-    )
-    s_out = row_grad(t_dot(comb, d_branch_all), core, plane)
-
-    g_gain_zero = jnp.sum(d_h_one * normed1 * (1.0 + scale1), axis=0)
-    d_scale1 = d_h_one * normed1 * gain_f[0]
-    token_grad = d_x_one + norm_back(d_h_one * gain_f[0] * (1.0 + scale1), normed1, inverse1)
-    d_token_mod = jnp.concatenate([d_scale1, d_gate1, d_scale2, d_gate2], axis=1)
-    pick = (seg[:, None] == jnp.arange(IMGS, dtype=jnp.int32)[None, :]).astype(full)
-    d_mod = jnp.dot(pick.T, d_token_mod, precision=HIGH)
-
-    gg = jnp.sum(gg, axis=0)[:4]
+        block_out, token_grad, d_branch_rows, d_query, d_keyed, d_valued, d_text_keys, d_text_vals,
+        d_mod, gg_full, gg_slice, s_ffn, s_down,
+    ) = back_layer(
+        [
+            d_h_two, ffn_out, x_one, branch, cotangent[0], jnp.full((1, 128), weight, full), mod,
+            seg[:, None], gain_f, tokens[0], seg_row, gain_s,
+        ],
+        [
+            out_w, attn_w, q_rot, k_rot, valued, text_rot, text_vals, cross_out, query, keyed,
+            text_keys, inv_qk[0], inv_qk[1], inv_t, cosine, sine, seg_col,
+        ],
+        g_ffn.reshape(2, 4, 4, 2, 48, ff),
+        g_down.reshape(4, 2, 128, D),
+    )
+    d_branch_all = d_branch_rows.reshape(CHIPS * ROW, D)
+    g_text = jnp.stack(
+        [t_dot(text_all, d_text_keys).astype(low), t_dot(text_all, d_text_vals).astype(low)]
+    )
+    g_attn = jnp.stack([t_dot(h_all, g).astype(low) for g in (d_query, d_keyed, d_valued)])
+    g_out = t_dot(comb, d_branch_all).astype(low)
+    s_text, s_attn, s_out = close_layer(
+        g_text.reshape(2, 4, 4, 2, 128, HW),
+        g_attn.reshape(3, 4, 4, 2, 48, HW),
+        g_out.reshape(4, 2, 48, D),
+    )
+
+    d_mod = jnp.concatenate([d_mod[:IMGS], d_mod[IMGS:]], axis=1)
+
+    gg = gg_slice[:4]
     cross_gate = jnp.tanh(gain_s[5])
     gg = gg.at[3].multiply(1.0 - cross_gate * cross_gate)
     spread = lax.dynamic_update_slice_in_dim(jnp.zeros((4, D), full), gg, chip * HW, axis=1)
     small = jnp.concatenate(
-        [g_gain_zero[None], g_gain_one[None], spread, jnp.sum(d_mod, axis=0).reshape(4, D)], axis=0
+        [gg_full[:2], spread, jnp.sum(d_mod, axis=0).reshape(4, D)], axis=0
     )
     small = small + at_core(small)
     small = sum4(small)

time: 838 us -> 690 us (0.82)
  Pallas kernels: 36.5 us -> 400 us
  waiting for transfers between devices: 303 us -> 34.9 us
  starting transfers between devices: 207 us -> 81.8 us
  other arithmetic: 120 us -> 45 us
  matrix products: 77.8 us -> 53.5 us
  local copies, waits for them, and re-layouts: 77.5 us -> 61.8 us
    pallas_call x1 -> x3, Pallas kernels: 22.1 us -> 386 us  [the longest x1 169 us: open_layer(): pl.pallas_call(open_kernel, in_specs=[V, V, V, V, V, V, V, ANY_SPEC, ANY_...]
    ppermute x108 -> x33, waiting for transfers between devices: 209 us -> 27.8 us  [swap(): return lax.ppermute(v, 'fsdp', [(i, i ^ mask) for i in range(8)])]
    ppermute x32 -> x0, starting transfers between devices: 80.8 us -> none  [the longest x15 61.2 us: reduce_buckets(): lax.ppermute(piece.astype(low), 'bucket', [(i, i + 1) for i in range(step)])]
    ppermute x32 -> x0, waiting for transfers between devices: 61.3 us -> none  [the longest x15 31.9 us: reduce_buckets(): lax.ppermute(piece.astype(low), 'bucket', [(i, i + 1) for i in range(step)])]
    ppermute x108 -> x33, starting transfers between devices: 114 us -> 64.5 us  [swap(): return lax.ppermute(v, 'fsdp', [(i, i ^ mask) for i in range(8)])]
    convert_element_type x28 -> x1, other arithmetic: 34.3 us -> 0.02 us  [per_device(): mod_low = d_mod.astype(low)]
    add x13 -> x0, other arithmetic: 21.9 us -> none  [the longest x5 16.3 us: core_half(): return keep + at_core(give.astype(low)).astype(jnp.float32)]
    dot_general x10 -> x4, matrix products: 29.6 us -> 8.35 us  [mult(): return jnp.dot(left, right, preferred_element_type=jnp.float32)]
  transfers between devices with their start and end apart: 148 -> 41, of which waited for: 46 -> 13; matrix products, arithmetic and copies ran while one was open for 30% -> 17% of each run, Pallas kernels for 4% -> 45%
where the time goes in v2:
time: 690 us; the launch traced here: 680 us
  Pallas kernels  400 us (58%)
  starting transfers between devices  81.8 us (12%)
  local copies, waits for them, and re-layouts  61.8 us (9%)
  matrix products  53.5 us (8%)
  other arithmetic  45 us (7%)
  waiting for transfers between devices  34.9 us (5%)
    pallas_call x1, Pallas kernels, open_layer(): pl.pallas_call(open_kernel, in_specs=[V, V, V, V, V, V, V, ANY_SPEC, ANY_...  169 us
    pallas_call x1, Pallas kernels, close_layer(): pl.pallas_call(close_kernel, in_specs=[V] * 3, out_specs=[V] * 3, out_sha...  120 us
    pallas_call x1, Pallas kernels, back_layer(): pl.pallas_call(back_kernel, in_specs=[V] * len(early) + [ANY_SPEC] * (LAT...  96.6 us
    ppermute x33, starting transfers between devices, swap(): return lax.ppermute(v, 'fsdp', [(i, i ^ mask) for i in range(8)])  64.5 us
    dot_general x10, matrix products, t_dot(): lax.dot_general(a, b, (((0,), (0,)), ((), ())), preferred_element_type=jn...  38.5 us
    ppermute x33, waiting for transfers between devices, swap(): return lax.ppermute(v, 'fsdp', [(i, i ^ mask) for i in range(8)])  27.8 us
    pallas_call x1, Pallas kernels, attend_all(): pl.pallas_call(attend_kernel, grid=(CHIPS,), in_specs=[big, big, big, one...  14.5 us
  transfers between devices with their start and end apart: 41, of which 13 were waited for; matrix products, arithmetic and copies ran while one was open for 17% of the time, Pallas kernels for 45%

profile of v2, /device:TPU:0, one launch (start us, length us, event | category | flops | bytes accessed | tf_op | source)
XLA Modules:
  0.0 680.2 jit_solution(1499191849560562393)
XLA Ops:
  1.4 3.0 collective-permute-start.20
  13.2 168.9 %shard_map.222 = (f32[8,3072]{1,0:T(8,128)}, f32[8,1536]{1,0:T(8,128)}, bf16[4,128,1536]{2,1,0:T(8,128)(2,1)}, s32[4,8,128]{2,1,0:T(8,128)}, bf16[3,1536,384]{2,...) custom-call(bf16[8,1024]{1,0:T(8,128)(2,1)} %pad_maximum_fusion.12.c, ...), custom_call_target="tpu_custom_call" | custom-call | flops 10000000000 | bytes 400000000 | tf_op jit(solution)/shard_map/pallas_call | solution.py:922
  189.4 10.4 %bitcast_select_fusion.8 = (f32[128]{0:T(128)S(1)}, f32[128]{0:T(128)S(1)}) fusion(f32[]{:T(128)} %bitcast.31, f32[]{:T(128)} %bitcast.32, f32[]{:T(128)} %bitcast.33, f32[]{:T(128)} %bitcast.34, f32[]{:T(128)} %bitcast.35, f32[]{:T(128)} %bitcast.37, f32[]{:T(128)} %bitcast.36, f32[]{:T(128)} %bitcast.14, f32[]{:T(128)} %bitcast.16, f32[]{:T(128)} %bitcast.18, ...), kind=kLoop, calls=%fused_computation.119 | loop fusion | flops 7680 | bytes 1088 | tf_op jit(solution)/shard_map/gather | solution.py:1649
  201.1 1.8 sine_multiply_fusion
  202.9 14.5 %shard_map.223 = (bf16[512,384]{1,0:T(8,128)(2,1)}, f32[512,384]{1,0:T(8,128)}, bf16[512,384]{1,0:T(8,128)(2,1)}, bf16[512,384]{1,0:T(8,128)(2,1)}, bf16[1024,384]{1,0:T(8,128)(2,1)}) custom-call(f32[512,384]{1,0:T(8,128)} %get-tuple-element.57.q_ref.rest_8_, f32[512,384]{1,0:T(8,128)} %get-tuple-element.58.k_ref.rest_9_, ...), custom_call_target="tpu_custom_call" | custom-call | flops 603979776 | bytes 10000000 | tf_op jit(solution)/shard_map/pallas_call | solution.py:1575
  224.4 3.4 collective-permute-done.7
  237.9 1.9 concatenate.61
  241.4 2.6 collective-permute-start.25
  245.8 1.9 fusion.7
  254.0 6.0 concatenate.62
  260.0 2.1 slice_reduce_fusion.12
  262.8 7.6 %concatenate.63 = bf16[128,1024]{1,0:T(8,128)(2,1)} concatenate(bf16[4,1024]{1,0:T(4,128)(2,1)S(1)} %fusion.15, bf16[4,1024]{1,0:T(4,128)(2,1)S(1)} %collective-permute-done.20, bf16[4,1024]{1,0:T(4,128)(2,1)} %collective-permute-done.21, bf16[2,1024]{1,0:T(2,128)(2,1)} %collective-permute-done.22, bf16[2,1024]{1,0:T(2,128)(2,1)} %collective-permute-done.23, ...), dimensions={0} | concatenate | bytes 524288 | tf_op jit(solution)/shard_map/concatenate | solution.py:1767
  271.9 2.3 multiply_reduce_fusion
  276.4 7.1 %collective-permute-done.17 = bf16[2,192,1024]{2,1,0:T(8,128)(2,1)} collective-permute-done((bf16[2,192,1024]{2,1,0:T(8,128)(2,1)}, bf16[2,192,1024]{2,1,0:T(8,128)(2,1)}, u32[]{:S(2)}, u32[]{:S(2)}) %collective-permute-start.17) | collective-permute-done | bytes 786464 | tf_op jit(solution)/shard_map/ppermute | solution.py:316
  283.4 2.8 select_bitcast_fusion.5
  286.2 1.9 collective-permute-start.13
  288.0 2.2 collective-permute-start
  292.7 5.5 collective-permute-done.13
  300.1 2.3 collective-permute-start.15
  302.4 4.3 collective-permute-done.1
  310.7 2.1 collective-permute-done.2
  319.7 2.6 multiply_convert_fusion
  324.1 1.8 convolution_convert_fusion.4
  326.0 3.0 convolution_convert_fusion.5.fo_ref
  329.0 3.5 convolution_convert_fusion.2
  332.5 1.8 convolution_convert_fusion.3
  334.3 3.0 fusion.1.dh2_ref
  337.3 3.4 pad_maximum_fusion.rest_17_
  341.2 96.6 %shard_map.224 = (bf16[128,1536]{1,0:T(8,128)(2,1)}, f32[128,1536]{1,0:T(8,128)}, bf16[4,128,1536]{2,1,0:T(8,128)(2,1)}, bf16[512,384]{1,0:T(8,128)(2,1)}, bf16[...) custom-call(bf16[512,1536]{1,0:T(8,128)(2,1)} %fusion.1.dh2_ref, ...), custom_call_target="tpu_custom_call" | custom-call | flops 10000000000 | bytes 400000000 | tf_op jit(solution)/shard_map/pallas_call | solution.py:1511
  438.8 28.9 %collective-permute-start.28 = (bf16[4,6144]{1,0:T(4,128)(2,1)S(1)}, bf16[4,6144]{1,0:T(4,128)(2,1)S(1)}, u32[]{:S(2)}, u32[]{:S(2)}) collective-permute-start(bf16[4,6144]{1,0:T(4,128)(2,1)S(1)} %fusion.10), channel_id=1, source_target_pairs={{0,2},{1,3},{2,0},{3,1},{4,6},{5,7},{6,4},{7,5},{8,10},{9,11},{10,... | collective-permute-start | bytes 147464 | tf_op jit(solution)/shard_map/ppermute | solution.py:316
  470.3 8.2 %convolution_convert_fusion = bf16[4096,384]{1,0:T(8,128)(2,1)S(1)} fusion(bf16[1024,4096]{1,0:T(8,128)(2,1)} %bitcast.170, bf16[1024,384]{1,0:T(8,128)(2,1)} %get-tuple-element.79), kind=kOutput, calls=%fused_computation.4 | convolution fusion | flops 3222798336 | bytes 12320768 | tf_op jit(solution)/shard_map/dot_general | solution.py:476
  478.5 9.8 %convolution_convert_fusion.1 = bf16[4096,384]{1,0:T(8,128)(2,1)} fusion(bf16[1024,4096]{1,0:T(8,128)(2,1)} %bitcast.171, bf16[1024,384]{1,0:T(8,128)(2,1)S(1)} %copy-done.47), kind=kOutput, calls=%fused_computation.5 | convolution fusion | flops 3222798336 | bytes 12320768 | tf_op jit(solution)/shard_map/dot_general | solution.py:476
  488.3 2.0 convolution_convert_fusion.7
  490.3 2.0 convolution_convert_fusion.8
  492.4 2.1 collective-permute-start.30
  495.3 2.0 collective-permute-start.37
  500.6 5.5 collective-permute-start.32
  506.1 2.4 collective-permute-start.34
  508.4 3.5 convolution_convert_fusion.9
  515.1 7.0 %collective-permute-done.33 = bf16[16,6144]{1,0:T(8,128)(2,1)S(1)} collective-permute-done((bf16[16,6144]{1,0:T(8,128)(2,1)}, bf16[16,6144]{1,0:T(8,128)(2,1)S(1)}, u32[]{:S(2)}, u32[]{:S(2)}) %collective-permute-start.33) | collective-permute-done | bytes 196640 | tf_op jit(solution)/shard_map/ppermute | solution.py:1756
  522.1 6.1 concatenate.66
  528.2 3.6 convolution_convert_fusion.6
  532.7 4.2 collective-permute-start.39
  536.9 3.4 pad_maximum_fusion.1.text_g
  541.2 2.1 pad_maximum_fusion.2.attn_g
  543.3 120.1 %shard_map.225 = (f32[2,128,1536]{2,1,0:T(8,128)}, f32[3,48,1536]{2,1,0:T(8,128)}, f32[48,1536]{1,0:T(8,128)}) custom-call(bf16[2,4,4,2,128,384]{5,4,3,2,1,0:T(8,128)(2,1)} %pad_maximum_fusion.1.text_g, bf16[3,4,4,2,48,384]{5,4,3,2,1,0:T(8,128)(2,1)} %pad_maximum_fusion.2.attn_g, bf16[4,2,48,1536]{3,2,1,0:T(8,128)(2,1)} %bitcast.158), custom_call_target="tpu_custom_call" | custom-call | flops 1000000 | bytes 400000000 | tf_op jit(solution)/shard_map/pallas_call | solution.py:1229
  664.9 5.7 concatenate.67
  670.6 2.2 fusion.11
  (251 shorter events, 86.1 us)
Async XLA Ops:
  1.4 230.2 %collective-permute-start.20 = (bf16[4,1024]{1,0:T(4,128)(2,1)S(1)}, bf16[4,1024]{1,0:T(4,128)(2,1)S(1)}, u32[]{:S(2)}, u32[]{:S(2)}) collective-permute-start(bf16[4,1024]{1,0:T(4,128)(2,1)S(1)} %fusion.15), channel_id=1, source_target_pairs={{0,2},{1,3},{2,0},{3,1},{4,6},{5,7},{6,4},{7,5},{8,10},{9,11},{10,... | collective-permute-start | bytes 24584 | tf_op jit(solution)/shard_map/ppermute | solution.py:316
  4.4 228.3 %collective-permute-start.21 = (bf16[4,1024]{1,0:T(4,128)(2,1)S(1)}, bf16[4,1024]{1,0:T(4,128)(2,1)}, u32[]{:S(2)}, u32[]{:S(2)}) collective-permute-start(bf16[4,1024]{1,0:T(4,128)(2,1)S(1)} %fusion.15), channel_id=1, source_target_pairs={{0,4},{1,5},{2,6},{3,7},{4,0},{5,1},{6,2},{7,3},{8,12},{9,13},{10,... | collective-permute-start | bytes 24584 | tf_op jit(solution)/shard_map/ppermute | solution.py:316
  5.9 211.5 %collective-permute-start.5 = (bf16[192,1536]{1,0:T(8,128)(2,1)}, bf16[192,1536]{1,0:T(8,128)(2,1)S(1)}, u32[]{:S(2)}, u32[]{:S(2)}) collective-permute-start(bf16[192,1536]{1,0:T(8,128)(2,1)} %param.27), channel_id=1, source_target_pairs={{0,1},{1,0},{2,3},{3,2},{4,5},{5,4},{6,7},{7,6},{8,9},{9,8},{10,11... | collective-permute-start | bytes 1769480 | tf_op jit(solution)/shard_map/ppermute | solution.py:316
  202.9 14.5 %copy-start.22 = (bf16[192,1536]{1,0:T(8,128)(2,1)S(1)}, bf16[192,1536]{1,0:T(8,128)(2,1)}, u32[]{:S(2)}) copy-start(bf16[192,1536]{1,0:T(8,128)(2,1)} %param.27) | copy-start | bytes 1769476
  220.2 7.7 %collective-permute-start.7 = (bf16[64,1536]{1,0:T(8,128)(2,1)S(1)}, bf16[64,1536]{1,0:T(8,128)(2,1)S(1)}, u32[]{:S(2)}, u32[]{:S(2)}) collective-permute-start(bf16[64,1536]{1,0:T(8,128)(2,1)S(1)} %get-tuple-element.131), channel_id=1, source_target_pairs={{0,2},{1,3},{2,0},{3,1},{4,6},{5,7},{6,4},{7,5},{8,10},{9,11},{10,... | collective-permute-start | bytes 589832 | tf_op jit(solution)/shard_map/ppermute | solution.py:316
  221.5 22.5 %collective-permute-start.6 = (bf16[64,1536]{1,0:T(8,128)(2,1)S(1)}, bf16[64,1536]{1,0:T(8,128)(2,1)}, u32[]{:S(2)}, u32[]{:S(2)}) collective-permute-start(bf16[64,1536]{1,0:T(8,128)(2,1)S(1)} %get-tuple-element.128), channel_id=1, source_target_pairs={{0,2},{1,3},{2,0},{3,1},{4,6},{5,7},{6,4},{7,5},{8,10},{9,11},{10,... | collective-permute-start | bytes 589832 | tf_op jit(solution)/shard_map/ppermute | solution.py:316
  222.8 21.4 %collective-permute-start.10 = (bf16[64,1536]{1,0:T(8,128)(2,1)S(1)}, bf16[64,1536]{1,0:T(8,128)(2,1)}, u32[]{:S(2)}, u32[]{:S(2)}) collective-permute-start(bf16[64,1536]{1,0:T(8,128)(2,1)S(1)} %get-tuple-element.129), channel_id=1, source_target_pairs={{0,4},{1,5},{2,6},{3,7},{4,0},{5,1},{6,2},{7,3},{8,12},{9,13},{10,... | collective-permute-start | bytes 589832 | tf_op jit(solution)/shard_map/ppermute | solution.py:316
  228.6 17.2 %collective-permute-start.8 = (bf16[64,1536]{1,0:T(8,128)(2,1)}, bf16[64,1536]{1,0:T(8,128)(2,1)}, u32[]{:S(2)}, u32[]{:S(2)}) collective-permute-start(bf16[64,1536]{1,0:T(8,128)(2,1)} %fusion.6), channel_id=1, source_target_pairs={{0,4},{1,5},{2,6},{3,7},{4,0},{5,1},{6,2},{7,3},{8,12},{9,13},{10,... | collective-permute-start | bytes 589832 | tf_op jit(solution)/shard_map/ppermute | solution.py:316
  232.2 3.9 collective-permute-start.22
  233.9 3.9 collective-permute-start.23
  239.8 11.3 %collective-permute-start.24 = (bf16[16,1024]{1,0:T(8,128)(2,1)}, bf16[16,1024]{1,0:T(8,128)(2,1)}, u32[]{:S(2)}, u32[]{:S(2)}) collective-permute-start(bf16[16,1024]{1,0:T(8,128)(2,1)} %concatenate.61), channel_id=1, source_target_pairs={{0,8},{8,0},{16,24},{24,16},{1,9},{9,1},{17,25},{25,17},{2,10},{10... | collective-permute-start | bytes 98312 | tf_op jit(solution)/shard_map/ppermute | solution.py:1764
  241.4 11.0 %collective-permute-start.25 = (bf16[16,1024]{1,0:T(8,128)(2,1)}, bf16[16,1024]{1,0:T(8,128)(2,1)}, u32[]{:S(2)}, u32[]{:S(2)}) collective-permute-start(bf16[16,1024]{1,0:T(8,128)(2,1)} %concatenate.61), channel_id=1, source_target_pairs={{0,16},{8,24},{16,0},{24,8},{1,17},{9,25},{17,1},{25,9},{2,18},{10... | collective-permute-start | bytes 98312 | tf_op jit(solution)/shard_map/ppermute | solution.py:1764
  244.0 10.0 %collective-permute-start.26 = (bf16[16,1024]{1,0:T(8,128)(2,1)}, bf16[16,1024]{1,0:T(8,128)(2,1)}, u32[]{:S(2)}, u32[]{:S(2)}) collective-permute-start(bf16[16,1024]{1,0:T(8,128)(2,1)} %concatenate.61), channel_id=1, source_target_pairs={{0,24},{8,16},{16,8},{24,0},{1,25},{9,17},{17,9},{25,1},{2,26},{10... | collective-permute-start | bytes 98312 | tf_op jit(solution)/shard_map/ppermute | solution.py:1764
  244.2 26.3 %collective-permute-start.9 = (bf16[64,1536]{1,0:T(8,128)(2,1)}, bf16[64,1536]{1,0:T(8,128)(2,1)}, u32[]{:S(2)}, u32[]{:S(2)}) collective-permute-start(bf16[64,1536]{1,0:T(8,128)(2,1)} %get-tuple-element.130), channel_id=1, source_target_pairs={{0,4},{1,5},{2,6},{3,7},{4,0},{5,1},{6,2},{7,3},{8,12},{9,13},{10,... | collective-permute-start | bytes 589832 | tf_op jit(solution)/shard_map/ppermute | solution.py:316
  247.7 23.1 %collective-permute-start.11 = (bf16[64,1536]{1,0:T(8,128)(2,1)}, bf16[64,1536]{1,0:T(8,128)(2,1)}, u32[]{:S(2)}, u32[]{:S(2)}) collective-permute-start(bf16[64,1536]{1,0:T(8,128)(2,1)} %get-tuple-element.127), channel_id=1, source_target_pairs={{0,2},{1,3},{2,0},{3,1},{4,6},{5,7},{6,4},{7,5},{8,10},{9,11},{10,... | collective-permute-start | bytes 589832 | tf_op jit(solution)/shard_map/ppermute | solution.py:316
  251.1 25.2 %collective-permute-start.16 = (bf16[2,192,1024]{2,1,0:T(8,128)(2,1)}, bf16[2,192,1024]{2,1,0:T(8,128)(2,1)}, u32[]{:S(2)}, u32[]{:S(2)}) collective-permute-start(bf16[2,192,1024]{2,1,0:T(8,128)(2,1)} %get-tuple-element.125), channel_id=1, source_target_pairs={{0,6},{1,7},{2,4},{3,5},{4,2},{5,3},{6,0},{7,1},{8,14},{9,15},{10,... | collective-permute-start | bytes 2359304 | tf_op jit(solution)/shard_map/ppermute | solution.py:316
  252.4 31.0 %collective-permute-start.17 = (bf16[2,192,1024]{2,1,0:T(8,128)(2,1)}, bf16[2,192,1024]{2,1,0:T(8,128)(2,1)}, u32[]{:S(2)}, u32[]{:S(2)}) collective-permute-start(bf16[2,192,1024]{2,1,0:T(8,128)(2,1)} %get-tuple-element.124), channel_id=1, source_target_pairs={{0,4},{1,5},{2,6},{3,7},{4,0},{5,1},{6,2},{7,3},{8,12},{9,13},{10,... | collective-permute-start | bytes 2359304 | tf_op jit(solution)/shard_map/ppermute | solution.py:316
  260.0 2.1 collective-permute-start.27
  262.1 21.3 %collective-permute-start.18 = (bf16[2,192,1024]{2,1,0:T(8,128)(2,1)}, bf16[2,192,1024]{2,1,0:T(8,128)(2,1)}, u32[]{:S(2)}, u32[]{:S(2)}) collective-permute-start(bf16[2,192,1024]{2,1,0:T(8,128)(2,1)} %get-tuple-element.123), channel_id=1, source_target_pairs={{0,2},{1,3},{2,0},{3,1},{4,6},{5,7},{6,4},{7,5},{8,10},{9,11},{10,... | collective-permute-start | bytes 2359304 | tf_op jit(solution)/shard_map/ppermute | solution.py:316
  270.5 38.1 %collective-permute-start.4 = (bf16[512,1536]{1,0:T(8,128)(2,1)}, bf16[512,1536]{1,0:T(8,128)(2,1)S(1)}, u32[]{:S(2)}, u32[]{:S(2)}) collective-permute-start(bf16[512,1536]{1,0:T(8,128)(2,1)} %param.30), channel_id=1, source_target_pairs={{0,1},{1,0},{2,3},{3,2},{4,5},{5,4},{6,7},{7,6},{8,9},{9,8},{10,11... | collective-permute-start | bytes 4718600 | tf_op jit(solution)/shard_map/ppermute | solution.py:316
  275.0 16.2 %collective-permute-start.12 = (bf16[128,1536]{1,0:T(8,128)(2,1)S(1)}, bf16[128,1536]{1,0:T(8,128)(2,1)S(1)}, u32[]{:S(2)}, u32[]{:S(2)}) collective-permute-start(bf16[128,1536]{1,0:T(8,128)(2,1)S(1)} %get-tuple-element.146), channel_id=1, source_target_pairs={{0,2},{1,3},{2,0},{3,1},{4,6},{5,7},{6,4},{7,5},{8,10},{9,11},{10,... | collective-permute-start | bytes 1179656 | tf_op jit(solution)/shard_map/ppermute | solution.py:316
  286.2 12.1 %collective-permute-start.13 = (bf16[128,1536]{1,0:T(8,128)(2,1)S(1)}, bf16[128,1536]{1,0:T(8,128)(2,1)S(1)}, u32[]{:S(2)}, u32[]{:S(2)}) collective-permute-start(bf16[128,1536]{1,0:T(8,128)(2,1)S(1)} %get-tuple-element.146), channel_id=1, source_target_pairs={{0,4},{1,5},{2,6},{3,7},{4,0},{5,1},{6,2},{7,3},{8,12},{9,13},{10,... | collective-permute-start | bytes 1179656 | tf_op jit(solution)/shard_map/ppermute | solution.py:316
  288.0 12.0 %collective-permute-start = (bf16[128,1536]{1,0:T(8,128)(2,1)S(1)}, bf16[128,1536]{1,0:T(8,128)(2,1)S(1)}, u32[]{:S(2)}, u32[]{:S(2)}) collective-permute-start(bf16[128,1536]{1,0:T(8,128)(2,1)S(1)} %get-tuple-element.105), channel_id=1, source_target_pairs={{0,2},{1,3},{2,0},{3,1},{4,6},{5,7},{6,4},{7,5},{8,10},{9,11},{10,... | collective-permute-start | bytes 1179656 | tf_op jit(solution)/shard_map/ppermute | solution.py:316
  290.3 16.4 %collective-permute-start.1 = (bf16[128,1536]{1,0:T(8,128)(2,1)S(1)}, bf16[128,1536]{1,0:T(8,128)(2,1)S(1)}, u32[]{:S(2)}, u32[]{:S(2)}) collective-permute-start(bf16[128,1536]{1,0:T(8,128)(2,1)S(1)} %get-tuple-element.105), channel_id=1, source_target_pairs={{0,4},{1,5},{2,6},{3,7},{4,0},{5,1},{6,2},{7,3},{8,12},{9,13},{10,... | collective-permute-start | bytes 1179656 | tf_op jit(solution)/shard_map/ppermute | solution.py:316
  291.1 25.0 %collective-permute-start.19 = (bf16[2,4,192,1024]{3,2,1,0:T(8,128)(2,1)S(1)}, bf16[2,4,192,1024]{3,2,1,0:T(8,128)(2,1)S(1)}, u32[]{:S(2)}, u32[]{:S(2)}) collective-permute-start(bf16[2,4,192,1024]{3,2,1,0:T(8,128)(2,1)S(1)} %pad_maximum_fusion.5), channel_id=1, source_target_pairs={{0,1},{1,0},{2,3},{3,2},{4,5},{5,4},{6,7},{7,6},{8,9},{9,8},{10,11... | collective-permute-start | bytes 9437192 | tf_op jit(solution)/shard_map/ppermute | solution.py:316
  292.7 17.4 %copy-start.9 = (bf16[512,1536]{1,0:T(8,128)(2,1)S(1)}, bf16[512,1536]{1,0:T(8,128)(2,1)}, u32[]{:S(2)}) copy-start(bf16[512,1536]{1,0:T(8,128)(2,1)} %param.30) | copy-start | bytes 4718596
  298.2 12.4 %collective-permute-start.14 = (bf16[64,1536]{1,0:T(8,128)(2,1)S(1)}, bf16[64,1536]{1,0:T(8,128)(2,1)S(1)}, u32[]{:S(2)}, u32[]{:S(2)}) collective-permute-start(bf16[64,1536]{1,0:T(8,128)(2,1)S(1)} %slice.275), channel_id=1, source_target_pairs={{0,4},{1,5},{2,6},{3,7},{4,0},{5,1},{6,2},{7,3},{8,12},{9,13},{10,... | collective-permute-start | bytes 589832 | tf_op jit(solution)/shard_map/ppermute | solution.py:316
  300.1 10.6 %collective-permute-start.15 = (bf16[64,1536]{1,0:T(8,128)(2,1)S(1)}, bf16[64,1536]{1,0:T(8,128)(2,1)S(1)}, u32[]{:S(2)}, u32[]{:S(2)}) collective-permute-start(bf16[64,1536]{1,0:T(8,128)(2,1)S(1)} %slice.276), channel_id=1, source_target_pairs={{0,2},{1,3},{2,0},{3,1},{4,6},{5,7},{6,4},{7,5},{8,10},{9,11},{10,... | collective-permute-start | bytes 589832 | tf_op jit(solution)/shard_map/ppermute | solution.py:316
  306.7 6.1 collective-permute-start.2
  308.6 5.7 collective-permute-start.3
  438.8 59.7 %copy-start.14 = (bf16[4,6144]{1,0:T(4,128)(2,1)}, bf16[4,6144]{1,0:T(4,128)(2,1)S(1)}, u32[]{:S(2)}) copy-start(bf16[4,6144]{1,0:T(4,128)(2,1)S(1)} %fusion.10) | copy-start | bytes 147460
  438.8 53.5 %collective-permute-start.28 = (bf16[4,6144]{1,0:T(4,128)(2,1)S(1)}, bf16[4,6144]{1,0:T(4,128)(2,1)S(1)}, u32[]{:S(2)}, u32[]{:S(2)}) collective-permute-start(bf16[4,6144]{1,0:T(4,128)(2,1)S(1)} %fusion.10), channel_id=1, source_target_pairs={{0,2},{1,3},{2,0},{3,1},{4,6},{5,7},{6,4},{7,5},{8,10},{9,11},{10,... | collective-permute-start | bytes 147464 | tf_op jit(solution)/shard_map/ppermute | solution.py:316
  467.7 26.7 %collective-permute-start.29 = (bf16[4,6144]{1,0:T(4,128)(2,1)S(1)}, bf16[4,6144]{1,0:T(4,128)(2,1)S(1)}, u32[]{:S(2)}, u32[]{:S(2)}) collective-permute-start(bf16[4,6144]{1,0:T(4,128)(2,1)S(1)} %fusion.10), channel_id=1, source_target_pairs={{0,4},{1,5},{2,6},{3,7},{4,0},{5,1},{6,2},{7,3},{8,12},{9,13},{10,... | collective-permute-start | bytes 147464 | tf_op jit(solution)/shard_map/ppermute | solution.py:316
  470.2 24.4 %collective-permute-start.36 = (f32[10,1536]{1,0:T(8,128)S(1)}, f32[10,1536]{1,0:T(8,128)S(1)}, u32[]{:S(2)}, u32[]{:S(2)}) collective-permute-start(f32[10,1536]{1,0:T(8,128)S(1)} %pad_maximum_fusion.11), channel_id=1, source_target_pairs={{0,1},{1,0},{2,3},{3,2},{4,5},{5,4},{6,7},{7,6},{8,9},{9,8},{10,11... | collective-permute-start | bytes 184328 | tf_op jit(solution)/shard_map/ppermute | solution.py:316
  492.4 4.9 collective-permute-start.30
  494.5 4.0 collective-permute-start.31
  495.3 16.6 %collective-permute-start.37 = (f32[10,1536]{1,0:T(8,128)}, f32[10,1536]{1,0:T(8,128)}, u32[]{:S(2)}, u32[]{:S(2)}) collective-permute-start(f32[10,1536]{1,0:T(8,128)} %fusion.25), channel_id=1, source_target_pairs={{0,2},{1,3},{2,0},{3,1},{4,6},{5,7},{6,4},{7,5},{8,10},{9,11},{10,... | collective-permute-start | bytes 184328 | tf_op jit(solution)/shard_map/ppermute | solution.py:316
  500.6 14.5 %collective-permute-start.32 = (bf16[16,6144]{1,0:T(8,128)(2,1)}, bf16[16,6144]{1,0:T(8,128)(2,1)S(1)}, u32[]{:S(2)}, u32[]{:S(2)}) collective-permute-start(bf16[16,6144]{1,0:T(8,128)(2,1)} %concatenate.65), channel_id=1, source_target_pairs={{0,8},{8,0},{16,24},{24,16},{1,9},{9,1},{17,25},{25,17},{2,10},{10... | collective-permute-start | bytes 589832 | tf_op jit(solution)/shard_map/ppermute | solution.py:1756
  506.1 16.0 %collective-permute-start.33 = (bf16[16,6144]{1,0:T(8,128)(2,1)}, bf16[16,6144]{1,0:T(8,128)(2,1)S(1)}, u32[]{:S(2)}, u32[]{:S(2)}) collective-permute-start(bf16[16,6144]{1,0:T(8,128)(2,1)} %concatenate.65), channel_id=1, source_target_pairs={{0,16},{8,24},{16,0},{24,8},{1,17},{9,25},{17,1},{25,9},{2,18},{10... | collective-permute-start | bytes 589832 | tf_op jit(solution)/shard_map/ppermute | solution.py:1756
  506.1 16.0 %collective-permute-start.34 = (bf16[16,6144]{1,0:T(8,128)(2,1)}, bf16[16,6144]{1,0:T(8,128)(2,1)}, u32[]{:S(2)}, u32[]{:S(2)}) collective-permute-start(bf16[16,6144]{1,0:T(8,128)(2,1)} %concatenate.65), channel_id=1, source_target_pairs={{0,24},{8,16},{16,8},{24,0},{1,25},{9,17},{17,9},{25,1},{2,26},{10... | collective-permute-start | bytes 589832 | tf_op jit(solution)/shard_map/ppermute | solution.py:1756
  513.5 18.2 %collective-permute-start.38 = (f32[10,1536]{1,0:T(8,128)}, f32[10,1536]{1,0:T(8,128)}, u32[]{:S(2)}, u32[]{:S(2)}) collective-permute-start(f32[10,1536]{1,0:T(8,128)} %add.198), channel_id=1, source_target_pairs={{0,4},{1,5},{2,6},{3,7},{4,0},{5,1},{6,2},{7,3},{8,12},{9,13},{10,... | collective-permute-start | bytes 184328 | tf_op jit(solution)/shard_map/ppermute | solution.py:316
  528.2 136.7 %collective-permute-start.35 = (bf16[64,6144]{1,0:T(8,128)(2,1)}, bf16[64,6144]{1,0:T(8,128)(2,1)}, u32[]{:S(2)}, u32[]{:S(2)}) collective-permute-start(bf16[64,6144]{1,0:T(8,128)(2,1)} %concatenate.66), channel_id=1, source_target_pairs={{0,1},{1,0},{2,3},{3,2},{4,5},{5,4},{6,7},{7,6},{8,9},{9,8},{10,11... | collective-permute-start | bytes 2359304 | tf_op jit(solution)/shard_map/ppermute | solution.py:316
  532.7 7.7 %collective-permute-start.39 = (f32[10,1536]{1,0:T(8,128)S(1)}, f32[10,1536]{1,0:T(8,128)S(1)}, u32[]{:S(2)}, u32[]{:S(2)}) collective-permute-start(f32[10,1536]{1,0:T(8,128)S(1)} %add.199), channel_id=1, source_target_pairs={{0,8},{8,0},{16,24},{24,16},{1,9},{9,1},{17,25},{25,17},{2,10},{10... | collective-permute-start | bytes 184328 | tf_op jit(solution)/shard_map/ppermute | solution.py:1745
  540.4 123.1 %collective-permute-start.40 = (f32[10,1536]{1,0:T(8,128)S(1)}, f32[10,1536]{1,0:T(8,128)S(1)}, u32[]{:S(2)}, u32[]{:S(2)}) collective-permute-start(f32[10,1536]{1,0:T(8,128)S(1)} %add.200), channel_id=1, source_target_pairs={{0,16},{8,24},{16,0},{24,8},{1,17},{9,25},{17,1},{25,9},{2,18},{10... | collective-permute-start | bytes 184328 | tf_op jit(solution)/shard_map/ppermute | solution.py:1746
  543.3 121.6 %copy-start.15 = (bf16[4,6144]{1,0:T(4,128)(2,1)S(1)}, bf16[4,6144]{1,0:T(4,128)(2,1)}, u32[]{:S(2)}) copy-start(bf16[4,6144]{1,0:T(4,128)(2,1)} %copy-done.14) | copy-start | bytes 147460
  543.3 121.6 %copy-start.19 = (bf16[4,6144]{1,0:T(4,128)(2,1)S(1)}, bf16[4,6144]{1,0:T(4,128)(2,1)}, u32[]{:S(2)}) copy-start(bf16[4,6144]{1,0:T(4,128)(2,1)} %copy-done.18) | copy-start | bytes 147460
  543.3 121.6 %copy-start.21 = (bf16[4,6144]{1,0:T(4,128)(2,1)S(1)}, bf16[4,6144]{1,0:T(4,128)(2,1)}, u32[]{:S(2)}) copy-start(bf16[4,6144]{1,0:T(4,128)(2,1)} %copy-done.20) | copy-start | bytes 147460
  543.3 121.6 %copy-start.28 = (bf16[2,6144]{1,0:T(2,128)(2,1)S(1)}, bf16[2,6144]{1,0:T(2,128)(2,1)}, u32[]{:S(2)}) copy-start(bf16[2,6144]{1,0:T(2,128)(2,1)} %copy-done.27) | copy-start | bytes 73732
  (41 other events, 170.7 us)

commit v3 on v2

--- a/solution.py
+++ b/solution.py
@@ -328,15 +328,6 @@
     return swap(v, 1)
 
 
-def reorder(parts, index):
-    bit = 1
-    while bit < len(parts):
-        odd = (index // bit) % 2 == 1
-        parts = [jnp.where(odd, parts[j ^ bit], parts[j]) for j in range(len(parts))]
-        bit *= 2
-    return parts
-
-
 def gather4(v):
     half = v.shape[0] // 2
     by_x = at_x(v)
@@ -345,116 +336,9 @@
     return [v, by_x, by_y, far]
 
 
-def reduce4(parts):
-    half = parts[0].shape[0] // 2
-    low = jnp.bfloat16
-    far_x = at_x(parts[3][:half].astype(low))
-    far_y = at_y(parts[3][half:].astype(low))
-    from_xa = at_x(parts[1][:half].astype(low))
-    from_yb = at_y(parts[2][half:].astype(low))
-    from_ya = at_y((parts[2][:half] + far_x.astype(jnp.float32)).astype(low))
-    from_xb = at_x((parts[1][half:] + far_y.astype(jnp.float32)).astype(low))
-    top = parts[0][:half] + from_xa.astype(jnp.float32) + from_ya.astype(jnp.float32)
-    bottom = parts[0][half:] + from_yb.astype(jnp.float32) + from_xb.astype(jnp.float32)
-    return jnp.concatenate([top, bottom], axis=0)
-
-
-def exchange4(pick):
-    return [pick(0), at_x(pick(1)), at_y(pick(2)), swap(pick(3), 6)]
-
-
 def sum4(v):
     v = v + at_x(v)
     return v + at_y(v)
-
-
-def sum4_rows(v):
-    rows = v.reshape(CHIPS, -1)
-    rows = rows + jnp.stack([at_x(rows)[j ^ 1] for j in range(CHIPS)])
-    rows = rows + jnp.stack([at_y(rows)[j ^ 2] for j in range(CHIPS)])
-    return rows.reshape(-1)
-
-
-def both_cores(mine, core, axis):
-    other = at_core(mine)
-    first = jnp.where(core == 0, mine, other)
-    second = jnp.where(core == 0, other, mine)
-    return first, second
-
-
-def column_weights(shard, chip, core, width):
-    count, rows, _ = shard.shape
-    got = exchange4(
-        lambda j: lax.dynamic_slice_in_dim(shard, jnp.bitwise_xor(chip, j) * width, width, axis=2)
-    )
-    mine = jnp.stack(reorder(got, chip), axis=1)
-    first, second = both_cores(mine, core, 0)
-    return jnp.stack([first, second], axis=2).reshape(count, 8 * rows, width)
-
-
-def row_weights(shard, core):
-    first, second = both_cores(shard, core, 0)
-    return jnp.concatenate([first, second], axis=0)
-
-
-def core_half(view, core, axis):
-    low = jnp.bfloat16
-    keep = lax.dynamic_index_in_dim(view, core, axis, keepdims=False)
-    give = lax.dynamic_index_in_dim(view, 1 - core, axis, keepdims=False)
-    return keep + at_core(give.astype(low)).astype(jnp.float32)
-
-
-def reduce_buckets(view, plane):
-    low = jnp.bfloat16
-    size = view.shape[0]
-    up = down = None
-    for step in range(1, size):
-        piece = lax.dynamic_index_in_dim(
-            view, jnp.minimum(plane + size - step, size - 1), 0, keepdims=False
-        )
-        if up is not None:
-            piece = piece + up.astype(jnp.float32)
-        up = lax.ppermute(piece.astype(low), "bucket", [(i, i + 1) for i in range(step)])
-        piece = lax.dynamic_index_in_dim(
-            view, jnp.maximum(plane - size + step, 0), 0, keepdims=False
-        )
-        if down is not None:
-            piece = piece + down.astype(jnp.float32)
-        down = lax.ppermute(
-            piece.astype(low), "bucket", [(size - 1 - i, size - 2 - i) for i in range(step)]
-        )
-    own = lax.dynamic_index_in_dim(view, plane, 0, keepdims=False)
-    return own + up.astype(jnp.float32) + down.astype(jnp.float32)
-
-
-def to_column_owner(block, chip):
-    got = exchange4(
-        lambda j: lax.dynamic_index_in_dim(
-            block, jnp.bitwise_xor(chip, j), 0, keepdims=False
-        ).astype(jnp.bfloat16)
-    )
-    return jnp.concatenate(reorder(got, chip), axis=-1).astype(jnp.float32)
-
-
-def to_row_owner(block):
-    pairs = [
-        (a * 8 + b * 2 + k, b * 8 + a * 2 + k) for a in range(4) for b in range(4) for k in range(2)
-    ]
-    return lax.ppermute(block.astype(jnp.bfloat16), ("bucket", "fsdp"), pairs).astype(jnp.float32)
-
-
-def column_grad(partial, chip, core, plane):
-    count, rows, width = partial.shape
-    view = partial.reshape(count, 4, 4, 2, rows // 32, width)
-    half = core_half(view, core, 3)
-    mine = reduce_buckets(jnp.transpose(half, (1, 0, 2, 3, 4)), plane)
-    return to_column_owner(jnp.transpose(mine, (1, 0, 2, 3)), chip)
-
-
-def row_grad(partial, core, plane):
-    rows, width = partial.shape
-    half = core_half(partial.reshape(4, 2, rows // 8, width), core, 1)
-    return to_row_owner(reduce_buckets(half, plane))
 
 
 def partner(u):
@@ -498,7 +382,7 @@
     q_ref, k_ref, v_ref, iq_ref, ik_ref, cos_ref, sin_ref, tk_ref, it_ref, tv_ref, sc_ref, sr_ref,
     g_ref, comb_ref, cross_ref, qr_ref, kr_ref, tr_ref,
 ):
-    same, mine = masks_of(sc_ref[...], sr_ref[0], tk_ref.shape[0])
+    same, mine = masks_of(sc_ref[...], sr_ref[...], tk_ref.shape[0])
     cosine = cos_ref[...]
     sine = sin_ref[...]
     low = jnp.bfloat16
@@ -620,6 +504,7 @@
         pl.semaphore_wait(sem, len(masks))
 
     def send(self, src, dst, mask):
+        assert self.count < self.send_sems.shape[0]
         copy = pltpu.make_async_remote_copy(
             src_ref=src,
             dst_ref=dst,
@@ -708,14 +593,43 @@
     return jnp.where(lax.broadcasted_iota(jnp.int32, got.shape, 0) < 4, got, one(b))
 
 
+def spread(net, src, dst, width, local):
+    count, rows, _ = src.shape
+
+    def cut(i, c):
+        return src.at[i, :, pl.ds(pl.multiple_of(c * width, 128), width)]
+
+    def put(i, f):
+        return dst.at[pl.ds(pl.multiple_of(f * rows, rows), rows), pl.ds(i * width, width)]
+
+    chip = net.me // 2
+    ids = range(count)
+    here = [local(cut(i, chip), put(i, net.me)) for i in ids]
+    core = [net.send(cut(i, chip), put(i, net.me), 1) for i in ids]
+
+    def away(m):
+        return [net.send(cut(i, net.peer(m) // 2), put(i, net.me), m) for i in ids]
+
+    def whole(f):
+        return dst.at[pl.ds(pl.multiple_of(f * rows, rows), rows), :]
+
+    def pass_on(copies, m):
+        for c in copies:
+            c.wait_recv()
+        return net.send(whole(net.peer(m)), whole(net.peer(m)), 1)
+
+    return here, core, away, pass_on
+
+
 ALL_PEERS = (1, 2, 3, 4, 5, 6, 7)
 
 
 def open_kernel(
     cond_ref, gain_ref, bias_ref, ada_ref, tok_ref, seg_ref, idx_ref, attn_ref, textw_ref, text_ref,
-    mod_ref, gains_ref, h_ref, idxs_ref, aw_ref, ta_ref, q_ref, k_ref, v_ref, tk_ref, tv_ref,
+    mod_ref, gains_ref, h_ref, idxs_ref, aw_ref, ta_out, q_ref, k_ref, v_ref, tk_ref, tv_ref,
     iqk_ref, it_ref,
-    conds, parts, mods, gbuf, tw_ref, sums, tsums, local_sems, send_sems, recv_sems,
+    conds, parts, mods, gbuf, tw_ref, ta_ref, sums, tsums, local_sems, out_sems, send_sems,
+    recv_sems,
 ):
     low = jnp.bfloat16
     full = jnp.float32
@@ -737,19 +651,6 @@
     iwaits = [net.send(idx_ref, idxs_ref.at[i], m) for i, m in ((1, 2), (2, 4), (3, 6))]
     idxs_ref[0] = idx_ref[...]
 
-    def spread(src, dst, rows, width, sem):
-        def cut(c):
-            return src.at[:, :, pl.ds(pl.multiple_of(c * width, 128), width)]
-
-        def put(f):
-            return dst.at[:, pl.ds(pl.multiple_of(f * rows, rows), rows), :]
-
-        here = pltpu.make_async_copy(cut(chip), put(me), sem)
-        here.start()
-        core = net.send(cut(chip), put(me), 1)
-        away = [net.send(cut(net.peer(m) // 2), put(me), m) for m in (2, 4, 6)]
-        return here, core, away, put
-
     for w in waits:
         w.wait_recv()
     lhs = jnp.concatenate([conds[m] for m in range(8)], axis=0).astype(low)
@@ -770,8 +671,21 @@
 
     lax.fori_loop(0, half_cols // step, mod_cols, 0)
     waits = [net.send(parts.at[m], mods.at[m], m) for m in ALL_PEERS]
-    attn_io = spread(attn_ref, aw_ref, attn_ref.shape[1], HW, local_sems.at[0])
-    text_io = spread(textw_ref, tw_ref, textw_ref.shape[1], HW, local_sems.at[1])
+
+    def local(slot):
+        def go(src, dst):
+            copy = pltpu.make_async_copy(src, dst, local_sems.at[slot[0]])
+            slot[0] += 1
+            copy.start()
+            return copy
+
+        return go
+
+    slot = [3]
+    attn_io = spread(net, attn_ref, aw_ref, HW, local(slot))
+    attn_away = [attn_io[2](m) for m in (2, 4, 6)]
+    text_io = spread(net, textw_ref, tw_ref, HW, local(slot))
+    text_away = [text_io[2](m) for m in (2, 4, 6)]
     own_text = pltpu.make_async_copy(text_ref, ta_ref.at[0], local_sems.at[2])
     own_text.start()
     for w in gwaits:
@@ -806,18 +720,22 @@
     lax.fori_loop(0, ROW // block, first_norm, 0)
     hx, hy = share4_start(net, h_ref)
 
-    def pass_on(io):
-        here, core, away, put = io
-        here.wait()
-        return [core] + [
-            (c.wait_recv(), net.send(put(net.peer(m)), put(net.peer(m)), 1))[1]
-            for c, m in zip(away, (2, 4, 6))
-        ]
-
-    attn_core = pass_on(attn_io)
-    text_core = pass_on(text_io)
+    def all_in(io, away):
+        for c in io[0]:
+            c.wait()
+        return io[1] + [io[3](c, m) for c, m in zip(away, (2, 4, 6))]
+
+    attn_core = all_in(attn_io, attn_away)
+    text_core = all_in(text_io, text_away)
     h_far = share4_relay(net, h_ref, hx, hy)
     own_text.wait()
+
+    def keep(j):
+        copy = pltpu.make_async_copy(ta_ref.at[j], ta_out.at[j], out_sems.at[j])
+        copy.start()
+        return copy
+
+    kept = [keep(0)]
     chunks = 4
     size = ta_ref.shape[1] // chunks
     tx, ty = [None] * chunks, [None] * chunks
@@ -836,11 +754,11 @@
     for j in range(CHIPS):
         h = h_ref[j]
         at = pl.ds(j * ROW, ROW)
-        qv = jnp.dot(h, aw_ref[0], preferred_element_type=full)
+        qv = jnp.dot(h, aw_ref[:, :HW], preferred_element_type=full)
         q_ref[at, :] = qv
-        kv = jnp.dot(h, aw_ref[1], preferred_element_type=full)
+        kv = jnp.dot(h, aw_ref[:, HW : 2 * HW], preferred_element_type=full)
         k_ref[at, :] = kv
-        v_ref[at, :] = jnp.dot(h, aw_ref[2], preferred_element_type=full).astype(low)
+        v_ref[at, :] = jnp.dot(h, aw_ref[:, 2 * HW :], preferred_element_type=full).astype(low)
         sums[0, :, at] = row_sums(qv * qv, kv * kv)
     sum_io = [net.send(sums.at[0], sums.at[i], m) for i, m in ((1, 2), (2, 4), (3, 6))]
 
@@ -853,13 +771,10 @@
         def body(i, acc):
             at = pl.ds(pl.multiple_of(i * kt, kt), kt)
             rows = ta_ref[j, pl.ds(lo, count), at]
-            return (
-                acc[0] + jnp.dot(rows, tw_ref[0, at, :], preferred_element_type=full),
-                acc[1] + jnp.dot(rows, tw_ref[1, at, :], preferred_element_type=full),
-            )
-
-        zero = jnp.zeros((count, HW), full)
-        keys, vals = lax.fori_loop(0, TXTD_OF(ta_ref) // kt, body, (zero, zero))
+            return acc + jnp.dot(rows, tw_ref[at, :], preferred_element_type=full)
+
+        both = lax.fori_loop(0, ta_ref.shape[2] // kt, body, jnp.zeros((count, 2 * HW), full))
+        keys, vals = both[:, :HW], both[:, HW:]
         at = pl.ds(j * ta_ref.shape[1] + lo, count)
         tk_ref[at, :] = keys
         tv_ref[at, :] = vals.astype(low)
@@ -890,10 +805,12 @@
     for s in range(chunks // 2):
         tx[s + chunks // 2].wait_recv()
         ty[s].wait_recv()
+    kept += [keep(1), keep(2)]
     text_rows(1, half, half)
     text_rows(2, 0, half)
     for c in relays:
         c.wait_recv()
+    kept.append(keep(3))
     for lo in (0, half):
         text_rows(3, lo, half)
     sum_io = [net.send(tsums.at[0], tsums.at[i], m) for i, m in ((1, 2), (2, 4), (3, 6))]
@@ -906,11 +823,9 @@
         it_ref[:, pl.ds(j * cap, cap)] = lax.rsqrt(total / D + EPS)
     for c in iwaits:
         c.wait_recv()
+    for c in kept:
+        c.wait()
     net.close()
-
-
-def TXTD_OF(ref):
-    return ref.shape[2]
 
 
 def open_layer(cond8, gain_pad, bias_pad, ada, tok, seg_col, idx, attn, textw, text):
@@ -922,13 +837,13 @@
     return pl.pallas_call(
         open_kernel,
         in_specs=[V, V, V, V, V, V, V, ANY_SPEC, ANY_SPEC, ANY_SPEC],
-        out_specs=[V] * 13,
+        out_specs=[V] * 5 + [ANY_SPEC] + [V] * 7,
         out_shape=[
             shape((8, 3072), full),
             shape((8, D), full),
             shape((CHIPS, ROW, D), low),
             shape((CHIPS, 8, ROW), jnp.int32),
-            shape((3, D, HW), low),
+            shape((D, 3 * HW), low),
             shape((CHIPS, cap, txtd), low),
             shape((CHIPS * ROW, HW), full),
             shape((CHIPS * ROW, HW), full),
@@ -943,11 +858,13 @@
             pltpu.VMEM((8, 8, 3072), full),
             pltpu.VMEM((8, 8, 3072), full),
             pltpu.VMEM((9, 8, D), full),
-            pltpu.VMEM((2, txtd, HW), low),
+            pltpu.VMEM((txtd, 2 * HW), low),
+            pltpu.VMEM((CHIPS, cap, txtd), low),
             pltpu.VMEM((CHIPS, 8, CHIPS * ROW), full),
             pltpu.VMEM((CHIPS, 8, CHIPS * cap), full),
-            pltpu.SemaphoreType.DMA((3,)),
-            *net_scratch(64),
+            pltpu.SemaphoreType.DMA((8,)),
+            pltpu.SemaphoreType.DMA((CHIPS,)),
+            *net_scratch(80),
         ],
         compiler_params=pltpu.CompilerParams(
             collective_id=1, has_side_effects=True, vmem_limit_bytes=56 * 1024 * 1024
@@ -1097,6 +1014,8 @@
         net = self.net
         chip = net.me // 2
         n, _, rows, width = self.total.shape
+        parts = self.wide.shape[0]
+        width = width // parts
         at = pl.ds(pl.multiple_of(chip * width, width), width)
 
         def cast(i, _):
@@ -1105,11 +1024,16 @@
 
         lax.fori_loop(0, n * 4, cast, 0)
         self.copies = [
-            net.send(self.stage.at[:, net.peer(m) // 2], self.wide.at[:, :, at], m)
+            net.send(
+                self.stage.at[0, net.peer(m) // 2, :, pl.ds(i * width, width)],
+                self.wide.at[i, :, at],
+                m,
+            )
             for m in (2, 4, 6)
+            for i in range(parts)
         ]
-        for i in range(n):
-            self.wide[i, :, at] = self.stage[i, chip]
+        for i in range(parts):
+            self.wide[i, :, at] = self.stage[0, chip, :, i * width : i * width + width]
 
     def finish(self):
         for c in self.copies:
@@ -1223,8 +1147,8 @@
     full = jnp.float32
     shape = jax.ShapeDtypeStruct
     V = VMEM_SPEC
-    tr, tw = text_g.shape[-2:]
-    ar, aw = attn_g.shape[-2:]
+    tr, tw = text_g.shape[-2], text_g.shape[-1] // 2
+    ar, aw = attn_g.shape[-2], attn_g.shape[-1] // 3
     orow, ow = out_g.shape[-2:]
     return pl.pallas_call(
         close_kernel,
@@ -1236,17 +1160,17 @@
             shape((orow, ow), full),
         ],
         scratch_shapes=[
-            *chain_scratch(True, (2, tr), tw),
-            *chain_scratch(True, (3, ar), aw),
+            *chain_scratch(True, (1, tr), 2 * tw),
+            *chain_scratch(True, (1, ar), 3 * aw),
             *chain_scratch(False, orow, ow),
             pltpu.VMEM((2, tr, 4 * tw), low),
             pltpu.VMEM((3, ar, 4 * aw), low),
-            pltpu.VMEM((2, 4, tr, tw), low),
-            pltpu.VMEM((3, 4, ar, aw), low),
+            pltpu.VMEM((1, 4, tr, 2 * tw), low),
+            pltpu.VMEM((1, 4, ar, 3 * aw), low),
             pltpu.VMEM((orow, ow), low),
             pltpu.VMEM((orow, ow), low),
             pltpu.SemaphoreType.DMA((2,)),
-            *net_scratch(16),
+            *net_scratch(32),
         ],
         compiler_params=pltpu.CompilerParams(
             collective_id=2, has_side_effects=True, vmem_limit_bytes=63 * 1024 * 1024
@@ -1284,7 +1208,7 @@
     dh2_ref, fo_ref, x1_ref, branch_ref, cot_ref, w_ref, mod_ref, seg_ref, gain_ref, tok_ref,
     ow_ref, aw_ref, qr_ref, kr_ref, v_ref, tr_ref, tv_ref, cross_ref, q_ref, k_ref, tk_ref,
     iq_ref, ik_ref, it_ref, cos_ref, sin_ref, sc_ref, sr_ref, gs_ref, ffn_g, down_g,
-    block_o, token_o, db_ref, dq_o, dk_o, dv_o, dt_o, dtv_o, dmod_o, gg_o, gs_o, ffn_o, down_o,
+    block_o, token_o, db_ref, dqkv_o, dtkv_o, dmod_o, gg_o, gs_o, ffn_o, down_o,
     dx_s, dc_s, dqf, dkf, dtf, part_s, sums, tsums, buf_a, far_a, buf_b, far_b, buf_c, far_c,
     fm, fa, ft, fs, dm, da, dt_c, ds_, f_wide, f_stage, d_stage, d_got, d_sem,
     f_keep, d_keep, keep_sem, send_sems, recv_sems, loads,
@@ -1392,7 +1316,7 @@
             dc_s, cross_ref.at[rows], q_ref.at[rows], k_ref.at[rows], tk_ref.at[text],
             iq_ref.at[rows], ik_ref.at[rows], it_ref.at[text], cos_ref.at[rows], sin_ref.at[rows],
             sc_ref.at[rows], sr_ref.at[j], gs_ref,
-            dqv, dkv, dv_o.at[rows], dtv, dtv_o.at[text], gs_o,
+            dqv, dkv, dqkv_o.at[rows, pl.ds(2 * HW, HW)], dtv, dtkv_o.at[text, pl.ds(HW, HW)], gs_o,
         )
         sums[0, :, rows] = row_sums(
             dqv[...] * (q_ref[rows, :] * iq_ref[rows, :]),
@@ -1432,21 +1356,17 @@
             words = words + tsums[i, :, pl.ds((j ^ i) * cap, cap)]
         mean = jnp.transpose(total / D)
         iq, ik, it = iq_ref[rows, :], ik_ref[rows, :], it_ref[text, :]
-        dq_o[rows, :] = (iq * (dqf[rows, :] - q_ref[rows, :] * iq * mean[:, 0:1])).astype(low)
-        dk_o[rows, :] = (ik * (dkf[rows, :] - k_ref[rows, :] * ik * mean[:, 4:5])).astype(low)
+        dqkv_o[rows, :HW] = (iq * (dqf[rows, :] - q_ref[rows, :] * iq * mean[:, 0:1])).astype(low)
+        dqkv_o[rows, HW : 2 * HW] = (ik * (dkf[rows, :] - k_ref[rows, :] * ik * mean[:, 4:5])).astype(low)
         mean = jnp.transpose(words / D)
-        dt_o[text, :] = (it * (dtf[text, :] - tk_ref[text, :] * it * mean[:, 0:1])).astype(low)
+        dtkv_o[text, :HW] = (it * (dtf[text, :] - tk_ref[text, :] * it * mean[:, 0:1])).astype(low)
 
     lax.fori_loop(0, ROW // block, block_rows, 0)
     wide = 256
 
     def first_grad(n, _):
         at = pl.ds(pl.multiple_of(n * wide, wide), wide)
-        part_s[:, at] = (
-            dot_t(dq_o[...], aw_ref[0, at, :])
-            + dot_t(dk_o[...], aw_ref[1, at, :])
-            + dot_t(dv_o[...], aw_ref[2, at, :])
-        )
+        part_s[:, at] = dot_t(dqkv_o[...], aw_ref[at, :])
         return 0
 
     lax.fori_loop(0, D // wide, first_grad, 0)
@@ -1504,23 +1424,20 @@
     shape = jax.ShapeDtypeStruct
     V = VMEM_SPEC
     cap = IMGS * TXT
-    fr, fw = ffn_g.shape[-2:]
+    fr, fw = ffn_g.shape[-2], ffn_g.shape[-1] // 2
     dr, dw = down_g.shape[-2:]
     tok = CHIPS * ROW
     reduce_scratch = [pltpu.VMEM((5, ROW, D), low), pltpu.VMEM((2, ROW // 2, D), low)]
     return pl.pallas_call(
         back_kernel,
         in_specs=[V] * len(early) + [ANY_SPEC] * (LATE + 2),
-        out_specs=[V] * 13,
+        out_specs=[V] * 10,
         out_shape=[
             shape((ROW, D), low),
             shape((ROW, D), full),
             shape((CHIPS, ROW, D), low),
-            shape((tok, HW), low),
-            shape((tok, HW), low),
-            shape((tok, HW), low),
-            shape((CHIPS * cap, HW), low),
-            shape((CHIPS * cap, HW), low),
+            shape((tok, 3 * HW), low),
+            shape((CHIPS * cap, 2 * HW), low),
             shape((8, 2 * D), full),
             shape((8, D), full),
             shape((8, HW), full),
@@ -1537,14 +1454,14 @@
             pltpu.VMEM((CHIPS, 8, tok), full),
             pltpu.VMEM((CHIPS, 8, CHIPS * cap), full),
             *reduce_scratch, *reduce_scratch, *reduce_scratch,
-            *chain_scratch(True, (2, fr), fw),
+            *chain_scratch(True, (1, fr), 2 * fw),
             *chain_scratch(False, dr, dw),
             pltpu.VMEM((2, fr, 4 * fw), low),
-            pltpu.VMEM((2, 4, fr, fw), low),
+            pltpu.VMEM((1, 4, fr, 2 * fw), low),
             pltpu.VMEM((dr, dw), low),
             pltpu.VMEM((dr, dw), low),
             pltpu.SemaphoreType.DMA((2,)),
-            pltpu.VMEM((2, 4, 4, fr, fw), low),
+            pltpu.VMEM((1, 4, 4, fr, 2 * fw), low),
             pltpu.VMEM((4, dr, dw), low),
             pltpu.SemaphoreType.DMA((2,)),
             *net_scratch(48),
@@ -1564,34 +1481,155 @@
     return pl.BlockSpec((rows, width), lambda i: (i, 0))
 
 
-def attend_all(q, k, v, iq, ik, cosine, sine, tk, it, tv, seg_col, seg_row, gains):
+def forward_kernel(
+    q_ref, k_ref, v_ref, iq_ref, ik_ref, cos_ref, sin_ref, tk_ref, it_ref, tv_ref, sc_ref, sr_ref,
+    gs_ref, mod_ref, seg_ref, gain_ref, tok_ref, cot_ref, w_ref, outw_ref, ffnw_ref, downw_ref,
+    comb_o, cross_o, qr_o, kr_o, tr_o, branch_o, x1_o, h_o, df_o, ow_o, fw_o, dw_o,
+    part_s, buf, far, f_own, d_own, local_sems, send_sems, recv_sems,
+):
+    low = jnp.bfloat16
+    full = jnp.float32
+    net = Net(send_sems, recv_sems)
+    net.meet((1, 2, 4, 6))
+    me = net.me
+    chip = me // 2
+    width = fw_o.shape[1] // 2
+    rows = outw_ref.shape[0]
+
+    def local(src, dst, i):
+        copy = pltpu.make_async_copy(src, dst, local_sems.at[i])
+        copy.start()
+        return copy
+
+    def own(ref, count):
+        return ref.at[pl.ds(pl.multiple_of((me % 2) * count, count), count), :]
+
+    out_here = local(outw_ref, own(ow_o, rows), 0)
+    out_core = net.send(outw_ref, own(ow_o, rows), 1)
+    down_rows = downw_ref.shape[0]
+    down_here = local(downw_ref, d_own, 1)
+    down_core = net.send(downw_ref, own(dw_o, down_rows), 1)
+    f_rows = ffnw_ref.shape[1]
+    place = [2]
+
+    def stage(src, dst):
+        i = place[0]
+        place[0] += 1
+        return local(src, f_own.at[:, pl.ds((i - 2) * width, width)], i)
+
+    f_here, f_core, f_away, f_pass = spread(net, ffnw_ref, fw_o, width, stage)
+    f_x, f_y = f_away(2), f_away(4)
+    block = 32
+    weight = w_ref[0:1, 0:1]
+
+    def ffn_grad(b, _):
+        at = pl.ds(pl.multiple_of(b * block, block), block)
+        gate = jnp.tanh(pick_rows(mod_ref[:, D:], seg_ref[at, :], 4))
+        df_o[0, at, :] = (cot_ref[at, :].astype(full) * weight * gate).astype(low)
+        return 0
+
+    lax.fori_loop(0, ROW // block, ffn_grad, 0)
+    out_here.wait()
+    out_core.wait_recv()
     cap = IMGS * TXT
+
+    def attention_row(i, _):
+        j = 3 - i
+        at = pl.ds(pl.multiple_of(j * ROW, ROW), ROW)
+        text = pl.ds(pl.multiple_of(j * cap, cap), cap)
+        attend_kernel(
+            q_ref.at[at], k_ref.at[at], v_ref.at[at], iq_ref.at[at], ik_ref.at[at],
+            cos_ref.at[at], sin_ref.at[at], tk_ref.at[text], it_ref.at[text], tv_ref.at[text],
+            sc_ref.at[at], sr_ref.at[j], gs_ref,
+            comb_o.at[at], cross_o.at[at], qr_o.at[at], kr_o.at[at], tr_o.at[text],
+        )
+        part_s[at, :] = jnp.dot(comb_o[at, :], ow_o[...], preferred_element_type=full)
+        return 0
+
+    lax.fori_loop(0, CHIPS, attention_row, 0)
+    half = ROW // 2
+    middle, finish = collect4(
+        net, lambda j, i: part_s[pl.ds(j * ROW + i * half, half), :], buf, far
+    )
+    f_far = f_away(6)
+    dx, dy = share4_start(net, df_o)
+
+    down_here.wait()
+    down_out = local(d_own, own(dw_o, down_rows), 4)
+    for c in f_here:
+        c.wait()
+    f_out = local(f_own, fw_o.at[pl.ds(pl.multiple_of(me * f_rows, f_rows), f_rows), :], 5)
+    middle()
+    for i in (0, 1):
+        branch_o[pl.ds(i * half, half), :] = finish(i)
+
+    def second(b, _):
+        at = pl.ds(pl.multiple_of(b * block, block), block)
+        seg = seg_ref[at, :]
+        gate = jnp.tanh(pick_rows(mod_ref[:, D:], seg, 0))
+        x1 = tok_ref[at, :].astype(full) + gate * branch_o[at, :]
+        x1_o[at, :] = x1
+        normed = x1 * lax.rsqrt(jnp.mean(x1 * x1, axis=-1, keepdims=True) + EPS)
+        scale = pick_rows(mod_ref[:, :D], seg, 4)
+        h_o[0, at, :] = (normed * gain_ref[1:2, :] * (1.0 + scale)).astype(low)
+        return 0
+
+    lax.fori_loop(0, ROW // block, second, 0)
+    hx, hy = share4_start(net, h_o)
+    last = [f_pass(f_x, 2), f_pass(f_y, 4)]
+    last += share4_relay(net, df_o, dx, dy)
+    last += share4_relay(net, h_o, hx, hy)
+    last.append(f_pass(f_far, 6))
+    for c in last + [down_core] + f_core:
+        c.wait_recv()
+    down_out.wait()
+    f_out.wait()
+    net.close()
+
+
+def forward_layer(*args):
     low = jnp.bfloat16
-    big = row_spec(ROW, HW)
-    text = row_spec(cap, HW)
-    one = row_spec(ROW, 1)
-    table = row_spec(ROW, 128)
+    full = jnp.float32
     shape = jax.ShapeDtypeStruct
+    V = VMEM_SPEC
+    cap = IMGS * TXT
+    tok = CHIPS * ROW
+    out_w, ffn_w, down_w = args[-3:]
+    width = ffn_w.shape[2] // CHIPS
     return pl.pallas_call(
-        attend_kernel,
-        grid=(CHIPS,),
-        in_specs=[
-            big, big, big, one, one, table, table, text, row_spec(cap, 1), text, one,
-            pl.BlockSpec((1, 1, ROW), lambda i: (i, 0, 0)),
-            pl.BlockSpec((6, HW), lambda i: (0, 0)),
+        forward_kernel,
+        in_specs=[V] * (len(args) - 3) + [ANY_SPEC] * 3,
+        out_specs=[V] * 10 + [ANY_SPEC] * 2,
+        out_shape=[
+            shape((tok, HW), low),
+            shape((tok, HW), full),
+            shape((tok, HW), low),
+            shape((tok, HW), low),
+            shape((CHIPS * cap, HW), low),
+            shape((ROW, D), full),
+            shape((ROW, D), full),
+            shape((CHIPS, ROW, D), low),
+            shape((CHIPS, ROW, D), low),
+            shape((2 * out_w.shape[0], D), low),
+            shape((D, 2 * width), low),
+            shape((2 * down_w.shape[0], D), low),
         ],
-        out_specs=[big, big, big, big, text],
-        out_shape=[
-            shape((CHIPS * ROW, HW), low),
-            shape((CHIPS * ROW, HW), jnp.float32),
-            shape((CHIPS * ROW, HW), low),
-            shape((CHIPS * ROW, HW), low),
-            shape((CHIPS * cap, HW), low),
+        scratch_shapes=[
+            pltpu.VMEM((tok, D), full),
+            pltpu.VMEM((5, ROW, D), low),
+            pltpu.VMEM((2, ROW // 2, D), low),
+            pltpu.VMEM((ffn_w.shape[1], 2 * width), low),
+            pltpu.VMEM(down_w.shape, low),
+            pltpu.SemaphoreType.DMA((6,)),
+            *net_scratch(40),
         ],
+        compiler_params=pltpu.CompilerParams(
+            collective_id=4, has_side_effects=True, vmem_limit_bytes=56 * 1024 * 1024
+        ),
         cost_estimate=pl.CostEstimate(
-            flops=4 * 24 * 128 * 384 * 128, bytes_accessed=10_000_000, transcendentals=1_200_000
+            flops=5_000_000_000, bytes_accessed=200_000_000, transcendentals=0
         ),
-    )(q, k, v, iq, ik, cosine, sine, tk, it, tv, seg_col, seg_row, gains)
+    )(*args)
 
 
 def per_device(
@@ -1653,81 +1691,58 @@
     cosine = jnp.cos(angle)
     sine = jnp.where(((lane // quarter) % 2 == 0)[None, :], -1.0, 1.0) * jnp.sin(angle)
 
-    ffn_w = column_weights(ffn_weight, chip, core, ff)
-    out_w = row_weights(out_weight, core)
-    down_w = row_weights(down_weight, core)
     gain_s = lax.dynamic_slice_in_dim(gain_f, chip * HW, HW, axis=1)[:6]
-
-    def per_token(part):
-        rows = mod[4 * (part // 2) :, (part % 2) * D : (part % 2 + 1) * D]
-        out = rows[IMGS - 1][None, :]
-        for i in range(IMGS - 2, -1, -1):
-            out = jnp.where(seg[:, None] == i, rows[i][None, :], out)
-        return out
-
-    scale1 = per_token(0)
-    gate1 = per_token(1)
-    scale2 = per_token(2)
-    gate2 = per_token(3)
-    tanh_one = jnp.tanh(gate1)
-    tanh_two = jnp.tanh(gate2)
-
-    x = tokens[0].astype(full)
-    normed1, inverse1 = norm_rows(x)
-    comb, cross_out, q_rot, k_rot, text_rot = attend_all(
-        query, keyed, valued, inv_qk[0], inv_qk[1], cosine, sine, text_keys, inv_t, text_vals,
-        seg_col, seg_row, gain_s,
-    )
-    branch = reduce4(list(mult(comb, out_w).reshape(CHIPS, ROW, D)))
-    x_one = x + tanh_one * branch
-    normed2, inverse2 = norm_rows(x_one)
-    h_two = (normed2 * gain_f[1] * (1.0 + scale2)).astype(low)
-    h_two_all = jnp.concatenate(gather4(h_two), axis=0)
 
     totals = counts.astype(full)
     here = jnp.sum(jnp.where(jnp.arange(totals.shape[0], dtype=jnp.int32) == plane, totals, 0.0))
     weight = lax.axis_size("bucket") * here / jnp.sum(totals)
-    grad = cotangent[0].astype(full) * weight
-    d_ffn = (grad * tanh_two).astype(low)
-    d_ffn_all = jnp.concatenate(gather4(d_ffn), axis=0)
-
-    gate_pre = mult(h_two_all, ffn_w[0])
-    upper = mult(h_two_all, ffn_w[1])
+    weight_row = jnp.full((1, 128), weight, full)
+    (
+        comb, cross_out, q_rot, k_rot, text_rot, branch, x_one, h_two_rows, d_ffn_rows, out_w, ffn_w,
+        down_w,
+    ) = forward_layer(
+        query, keyed, valued, inv_qk[0], inv_qk[1], cosine, sine, text_keys, inv_t, text_vals,
+        seg_col, seg_row, gain_s, mod, seg[:, None], gain_f, tokens[0], cotangent[0], weight_row,
+        out_weight, ffn_weight, down_weight,
+    )
+    h_two_all = h_two_rows.reshape(CHIPS * ROW, D)
+    d_ffn_all = d_ffn_rows.reshape(CHIPS * ROW, D)
+    both = mult(h_two_all, ffn_w)
+    gate_pre = both[:, :ff]
+    upper = both[:, ff:]
     d_hidden = dot_t(d_ffn_all, down_w)
     sigm = jax.nn.sigmoid(gate_pre)
     silu_pre = gate_pre * sigm
     hidden = (silu_pre * upper).astype(low)
     d_pre = (d_hidden * upper * sigm * (1.0 + gate_pre * (1.0 - sigm))).astype(low)
     d_up = (d_hidden * silu_pre).astype(low)
-    d_h_two = (dot_t(d_pre, ffn_w[0]) + dot_t(d_up, ffn_w[1])).astype(low)
+    d_both = jnp.concatenate([d_pre, d_up], axis=1)
+    d_h_two = dot_t(d_both, ffn_w).astype(low)
     ffn_out = mult(hidden, down_w).astype(low)
     g_down = t_dot(hidden, d_ffn_all).astype(low)
-    g_ffn = jnp.stack([t_dot(h_two_all, d_pre).astype(low), t_dot(h_two_all, d_up).astype(low)])
+    g_ffn = t_dot(h_two_all, d_both).astype(low)
 
     (
-        block_out, token_grad, d_branch_rows, d_query, d_keyed, d_valued, d_text_keys, d_text_vals,
-        d_mod, gg_full, gg_slice, s_ffn, s_down,
+        block_out, token_grad, d_branch_rows, d_qkv, d_text, d_mod, gg_full, gg_slice, s_ffn, s_down,
     ) = back_layer(
         [
-            d_h_two, ffn_out, x_one, branch, cotangent[0], jnp.full((1, 128), weight, full), mod,
+            d_h_two, ffn_out, x_one, branch, cotangent[0], weight_row, mod,
             seg[:, None], gain_f, tokens[0], seg_row, gain_s,
         ],
         [
             out_w, attn_w, q_rot, k_rot, valued, text_rot, text_vals, cross_out, query, keyed,
             text_keys, inv_qk[0], inv_qk[1], inv_t, cosine, sine, seg_col,
         ],
-        g_ffn.reshape(2, 4, 4, 2, 48, ff),
+        g_ffn.reshape(1, 4, 4, 2, 48, 2 * ff),
         g_down.reshape(4, 2, 128, D),
     )
     d_branch_all = d_branch_rows.reshape(CHIPS * ROW, D)
-    g_text = jnp.stack(
-        [t_dot(text_all, d_text_keys).astype(low), t_dot(text_all, d_text_vals).astype(low)]
-    )
-    g_attn = jnp.stack([t_dot(h_all, g).astype(low) for g in (d_query, d_keyed, d_valued)])
+    g_text = t_dot(text_all, d_text).astype(low)
+    g_attn = t_dot(h_all, d_qkv).astype(low)
     g_out = t_dot(comb, d_branch_all).astype(low)
     s_text, s_attn, s_out = close_layer(
-        g_text.reshape(2, 4, 4, 2, 128, HW),
-        g_attn.reshape(3, 4, 4, 2, 48, HW),
+        g_text.reshape(1, 4, 4, 2, 128, 2 * HW),
+        g_attn.reshape(1, 4, 4, 2, 48, 3 * HW),
         g_out.reshape(4, 2, 48, D),
     )
 

time: 690 us -> 638 us (0.925)
  Pallas kernels: 400 us -> 467 us
  waiting for transfers between devices: 34.9 us -> 5.52 us
  starting transfers between devices: 81.8 us -> 52.8 us
  other arithmetic: 45 us -> 18.8 us
  local copies, waits for them, and re-layouts: 61.8 us -> 36 us
    pallas_call x1, Pallas kernels: 14.5 us -> 83.7 us  [forward_layer(): pl.pallas_call(forward_kernel, in_specs=[V] * (len(args) - 3) + [ANY_SPEC...]
    ppermute x33 -> x13, starting transfers between devices: 64.5 us -> 34.5 us  [swap(): return lax.ppermute(v, 'fsdp', [(i, i ^ mask) for i in range(8)])]
    ppermute x33 -> x13, waiting for transfers between devices: 27.8 us -> 5.5 us  [swap(): return lax.ppermute(v, 'fsdp', [(i, i ^ mask) for i in range(8)])]
    another operation x7 -> x0, other arithmetic: 13.7 us -> none  [the longest x1 3.4 us: per_device(): jnp.stack([t_dot(h_two_all, d_pre).astype(low), t_dot(h_two_all, d_up).as...]
    dot_general x10 -> x6, matrix products: 38.5 us -> 30.6 us  [t_dot(): lax.dot_general(a, b, (((0,), (0,)), ((), ())), preferred_element_type=jn...]
    ppermute x3, waiting for transfers between devices: 7.03 us -> 0.01 us  [per_device(): lax.ppermute(mods, 'bucket', [(i, i ^ shift) for i in range(4)])]
  transfers between devices with their start and end apart: 41 -> 21, of which waited for: 13 -> 3; matrix products, arithmetic and copies ran while one was open for 17% -> 5% of each run, Pallas kernels for 45% -> 19%
where the time goes in v3:
time: 638 us; the launch traced here: 629 us
  Pallas kernels  467 us (73%)
  starting transfers between devices  52.8 us (8%)
  matrix products  46.8 us (7%)
  local copies, waits for them, and re-layouts  36 us (6%)
  other arithmetic  18.8 us (3%)
    pallas_call x1, Pallas kernels, open_layer(): pl.pallas_call(open_kernel, in_specs=[V, V, V, V, V, V, V, ANY_SPEC, ANY_...  169 us
    pallas_call x1, Pallas kernels, close_layer(): pl.pallas_call(close_kernel, in_specs=[V] * 3, out_specs=[V] * 3, out_sha...  118 us
    pallas_call x1, Pallas kernels, back_layer(): pl.pallas_call(back_kernel, in_specs=[V] * len(early) + [ANY_SPEC] * (LAT...  96.1 us
    pallas_call x1, Pallas kernels, forward_layer(): pl.pallas_call(forward_kernel, in_specs=[V] * (len(args) - 3) + [ANY_SPEC...  83.7 us
    ppermute x13, starting transfers between devices, swap(): return lax.ppermute(v, 'fsdp', [(i, i ^ mask) for i in range(8)])  34.5 us
    dot_general x6, matrix products, t_dot(): lax.dot_general(a, b, (((0,), (0,)), ((), ())), preferred_element_type=jn...  30.6 us
  transfers between devices with their start and end apart: 21, of which 3 were waited for; matrix products, arithmetic and copies ran while one was open for 5% of the time, Pallas kernels for 19%

profile of v3, /device:TPU:0, one launch (start us, length us, event | category | flops | bytes accessed | tf_op | source)
XLA Modules:
  0.0 629.4 jit_solution(5053161808026539483)
XLA Ops:
  0.7 1.4 pad_maximum_fusion.5.cond_ref
  4.3 1.4 copy.28.seg_ref
  5.7 1.3 add_add_fusion.idx_ref
  8.0 169.0 %shard_map.222 = (f32[8,3072]{1,0:T(8,128)}, f32[8,1536]{1,0:T(8,128)}, bf16[4,128,1536]{2,1,0:T(8,128)(2,1)}, s32[4,8,128]{2,1,0:T(8,128)}, bf16[1536,1152]{1,0...) custom-call(bf16[8,1024]{1,0:T(8,128)(2,1)} %pad_maximum_fusion.5.co, ...), custom_call_target="tpu_custom_call" | custom-call | flops 10000000000 | bytes 400000000 | tf_op jit(solution)/shard_map/pallas_call | solution.py:837
  180.2 1.4 fusion.20
  182.4 1.0 copy.31.it_ref.rest_13_
  184.3 1.3 constant_dynamic-slice_fusion.gs_ref
  187.7 10.2 %bitcast_select_fusion.8 = (f32[128]{0:T(128)S(1)}, f32[128]{0:T(128)S(1)}) fusion(f32[]{:T(128)} %bitcast.27, f32[]{:T(128)} %bitcast.28, f32[]{:T(128)} %bitcast.29, f32[]{:T(128)} %bitcast.30, f32[]{:T(128)} %bitcast.31, f32[]{:T(128)} %bitcast.33, f32[]{:T(128)} %bitcast.32, f32[]{:T(128)} %bitcast.10, f32[]{:T(128)} %bitcast.12, f32[]{:T(128)} %bitcast.14, ...), kind=kLoop, calls=%fused_computation.47 | loop fusion | flops 7680 | bytes 1088 | tf_op jit(solution)/shard_map/gather | solution.py:1687
  197.8 1.8 sine_multiply_fusion
  200.2 83.7 %shard_map.223 = (bf16[512,384]{1,0:T(8,128)(2,1)}, f32[512,384]{1,0:T(8,128)}, bf16[512,384]{1,0:T(8,128)(2,1)}, bf16[512,384]{1,0:T(8,128)(2,1)}, bf16[1024,38...) custom-call(f32[512,384]{1,0:T(8,128)} %get-tuple-element.60.q_ref.r, ...), custom_call_target="tpu_custom_call" | custom-call | flops 5000000000 | bytes 200000000 | tf_op jit(solution)/shard_map/pallas_call | solution.py:1599
  283.9 6.1 fusion.22
  290.1 2.6 multiply_convert_fusion.2
  292.9 4.5 convolution_convert_fusion.5.dh2_ref
  297.4 5.6 convolution_convert_fusion
  303.1 2.9 convolution_convert_fusion.4.fo_ref
  306.0 3.5 convolution_convert_fusion.3
  309.6 96.1 %shard_map.224 = (bf16[128,1536]{1,0:T(8,128)(2,1)}, f32[128,1536]{1,0:T(8,128)}, bf16[4,128,1536]{2,1,0:T(8,128)(2,1)}, bf16[512,1152]{1,0:T(8,128)(2,1)}, bf16...) custom-call(bf16[512,1536]{1,0:T(8,128)(2,1)} %convolution_convert_f, ...), custom_call_target="tpu_custom_call" | custom-call | flops 10000000000 | bytes 400000000 | tf_op jit(solution)/shard_map/pallas_call | solution.py:1431
  405.7 1.0 fusion.19
  409.3 26.2 %collective-permute-start.8 = (bf16[4,6144]{1,0:T(4,128)(2,1)S(1)}, bf16[4,6144]{1,0:T(4,128)(2,1)S(1)}, u32[]{:S(2)}, u32[]{:S(2)}) collective-permute-start(bf16[4,6144]{1,0:T(4,128)(2,1)S(1)} %fusion.3), channel_id=1, source_target_pairs={{0,2},{1,3},{2,0},{3,1},{4,6},{5,7},{6,4},{7,5},{8,10},{9,11},{10,... | collective-permute-start | bytes 147464 | tf_op jit(solution)/shard_map/ppermute | solution.py:316
  435.5 2.4 collective-permute-done.8
  438.0 1.6 collective-permute-done.9
  439.9 1.9 collective-permute-start.17
  442.1 2.0 collective-permute-start.1
  444.1 1.5 collective-permute-done
  445.6 1.1 collective-permute-start.2
  446.7 1.1 collective-permute-start.3
  448.0 9.2 %collective-permute-start.12 = (bf16[16,6144]{1,0:T(8,128)(2,1)S(1)}, bf16[16,6144]{1,0:T(8,128)(2,1)S(1)}, u32[]{:S(2)}, u32[]{:S(2)}) collective-permute-start(bf16[16,6144]{1,0:T(8,128)(2,1)S(1)} %concatenate.46), channel_id=1, source_target_pairs={{0,8},{8,0},{16,24},{24,16},{1,9},{9,1},{17,25},{25,17},{2,10},{10... | collective-permute-start | bytes 589832 | tf_op jit(solution)/shard_map/ppermute | solution.py:1771
  457.3 2.4 collective-permute-start.14
  459.8 1.0 collective-permute-start.18
  460.8 11.6 %convolution_convert_fusion.2 = bf16[4096,768]{1,0:T(8,128)(2,1)} fusion(bf16[1024,4096]{1,0:T(8,128)(2,1)} %bitcast.116, bf16[1024,768]{1,0:T(8,128)(2,1)} %get-tuple-element.88), kind=kOutput, calls=%fused_computation.2 | convolution fusion | flops 6445596672 | bytes 16252928 | tf_op jit(solution)/shard_map/dot_general | solution.py:360
  472.4 1.1 collective-permute-start.4
  473.5 0.9 collective-permute-start.5
  474.5 2.5 collective-permute-start.6
  477.1 3.5 concatenate.47
  480.7 5.3 convolution_convert_fusion.1
  486.0 3.1 concatenate.43
  489.6 1.9 collective-permute-start.20
  491.5 3.2 convolution_convert_fusion.6
  494.7 117.7 %shard_map.225 = (f32[2,128,1536]{2,1,0:T(8,128)}, f32[3,48,1536]{2,1,0:T(8,128)}, f32[48,1536]{1,0:T(8,128)}) custom-call(bf16[1,4,4,2,128,768]{5,4,3,2,1,0:T(8,128)(2,1)} %bitcast.100, bf16[1,4,4,2,48,1152]{5,4,3,2,1,0:T(8,128)(2,1)} %bitcast.101, bf16[4,2,48,1536]{3,2,1,0:T(8,128)(2,1)} %bitcast.102), custom_call_target="tpu_custom_call" | custom-call | flops 1000000 | bytes 400000000 | tf_op jit(solution)/shard_map/pallas_call | solution.py:1153
  612.5 1.7 concatenate.44
  614.2 0.9 add.117
  616.5 4.1 concatenate.48
  620.6 1.3 fusion.4
  622.7 0.9 copy.51
  623.6 0.9 copy.52
  625.2 1.1 copy.54
  626.4 1.1 copy.55
  628.1 0.9 copy.56
  (109 shorter events, 17.0 us)
Async XLA Ops:
  7.3 0.6 copy-start.8
  8.0 177.6 %copy-start.10 = (s32[4]{0:T(128)S(1)}, s32[4]{0:T(128)}, u32[]{:S(2)}) copy-start(s32[4]{0:T(128)} %param.22) | copy-start | bytes 52
  283.9 6.2 copy-start.12
  283.9 6.2 copy-start.16
  290.1 2.8 copy-start.15
  292.9 4.6 copy-start.13
  309.5 132.3 %copy-start.9 = (bf16[1,4,1024]{2,1,0:T(4,128)(2,1)S(1)}, bf16[1,4,1024]{2,1,0:T(4,128)(2,1)}, u32[]{:S(2)}) copy-start(bf16[1,4,1024]{2,1,0:T(4,128)(2,1)} %param.18) | copy-start | bytes 24580
  409.2 30.7 %collective-permute-start.16 = (f32[10,1536]{1,0:T(8,128)S(1)}, f32[10,1536]{1,0:T(8,128)S(1)}, u32[]{:S(2)}, u32[]{:S(2)}) collective-permute-start(f32[10,1536]{1,0:T(8,128)S(1)} %pad_maximum_fusion.4), channel_id=1, source_target_pairs={{0,1},{1,0},{2,3},{3,2},{4,5},{5,4},{6,7},{7,6},{8,9},{9,8},{10,11... | collective-permute-start | bytes 184328 | tf_op jit(solution)/shard_map/ppermute | solution.py:316
  409.3 28.6 %collective-permute-start.8 = (bf16[4,6144]{1,0:T(4,128)(2,1)S(1)}, bf16[4,6144]{1,0:T(4,128)(2,1)S(1)}, u32[]{:S(2)}, u32[]{:S(2)}) collective-permute-start(bf16[4,6144]{1,0:T(4,128)(2,1)S(1)} %fusion.3), channel_id=1, source_target_pairs={{0,2},{1,3},{2,0},{3,1},{4,6},{5,7},{6,4},{7,5},{8,10},{9,11},{10,... | collective-permute-start | bytes 147464 | tf_op jit(solution)/shard_map/ppermute | solution.py:316
  435.5 4.1 collective-permute-start.9
  438.0 9.9 %collective-permute-start.10 = (bf16[2,6144]{1,0:T(2,128)(2,1)S(1)}, bf16[2,6144]{1,0:T(2,128)(2,1)S(1)}, u32[]{:S(2)}, u32[]{:S(2)}) collective-permute-start(bf16[2,6144]{1,0:T(2,128)(2,1)S(1)} %slice.130), channel_id=1, source_target_pairs={{0,4},{1,5},{2,6},{3,7},{4,0},{5,1},{6,2},{7,3},{8,12},{9,13},{10,... | collective-permute-start | bytes 73736 | tf_op jit(solution)/shard_map/ppermute | solution.py:316
  439.7 8.2 %collective-permute-start.11 = (bf16[2,6144]{1,0:T(2,128)(2,1)S(1)}, bf16[2,6144]{1,0:T(2,128)(2,1)S(1)}, u32[]{:S(2)}, u32[]{:S(2)}) collective-permute-start(bf16[2,6144]{1,0:T(2,128)(2,1)S(1)} %slice.131), channel_id=1, source_target_pairs={{0,2},{1,3},{2,0},{3,1},{4,6},{5,7},{6,4},{7,5},{8,10},{9,11},{10,... | collective-permute-start | bytes 73736 | tf_op jit(solution)/shard_map/ppermute | solution.py:316
  439.9 17.4 %collective-permute-start.17 = (f32[10,1536]{1,0:T(8,128)S(1)}, f32[10,1536]{1,0:T(8,128)S(1)}, u32[]{:S(2)}, u32[]{:S(2)}) collective-permute-start(f32[10,1536]{1,0:T(8,128)S(1)} %fusion.18), channel_id=1, source_target_pairs={{0,2},{1,3},{2,0},{3,1},{4,6},{5,7},{6,4},{7,5},{8,10},{9,11},{10,... | collective-permute-start | bytes 184328 | tf_op jit(solution)/shard_map/ppermute | solution.py:316
  441.9 3.7 collective-permute-start
  442.1 4.6 collective-permute-start.1
  445.6 14.1 %collective-permute-start.2 = (bf16[2,1024]{1,0:T(2,128)(2,1)S(1)}, bf16[2,1024]{1,0:T(2,128)(2,1)S(1)}, u32[]{:S(2)}, u32[]{:S(2)}) collective-permute-start(bf16[2,1024]{1,0:T(2,128)(2,1)S(1)} %slice.128), channel_id=1, source_target_pairs={{0,4},{1,5},{2,6},{3,7},{4,0},{5,1},{6,2},{7,3},{8,12},{9,13},{10,... | collective-permute-start | bytes 12296 | tf_op jit(solution)/shard_map/ppermute | solution.py:316
  446.7 25.6 %collective-permute-start.3 = (bf16[2,1024]{1,0:T(2,128)(2,1)S(1)}, bf16[2,1024]{1,0:T(2,128)(2,1)S(1)}, u32[]{:S(2)}, u32[]{:S(2)}) collective-permute-start(bf16[2,1024]{1,0:T(2,128)(2,1)S(1)} %slice.129), channel_id=1, source_target_pairs={{0,2},{1,3},{2,0},{3,1},{4,6},{5,7},{6,4},{7,5},{8,10},{9,11},{10,... | collective-permute-start | bytes 12296 | tf_op jit(solution)/shard_map/ppermute | solution.py:316
  448.0 26.4 %collective-permute-start.12 = (bf16[16,6144]{1,0:T(8,128)(2,1)S(1)}, bf16[16,6144]{1,0:T(8,128)(2,1)S(1)}, u32[]{:S(2)}, u32[]{:S(2)}) collective-permute-start(bf16[16,6144]{1,0:T(8,128)(2,1)S(1)} %concatenate.46), channel_id=1, source_target_pairs={{0,8},{8,0},{16,24},{24,16},{1,9},{9,1},{17,25},{25,17},{2,10},{10... | collective-permute-start | bytes 589832 | tf_op jit(solution)/shard_map/ppermute | solution.py:1771
  457.3 19.7 %collective-permute-start.13 = (bf16[16,6144]{1,0:T(8,128)(2,1)S(1)}, bf16[16,6144]{1,0:T(8,128)(2,1)S(1)}, u32[]{:S(2)}, u32[]{:S(2)}) collective-permute-start(bf16[16,6144]{1,0:T(8,128)(2,1)S(1)} %concatenate.46), channel_id=1, source_target_pairs={{0,16},{8,24},{16,0},{24,8},{1,17},{9,25},{17,1},{25,9},{2,18},{10... | collective-permute-start | bytes 589832 | tf_op jit(solution)/shard_map/ppermute | solution.py:1771
  457.3 19.8 %collective-permute-start.14 = (bf16[16,6144]{1,0:T(8,128)(2,1)S(1)}, bf16[16,6144]{1,0:T(8,128)(2,1)S(1)}, u32[]{:S(2)}, u32[]{:S(2)}) collective-permute-start(bf16[16,6144]{1,0:T(8,128)(2,1)S(1)} %concatenate.46), channel_id=1, source_target_pairs={{0,24},{8,16},{16,8},{24,0},{1,25},{9,17},{17,9},{25,1},{2,26},{10... | collective-permute-start | bytes 589832 | tf_op jit(solution)/shard_map/ppermute | solution.py:1771
  459.8 13.8 %collective-permute-start.18 = (f32[10,1536]{1,0:T(8,128)S(1)}, f32[10,1536]{1,0:T(8,128)S(1)}, u32[]{:S(2)}, u32[]{:S(2)}) collective-permute-start(f32[10,1536]{1,0:T(8,128)S(1)} %add.114), channel_id=1, source_target_pairs={{0,4},{1,5},{2,6},{3,7},{4,0},{5,1},{6,2},{7,3},{8,12},{9,13},{10,... | collective-permute-start | bytes 184328 | tf_op jit(solution)/shard_map/ppermute | solution.py:316
  460.8 19.9 %copy-start.11 = (bf16[4,128,1536]{2,1,0:T(8,128)(2,1)S(1)}, bf16[4,128,1536]{2,1,0:T(8,128)(2,1)}, u32[]{:S(2)}) copy-start(bf16[4,128,1536]{2,1,0:T(8,128)(2,1)} %get-tuple-element.89) | copy-start | bytes 4718596
  472.4 13.6 %collective-permute-start.4 = (bf16[16,1024]{1,0:T(8,128)(2,1)S(1)}, bf16[16,1024]{1,0:T(8,128)(2,1)S(1)}, u32[]{:S(2)}, u32[]{:S(2)}) collective-permute-start(bf16[16,1024]{1,0:T(8,128)(2,1)S(1)} %concatenate.42), channel_id=1, source_target_pairs={{0,8},{8,0},{16,24},{24,16},{1,9},{9,1},{17,25},{25,17},{2,10},{10... | collective-permute-start | bytes 98312 | tf_op jit(solution)/shard_map/ppermute | solution.py:1779
  473.5 12.5 %collective-permute-start.5 = (bf16[16,1024]{1,0:T(8,128)(2,1)S(1)}, bf16[16,1024]{1,0:T(8,128)(2,1)S(1)}, u32[]{:S(2)}, u32[]{:S(2)}) collective-permute-start(bf16[16,1024]{1,0:T(8,128)(2,1)S(1)} %concatenate.42), channel_id=1, source_target_pairs={{0,16},{8,24},{16,0},{24,8},{1,17},{9,25},{17,1},{25,9},{2,18},{10... | collective-permute-start | bytes 98312 | tf_op jit(solution)/shard_map/ppermute | solution.py:1779
  474.5 11.5 %collective-permute-start.6 = (bf16[16,1024]{1,0:T(8,128)(2,1)S(1)}, bf16[16,1024]{1,0:T(8,128)(2,1)S(1)}, u32[]{:S(2)}, u32[]{:S(2)}) collective-permute-start(bf16[16,1024]{1,0:T(8,128)(2,1)S(1)} %concatenate.42), channel_id=1, source_target_pairs={{0,24},{8,16},{16,8},{24,0},{1,25},{9,17},{17,9},{25,1},{2,26},{10... | collective-permute-start | bytes 98312 | tf_op jit(solution)/shard_map/ppermute | solution.py:1779
  477.0 12.7 %collective-permute-start.19 = (f32[10,1536]{1,0:T(8,128)S(1)}, f32[10,1536]{1,0:T(8,128)S(1)}, u32[]{:S(2)}, u32[]{:S(2)}) collective-permute-start(f32[10,1536]{1,0:T(8,128)S(1)} %add.115), channel_id=1, source_target_pairs={{0,8},{8,0},{16,24},{24,16},{1,9},{9,1},{17,25},{25,17},{2,10},{10... | collective-permute-start | bytes 184328 | tf_op jit(solution)/shard_map/ppermute | solution.py:1760
  480.7 135.8 %collective-permute-start.15 = (bf16[64,6144]{1,0:T(8,128)(2,1)}, bf16[64,6144]{1,0:T(8,128)(2,1)}, u32[]{:S(2)}, u32[]{:S(2)}) collective-permute-start(bf16[64,6144]{1,0:T(8,128)(2,1)} %concatenate.47), channel_id=1, source_target_pairs={{0,1},{1,0},{2,3},{3,2},{4,5},{5,4},{6,7},{7,6},{8,9},{9,8},{10,11... | collective-permute-start | bytes 2359304 | tf_op jit(solution)/shard_map/ppermute | solution.py:316
  480.7 10.8 %copy-start.14 = (bf16[512,384]{1,0:T(8,128)(2,1)S(1)}, bf16[512,384]{1,0:T(8,128)(2,1)}, u32[]{:S(2)}) copy-start(bf16[512,384]{1,0:T(8,128)(2,1)} %get-tuple-element.91) | copy-start | bytes 1179652
  486.0 8.7 %copy-start.7 = (bf16[16,1024]{1,0:T(8,128)(2,1)}, bf16[16,1024]{1,0:T(8,128)(2,1)S(1)}, u32[]{:S(2)}) copy-start(bf16[16,1024]{1,0:T(8,128)(2,1)S(1)} %collective-permute-done.6) | copy-start | bytes 98308
  489.1 123.4 %collective-permute-start.7 = (bf16[64,1024]{1,0:T(8,128)(2,1)}, bf16[64,1024]{1,0:T(8,128)(2,1)}, u32[]{:S(2)}, u32[]{:S(2)}) collective-permute-start(bf16[64,1024]{1,0:T(8,128)(2,1)} %concatenate.43), channel_id=1, source_target_pairs={{0,1},{1,0},{2,3},{3,2},{4,5},{5,4},{6,7},{7,6},{8,9},{9,8},{10,11... | collective-permute-start | bytes 393224 | tf_op jit(solution)/shard_map/ppermute | solution.py:316
  489.6 124.6 %collective-permute-start.20 = (f32[10,1536]{1,0:T(8,128)S(1)}, f32[10,1536]{1,0:T(8,128)}, u32[]{:S(2)}, u32[]{:S(2)}) collective-permute-start(f32[10,1536]{1,0:T(8,128)S(1)} %add.116), channel_id=1, source_target_pairs={{0,16},{8,24},{16,0},{24,8},{1,17},{9,25},{17,1},{25,9},{2,18},{10... | collective-permute-start | bytes 184328 | tf_op jit(solution)/shard_map/ppermute | solution.py:1761
  616.5 5.5 copy-start.5
  620.6 2.1 copy-start.4
  620.6 3.0 copy-start.2
  622.0 2.5 copy-start.6
  622.7 2.5 copy-start.1
  624.5 1.9 copy-start
  626.4 1.7 copy-start.3

commit v4 on v3

--- a/solution.py
+++ b/solution.py
@@ -310,35 +310,6 @@
 CHIPS = 4
 HW = D // CHIPS
 PAIRS = HW // 128
-
-
-def swap(v, mask):
-    return lax.ppermute(v, "fsdp", [(i, i ^ mask) for i in range(8)])
-
-
-def at_x(v):
-    return swap(v, 2)
-
-
-def at_y(v):
-    return swap(v, 4)
-
-
-def at_core(v):
-    return swap(v, 1)
-
-
-def gather4(v):
-    half = v.shape[0] // 2
-    by_x = at_x(v)
-    by_y = at_y(v)
-    far = jnp.concatenate([at_y(by_x[:half]), at_x(by_y[half:])], axis=0)
-    return [v, by_x, by_y, far]
-
-
-def sum4(v):
-    v = v + at_x(v)
-    return v + at_y(v)
 
 
 def partner(u):
@@ -480,6 +451,13 @@
 ANY_SPEC = pl.BlockSpec(memory_space=pl.ANY)
 
 
+def to_row_owner(block):
+    pairs = [
+        (a * 8 + b * 2 + k, b * 8 + a * 2 + k) for a in range(4) for b in range(4) for k in range(2)
+    ]
+    return lax.ppermute(block, ("bucket", "fsdp"), pairs).astype(jnp.float32)
+
+
 class Net:
     def __init__(self, send_sems, recv_sems):
         self.me = lax.axis_index("fsdp")
@@ -1013,7 +991,7 @@
     def start(self):
         net = self.net
         chip = net.me // 2
-        n, _, rows, width = self.total.shape
+        n, _, rows, width = self.stage.shape
         parts = self.wide.shape[0]
         width = width // parts
         at = pl.ds(pl.multiple_of(chip * width, width), width)
@@ -1022,7 +1000,8 @@
             self.stage[i // 4, i % 4] = self.total[i // 4, i % 4].astype(jnp.bfloat16)
             return 0
 
-        lax.fori_loop(0, n * 4, cast, 0)
+        if self.total is not None:
+            lax.fori_loop(0, n * 4, cast, 0)
         self.copies = [
             net.send(
                 self.stage.at[0, net.peer(m) // 2, :, pl.ds(i * width, width)],
@@ -1042,7 +1021,7 @@
             self.out[i] = self.wide[i].astype(jnp.float32)
 
 
-def meet_all(net):
+def meet_all(net, far=False):
     plane = lax.axis_index("bucket")
     chip = net.me // 2
     sem = pltpu.get_barrier_semaphore()
@@ -1067,10 +1046,17 @@
             device_id_type=MESH_IDS,
         )
 
+    if far:
+        pl.semaphore_signal(
+            sem,
+            inc=1,
+            device_id={"bucket": plane + 2 - 4 * (plane // 2)},
+            device_id_type=MESH_IDS,
+        )
     one = jnp.int32(1)
     zero = jnp.int32(0)
     count = (
-        7
+        (8 if far else 7)
         + jnp.where(plane >= 1, one, zero)
         + jnp.where(plane <= 2, one, zero)
         + jnp.where(chip != plane, one, zero)
@@ -1090,38 +1076,169 @@
     )
 
 
+class Spread:
+    def __init__(self, buf, sems):
+        self.buf, self.sems = buf, sems
+        self.plane = lax.axis_index("bucket")
+
+    def copy(self, up, slab):
+        first = 0 if up else 8
+        return pltpu.make_async_remote_copy(
+            src_ref=self.buf.at[slab],
+            dst_ref=self.buf.at[slab],
+            send_sem=self.sems.at[first + slab],
+            recv_sem=self.sems.at[first + 4 + slab],
+            device_id={"bucket": self.plane + (1 if up else -1)},
+            device_id_type=MESH_IDS,
+        )
+
+    def hop(self, h):
+        for up in (True, False):
+            slab = self.plane - h if up else self.plane + h
+            there = (slab >= 0) if up else (slab <= 3)
+            sends = (self.plane <= 2) if up else (self.plane >= 1)
+
+            @pl.when(there)
+            def _(up=up, slab=slab, sends=sends):
+                if h > 0:
+                    self.copy(up, slab).wait_recv()
+
+                @pl.when(sends)
+                def _():
+                    self.copy(up, slab).start()
+
+    def close(self):
+        for h in range(4):
+            for up in (True, False):
+                slab = self.plane - h if up else self.plane + h
+                there = (slab >= 0) if up else (slab <= 3)
+                sends = (self.plane <= 2) if up else (self.plane >= 1)
+
+                @pl.when(there & sends)
+                def _(up=up, slab=slab):
+                    self.copy(up, slab).wait_send()
+
+
 def close_kernel(
-    text_g, attn_g, out_g,
-    text_o, attn_o, out_o,
+    text_g, attn_g, out_g, ffn_t, dmod_ref, gg_ref, gs_ref, cond_ref,
+    text_o, attn_o, out_o, ffn_o, ada_o, small_o,
     tm, ta, tt, ts, am, aa, at_, as_, om, oa, ot, os_,
-    t_wide, a_wide, t_stage, a_stage, o_stage, o_got, o_sem, send_sems, recv_sems,
+    t_wide, a_wide, f_wide, t_stage, a_stage, o_stage, o_got, o_sem,
+    mods, mods_other, mod_sems, smalls, got, z_sems, ada_s, send_sems, recv_sems,
 ):
+    low = jnp.bfloat16
+    full = jnp.float32
     net = Net(send_sems, recv_sems)
-    meet_all(net)
+    meet_all(net, True)
     plane = lax.axis_index("bucket")
-    chip = net.me // 2
+    me = net.me
+    chip = me // 2
     out = Chain(net, out_g, om, oa, ot, os_, False)
     attn = Chain(net, attn_g, am, aa, at_, as_, True)
     text = Chain(net, text_g, tm, ta, tt, ts, True)
-    chains = [out, attn, text]
+    chains = [out, text, attn]
     for c in chains:
         c.core_start()
+
+    act = cond_ref[...].astype(full)
+    mods[plane, 0, :, 2 * D :] = (act * jax.nn.sigmoid(act)).astype(low)
+    mods[plane, 0, :, : 2 * D] = dmod_ref[...].astype(low)
+    mine = mods.at[plane, 0]
+    mod_io = [net.send(mine, mods.at[plane, i], m) for i, m in ((1, 2), (2, 4), (3, 6))]
+
+    smalls[...] = jnp.zeros(smalls.shape, full)
+    smalls[0:2, :] = gg_ref[0:2, :]
+    smalls[2:6, pl.ds(pl.multiple_of(chip * HW, 128), HW)] = gs_ref[0:4, :]
+    for p in range(4):
+        rows = dmod_ref[4 * (p // 2) : 4 * (p // 2) + 4, (p % 2) * D : (p % 2 + 1) * D]
+        smalls[8 + p : 9 + p, :] = jnp.sum(rows, axis=0, keepdims=True)
+    order = [None]
+
+    def small_send(i):
+        if i < 3:
+            order[0] = net.send(smalls, got.at[i], (1, 2, 4)[i])
+            return
+        there = plane + 1 - 2 * (plane % 2) if i == 3 else plane + 2 - 4 * (plane // 2)
+        copy = pltpu.make_async_remote_copy(
+            src_ref=smalls,
+            dst_ref=got.at[i],
+            send_sem=z_sems.at[2 * (i - 3)],
+            recv_sem=z_sems.at[2 * (i - 3) + 1],
+            device_id={"bucket": there},
+            device_id_type=MESH_IDS,
+        )
+        copy.start()
+        order[0] = copy
+
+    def small_add(i):
+        order[0].wait()
+        net.all = [c for c in net.all if c is not order[0]]
+        smalls[...] = smalls[...] + got[i]
+
+    small_send(0)
+    f_cols = Columns(net, None, ffn_t, f_wide, ffn_o)
+    f_cols.start()
     for c in chains:
         c.core_finish()
         c.step(0)
-    for t in (1, 2):
-        for c in chains:
-            c.step(t)
+    small_add(0)
+    small_send(1)
+    for c in mod_io:
+        c.wait_recv()
+    lines = Spread(mods, mod_sems)
+    lines.hop(0)
+    small_add(1)
+    small_send(2)
+    for c in chains:
+        c.step(1)
+    lines.hop(1)
+    small_add(2)
+    small_send(3)
+    f_cols.finish()
+    for c in chains:
+        c.step(2)
+    lines.hop(2)
+    small_add(3)
+    small_send(4)
+    lines.hop(3)
+    other = net.send(mods, mods_other, 1)
+    small_add(4)
+    small_o[...] = smalls[...]
     out.finish()
-    o_stage[...] = ot[...].astype(jnp.bfloat16)
+    o_stage[...] = ot[...].astype(low)
 
     @pl.when(chip != plane)
     def _():
         transposed(net, o_stage, o_got, o_sem).start()
 
-    attn.finish()
-    attn_cols = Columns(net, at_, a_stage, a_wide, attn_o)
-    attn_cols.start()
+    other.wait_recv()
+    rank = plane * 8 + me
+    lanes = pl.ds(pl.multiple_of(2 * D + (rank // 4) * 128, 128), 128)
+    total = 128
+    both = []
+    for ref in (mods, mods_other):
+        acts = ref[:, :, :, lanes].astype(full).reshape(total, 128)
+        both.append(acts)
+    acts = jnp.concatenate(both, axis=0)
+    upper = (lax.broadcasted_iota(jnp.int32, acts.shape, 0) % 8) < 4
+    parts = (jnp.where(upper, acts, 0.0).astype(low), jnp.where(upper, 0.0, acts).astype(low))
+    wide = 512
+
+    def ada_cols(i, _):
+        at = pl.ds(pl.multiple_of(i * wide, wide), wide)
+        rows = jnp.concatenate(
+            [r[:, :, :, at].astype(full).reshape(total, wide) for r in (mods, mods_other)], axis=0
+        ).astype(low)
+        for p in range(2):
+            ada_s[...] = t_dot(parts[p], rows)
+            to = pl.ds(pl.multiple_of(p * 2 * D + i * wide, wide), wide)
+            ada_o[:, to] = ada_s[pl.ds(pl.multiple_of((rank % 4) * 32, 32), 32), :]
+        return 0
+
+    lax.fori_loop(0, 2 * D // wide, ada_cols, 0)
+    text.finish()
+    text_cols = Columns(net, tt, t_stage, t_wide, text_o)
+    text_cols.start()
 
     @pl.when(chip != plane)
     def _():
@@ -1132,17 +1249,18 @@
     def _():
         out_o[...] = ot[...]
 
+    attn.finish()
+    attn_cols = Columns(net, at_, a_stage, a_wide, attn_o)
+    attn_cols.start()
+    text_cols.finish()
     attn_cols.finish()
-    text.finish()
-    text_cols = Columns(net, tt, t_stage, t_wide, text_o)
-    text_cols.start()
-    text_cols.finish()
     for c in chains:
         c.close()
+    lines.close()
     net.close()
 
 
-def close_layer(text_g, attn_g, out_g):
+def close_layer(text_g, attn_g, out_g, ffn_t, dmod, gg, gs, cond8):
     low = jnp.bfloat16
     full = jnp.float32
     shape = jax.ShapeDtypeStruct
@@ -1150,14 +1268,18 @@
     tr, tw = text_g.shape[-2], text_g.shape[-1] // 2
     ar, aw = attn_g.shape[-2], attn_g.shape[-1] // 3
     orow, ow = out_g.shape[-2:]
+    fr, fw = ffn_t.shape[-2], ffn_t.shape[-1] // 2
     return pl.pallas_call(
         close_kernel,
-        in_specs=[V] * 3,
-        out_specs=[V] * 3,
+        in_specs=[V] * 8,
+        out_specs=[V] * 6,
         out_shape=[
             shape((2, tr, 4 * tw), full),
             shape((3, ar, 4 * aw), full),
             shape((orow, ow), full),
+            shape((2, fr, 4 * fw), full),
+            shape((32, 4 * D), full),
+            shape((16, D), full),
         ],
         scratch_shapes=[
             *chain_scratch(True, (1, tr), 2 * tw),
@@ -1165,24 +1287,28 @@
             *chain_scratch(False, orow, ow),
             pltpu.VMEM((2, tr, 4 * tw), low),
             pltpu.VMEM((3, ar, 4 * aw), low),
+            pltpu.VMEM((2, fr, 4 * fw), low),
             pltpu.VMEM((1, 4, tr, 2 * tw), low),
             pltpu.VMEM((1, 4, ar, 3 * aw), low),
             pltpu.VMEM((orow, ow), low),
             pltpu.VMEM((orow, ow), low),
             pltpu.SemaphoreType.DMA((2,)),
-            *net_scratch(32),
+            pltpu.VMEM((4, CHIPS, 8, 2 * D + cond8.shape[1]), low),
+            pltpu.VMEM((4, CHIPS, 8, 2 * D + cond8.shape[1]), low),
+            pltpu.SemaphoreType.DMA((16,)),
+            pltpu.VMEM((16, D), full),
+            pltpu.VMEM((5, 16, D), full),
+            pltpu.SemaphoreType.DMA((4,)),
+            pltpu.VMEM((128, 512), full),
+            *net_scratch(40),
         ],
         compiler_params=pltpu.CompilerParams(
-            collective_id=2, has_side_effects=True, vmem_limit_bytes=63 * 1024 * 1024
+            collective_id=2, has_side_effects=True, vmem_limit_bytes=60 * 1024 * 1024
         ),
         cost_estimate=pl.CostEstimate(
             flops=1_000_000, bytes_accessed=400_000_000, transcendentals=0
         ),
-    )(text_g, attn_g, out_g)
-
-
-def column_of(v):
-    return jnp.transpose(v)[:, 0:1]
+    )(text_g, attn_g, out_g, ffn_t, dmod, gg, gs, cond8)
 
 
 def back_kernel(
@@ -1210,8 +1336,7 @@
     iq_ref, ik_ref, it_ref, cos_ref, sin_ref, sc_ref, sr_ref, gs_ref, ffn_g, down_g,
     block_o, token_o, db_ref, dqkv_o, dtkv_o, dmod_o, gg_o, gs_o, ffn_o, down_o,
     dx_s, dc_s, dqf, dkf, dtf, part_s, sums, tsums, buf_a, far_a, buf_b, far_b, buf_c, far_c,
-    fm, fa, ft, fs, dm, da, dt_c, ds_, f_wide, f_stage, d_stage, d_got, d_sem,
-    f_keep, d_keep, keep_sem, send_sems, recv_sems, loads,
+    fm, fa, ft, fs, dm, da, dt_c, ds_, f_keep, d_keep, keep_sem, send_sems, recv_sems, loads,
 ):
     low = jnp.bfloat16
     full = jnp.float32
@@ -1372,16 +1497,17 @@
     lax.fori_loop(0, D // wide, first_grad, 0)
     middle_c, finish_c = collect4(net, rows_of(part_s), buf_c, far_c)
     ffn.finish()
-    f_cols = Columns(net, ft, f_stage, f_wide, ffn_o)
     middle_c()
-    f_cols.start()
+
+    def ffn_cast(i, _):
+        ffn_o[0, i] = ft[0, i].astype(low)
+        return 0
+
+    lax.fori_loop(0, 4, ffn_cast, 0)
     down.finish()
-    d_stage[...] = dt_c[...].astype(low)
-
-    @pl.when(chip != plane)
-    def _():
-        transposed(net, d_stage, d_got, d_sem).start()
-
+    down_o[...] = dt_c[...].astype(low)
+    gate = jnp.tanh(gs_ref[5:6, :])
+    gs_o[3:4, :] = gs_o[3:4, :] * (1.0 - gate * gate)
     for i in (0, 1):
         part_s[pl.ds(i * half, half), :] = finish_c(i)
 
@@ -1402,17 +1528,6 @@
         return 0
 
     lax.fori_loop(0, ROW // block, first_rows, 0)
-    f_cols.finish()
-
-    @pl.when(chip != plane)
-    def _():
-        transposed(net, d_stage, d_got, d_sem).wait()
-        down_o[...] = d_got[...].astype(full)
-
-    @pl.when(chip == plane)
-    def _():
-        down_o[...] = dt_c[...]
-
     ffn.close()
     down.close()
     net.close()
@@ -1441,8 +1556,8 @@
             shape((8, 2 * D), full),
             shape((8, D), full),
             shape((8, HW), full),
-            shape((2, fr, 4 * fw), full),
-            shape((dr, dw), full),
+            shape((1, 4, fr, 2 * fw), low),
+            shape((dr, dw), low),
         ],
         scratch_shapes=[
             pltpu.VMEM((ROW, D), full),
@@ -1456,11 +1571,6 @@
             *reduce_scratch, *reduce_scratch, *reduce_scratch,
             *chain_scratch(True, (1, fr), 2 * fw),
             *chain_scratch(False, dr, dw),
-            pltpu.VMEM((2, fr, 4 * fw), low),
-            pltpu.VMEM((1, 4, fr, 2 * fw), low),
-            pltpu.VMEM((dr, dw), low),
-            pltpu.VMEM((dr, dw), low),
-            pltpu.SemaphoreType.DMA((2,)),
             pltpu.VMEM((1, 4, 4, fr, 2 * fw), low),
             pltpu.VMEM((4, dr, dw), low),
             pltpu.SemaphoreType.DMA((2,)),
@@ -1664,16 +1774,16 @@
         jnp.zeros((ada_weight.shape[1],), full), ada_bias.astype(full), slot * ada_bias.shape[0], 0
     )
     bias_pad = jnp.repeat(bias.reshape(2, 3072), 4, axis=0)
+    cond8 = jnp.concatenate([cond[0], cond[0]], axis=0)
     seg = segments[0]
     idx = jnp.concatenate([seg[None, :], positions[0], jnp.zeros((5, ROW), jnp.int32)], axis=0)
     (
         mod, gain_f, h_rows, idx_all, attn_w, text_rows, query, keyed, valued, text_keys, text_vals,
         inv_qk, inv_t,
     ) = open_layer(
-        jnp.concatenate([cond[0], cond[0]], axis=0), gain_pad, bias_pad, ada_weight, tokens[0],
+        cond8, gain_pad, bias_pad, ada_weight, tokens[0],
         seg[:, None], idx, attn_weight, text_weight, text[0],
     )
-    cond_act = silu(cond[0].astype(full)).astype(low)
     h_all = h_rows.reshape(CHIPS * ROW, D)
     text_all = text_rows.reshape(CHIPS * IMGS * TXT, -1)
     inv_qk = jnp.stack([inv_qk[0], inv_qk[4]])[:, :, None]
@@ -1723,7 +1833,7 @@
     g_ffn = t_dot(h_two_all, d_both).astype(low)
 
     (
-        block_out, token_grad, d_branch_rows, d_qkv, d_text, d_mod, gg_full, gg_slice, s_ffn, s_down,
+        block_out, token_grad, d_branch_rows, d_qkv, d_text, d_mod, gg_full, gg_slice, ffn_sum, down_sum,
     ) = back_layer(
         [
             d_h_two, ffn_out, x_one, branch, cotangent[0], weight_row, mod,
@@ -1740,48 +1850,20 @@
     g_text = t_dot(text_all, d_text).astype(low)
     g_attn = t_dot(h_all, d_qkv).astype(low)
     g_out = t_dot(comb, d_branch_all).astype(low)
-    s_text, s_attn, s_out = close_layer(
+    s_down = to_row_owner(down_sum)
+    s_text, s_attn, s_out, s_ffn, s_ada_w, small = close_layer(
         g_text.reshape(1, 4, 4, 2, 128, 2 * HW),
         g_attn.reshape(1, 4, 4, 2, 48, 3 * HW),
         g_out.reshape(4, 2, 48, D),
-    )
-
-    d_mod = jnp.concatenate([d_mod[:IMGS], d_mod[IMGS:]], axis=1)
-
-    gg = gg_slice[:4]
-    cross_gate = jnp.tanh(gain_s[5])
-    gg = gg.at[3].multiply(1.0 - cross_gate * cross_gate)
-    spread = lax.dynamic_update_slice_in_dim(jnp.zeros((4, D), full), gg, chip * HW, axis=1)
-    small = jnp.concatenate(
-        [gg_full[:2], spread, jnp.sum(d_mod, axis=0).reshape(4, D)], axis=0
-    )
-    small = small + at_core(small)
-    small = sum4(small)
-    small = small + lax.ppermute(small, "bucket", [(i, i ^ 1) for i in range(4)])
-    small = small + lax.ppermute(small, "bucket", [(i, i ^ 2) for i in range(4)])
+        ffn_sum,
+        d_mod,
+        gg_full,
+        gg_slice,
+        cond8,
+    )
     rank = plane * 8 + slot
     s_gains = lax.dynamic_slice_in_dim(small[:6], rank * 48, 48, axis=1)
-    s_ada_b = lax.dynamic_slice_in_dim(small[6:].reshape(-1), rank * 192, 192, axis=0)
-
-    mod_low = d_mod.astype(low)
-    mods = jnp.concatenate(gather4(mod_low), axis=0)
-    planes_m = [mods]
-    for shift in (1, 2, 3):
-        planes_m.append(
-            lax.ppermute(mods, "bucket", [(i, i ^ shift) for i in range(4)])
-        )
-    mods = jnp.concatenate(planes_m, axis=0)
-    mods = jnp.concatenate([mods, at_core(mods)], axis=0)
-    conds_all = jnp.concatenate(gather4(cond_act), axis=0)
-    planes_c = [conds_all]
-    for shift in (1, 2, 3):
-        planes_c.append(
-            lax.ppermute(conds_all, "bucket", [(i, i ^ shift) for i in range(4)])
-        )
-    conds_all = jnp.concatenate(planes_c, axis=0)
-    conds_all = jnp.concatenate([conds_all, at_core(conds_all)], axis=0)
-    s_ada_w = t_dot(lax.dynamic_slice_in_dim(conds_all, rank * 32, 32, axis=1), mods)
-
+    s_ada_b = lax.dynamic_slice_in_dim(small[8:12].reshape(-1), rank * 192, 192, axis=0)
     return (
         block_out[None],
         token_grad[None],

time: 638 us -> 590 us (0.925)
  starting transfers between devices: 52.8 us -> 1.65 us
  Pallas kernels: 467 us -> 493 us
  local copies, waits for them, and re-layouts: 36 us -> 21.7 us
    ppermute x21 -> x1, starting transfers between devices: 52.8 us -> 1.65 us  [to_row_owner(): return lax.ppermute(block, ('bucket', 'fsdp'), pairs).astype(jnp.float32)]
    pallas_call x1, Pallas kernels: 118 us -> 149 us  [close_layer(): pl.pallas_call(close_kernel, in_specs=[V] * 8, out_specs=[V] * 6, out_sha...]
    concatenate x6 -> x0, local copies, waits for them, and re-layouts: 12.7 us -> none  [the longest x1 4.11 us: per_device(): mods = jnp.concatenate([mods, at_core(mods)], axis=0)]
    dot_general x6 -> x5, matrix products: 30.6 us -> 26.7 us  [t_dot(): lax.dot_general(a, b, (((0,), (0,)), ((), ())), preferred_element_type=jn...]
  transfers between devices with their start and end apart: 21 -> 1, of which waited for: 3 -> 0; matrix products, arithmetic and copies ran while one was open for 5% -> 4% of each run, Pallas kernels for 19% -> 26%
where the time goes in v4:
time: 590 us; the launch traced here: 580 us
  Pallas kernels  493 us (84%)
  matrix products  42.9 us (7%)
  local copies, waits for them, and re-layouts  21.7 us (4%)
  other arithmetic  17.8 us (3%)
    pallas_call x1, Pallas kernels, open_layer(): pl.pallas_call(open_kernel, in_specs=[V, V, V, V, V, V, V, ANY_SPEC, ANY_...  169 us
    pallas_call x1, Pallas kernels, close_layer(): pl.pallas_call(close_kernel, in_specs=[V] * 8, out_specs=[V] * 6, out_sha...  149 us
    pallas_call x1, Pallas kernels, back_layer(): pl.pallas_call(back_kernel, in_specs=[V] * len(early) + [ANY_SPEC] * (LAT...  91.5 us
    pallas_call x1, Pallas kernels, forward_layer(): pl.pallas_call(forward_kernel, in_specs=[V] * (len(args) - 3) + [ANY_SPEC...  83.7 us
    dot_general x5, matrix products, t_dot(): lax.dot_general(a, b, (((0,), (0,)), ((), ())), preferred_element_type=jn...  26.7 us
  transfers between devices with their start and end apart: 1, of which 0 were waited for; matrix products, arithmetic and copies ran while one was open for 4% of the time, Pallas kernels for 26%

profile of v4, /device:TPU:0, one launch (start us, length us, event | category | flops | bytes accessed | tf_op | source)
XLA Modules:
  0.0 579.9 jit_solution(10516076731377684929)
XLA Ops:
  0.7 0.1 pad.13.clone
  0.8 0.7 fusion.10
  1.5 0.7 pad_convert_fusion
  2.2 1.4 pad_maximum_fusion.3.cond_ref
  3.6 0.8 convert_dynamic-update-slice_fusion
  4.4 1.4 copy.28.seg_ref
  5.8 0.7 reshape.155.bias_ref
  6.4 1.3 add_add_fusion.idx_ref
  7.8 0.2 dynamic_update_slice.6.gain_ref
  8.1 0.6 copy-done.7
  8.7 169.1 %shard_map.222 = (f32[8,3072]{1,0:T(8,128)}, f32[8,1536]{1,0:T(8,128)}, bf16[4,128,1536]{2,1,0:T(8,128)(2,1)}, s32[4,8,128]{2,1,0:T(8,128)}, bf16[1536,1152]{1,0...) custom-call(bf16[8,1024]{1,0:T(8,128)(2,1)} %pad_maximum_fusion.3.co, ...), custom_call_target="tpu_custom_call" | custom-call | flops 10000000000 | bytes 400000000 | tf_op jit(solution)/shard_map/pallas_call | solution.py:815
  177.7 0.8 slice_bitcast_fusion.1
  178.5 0.8 slice_bitcast_fusion
  179.3 1.4 fusion.9
  180.7 0.9 copy.32.sc_ref.rest_16_
  181.6 0.9 copy.30.ik_ref.rest_12_
  182.4 0.9 copy.29.iq_ref.rest_11_
  183.3 1.0 copy.31.it_ref.rest_13_
  184.3 0.6 convert_reduce_fusion
  186.1 1.3 constant_dynamic-slice_fusion.1.gs_ref
  187.4 10.2 %bitcast_select_fusion.8 = (f32[128]{0:T(128)S(1)}, f32[128]{0:T(128)S(1)}) fusion(f32[]{:T(128)} %bitcast.27, f32[]{:T(128)} %bitcast.28, f32[]{:T(128)} %bitcast.29, f32[]{:T(128)} %bitcast.30, f32[]{:T(128)} %bitcast.31, f32[]{:T(128)} %bitcast.33, f32[]{:T(128)} %bitcast.32, f32[]{:T(128)} %bitcast.10, f32[]{:T(128)} %bitcast.12, f32[]{:T(128)} %bitcast.14, ...), kind=kLoop, calls=%fused_computation.36 | loop fusion | flops 7680 | bytes 1088 | tf_op jit(solution)/shard_map/gather | solution.py:1797
  197.6 1.8 sine_multiply_fusion
  199.4 0.5 broadcast_in_dim.78.w_ref
  199.9 83.7 %shard_map.223 = (bf16[512,384]{1,0:T(8,128)(2,1)}, f32[512,384]{1,0:T(8,128)}, bf16[512,384]{1,0:T(8,128)(2,1)}, bf16[512,384]{1,0:T(8,128)(2,1)}, bf16[1024,38...) custom-call(f32[512,384]{1,0:T(8,128)} %get-tuple-element.51.q_ref.r, ...), custom_call_target="tpu_custom_call" | custom-call | flops 5000000000 | bytes 200000000 | tf_op jit(solution)/shard_map/pallas_call | solution.py:1709
  283.7 6.1 %fusion.11 = f32[512,2048]{1,0:T(8,128)S(1)} fusion(bf16[512,1536]{1,0:T(8,128)(2,1)} %bitcast.119, bf16[1536,2048]{1,0:T(8,128)(2,1)} %get-tuple-element.64), kind=kOutput, calls=%fused_computation.69 | convolution fusion | flops 3221225472 | bytes 12058624 | tf_op jit(solution)/shard_map/dot_general | solution.py:142
  289.8 2.6 multiply_convert_fusion.2
  292.4 3.0 convolution_convert_fusion.4.fo_ref
  295.4 3.5 convolution_convert_fusion.3
  298.9 4.6 convolution_convert_fusion.5.dh2_ref
  303.5 5.5 convolution_convert_fusion
  309.0 91.5 %shard_map.224 = (bf16[128,1536]{1,0:T(8,128)(2,1)}, f32[128,1536]{1,0:T(8,128)}, bf16[4,128,1536]{2,1,0:T(8,128)(2,1)}, bf16[512,1152]{1,0:T(8,128)(2,1)}, bf16...) custom-call(bf16[512,1536]{1,0:T(8,128)(2,1)} %convolution_convert_f, ...), custom_call_target="tpu_custom_call" | custom-call | flops 10000000000 | bytes 400000000 | tf_op jit(solution)/shard_map/pallas_call | solution.py:1546
  400.5 1.7 collective-permute-start
  402.2 11.8 %convolution_convert_fusion.2 = bf16[4096,768]{1,0:T(8,128)(2,1)} fusion(bf16[1024,4096]{1,0:T(8,128)(2,1)} %bitcast.114, bf16[1024,768]{1,0:T(8,128)(2,1)} %get-tuple-element.76), kind=kOutput, calls=%fused_computation.2 | convolution fusion | flops 6445596672 | bytes 16252928 | tf_op jit(solution)/shard_map/dot_general | solution.py:331
  414.1 4.0 convolution_convert_fusion.1
  418.1 1.8 convolution_convert_fusion.6
  419.9 149.1 %shard_map.225 = (f32[2,128,1536]{2,1,0:T(8,128)}, f32[3,48,1536]{2,1,0:T(8,128)}, f32[48,1536]{1,0:T(8,128)}, f32[2,48,4096]{2,1,0:T(8,128)}, f32[32,6144]{1,0:T(8,128)}, /*index=5*/f32[16,1536]{1,0:T(8,128)}) custom-call(bf16[1,4,4,2,128,768]{5,4,3,2,1,0:T(8,128)(2,1)} %bitcast.98, bf16[1,4,4,2,48,1152]{5,4,3,2,1,0:T(8,128)(2,1)} %bitcast.99, ...), custom_call_target="tpu_custom_call" | custom-call | flops 1000000 | bytes 400000000 | tf_op jit(solution)/shard_map/pallas_call | solution.py:1272
  569.0 0.9 slice.51
  569.9 0.8 slice.52
  570.7 0.6 dynamic_slice.10
  571.4 0.7 constant_dynamic-slice_fusion
  572.0 1.0 convert_element_type.59
  573.0 0.7 copy.48
  573.8 0.9 copy.49
  574.6 0.9 copy.50
  575.5 0.9 copy.51
  576.4 0.7 copy.52
  577.2 1.1 copy.53
  578.3 1.1 copy.54
  (45 shorter events, 0.2 us)
Async XLA Ops:
  8.0 0.6 copy-start.7
  8.7 175.6 %copy-start.8 = (s32[4]{0:T(128)S(1)}, s32[4]{0:T(128)}, u32[]{:S(2)}) copy-start(s32[4]{0:T(128)} %param.20) | copy-start | bytes 52
  283.7 6.2 %copy-start.12 = (bf16[4,128,1536]{2,1,0:T(8,128)(2,1)S(1)}, bf16[4,128,1536]{2,1,0:T(8,128)(2,1)}, u32[]{:S(2)}) copy-start(bf16[4,128,1536]{2,1,0:T(8,128)(2,1)} %get-tuple-element.61) | copy-start | bytes 4718596
  283.7 6.2 %copy-start.14 = (bf16[1024,1536]{1,0:T(8,128)(2,1)S(1)}, bf16[1024,1536]{1,0:T(8,128)(2,1)}, u32[]{:S(2)}) copy-start(bf16[1024,1536]{1,0:T(8,128)(2,1)} %get-tuple-element.62) | copy-start | bytes 9437188
  292.4 6.5 %slice-start = ((s8[6291456]{0:T(1024)(128)(4,1)}), s8[4194304]{0:T(1024)(128)(4,1)S(1)}, s32[]{:S(2)}) async-start(s8[6291456]{0:T(1024)(128)(4,1)} %bitcast.123), calls=%async_computation | async-start | bytes 8388608
  295.4 3.5 slice-start.1
  298.9 4.6 copy-start.11
  400.5 171.5 %collective-permute-start = (bf16[128,1536]{1,0:T(8,128)(2,1)}, bf16[128,1536]{1,0:T(8,128)(2,1)S(1)}, u32[]{:S(2)}, u32[]{:S(2)}) collective-permute-start(bf16[128,1536]{1,0:T(8,128)(2,1)} %get-tuple-element.91), channel_id=1, source_target_pairs={{0,0},{1,1},{2,8},{3,9},{4,16},{5,17},{6,24},{7,25},{8,2},{9,3},{1... | collective-permute-start | bytes 1179656 | tf_op jit(solution)/shard_map/ppermute | solution.py:458
  402.2 11.8 %copy-start.9 = (bf16[4,128,1536]{2,1,0:T(8,128)(2,1)S(1)}, bf16[4,128,1536]{2,1,0:T(8,128)(2,1)}, u32[]{:S(2)}) copy-start(bf16[4,128,1536]{2,1,0:T(8,128)(2,1)} %get-tuple-element.77) | copy-start | bytes 4718596
  402.2 11.8 %copy-start.15 = (bf16[512,1152]{1,0:T(8,128)(2,1)S(1)}, bf16[512,1152]{1,0:T(8,128)(2,1)}, u32[]{:S(2)}) copy-start(bf16[512,1152]{1,0:T(8,128)(2,1)} %get-tuple-element.78) | copy-start | bytes 3538948
  414.0 4.0 copy-start.10
  414.0 4.0 copy-start.13
  419.9 153.1 %copy-start.5 = (bf16[128,1536]{1,0:T(8,128)(2,1)S(1)}, bf16[128,1536]{1,0:T(8,128)(2,1)}, u32[]{:S(2)}) copy-start(bf16[128,1536]{1,0:T(8,128)(2,1)} %get-tuple-element.73) | copy-start | bytes 1179652
  569.0 4.8 copy-start.3
  569.0 5.7 copy-start.4
  573.0 2.5 copy-start.2
  573.8 2.7 copy-start.6
  574.6 2.5 copy-start.1
  576.4 1.9 copy-start

commit v5 on v4

--- a/solution.py
+++ b/solution.py
@@ -1,5 +1,6 @@
 import jax
 import jax.numpy as jnp
+import numpy as np
 from jax import lax
 from jax.experimental import pallas as pl
 from jax.experimental.pallas import tpu as pltpu
@@ -571,50 +572,137 @@
     return jnp.where(lax.broadcasted_iota(jnp.int32, got.shape, 0) < 4, got, one(b))
 
 
-def spread(net, src, dst, width, local):
-    count, rows, _ = src.shape
-
-    def cut(i, c):
-        return src.at[i, :, pl.ds(pl.multiple_of(c * width, 128), width)]
-
-    def put(i, f):
-        return dst.at[pl.ds(pl.multiple_of(f * rows, rows), rows), pl.ds(i * width, width)]
-
-    chip = net.me // 2
-    ids = range(count)
-    here = [local(cut(i, chip), put(i, net.me)) for i in ids]
-    core = [net.send(cut(i, chip), put(i, net.me), 1) for i in ids]
-
-    def away(m):
-        return [net.send(cut(i, net.peer(m) // 2), put(i, net.me), m) for i in ids]
-
-    def whole(f):
-        return dst.at[pl.ds(pl.multiple_of(f * rows, rows), rows), :]
-
-    def pass_on(copies, m):
-        for c in copies:
+class Lines:
+    MASKS = (2, 4, 6)
+
+    def __init__(self, net, src, dst, width, sems, local):
+        self.net, self.src, self.dst, self.width, self.sems = net, src, dst, width, sems
+        self.plane = lax.axis_index("bucket")
+        self.chip = net.me // 2
+        self.core = net.me % 2
+        self.local = local
+        self.ids = range(src.shape[0])
+
+    def columns(self, c):
+        return pl.ds(pl.multiple_of(c * self.width, 128), self.width)
+
+    def lanes(self, i):
+        return pl.ds(i * self.width, self.width)
+
+    def away_start(self):
+        own = self.dst.at[self.chip, self.core, self.plane]
+        self.away = [
+            self.net.send(
+                self.src.at[i, self.plane, :, self.columns(self.net.peer(m) // 2)],
+                own.at[:, self.lanes(i)],
+                m,
+            )
+            for m in self.MASKS
+            for i in self.ids
+        ]
+
+    def own_start(self):
+        own = self.dst.at[self.chip, self.core]
+        cuts = [self.src.at[i, :, :, self.columns(self.chip)] for i in self.ids]
+        puts = [own.at[:, :, self.lanes(i)] for i in self.ids]
+        self.ready = [self.net.send(a, b, 1) for a, b in zip(cuts, puts)]
+        self.here = [self.local(i, a, b) for i, (a, b) in enumerate(zip(cuts, puts))]
+
+    def copy(self, up, k, slab):
+        at = self.dst.at[self.net.peer(self.MASKS[k]) // 2, self.core, slab]
+        first = ((k * 2 + (0 if up else 1)) * 4 + slab) * 2
+        return pltpu.make_async_remote_copy(
+            src_ref=at,
+            dst_ref=at,
+            send_sem=self.sems.at[first],
+            recv_sem=self.sems.at[first + 1],
+            device_id={"bucket": self.plane + (1 if up else -1)},
+            device_id_type=MESH_IDS,
+        )
+
+    def moves(self, h):
+        for up in (True, False):
+            slab = self.plane - h if up else self.plane + h
+            there = (slab >= 0) if up else (slab <= 3)
+            sends = (self.plane <= 2) if up else (self.plane >= 1)
+            yield up, slab, there, sends
+
+    def hop(self, h):
+        if h == 0:
+            for c in self.away:
+                c.wait_recv()
+        for up, slab, there, sends in self.moves(h):
+
+            @pl.when(there)
+            def _(up=up, slab=slab, sends=sends):
+                for k in range(3):
+                    if h > 0:
+                        self.copy(up, k, slab).wait_recv()
+                    if h < 3:
+
+                        @pl.when(sends)
+                        def _(k=k):
+                            self.copy(up, k, slab).start()
+
+    def finish(self):
+        self.hop(3)
+        for m in self.MASKS:
+            at = self.dst.at[self.net.peer(m) // 2, self.core]
+            self.ready.append(self.net.send(at, at, 1))
+
+    def wait(self):
+        for c in self.ready:
             c.wait_recv()
-        return net.send(whole(net.peer(m)), whole(net.peer(m)), 1)
-
-    return here, core, away, pass_on
+
+    def close(self):
+        for h in range(3):
+            for up, slab, there, sends in self.moves(h):
+
+                @pl.when(there & sends)
+                def _(up=up, slab=slab):
+                    for k in range(3):
+                        self.copy(up, k, slab).wait_send()
+
+
+def meet_line(net, masks):
+    plane = lax.axis_index("bucket")
+    sem = pltpu.get_barrier_semaphore()
+    for mask in masks:
+        pl.semaphore_signal(
+            sem, inc=1, device_id={"fsdp": net.peer(mask)}, device_id_type=MESH_IDS
+        )
+    for inner, step in ((plane >= 1, -1), (plane <= 2, 1)):
+
+        @pl.when(inner)
+        def _(step=step):
+            pl.semaphore_signal(
+                sem, inc=1, device_id={"bucket": plane + step}, device_id_type=MESH_IDS
+            )
+
+    one = jnp.int32(1)
+    zero = jnp.int32(0)
+    pl.semaphore_wait(
+        sem, len(masks) + jnp.where(plane >= 1, one, zero) + jnp.where(plane <= 2, one, zero)
+    )
 
 
 ALL_PEERS = (1, 2, 3, 4, 5, 6, 7)
 
 
 def open_kernel(
-    cond_ref, gain_ref, bias_ref, ada_ref, tok_ref, seg_ref, idx_ref, attn_ref, textw_ref, text_ref,
+    cond_ref, gain_ref, bias_ref, ada_ref, tok_ref, seg_ref, idx_ref, freq_ref, attn_ref, textw_ref,
+    text_ref,
     mod_ref, gains_ref, h_ref, idxs_ref, aw_ref, ta_out, q_ref, k_ref, v_ref, tk_ref, tv_ref,
-    iqk_ref, it_ref,
-    conds, parts, mods, gbuf, tw_ref, ta_ref, sums, tsums, local_sems, out_sems, send_sems,
-    recv_sems,
+    iq_ref, ik_ref, it_ref, cos_ref, sin_ref, sc_ref, gs_ref,
+    conds, parts, mods, gbuf, tw_ref, ta_ref, sums, tsums, local_sems, out_sems, attn_sems, text_sems,
+    send_sems, recv_sems,
 ):
     low = jnp.bfloat16
     full = jnp.float32
     net = Net(send_sems, recv_sems)
     me = net.me
     chip = me // 2
-    net.meet(ALL_PEERS)
+    meet_line(net, ALL_PEERS)
 
     act = cond_ref[...].astype(full)
     act = (act * jax.nn.sigmoid(act)).astype(low).astype(full)
@@ -629,6 +717,20 @@
     iwaits = [net.send(idx_ref, idxs_ref.at[i], m) for i, m in ((1, 2), (2, 4), (3, 6))]
     idxs_ref[0] = idx_ref[...]
 
+    def local(first):
+        def go(i, src, dst):
+            copy = pltpu.make_async_copy(src, dst, local_sems.at[first + i])
+            copy.start()
+            return copy
+
+        return go
+
+    attn_io = Lines(net, attn_ref, aw_ref, HW, attn_sems, local(3))
+    text_io = Lines(net, textw_ref, tw_ref, HW, text_sems, local(6))
+    attn_io.away_start()
+    text_io.away_start()
+    own_text = local(2)(0, text_ref, ta_ref.at[0])
+
     for w in waits:
         w.wait_recv()
     lhs = jnp.concatenate([conds[m] for m in range(8)], axis=0).astype(low)
@@ -650,22 +752,30 @@
     lax.fori_loop(0, half_cols // step, mod_cols, 0)
     waits = [net.send(parts.at[m], mods.at[m], m) for m in ALL_PEERS]
 
-    def local(slot):
-        def go(src, dst):
-            copy = pltpu.make_async_copy(src, dst, local_sems.at[slot[0]])
-            slot[0] += 1
-            copy.start()
-            return copy
-
-        return go
-
-    slot = [3]
-    attn_io = spread(net, attn_ref, aw_ref, HW, local(slot))
-    attn_away = [attn_io[2](m) for m in (2, 4, 6)]
-    text_io = spread(net, textw_ref, tw_ref, HW, local(slot))
-    text_away = [text_io[2](m) for m in (2, 4, 6)]
-    own_text = pltpu.make_async_copy(text_ref, ta_ref.at[0], local_sems.at[2])
-    own_text.start()
+    attn_io.own_start()
+    text_io.own_start()
+    own_text.wait()
+
+    def keep(j):
+        copy = pltpu.make_async_copy(ta_ref.at[j], ta_out.at[j], out_sems.at[j])
+        copy.start()
+        return copy
+
+    kept = [keep(0)]
+    chunks = 4
+    size = ta_ref.shape[1] // chunks
+    tx, ty = [None] * chunks, [None] * chunks
+
+    def text_send(s):
+        i, j = s, (s + chunks // 2) % chunks
+        at = pl.ds(i * size, size)
+        tx[i] = net.send(ta_ref.at[0, at], ta_ref.at[1, at], 2)
+        at = pl.ds(j * size, size)
+        ty[j] = net.send(ta_ref.at[0, at], ta_ref.at[2, at], 4)
+
+    text_send(0)
+    attn_io.hop(0)
+    text_io.hop(0)
     for w in gwaits:
         w.wait_recv()
     gains = gain_ref[...]
@@ -698,70 +808,15 @@
     lax.fori_loop(0, ROW // block, first_norm, 0)
     hx, hy = share4_start(net, h_ref)
 
-    def all_in(io, away):
-        for c in io[0]:
-            c.wait()
-        return io[1] + [io[3](c, m) for c, m in zip(away, (2, 4, 6))]
-
-    attn_core = all_in(attn_io, attn_away)
-    text_core = all_in(text_io, text_away)
+    text_send(1)
+    attn_io.hop(1)
     h_far = share4_relay(net, h_ref, hx, hy)
-    own_text.wait()
-
-    def keep(j):
-        copy = pltpu.make_async_copy(ta_ref.at[j], ta_out.at[j], out_sems.at[j])
-        copy.start()
-        return copy
-
-    kept = [keep(0)]
-    chunks = 4
-    size = ta_ref.shape[1] // chunks
-    tx, ty = [None] * chunks, [None] * chunks
-    for s in range(chunks):
-        i, j = s, (s + chunks // 2) % chunks
-        at = pl.ds(i * size, size)
-        tx[i] = net.send(ta_ref.at[0, at], ta_ref.at[1, at], 2)
-        at = pl.ds(j * size, size)
-        ty[j] = net.send(ta_ref.at[0, at], ta_ref.at[2, at], 4)
-
-    for c in attn_core:
-        c.wait_recv()
-    for c in h_far:
-        c.wait_recv()
-
-    for j in range(CHIPS):
-        h = h_ref[j]
-        at = pl.ds(j * ROW, ROW)
-        qv = jnp.dot(h, aw_ref[:, :HW], preferred_element_type=full)
-        q_ref[at, :] = qv
-        kv = jnp.dot(h, aw_ref[:, HW : 2 * HW], preferred_element_type=full)
-        k_ref[at, :] = kv
-        v_ref[at, :] = jnp.dot(h, aw_ref[:, 2 * HW :], preferred_element_type=full).astype(low)
-        sums[0, :, at] = row_sums(qv * qv, kv * kv)
-    sum_io = [net.send(sums.at[0], sums.at[i], m) for i, m in ((1, 2), (2, 4), (3, 6))]
-
-    for c in text_core:
-        c.wait_recv()
-
-    def text_rows(j, lo, count):
-        kt = 1024
-
-        def body(i, acc):
-            at = pl.ds(pl.multiple_of(i * kt, kt), kt)
-            rows = ta_ref[j, pl.ds(lo, count), at]
-            return acc + jnp.dot(rows, tw_ref[at, :], preferred_element_type=full)
-
-        both = lax.fori_loop(0, ta_ref.shape[2] // kt, body, jnp.zeros((count, 2 * HW), full))
-        keys, vals = both[:, :HW], both[:, HW:]
-        at = pl.ds(j * ta_ref.shape[1] + lo, count)
-        tk_ref[at, :] = keys
-        tv_ref[at, :] = vals.astype(low)
-        tsums[0, :, at] = row_sums(keys * keys, None)
-
-    cap = ta_ref.shape[1]
-    half = cap // 2
-    for lo in (0, half):
-        text_rows(0, lo, half)
+    for i in range(2, chunks):
+        text_send(i)
+    text_io.hop(1)
+    attn_io.hop(2)
+    attn_io.finish()
+    text_io.hop(2)
     relays = []
     for s in range(chunks // 2):
         i, j = s, s + chunks // 2
@@ -771,13 +826,74 @@
         ty[j].wait_recv()
         at = pl.ds(j * size, size)
         relays.append(net.send(ta_ref.at[2, at], ta_ref.at[3, at], 2))
+
+    for c in iwaits:
+        c.wait_recv()
+    gs_ref[...] = gains_ref[:, pl.ds(pl.multiple_of(chip * HW, 128), HW)]
+    lane = lax.broadcasted_iota(jnp.int32, (ROW, 128), 1)
+    sign = jnp.where((lane // 16) % 2 == 0, -1.0, 1.0)
+    for j in range(CHIPS):
+        at = pl.ds(j * ROW, ROW)
+        cols = jnp.transpose(idxs_ref[j].astype(full))
+        sc_ref[at, :] = cols[:, 0:1].astype(jnp.int32)
+        place = jnp.where((lane // 32) % 2 == 0, cols[:, 1:2], cols[:, 2:3])
+        angle = place * freq_ref[0:1, :]
+        cos_ref[at, :] = jnp.cos(angle)
+        sin_ref[at, :] = sign * jnp.sin(angle)
+
+    attn_io.wait()
+    for c in attn_io.here:
+        c.wait()
+    for c in h_far:
+        c.wait_recv()
+
+    def columns(lo, hi):
+        return aw_ref[:, :, :, :, lo:hi].reshape(D, hi - lo)
+
+    for j in range(CHIPS):
+        h = h_ref[j]
+        at = pl.ds(j * ROW, ROW)
+        qv = jnp.dot(h, columns(0, HW), preferred_element_type=full)
+        q_ref[at, :] = qv
+        kv = jnp.dot(h, columns(HW, 2 * HW), preferred_element_type=full)
+        k_ref[at, :] = kv
+        v_ref[at, :] = jnp.dot(h, columns(2 * HW, 3 * HW), preferred_element_type=full).astype(low)
+        sums[0, :, at] = row_sums(qv * qv, kv * kv)
+    sum_io = [net.send(sums.at[0], sums.at[i], m) for i, m in ((1, 2), (2, 4), (3, 6))]
+
+    text_io.finish()
+    text_io.wait()
+    for c in text_io.here:
+        c.wait()
+
+    def text_rows(j, lo, count):
+        kt = 1024
+
+        def body(i, acc):
+            at = pl.ds(pl.multiple_of(i * kt, kt), kt)
+            rows = ta_ref[j, pl.ds(lo, count), at]
+            return acc + jnp.dot(rows, tw_ref[i].reshape(kt, 2 * HW), preferred_element_type=full)
+
+        both = lax.fori_loop(0, ta_ref.shape[2] // kt, body, jnp.zeros((count, 2 * HW), full))
+        keys, vals = both[:, :HW], both[:, HW:]
+        at = pl.ds(j * ta_ref.shape[1] + lo, count)
+        tk_ref[at, :] = keys
+        tv_ref[at, :] = vals.astype(low)
+        tsums[0, :, at] = row_sums(keys * keys, None)
+
+    cap = ta_ref.shape[1]
+    half = cap // 2
+    for lo in (0, half):
+        text_rows(0, lo, half)
     for i, c in enumerate(sum_io):
         c.wait_recv()
     for j in range(CHIPS):
         total = sums[0, :, pl.ds(j * ROW, ROW)]
         for i in (1, 2, 3):
             total = total + sums[i, :, pl.ds((j ^ i) * ROW, ROW)]
-        iqk_ref[:, pl.ds(j * ROW, ROW)] = lax.rsqrt(total / D + EPS)
+        both = jnp.transpose(lax.rsqrt(total / D + EPS))
+        iq_ref[pl.ds(j * ROW, ROW), :] = both[:, 0:1]
+        ik_ref[pl.ds(j * ROW, ROW), :] = both[:, 4:5]
     text_rows(1, 0, half)
     text_rows(2, half, half)
     for s in range(chunks // 2):
@@ -798,15 +914,15 @@
         total = tsums[0, :, pl.ds(j * cap, cap)]
         for i in (1, 2, 3):
             total = total + tsums[i, :, pl.ds((j ^ i) * cap, cap)]
-        it_ref[:, pl.ds(j * cap, cap)] = lax.rsqrt(total / D + EPS)
-    for c in iwaits:
-        c.wait_recv()
+        it_ref[pl.ds(j * cap, cap), :] = jnp.transpose(lax.rsqrt(total / D + EPS))[:, 0:1]
     for c in kept:
         c.wait()
+    attn_io.close()
+    text_io.close()
     net.close()
 
 
-def open_layer(cond8, gain_pad, bias_pad, ada, tok, seg_col, idx, attn, textw, text):
+def open_layer(cond8, gain_pad, bias_pad, ada, tok, seg_col, idx, freq, attn, textw, text):
     low = jnp.bfloat16
     full = jnp.float32
     shape = jax.ShapeDtypeStruct
@@ -814,34 +930,41 @@
     V = VMEM_SPEC
     return pl.pallas_call(
         open_kernel,
-        in_specs=[V, V, V, V, V, V, V, ANY_SPEC, ANY_SPEC, ANY_SPEC],
-        out_specs=[V] * 5 + [ANY_SPEC] + [V] * 7,
+        in_specs=[V] * 8 + [ANY_SPEC] * 3,
+        out_specs=[V] * 5 + [ANY_SPEC] + [V] * 12,
         out_shape=[
             shape((8, 3072), full),
             shape((8, D), full),
             shape((CHIPS, ROW, D), low),
             shape((CHIPS, 8, ROW), jnp.int32),
-            shape((D, 3 * HW), low),
+            shape((CHIPS, 2, *attn.shape[1:3], 3 * HW), low),
             shape((CHIPS, cap, txtd), low),
             shape((CHIPS * ROW, HW), full),
             shape((CHIPS * ROW, HW), full),
             shape((CHIPS * ROW, HW), low),
             shape((CHIPS * cap, HW), full),
             shape((CHIPS * cap, HW), low),
-            shape((8, CHIPS * ROW), full),
-            shape((8, CHIPS * cap), full),
+            shape((CHIPS * ROW, 1), full),
+            shape((CHIPS * ROW, 1), full),
+            shape((CHIPS * cap, 1), full),
+            shape((CHIPS * ROW, 128), full),
+            shape((CHIPS * ROW, 128), full),
+            shape((CHIPS * ROW, 1), jnp.int32),
+            shape((8, HW), full),
         ],
         scratch_shapes=[
             pltpu.VMEM((8, 8, 128), full),
             pltpu.VMEM((8, 8, 3072), full),
             pltpu.VMEM((8, 8, 3072), full),
             pltpu.VMEM((9, 8, D), full),
-            pltpu.VMEM((txtd, 2 * HW), low),
+            pltpu.VMEM((CHIPS, 2, *textw.shape[1:3], 2 * HW), low),
             pltpu.VMEM((CHIPS, cap, txtd), low),
             pltpu.VMEM((CHIPS, 8, CHIPS * ROW), full),
             pltpu.VMEM((CHIPS, 8, CHIPS * cap), full),
             pltpu.SemaphoreType.DMA((8,)),
             pltpu.SemaphoreType.DMA((CHIPS,)),
+            pltpu.SemaphoreType.DMA((48,)),
+            pltpu.SemaphoreType.DMA((48,)),
             *net_scratch(80),
         ],
         compiler_params=pltpu.CompilerParams(
@@ -850,7 +973,7 @@
         cost_estimate=pl.CostEstimate(
             flops=10_000_000_000, bytes_accessed=400_000_000, transcendentals=0
         ),
-    )(cond8, gain_pad, bias_pad, ada, tok, seg_col, idx, attn, textw, text)
+    )(cond8, gain_pad, bias_pad, ada, tok, seg_col, idx, freq, attn, textw, text)
 
 
 class Chain:
@@ -1440,7 +1563,7 @@
             qr_ref.at[rows], kr_ref.at[rows], v_ref.at[rows], tr_ref.at[text], tv_ref.at[text],
             dc_s, cross_ref.at[rows], q_ref.at[rows], k_ref.at[rows], tk_ref.at[text],
             iq_ref.at[rows], ik_ref.at[rows], it_ref.at[text], cos_ref.at[rows], sin_ref.at[rows],
-            sc_ref.at[rows], sr_ref.at[j], gs_ref,
+            sc_ref.at[rows], sr_ref.at[j, pl.ds(0, 1)], gs_ref,
             dqv, dkv, dqkv_o.at[rows, pl.ds(2 * HW, HW)], dtv, dtkv_o.at[text, pl.ds(HW, HW)], gs_o,
         )
         sums[0, :, rows] = row_sums(
@@ -1595,15 +1718,15 @@
     q_ref, k_ref, v_ref, iq_ref, ik_ref, cos_ref, sin_ref, tk_ref, it_ref, tv_ref, sc_ref, sr_ref,
     gs_ref, mod_ref, seg_ref, gain_ref, tok_ref, cot_ref, w_ref, outw_ref, ffnw_ref, downw_ref,
     comb_o, cross_o, qr_o, kr_o, tr_o, branch_o, x1_o, h_o, df_o, ow_o, fw_o, dw_o,
-    part_s, buf, far, f_own, d_own, local_sems, send_sems, recv_sems,
+    part_s, buf, far, f_own, d_own, local_sems, line_sems, send_sems, recv_sems,
 ):
     low = jnp.bfloat16
     full = jnp.float32
     net = Net(send_sems, recv_sems)
-    net.meet((1, 2, 4, 6))
+    meet_line(net, (1, 2, 4, 6))
     me = net.me
     chip = me // 2
-    width = fw_o.shape[1] // 2
+    width = fw_o.shape[4] // 2
     rows = outw_ref.shape[0]
 
     def local(src, dst, i):
@@ -1619,16 +1742,13 @@
     down_rows = downw_ref.shape[0]
     down_here = local(downw_ref, d_own, 1)
     down_core = net.send(downw_ref, own(dw_o, down_rows), 1)
-    f_rows = ffnw_ref.shape[1]
-    place = [2]
-
-    def stage(src, dst):
-        i = place[0]
-        place[0] += 1
-        return local(src, f_own.at[:, pl.ds((i - 2) * width, width)], i)
-
-    f_here, f_core, f_away, f_pass = spread(net, ffnw_ref, fw_o, width, stage)
-    f_x, f_y = f_away(2), f_away(4)
+
+    def stage(i, src, dst):
+        return local(src, f_own.at[:, :, pl.ds(i * width, width)], 2 + i)
+
+    ffn_io = Lines(net, ffnw_ref, fw_o, width, line_sems, stage)
+    ffn_io.away_start()
+    ffn_io.own_start()
     block = 32
     weight = w_ref[0:1, 0:1]
 
@@ -1639,18 +1759,27 @@
         return 0
 
     lax.fori_loop(0, ROW // block, ffn_grad, 0)
+    dx, dy = share4_start(net, df_o)
     out_here.wait()
     out_core.wait_recv()
     cap = IMGS * TXT
 
     def attention_row(i, _):
+        @pl.when(i == 1)
+        def _():
+            ffn_io.hop(0)
+
+        @pl.when(i == 3)
+        def _():
+            ffn_io.hop(1)
+
         j = 3 - i
         at = pl.ds(pl.multiple_of(j * ROW, ROW), ROW)
         text = pl.ds(pl.multiple_of(j * cap, cap), cap)
         attend_kernel(
             q_ref.at[at], k_ref.at[at], v_ref.at[at], iq_ref.at[at], ik_ref.at[at],
             cos_ref.at[at], sin_ref.at[at], tk_ref.at[text], it_ref.at[text], tv_ref.at[text],
-            sc_ref.at[at], sr_ref.at[j], gs_ref,
+            sc_ref.at[at], sr_ref.at[j, pl.ds(0, 1)], gs_ref,
             comb_o.at[at], cross_o.at[at], qr_o.at[at], kr_o.at[at], tr_o.at[text],
         )
         part_s[at, :] = jnp.dot(comb_o[at, :], ow_o[...], preferred_element_type=full)
@@ -1661,15 +1790,15 @@
     middle, finish = collect4(
         net, lambda j, i: part_s[pl.ds(j * ROW + i * half, half), :], buf, far
     )
-    f_far = f_away(6)
-    dx, dy = share4_start(net, df_o)
+    df_far = share4_relay(net, df_o, dx, dy)
 
     down_here.wait()
     down_out = local(d_own, own(dw_o, down_rows), 4)
-    for c in f_here:
+    for c in ffn_io.here:
         c.wait()
-    f_out = local(f_own, fw_o.at[pl.ds(pl.multiple_of(me * f_rows, f_rows), f_rows), :], 5)
+    f_out = local(f_own, fw_o.at[chip, me % 2], 5)
     middle()
+    ffn_io.hop(2)
     for i in (0, 1):
         branch_o[pl.ds(i * half, half), :] = finish(i)
 
@@ -1686,14 +1815,14 @@
 
     lax.fori_loop(0, ROW // block, second, 0)
     hx, hy = share4_start(net, h_o)
-    last = [f_pass(f_x, 2), f_pass(f_y, 4)]
-    last += share4_relay(net, df_o, dx, dy)
-    last += share4_relay(net, h_o, hx, hy)
-    last.append(f_pass(f_far, 6))
-    for c in last + [down_core] + f_core:
+    ffn_io.finish()
+    last = share4_relay(net, h_o, hx, hy)
+    for c in (*df_far, *last, down_core):
         c.wait_recv()
+    ffn_io.wait()
     down_out.wait()
     f_out.wait()
+    ffn_io.close()
     net.close()
 
 
@@ -1705,7 +1834,7 @@
     cap = IMGS * TXT
     tok = CHIPS * ROW
     out_w, ffn_w, down_w = args[-3:]
-    width = ffn_w.shape[2] // CHIPS
+    width = ffn_w.shape[3] // CHIPS
     return pl.pallas_call(
         forward_kernel,
         in_specs=[V] * (len(args) - 3) + [ANY_SPEC] * 3,
@@ -1721,16 +1850,17 @@
             shape((CHIPS, ROW, D), low),
             shape((CHIPS, ROW, D), low),
             shape((2 * out_w.shape[0], D), low),
-            shape((D, 2 * width), low),
+            shape((CHIPS, 2, *ffn_w.shape[1:3], 2 * width), low),
             shape((2 * down_w.shape[0], D), low),
         ],
         scratch_shapes=[
             pltpu.VMEM((tok, D), full),
             pltpu.VMEM((5, ROW, D), low),
             pltpu.VMEM((2, ROW // 2, D), low),
-            pltpu.VMEM((ffn_w.shape[1], 2 * width), low),
+            pltpu.VMEM((*ffn_w.shape[1:3], 2 * width), low),
             pltpu.VMEM(down_w.shape, low),
             pltpu.SemaphoreType.DMA((6,)),
+            pltpu.SemaphoreType.DMA((48,)),
             *net_scratch(40),
         ],
         compiler_params=pltpu.CompilerParams(
@@ -1740,6 +1870,11 @@
             flops=5_000_000_000, bytes_accessed=200_000_000, transcendentals=0
         ),
     )(*args)
+
+
+def quarters(w):
+    n, rows, columns = w.shape
+    return w.reshape(n, 4, rows // 4, columns)
 
 
 def per_device(
@@ -1777,32 +1912,19 @@
     cond8 = jnp.concatenate([cond[0], cond[0]], axis=0)
     seg = segments[0]
     idx = jnp.concatenate([seg[None, :], positions[0], jnp.zeros((5, ROW), jnp.int32)], axis=0)
+    quarter = HDIM // 4
+    freq = np.tile(10000.0 ** (-np.arange(quarter) / quarter), (8, 128 // quarter))
+    freq_row = jnp.asarray(freq.astype(np.float32))
     (
         mod, gain_f, h_rows, idx_all, attn_w, text_rows, query, keyed, valued, text_keys, text_vals,
-        inv_qk, inv_t,
+        inv_q, inv_k, inv_t, cosine, sine, seg_col, gain_s,
     ) = open_layer(
         cond8, gain_pad, bias_pad, ada_weight, tokens[0],
-        seg[:, None], idx, attn_weight, text_weight, text[0],
-    )
+        seg[:, None], idx, freq_row, quarters(attn_weight), quarters(text_weight), text[0],
+    )
+    attn_w = attn_w.reshape(D, 3 * HW)
     h_all = h_rows.reshape(CHIPS * ROW, D)
     text_all = text_rows.reshape(CHIPS * IMGS * TXT, -1)
-    inv_qk = jnp.stack([inv_qk[0], inv_qk[4]])[:, :, None]
-    inv_t = inv_t[0][:, None]
-    seg_all = idx_all[:, 0]
-    pos_all = idx_all[:, 1:3]
-    seg_col = seg_all.reshape(CHIPS * ROW, 1)
-    seg_row = seg_all.reshape(CHIPS, 1, ROW)
-    lane = jnp.arange(128, dtype=jnp.int32)
-    quarter = HDIM // 4
-    freq = (10000.0 ** (-jnp.arange(quarter, dtype=full) / quarter))[lane % quarter]
-    where_row = ((lane // 32) % 2 == 0)[None, None, :]
-    pos_lane = jnp.where(where_row, pos_all[:, 0, :, None], pos_all[:, 1, :, None]).astype(full)
-    angle = (pos_lane * freq[None, None, :]).reshape(CHIPS * ROW, 128)
-    cosine = jnp.cos(angle)
-    sine = jnp.where(((lane // quarter) % 2 == 0)[None, :], -1.0, 1.0) * jnp.sin(angle)
-
-    gain_s = lax.dynamic_slice_in_dim(gain_f, chip * HW, HW, axis=1)[:6]
-
     totals = counts.astype(full)
     here = jnp.sum(jnp.where(jnp.arange(totals.shape[0], dtype=jnp.int32) == plane, totals, 0.0))
     weight = lax.axis_size("bucket") * here / jnp.sum(totals)
@@ -1811,10 +1933,11 @@
         comb, cross_out, q_rot, k_rot, text_rot, branch, x_one, h_two_rows, d_ffn_rows, out_w, ffn_w,
         down_w,
     ) = forward_layer(
-        query, keyed, valued, inv_qk[0], inv_qk[1], cosine, sine, text_keys, inv_t, text_vals,
-        seg_col, seg_row, gain_s, mod, seg[:, None], gain_f, tokens[0], cotangent[0], weight_row,
-        out_weight, ffn_weight, down_weight,
-    )
+        query, keyed, valued, inv_q, inv_k, cosine, sine, text_keys, inv_t, text_vals,
+        seg_col, idx_all, gain_s, mod, seg[:, None], gain_f, tokens[0], cotangent[0], weight_row,
+        out_weight, quarters(ffn_weight), down_weight,
+    )
+    ffn_w = ffn_w.reshape(D, 2 * ff)
     h_two_all = h_two_rows.reshape(CHIPS * ROW, D)
     d_ffn_all = d_ffn_rows.reshape(CHIPS * ROW, D)
     both = mult(h_two_all, ffn_w)
@@ -1837,11 +1960,11 @@
     ) = back_layer(
         [
             d_h_two, ffn_out, x_one, branch, cotangent[0], weight_row, mod,
-            seg[:, None], gain_f, tokens[0], seg_row, gain_s,
+            seg[:, None], gain_f, tokens[0], idx_all, gain_s,
         ],
         [
             out_w, attn_w, q_rot, k_rot, valued, text_rot, text_vals, cross_out, query, keyed,
-            text_keys, inv_qk[0], inv_qk[1], inv_t, cosine, sine, seg_col,
+            text_keys, inv_q, inv_k, inv_t, cosine, sine, seg_col,
         ],
         g_ffn.reshape(1, 4, 4, 2, 48, 2 * ff),
         g_down.reshape(4, 2, 128, D),

time: 590 us -> 520 us (0.88)
  Pallas kernels: 493 us -> 445 us
  other arithmetic: 17.8 us -> 6.41 us
  local copies, waits for them, and re-layouts: 21.7 us -> 13.1 us
    pallas_call x1, Pallas kernels: 169 us -> 138 us  [open_layer(): pl.pallas_call(open_kernel, in_specs=[V] * 8 + [ANY_SPEC] * 3, out_specs=...]
    pallas_call x1, Pallas kernels: 83.7 us -> 68.7 us  [forward_layer(): pl.pallas_call(forward_kernel, in_specs=[V] * (len(args) - 3) + [ANY_SPEC...]
    gather x1 -> x0, other arithmetic: 10.2 us -> none  [per_device(): (10000.0 ** (-jnp.arange(quarter, dtype=full) / quarter))[lane % quarter]]
  transfers between devices with their start and end apart: 1 -> 1, of which waited for: 0 -> 0; matrix products, arithmetic and copies ran while one was open for 4% -> 4% of each run, Pallas kernels for 26% -> 29%
where the time goes in v5:
time: 520 us; the launch traced here: 512 us
  Pallas kernels  445 us (86%)
  matrix products  43.2 us (8%)
  local copies, waits for them, and re-layouts  13.1 us (3%)
  other arithmetic  6.41 us (1%)
    pallas_call x1, Pallas kernels, close_layer(): pl.pallas_call(close_kernel, in_specs=[V] * 8, out_specs=[V] * 6, out_sha...  147 us
    pallas_call x1, Pallas kernels, open_layer(): pl.pallas_call(open_kernel, in_specs=[V] * 8 + [ANY_SPEC] * 3, out_specs=...  138 us
    pallas_call x1, Pallas kernels, back_layer(): pl.pallas_call(back_kernel, in_specs=[V] * len(early) + [ANY_SPEC] * (LAT...  91.3 us
    pallas_call x1, Pallas kernels, forward_layer(): pl.pallas_call(forward_kernel, in_specs=[V] * (len(args) - 3) + [ANY_SPEC...  68.7 us
    dot_general x5, matrix products, t_dot(): lax.dot_general(a, b, (((0,), (0,)), ((), ())), preferred_element_type=jn...  26.9 us
  transfers between devices with their start and end apart: 1, of which 0 were waited for; matrix products, arithmetic and copies ran while one was open for 4% of the time, Pallas kernels for 29%

profile of v5, /device:TPU:0, one launch (start us, length us, event | category | flops | bytes accessed | tf_op | source)
XLA Modules:
  0.0 511.5 jit_solution(10536750290674185064)
XLA Ops:
  0.7 0.1 pad.13.clone
  0.7 0.7 pad_convert_fusion
  1.4 1.4 pad_maximum_fusion.3.cond_ref
  2.8 0.8 convert_dynamic-update-slice_fusion
  3.6 1.4 copy.26.seg_ref
  5.0 0.7 reshape.75.bias_ref
  5.7 1.3 convert_reduce_fusion
  8.3 1.3 add_add_fusion.idx_ref
  9.6 0.2 dynamic_update_slice.6.gain_ref
  9.9 0.0 copy-start.7
  9.9 0.6 copy-done.7
  10.5 138.0 %shard_map.231 = (f32[8,3072]{1,0:T(8,128)}, f32[8,1536]{1,0:T(8,128)}, bf16[4,128,1536]{2,1,0:T(8,128)(2,1)}, s32[4,8,128]{2,1,0:T(8,128)}, bf16[4,2,4,48,1152]...) custom-call(bf16[8,1024]{1,0:T(8,128)(2,1)} %pad_maximum_fusion.3.co, ...), custom_call_target="tpu_custom_call" | custom-call | flops 10000000000 | bytes 400000000 | tf_op jit(solution)/shard_map/pallas_call | solution.py:931
  148.5 0.5 broadcast_in_dim.30.w_ref
  149.0 68.7 %shard_map.232 = (bf16[512,384]{1,0:T(8,128)(2,1)}, f32[512,384]{1,0:T(8,128)}, bf16[512,384]{1,0:T(8,128)(2,1)}, bf16[512,384]{1,0:T(8,128)(2,1)}, bf16[1024,38...) custom-call(f32[512,384]{1,0:T(8,128)} %get-tuple-element.56.q_ref.r, ...), custom_call_target="tpu_custom_call" | custom-call | flops 5000000000 | bytes 200000000 | tf_op jit(solution)/shard_map/pallas_call | solution.py:1838
  217.8 6.1 %fusion.4 = f32[512,2048]{1,0:T(8,128)S(1)} fusion(bf16[512,1536]{1,0:T(8,128)(2,1)} %bitcast.66, bf16[1536,2048]{1,0:T(8,128)(2,1)} %bitcast.58), kind=kOutput, calls=%fused_computation.23 | convolution fusion | flops 3221225472 | bytes 12058624 | tf_op jit(solution)/shard_map/dot_general | solution.py:143
  223.9 0.0 copy-done.11
  223.9 0.0 copy-done.13
  224.0 2.6 multiply_convert_fusion.2
  226.5 0.0 slice-start
  226.6 3.0 convolution_convert_fusion.4.fo_ref
  229.5 3.5 convolution_convert_fusion.3
  233.0 4.6 convolution_convert_fusion.5.dh2_ref
  237.6 5.7 %convolution_convert_fusion = bf16[1536,2048]{1,0:T(8,128)(2,1)} fusion(bf16[512,1536]{1,0:T(8,128)(2,1)S(1)} %bitcast.67, bf16[512,1024]{1,0:T(8,128)(2,1)S(1)} %get-tuple-element.105, bf16[512,1024]{1,0:T(8,128)(2,1)S(1)} %get-tuple-element.104), kind=kOutput, calls=%fused_computation | convolution fusion | flops 3228565504 | bytes 9961472 | tf_op jit(solution)/shard_map/dot_general | solution.py:332
  243.3 91.3 %shard_map.233 = (bf16[128,1536]{1,0:T(8,128)(2,1)}, f32[128,1536]{1,0:T(8,128)}, bf16[4,128,1536]{2,1,0:T(8,128)(2,1)}, bf16[512,1152]{1,0:T(8,128)(2,1)}, bf16...) custom-call(bf16[512,1536]{1,0:T(8,128)(2,1)} %convolution_convert_f, ...), custom_call_target="tpu_custom_call" | custom-call | flops 10000000000 | bytes 400000000 | tf_op jit(solution)/shard_map/pallas_call | solution.py:1669
  334.7 1.7 collective-permute-start
  336.4 11.9 %convolution_convert_fusion.2 = bf16[4096,768]{1,0:T(8,128)(2,1)} fusion(bf16[1024,4096]{1,0:T(8,128)(2,1)} %bitcast.56, bf16[1024,768]{1,0:T(8,128)(2,1)} %get-tuple-element.86), kind=kOutput, calls=%fused_computation.2 | convolution fusion | flops 6445596672 | bytes 16252928 | tf_op jit(solution)/shard_map/dot_general | solution.py:332
  348.2 0.0 copy-done.14
  348.2 4.0 convolution_convert_fusion.1
  352.3 0.0 copy-done.9
  352.3 1.8 convolution_convert_fusion.6
  354.1 146.6 %shard_map.234 = (f32[2,128,1536]{2,1,0:T(8,128)}, f32[3,48,1536]{2,1,0:T(8,128)}, f32[48,1536]{1,0:T(8,128)}, f32[2,48,4096]{2,1,0:T(8,128)}, f32[32,6144]{1,0:T(8,128)}, /*index=5*/f32[16,1536]{1,0:T(8,128)}) custom-call(bf16[1,4,4,2,128,768]{5,4,3,2,1,0:T(8,128)(2,1)} %bitcast.39, bf16[1,4,4,2,48,1152]{5,4,3,2,1,0:T(8,128)(2,1)} %bitcast.40, ...), custom_call_target="tpu_custom_call" | custom-call | flops 1000000 | bytes 400000000 | tf_op jit(solution)/shard_map/pallas_call | solution.py:1395
  500.6 0.0 copy-start.3
  500.6 0.0 copy-start.4
  500.6 0.9 slice.14
  501.6 0.8 slice.15
  502.4 0.6 dynamic_slice.6
  503.0 0.7 constant_dynamic-slice_fusion
  503.7 0.0 collective-permute-done
  503.7 1.0 convert_element_type.54
  504.7 0.7 copy.38
  505.4 0.0 copy-done.3
  505.4 0.9 copy.39
  506.3 0.0 copy-done.4
  506.3 0.9 copy.40
  507.2 0.9 copy.41
  508.1 0.7 copy.42
  508.8 1.1 copy.43
  510.0 1.1 copy.44
  (30 shorter events, 0.1 us)
Async XLA Ops:
  9.9 0.6 copy-start.7
  217.8 6.2 %copy-start.11 = (bf16[4,128,1536]{2,1,0:T(8,128)(2,1)S(1)}, bf16[4,128,1536]{2,1,0:T(8,128)(2,1)}, u32[]{:S(2)}) copy-start(bf16[4,128,1536]{2,1,0:T(8,128)(2,1)} %get-tuple-element.71) | copy-start | bytes 4718596
  217.8 6.2 %copy-start.13 = (bf16[1024,1536]{1,0:T(8,128)(2,1)S(1)}, bf16[1024,1536]{1,0:T(8,128)(2,1)}, u32[]{:S(2)}) copy-start(bf16[1024,1536]{1,0:T(8,128)(2,1)} %get-tuple-element.72) | copy-start | bytes 9437188
  226.5 6.5 %slice-start = ((s8[6291456]{0:T(1024)(128)(4,1)}), s8[4194304]{0:T(1024)(128)(4,1)S(1)}, s32[]{:S(2)}) async-start(s8[6291456]{0:T(1024)(128)(4,1)} %bitcast.59), calls=%async_computation | async-start | bytes 8388608
  229.5 3.5 slice-start.1
  233.0 4.6 copy-start.10
  334.7 169.0 %collective-permute-start = (bf16[128,1536]{1,0:T(8,128)(2,1)}, bf16[128,1536]{1,0:T(8,128)(2,1)S(1)}, u32[]{:S(2)}, u32[]{:S(2)}) collective-permute-start(bf16[128,1536]{1,0:T(8,128)(2,1)} %get-tuple-element.101), channel_id=1, source_target_pairs={{0,0},{1,1},{2,8},{3,9},{4,16},{5,17},{6,24},{7,25},{8,2},{9,3},{1... | collective-permute-start | bytes 1179656 | tf_op jit(solution)/shard_map/ppermute | solution.py:459
  336.3 11.9 %copy-start.8 = (bf16[4,128,1536]{2,1,0:T(8,128)(2,1)S(1)}, bf16[4,128,1536]{2,1,0:T(8,128)(2,1)}, u32[]{:S(2)}) copy-start(bf16[4,128,1536]{2,1,0:T(8,128)(2,1)} %get-tuple-element.87) | copy-start | bytes 4718596
  336.3 11.9 %copy-start.14 = (bf16[512,1152]{1,0:T(8,128)(2,1)S(1)}, bf16[512,1152]{1,0:T(8,128)(2,1)}, u32[]{:S(2)}) copy-start(bf16[512,1152]{1,0:T(8,128)(2,1)} %get-tuple-element.88) | copy-start | bytes 3538948
  348.2 4.0 copy-start.9
  348.2 4.0 copy-start.12
  354.1 150.6 %copy-start.5 = (bf16[128,1536]{1,0:T(8,128)(2,1)S(1)}, bf16[128,1536]{1,0:T(8,128)(2,1)}, u32[]{:S(2)}) copy-start(bf16[128,1536]{1,0:T(8,128)(2,1)} %get-tuple-element.83) | copy-start | bytes 1179652
  500.6 4.8 copy-start.3
  500.6 5.7 %copy-start.4 = (f32[32,6144]{1,0:T(8,128)S(1)}, f32[32,6144]{1,0:T(8,128)}, u32[]{:S(2)}) copy-start(f32[32,6144]{1,0:T(8,128)} %get-tuple-element.119) | copy-start | bytes 2359300
  504.7 2.5 copy-start.2
  505.4 2.7 copy-start.6
  506.3 2.5 copy-start.1
  508.1 1.9 copy-start

commit v6 on v5

--- a/solution.py
+++ b/solution.py
@@ -690,11 +690,11 @@
 
 
 def open_kernel(
-    cond_ref, gain_ref, bias_ref, ada_ref, tok_ref, seg_ref, idx_ref, freq_ref, attn_ref, textw_ref,
+    cond_ref, gain_ref, bias_ref, ada_ref, tok_ref, counts_ref, idx_ref, freq_ref, attn_ref, textw_ref,
     text_ref,
-    mod_ref, gains_ref, h_ref, idxs_ref, aw_ref, ta_out, q_ref, k_ref, v_ref, tk_ref, tv_ref,
+    mod_ref, gains_ref, h_out, idxs_ref, aw_out, ta_out, q_out, k_out, v_out, tk_ref, tv_ref,
     iq_ref, ik_ref, it_ref, cos_ref, sin_ref, sc_ref, gs_ref,
-    conds, parts, mods, gbuf, tw_ref, ta_ref, sums, tsums, local_sems, out_sems, attn_sems, text_sems,
+    seg_ref, w_ref, h_ref, aw_ref, q_ref, k_ref, v_ref, conds, parts, mods, gbuf, tw_ref, ta_ref, sums, tsums, local_sems, out_sems, attn_sems, text_sems,
     send_sems, recv_sems,
 ):
     low = jnp.bfloat16
@@ -706,6 +706,7 @@
 
     act = cond_ref[...].astype(full)
     act = (act * jax.nn.sigmoid(act)).astype(low).astype(full)
+    act = jnp.concatenate([act, act], axis=0)
     for j in range(8):
         gbuf[8, :, 128 * j : 128 * j + 128] = act[:, 128 * j : 128 * j + 128]
     waits = []
@@ -776,6 +777,12 @@
     text_send(0)
     attn_io.hop(0)
     text_io.hop(0)
+    seg_ref[...] = jnp.transpose(idx_ref[...].astype(full))[:, 0:1].astype(jnp.int32)
+    totals = counts_ref[...].astype(full)
+    bucket = lax.broadcasted_iota(jnp.int32, totals.shape, 1) == lax.axis_index("bucket")
+    here = jnp.sum(jnp.where(bucket, totals, 0.0), axis=-1, keepdims=True)
+    weight = CHIPS * here / jnp.sum(totals, axis=-1, keepdims=True)
+    w_ref[...] = jnp.broadcast_to(weight, w_ref.shape)
     for w in gwaits:
         w.wait_recv()
     gains = gain_ref[...]
@@ -860,6 +867,10 @@
         v_ref[at, :] = jnp.dot(h, columns(2 * HW, 3 * HW), preferred_element_type=full).astype(low)
         sums[0, :, at] = row_sums(qv * qv, kv * kv)
     sum_io = [net.send(sums.at[0], sums.at[i], m) for i, m in ((1, 2), (2, 4), (3, 6))]
+    early = ((h_ref, h_out), (aw_ref, aw_out), (q_ref, q_out), (k_ref, k_out), (v_ref, v_out))
+    for i, (src, dst) in enumerate(early):
+        kept.append(pltpu.make_async_copy(src, dst, out_sems.at[CHIPS + i]))
+        kept[-1].start()
 
     text_io.finish()
     text_io.wait()
@@ -883,8 +894,7 @@
 
     cap = ta_ref.shape[1]
     half = cap // 2
-    for lo in (0, half):
-        text_rows(0, lo, half)
+    text_rows(0, 0, cap)
     for i, c in enumerate(sum_io):
         c.wait_recv()
     for j in range(CHIPS):
@@ -905,8 +915,7 @@
     for c in relays:
         c.wait_recv()
     kept.append(keep(3))
-    for lo in (0, half):
-        text_rows(3, lo, half)
+    text_rows(3, 0, cap)
     sum_io = [net.send(tsums.at[0], tsums.at[i], m) for i, m in ((1, 2), (2, 4), (3, 6))]
     for c in sum_io:
         c.wait_recv()
@@ -922,7 +931,7 @@
     net.close()
 
 
-def open_layer(cond8, gain_pad, bias_pad, ada, tok, seg_col, idx, freq, attn, textw, text):
+def open_layer(cond, gain_pad, bias_pad, ada, tok, counts, idx, freq, attn, textw, text):
     low = jnp.bfloat16
     full = jnp.float32
     shape = jax.ShapeDtypeStruct
@@ -931,7 +940,7 @@
     return pl.pallas_call(
         open_kernel,
         in_specs=[V] * 8 + [ANY_SPEC] * 3,
-        out_specs=[V] * 5 + [ANY_SPEC] + [V] * 12,
+        out_specs=[V, V, ANY_SPEC, V] + [ANY_SPEC] * 5 + [V] * 11,
         out_shape=[
             shape((8, 3072), full),
             shape((8, D), full),
@@ -951,8 +960,15 @@
             shape((CHIPS * ROW, 128), full),
             shape((CHIPS * ROW, 1), jnp.int32),
             shape((8, HW), full),
+            shape((ROW, 1), jnp.int32),
+            shape((8, 128), full),
         ],
         scratch_shapes=[
+            pltpu.VMEM((CHIPS, ROW, D), low),
+            pltpu.VMEM((CHIPS, 2, *attn.shape[1:3], 3 * HW), low),
+            pltpu.VMEM((CHIPS * ROW, HW), full),
+            pltpu.VMEM((CHIPS * ROW, HW), full),
+            pltpu.VMEM((CHIPS * ROW, HW), low),
             pltpu.VMEM((8, 8, 128), full),
             pltpu.VMEM((8, 8, 3072), full),
             pltpu.VMEM((8, 8, 3072), full),
@@ -962,7 +978,7 @@
             pltpu.VMEM((CHIPS, 8, CHIPS * ROW), full),
             pltpu.VMEM((CHIPS, 8, CHIPS * cap), full),
             pltpu.SemaphoreType.DMA((8,)),
-            pltpu.SemaphoreType.DMA((CHIPS,)),
+            pltpu.SemaphoreType.DMA((CHIPS + 5,)),
             pltpu.SemaphoreType.DMA((48,)),
             pltpu.SemaphoreType.DMA((48,)),
             *net_scratch(80),
@@ -973,7 +989,7 @@
         cost_estimate=pl.CostEstimate(
             flops=10_000_000_000, bytes_accessed=400_000_000, transcendentals=0
         ),
-    )(cond8, gain_pad, bias_pad, ada, tok, seg_col, idx, freq, attn, textw, text)
+    )(cond, gain_pad, bias_pad, ada, tok, counts, idx, freq, attn, textw, text)
 
 
 class Chain:
@@ -1108,8 +1124,8 @@
 
 
 class Columns:
-    def __init__(self, net, total, stage, wide, out):
-        self.net, self.total, self.stage, self.wide, self.out = net, total, stage, wide, out
+    def __init__(self, net, total, stage, wide):
+        self.net, self.total, self.stage, self.wide = net, total, stage, wide
 
     def start(self):
         net = self.net
@@ -1140,8 +1156,6 @@
     def finish(self):
         for c in self.copies:
             c.wait_recv()
-        for i in range(self.out.shape[0]):
-            self.out[i] = self.wide[i].astype(jnp.float32)
 
 
 def meet_all(net, far=False):
@@ -1244,9 +1258,9 @@
 
 def close_kernel(
     text_g, attn_g, out_g, ffn_t, dmod_ref, gg_ref, gs_ref, cond_ref,
-    text_o, attn_o, out_o, ffn_o, ada_o, small_o,
+    t_wide, a_wide, out_o, f_wide, ada_o, small_o,
     tm, ta, tt, ts, am, aa, at_, as_, om, oa, ot, os_,
-    t_wide, a_wide, f_wide, t_stage, a_stage, o_stage, o_got, o_sem,
+    t_stage, a_stage, o_stage, o_got, o_sem,
     mods, mods_other, mod_sems, smalls, got, z_sems, ada_s, send_sems, recv_sems,
 ):
     low = jnp.bfloat16
@@ -1264,7 +1278,8 @@
         c.core_start()
 
     act = cond_ref[...].astype(full)
-    mods[plane, 0, :, 2 * D :] = (act * jax.nn.sigmoid(act)).astype(low)
+    act = act * jax.nn.sigmoid(act)
+    mods[plane, 0, :, 2 * D :] = jnp.concatenate([act, act], axis=0).astype(low)
     mods[plane, 0, :, : 2 * D] = dmod_ref[...].astype(low)
     mine = mods.at[plane, 0]
     mod_io = [net.send(mine, mods.at[plane, i], m) for i, m in ((1, 2), (2, 4), (3, 6))]
@@ -1299,7 +1314,7 @@
         smalls[...] = smalls[...] + got[i]
 
     small_send(0)
-    f_cols = Columns(net, None, ffn_t, f_wide, ffn_o)
+    f_cols = Columns(net, None, ffn_t, f_wide)
     f_cols.start()
     for c in chains:
         c.core_finish()
@@ -1360,20 +1375,20 @@
 
     lax.fori_loop(0, 2 * D // wide, ada_cols, 0)
     text.finish()
-    text_cols = Columns(net, tt, t_stage, t_wide, text_o)
+    text_cols = Columns(net, tt, t_stage, t_wide)
     text_cols.start()
 
     @pl.when(chip != plane)
     def _():
         transposed(net, o_stage, o_got, o_sem).wait()
-        out_o[...] = o_got[...].astype(jnp.float32)
+        out_o[...] = o_got[...]
 
     @pl.when(chip == plane)
     def _():
-        out_o[...] = ot[...]
+        out_o[...] = o_stage[...]
 
     attn.finish()
-    attn_cols = Columns(net, at_, a_stage, a_wide, attn_o)
+    attn_cols = Columns(net, at_, a_stage, a_wide)
     attn_cols.start()
     text_cols.finish()
     attn_cols.finish()
@@ -1397,10 +1412,10 @@
         in_specs=[V] * 8,
         out_specs=[V] * 6,
         out_shape=[
-            shape((2, tr, 4 * tw), full),
-            shape((3, ar, 4 * aw), full),
-            shape((orow, ow), full),
-            shape((2, fr, 4 * fw), full),
+            shape((2, tr, 4 * tw), low),
+            shape((3, ar, 4 * aw), low),
+            shape((orow, ow), low),
+            shape((2, fr, 4 * fw), low),
             shape((32, 4 * D), full),
             shape((16, D), full),
         ],
@@ -1408,9 +1423,6 @@
             *chain_scratch(True, (1, tr), 2 * tw),
             *chain_scratch(True, (1, ar), 3 * aw),
             *chain_scratch(False, orow, ow),
-            pltpu.VMEM((2, tr, 4 * tw), low),
-            pltpu.VMEM((3, ar, 4 * aw), low),
-            pltpu.VMEM((2, fr, 4 * fw), low),
             pltpu.VMEM((1, 4, tr, 2 * tw), low),
             pltpu.VMEM((1, 4, ar, 3 * aw), low),
             pltpu.VMEM((orow, ow), low),
@@ -1909,7 +1921,6 @@
         jnp.zeros((ada_weight.shape[1],), full), ada_bias.astype(full), slot * ada_bias.shape[0], 0
     )
     bias_pad = jnp.repeat(bias.reshape(2, 3072), 4, axis=0)
-    cond8 = jnp.concatenate([cond[0], cond[0]], axis=0)
     seg = segments[0]
     idx = jnp.concatenate([seg[None, :], positions[0], jnp.zeros((5, ROW), jnp.int32)], axis=0)
     quarter = HDIM // 4
@@ -1917,24 +1928,20 @@
     freq_row = jnp.asarray(freq.astype(np.float32))
     (
         mod, gain_f, h_rows, idx_all, attn_w, text_rows, query, keyed, valued, text_keys, text_vals,
-        inv_q, inv_k, inv_t, cosine, sine, seg_col, gain_s,
+        inv_q, inv_k, inv_t, cosine, sine, seg_col, gain_s, seg_own, weight_row,
     ) = open_layer(
-        cond8, gain_pad, bias_pad, ada_weight, tokens[0],
-        seg[:, None], idx, freq_row, quarters(attn_weight), quarters(text_weight), text[0],
+        cond[0], gain_pad, bias_pad, ada_weight, tokens[0],
+        counts[None, :], idx, freq_row, quarters(attn_weight), quarters(text_weight), text[0],
     )
     attn_w = attn_w.reshape(D, 3 * HW)
     h_all = h_rows.reshape(CHIPS * ROW, D)
     text_all = text_rows.reshape(CHIPS * IMGS * TXT, -1)
-    totals = counts.astype(full)
-    here = jnp.sum(jnp.where(jnp.arange(totals.shape[0], dtype=jnp.int32) == plane, totals, 0.0))
-    weight = lax.axis_size("bucket") * here / jnp.sum(totals)
-    weight_row = jnp.full((1, 128), weight, full)
     (
         comb, cross_out, q_rot, k_rot, text_rot, branch, x_one, h_two_rows, d_ffn_rows, out_w, ffn_w,
         down_w,
     ) = forward_layer(
         query, keyed, valued, inv_q, inv_k, cosine, sine, text_keys, inv_t, text_vals,
-        seg_col, idx_all, gain_s, mod, seg[:, None], gain_f, tokens[0], cotangent[0], weight_row,
+        seg_col, idx_all, gain_s, mod, seg_own, gain_f, tokens[0], cotangent[0], weight_row,
         out_weight, quarters(ffn_weight), down_weight,
     )
     ffn_w = ffn_w.reshape(D, 2 * ff)
@@ -1960,7 +1967,7 @@
     ) = back_layer(
         [
             d_h_two, ffn_out, x_one, branch, cotangent[0], weight_row, mod,
-            seg[:, None], gain_f, tokens[0], idx_all, gain_s,
+            seg_own, gain_f, tokens[0], idx_all, gain_s,
         ],
         [
             out_w, attn_w, q_rot, k_rot, valued, text_rot, text_vals, cross_out, query, keyed,
@@ -1982,7 +1989,7 @@
         d_mod,
         gg_full,
         gg_slice,
-        cond8,
+        cond[0],
     )
     rank = plane * 8 + slot
     s_gains = lax.dynamic_slice_in_dim(small[:6], rank * 48, 48, axis=1)
@@ -1993,10 +2000,10 @@
         s_ada_w,
         s_ada_b,
         s_gains,
-        s_attn,
-        s_out,
-        s_text,
-        s_ffn,
+        s_attn.astype(full),
+        s_out.astype(full),
+        s_text.astype(full),
+        s_ffn.astype(full),
         s_down,
     )
 

time: 520 us -> 512 us (0.985)
  local copies, waits for them, and re-layouts: 13.1 us -> 7.21 us
    convert_element_type x0 -> x4, other arithmetic: none -> 6.34 us  [the longest x1 2.01 us: per_device(): s_attn.astype(full)]
  transfers between devices with their start and end apart: 1 -> 1, of which waited for: 0 -> 0; matrix products, arithmetic and copies ran while one was open for 4% -> 5% of each run, Pallas kernels for 29% -> 29%
where the time goes in v6:
time: 512 us; the launch traced here: 504 us
  Pallas kernels  441 us (86%)
  matrix products  43.2 us (8%)
  other arithmetic  10.1 us (2%)
  local copies, waits for them, and re-layouts  7.21 us (1%)
    pallas_call x1, Pallas kernels, close_layer(): pl.pallas_call(close_kernel, in_specs=[V] * 8, out_specs=[V] * 6, out_sha...  146 us
    pallas_call x1, Pallas kernels, open_layer(): pl.pallas_call(open_kernel, in_specs=[V] * 8 + [ANY_SPEC] * 3, out_specs=...  135 us
    pallas_call x1, Pallas kernels, back_layer(): pl.pallas_call(back_kernel, in_specs=[V] * len(early) + [ANY_SPEC] * (LAT...  91.3 us
    pallas_call x1, Pallas kernels, forward_layer(): pl.pallas_call(forward_kernel, in_specs=[V] * (len(args) - 3) + [ANY_SPEC...  68.8 us
    dot_general x5, matrix products, t_dot(): lax.dot_general(a, b, (((0,), (0,)), ((), ())), preferred_element_type=jn...  26.9 us
  transfers between devices with their start and end apart: 1, of which 0 were waited for; matrix products, arithmetic and copies ran while one was open for 5% of the time, Pallas kernels for 29%

profile of v6, /device:TPU:0, one launch (start us, length us, event | category | flops | bytes accessed | tf_op | source)
XLA Modules:
  0.0 504.2 jit_solution(8515719488865503829)
XLA Ops:
  0.7 0.1 pad.13.clone
  0.7 0.7 pad_convert_fusion
  1.4 0.8 convert_dynamic-update-slice_fusion
  2.3 0.7 reshape.75.bias_ref
  2.9 1.3 add_add_fusion.idx_ref
  4.3 0.2 dynamic_update_slice.6.gain_ref
  4.5 0.0 copy-start.5
  4.5 0.6 copy-done.5
  5.2 135.1 %shard_map.231 = (f32[8,3072]{1,0:T(8,128)}, f32[8,1536]{1,0:T(8,128)}, bf16[4,128,1536]{2,1,0:T(8,128)(2,1)}, s32[4,8,128]{2,1,0:T(8,128)}, bf16[4,2,4,48,1152]...) custom-call(bf16[4,1024]{1,0:T(4,128)(2,1)} %bitcast.44, ...), custom_call_target="tpu_custom_call" | custom-call | flops 10000000000 | bytes 400000000 | tf_op jit(solution)/shard_map/pallas_call | solution.py:940
  140.3 68.8 %shard_map.232 = (bf16[512,384]{1,0:T(8,128)(2,1)}, f32[512,384]{1,0:T(8,128)}, bf16[512,384]{1,0:T(8,128)(2,1)}, bf16[512,384]{1,0:T(8,128)(2,1)}, bf16[1024,38...) custom-call(f32[512,384]{1,0:T(8,128)} %get-tuple-element.58.q_ref.r, ...), custom_call_target="tpu_custom_call" | custom-call | flops 5000000000 | bytes 200000000 | tf_op jit(solution)/shard_map/pallas_call | solution.py:1850
  209.1 0.0 copy-start.9
  209.1 0.0 copy-start.11
  209.1 6.1 %fusion.3 = f32[512,2048]{1,0:T(8,128)S(1)} fusion(bf16[512,1536]{1,0:T(8,128)(2,1)} %bitcast.67, bf16[1536,2048]{1,0:T(8,128)(2,1)} %bitcast.59), kind=kOutput, calls=%fused_computation.19 | convolution fusion | flops 3221225472 | bytes 12058624 | tf_op jit(solution)/shard_map/dot_general | solution.py:143
  215.3 0.0 copy-done.9
  215.3 0.0 copy-done.11
  215.3 2.6 multiply_convert_fusion.2
  217.9 0.0 slice-start
  217.9 3.0 convolution_convert_fusion.4.fo_ref
  220.8 3.5 convolution_convert_fusion.3
  224.4 0.0 slice-done
  224.4 0.0 slice-done.1
  224.4 4.6 convolution_convert_fusion.5.dh2_ref
  228.9 0.0 copy-done.8
  228.9 5.7 %convolution_convert_fusion = bf16[1536,2048]{1,0:T(8,128)(2,1)} fusion(bf16[512,1536]{1,0:T(8,128)(2,1)S(1)} %bitcast.68, bf16[512,1024]{1,0:T(8,128)(2,1)S(1)} %get-tuple-element.107, bf16[512,1024]{1,0:T(8,128)(2,1)S(1)} %get-tuple-element.106), kind=kOutput, calls=%fused_computation | convolution fusion | flops 3228565504 | bytes 9961472 | tf_op jit(solution)/shard_map/dot_general | solution.py:332
  234.7 91.3 %shard_map.233 = (bf16[128,1536]{1,0:T(8,128)(2,1)}, f32[128,1536]{1,0:T(8,128)}, bf16[4,128,1536]{2,1,0:T(8,128)(2,1)}, bf16[512,1152]{1,0:T(8,128)(2,1)}, bf16...) custom-call(bf16[512,1536]{1,0:T(8,128)(2,1)} %convolution_convert_f, ...), custom_call_target="tpu_custom_call" | custom-call | flops 10000000000 | bytes 400000000 | tf_op jit(solution)/shard_map/pallas_call | solution.py:1681
  326.0 1.7 collective-permute-start
  327.6 11.9 %convolution_convert_fusion.2 = bf16[4096,768]{1,0:T(8,128)(2,1)} fusion(bf16[1024,4096]{1,0:T(8,128)(2,1)} %bitcast.57, bf16[1024,768]{1,0:T(8,128)(2,1)} %get-tuple-element.90), kind=kOutput, calls=%fused_computation.2 | convolution fusion | flops 6445596672 | bytes 16252928 | tf_op jit(solution)/shard_map/dot_general | solution.py:332
  339.5 0.0 copy-done.6
  339.5 0.0 copy-done.12
  339.5 0.0 copy-start.10
  339.5 4.0 convolution_convert_fusion.1
  343.5 0.0 copy-done.10
  343.5 1.8 convolution_convert_fusion.6
  345.4 145.6 %shard_map.234 = (bf16[2,128,1536]{2,1,0:T(8,128)(2,1)}, bf16[3,48,1536]{2,1,0:T(8,128)(2,1)}, bf16[48,1536]{1,0:T(8,128)(2,1)}, bf16[2,48,4096]{2,1,0:T(8,128)(...) custom-call(bf16[1,4,4,2,128,768]{5,4,3,2,1,0:T(8,128)(2,1)} %bitcast.39, bf16[1,4,4,2,48,1152]{5,4,3,2,1,0:T(8,128)(2,1)} %bitcast.40, ...), custom_call_target="tpu_custom_call" | custom-call | flops 1000000 | bytes 400000000 | tf_op jit(solution)/shard_map/pallas_call | solution.py:1410
  491.0 0.9 slice.14
  491.8 0.8 slice.15
  492.7 1.7 convert_element_type.63
  494.4 2.0 convert_element_type.62
  496.4 1.3 convert_element_type.64
  497.7 0.0 copy-done.2
  497.7 1.3 convert_element_type.65
  499.0 0.6 dynamic_slice.6
  499.6 0.7 constant_dynamic-slice_fusion
  500.3 0.0 collective-permute-done
  500.3 1.0 convert_element_type.66
  501.3 0.7 copy.31
  502.0 0.9 copy.32
  502.9 0.9 copy.33
  (22 shorter events, 0.1 us)
Async XLA Ops:
  4.5 0.6 copy-start.5
  209.1 6.2 %copy-start.9 = (bf16[4,128,1536]{2,1,0:T(8,128)(2,1)S(1)}, bf16[4,128,1536]{2,1,0:T(8,128)(2,1)}, u32[]{:S(2)}) copy-start(bf16[4,128,1536]{2,1,0:T(8,128)(2,1)} %get-tuple-element.75) | copy-start | bytes 4718596
  209.1 6.2 %copy-start.11 = (bf16[1024,1536]{1,0:T(8,128)(2,1)S(1)}, bf16[1024,1536]{1,0:T(8,128)(2,1)}, u32[]{:S(2)}) copy-start(bf16[1024,1536]{1,0:T(8,128)(2,1)} %get-tuple-element.76) | copy-start | bytes 9437188
  217.9 6.5 %slice-start = ((s8[6291456]{0:T(1024)(128)(4,1)}), s8[4194304]{0:T(1024)(128)(4,1)S(1)}, s32[]{:S(2)}) async-start(s8[6291456]{0:T(1024)(128)(4,1)} %bitcast.60), calls=%async_computation | async-start | bytes 8388608
  220.8 3.5 slice-start.1
  224.4 4.6 copy-start.8
  326.0 174.3 %collective-permute-start = (bf16[128,1536]{1,0:T(8,128)(2,1)}, bf16[128,1536]{1,0:T(8,128)(2,1)S(1)}, u32[]{:S(2)}, u32[]{:S(2)}) collective-permute-start(bf16[128,1536]{1,0:T(8,128)(2,1)} %get-tuple-element.105), channel_id=1, source_target_pairs={{0,0},{1,1},{2,8},{3,9},{4,16},{5,17},{6,24},{7,25},{8,2},{9,3},{1... | collective-permute-start | bytes 1179656 | tf_op jit(solution)/shard_map/ppermute | solution.py:459
  327.6 11.9 %copy-start.6 = (bf16[4,128,1536]{2,1,0:T(8,128)(2,1)S(1)}, bf16[4,128,1536]{2,1,0:T(8,128)(2,1)}, u32[]{:S(2)}) copy-start(bf16[4,128,1536]{2,1,0:T(8,128)(2,1)} %get-tuple-element.91) | copy-start | bytes 4718596
  327.6 11.9 %copy-start.12 = (bf16[512,1152]{1,0:T(8,128)(2,1)S(1)}, bf16[512,1152]{1,0:T(8,128)(2,1)}, u32[]{:S(2)}) copy-start(bf16[512,1152]{1,0:T(8,128)(2,1)} %get-tuple-element.92) | copy-start | bytes 3538948
  339.5 4.0 copy-start.7
  339.5 4.0 copy-start.10
  491.0 5.4 %copy-start.3 = (bf16[2,128,1536]{2,1,0:T(8,128)(2,1)S(1)}, bf16[2,128,1536]{2,1,0:T(8,128)(2,1)}, u32[]{:S(2)}) copy-start(bf16[2,128,1536]{2,1,0:T(8,128)(2,1)} %get-tuple-element.103) | copy-start | bytes 2359300
  492.6 5.1 %copy-start.2 = (bf16[2,48,4096]{2,1,0:T(8,128)(2,1)S(1)}, bf16[2,48,4096]{2,1,0:T(8,128)(2,1)}, u32[]{:S(2)}) copy-start(bf16[2,48,4096]{2,1,0:T(8,128)(2,1)} %get-tuple-element.104) | copy-start | bytes 2359300
  497.7 3.6 copy-start.4
  497.7 4.3 copy-start
  499.0 3.9 copy-start.1

commit v7 on v6

--- a/solution.py
+++ b/solution.py
@@ -1257,15 +1257,17 @@
 
 
 def close_kernel(
-    text_g, attn_g, out_g, ffn_t, dmod_ref, gg_ref, gs_ref, cond_ref,
+    ta_ref, dt_ref, attn_g, out_g, ffn_t, dmod_ref, gg_ref, gs_ref, cond_ref,
     t_wide, a_wide, out_o, f_wide, ada_o, small_o,
     tm, ta, tt, ts, am, aa, at_, as_, om, oa, ot, os_,
     t_stage, a_stage, o_stage, o_got, o_sem,
-    mods, mods_other, mod_sems, smalls, got, z_sems, ada_s, send_sems, recv_sems,
+    mods, mods_other, mod_sems, smalls, got, z_sems, ada_s, ta_s, text_g, ta_sem, send_sems, recv_sems,
 ):
     low = jnp.bfloat16
     full = jnp.float32
     net = Net(send_sems, recv_sems)
+    load = pltpu.make_async_copy(ta_ref, ta_s, ta_sem.at[0])
+    load.start()
     meet_all(net, True)
     plane = lax.axis_index("bucket")
     me = net.me
@@ -1273,9 +1275,19 @@
     out = Chain(net, out_g, om, oa, ot, os_, False)
     attn = Chain(net, attn_g, am, aa, at_, as_, True)
     text = Chain(net, text_g, tm, ta, tt, ts, True)
-    chains = [out, text, attn]
-    for c in chains:
+    chains = [out, attn, text]
+    first = [out, attn]
+    for c in first:
         c.core_start()
+
+    def caption_grad(core):
+        def block(i, _):
+            at = (i // 4) * 1024 + (i % 4) * 256 + core * 128
+            part = t_dot(ta_s[:, pl.ds(pl.multiple_of(at, 128), 128)], dt_ref[...])
+            text_g[0, i // 4, i % 4, core] = part.astype(low)
+            return 0
+
+        lax.fori_loop(0, 16, block, 0)
 
     act = cond_ref[...].astype(full)
     act = act * jax.nn.sigmoid(act)
@@ -1316,28 +1328,36 @@
     small_send(0)
     f_cols = Columns(net, None, ffn_t, f_wide)
     f_cols.start()
-    for c in chains:
+    for c in first:
         c.core_finish()
         c.step(0)
+    load.wait()
+    caption_grad(1 - me % 2)
+    text.core_start()
     small_add(0)
     small_send(1)
+    for c in first:
+        c.step(1)
     for c in mod_io:
         c.wait_recv()
     lines = Spread(mods, mod_sems)
     lines.hop(0)
+    caption_grad(me % 2)
+    text.core_finish()
+    text.step(0)
     small_add(1)
     small_send(2)
-    for c in chains:
-        c.step(1)
+    for c in first:
+        c.step(2)
     lines.hop(1)
     small_add(2)
     small_send(3)
     f_cols.finish()
-    for c in chains:
-        c.step(2)
+    text.step(1)
     lines.hop(2)
     small_add(3)
     small_send(4)
+    text.step(2)
     lines.hop(3)
     other = net.send(mods, mods_other, 1)
     small_add(4)
@@ -1374,9 +1394,9 @@
         return 0
 
     lax.fori_loop(0, 2 * D // wide, ada_cols, 0)
-    text.finish()
-    text_cols = Columns(net, tt, t_stage, t_wide)
-    text_cols.start()
+    attn.finish()
+    attn_cols = Columns(net, at_, a_stage, a_wide)
+    attn_cols.start()
 
     @pl.when(chip != plane)
     def _():
@@ -1387,29 +1407,29 @@
     def _():
         out_o[...] = o_stage[...]
 
-    attn.finish()
-    attn_cols = Columns(net, at_, a_stage, a_wide)
-    attn_cols.start()
+    text.finish()
+    text_cols = Columns(net, tt, t_stage, t_wide)
+    text_cols.start()
+    attn_cols.finish()
     text_cols.finish()
-    attn_cols.finish()
     for c in chains:
         c.close()
     lines.close()
     net.close()
 
 
-def close_layer(text_g, attn_g, out_g, ffn_t, dmod, gg, gs, cond8):
+def close_layer(text_all, d_text, attn_g, out_g, ffn_t, dmod, gg, gs, cond):
     low = jnp.bfloat16
     full = jnp.float32
     shape = jax.ShapeDtypeStruct
     V = VMEM_SPEC
-    tr, tw = text_g.shape[-2], text_g.shape[-1] // 2
+    tr, tw = text_all.shape[1] // 32, d_text.shape[1] // 2
     ar, aw = attn_g.shape[-2], attn_g.shape[-1] // 3
     orow, ow = out_g.shape[-2:]
     fr, fw = ffn_t.shape[-2], ffn_t.shape[-1] // 2
     return pl.pallas_call(
         close_kernel,
-        in_specs=[V] * 8,
+        in_specs=[ANY_SPEC] + [V] * 8,
         out_specs=[V] * 6,
         out_shape=[
             shape((2, tr, 4 * tw), low),
@@ -1428,13 +1448,16 @@
             pltpu.VMEM((orow, ow), low),
             pltpu.VMEM((orow, ow), low),
             pltpu.SemaphoreType.DMA((2,)),
-            pltpu.VMEM((4, CHIPS, 8, 2 * D + cond8.shape[1]), low),
-            pltpu.VMEM((4, CHIPS, 8, 2 * D + cond8.shape[1]), low),
+            pltpu.VMEM((4, CHIPS, 8, 2 * D + cond.shape[1]), low),
+            pltpu.VMEM((4, CHIPS, 8, 2 * D + cond.shape[1]), low),
             pltpu.SemaphoreType.DMA((16,)),
             pltpu.VMEM((16, D), full),
             pltpu.VMEM((5, 16, D), full),
             pltpu.SemaphoreType.DMA((4,)),
             pltpu.VMEM((128, 512), full),
+            pltpu.VMEM(text_all.shape, low),
+            pltpu.VMEM((1, 4, 4, 2, tr, 2 * tw), low),
+            pltpu.SemaphoreType.DMA((1,)),
             *net_scratch(40),
         ],
         compiler_params=pltpu.CompilerParams(
@@ -1443,7 +1466,7 @@
         cost_estimate=pl.CostEstimate(
             flops=1_000_000, bytes_accessed=400_000_000, transcendentals=0
         ),
-    )(text_g, attn_g, out_g, ffn_t, dmod, gg, gs, cond8)
+    )(text_all, d_text, attn_g, out_g, ffn_t, dmod, gg, gs, cond)
 
 
 def back_kernel(
@@ -1977,12 +2000,12 @@
         g_down.reshape(4, 2, 128, D),
     )
     d_branch_all = d_branch_rows.reshape(CHIPS * ROW, D)
-    g_text = t_dot(text_all, d_text).astype(low)
     g_attn = t_dot(h_all, d_qkv).astype(low)
     g_out = t_dot(comb, d_branch_all).astype(low)
     s_down = to_row_owner(down_sum)
     s_text, s_attn, s_out, s_ffn, s_ada_w, small = close_layer(
-        g_text.reshape(1, 4, 4, 2, 128, 2 * HW),
+        text_all,
+        d_text,
         g_attn.reshape(1, 4, 4, 2, 48, 3 * HW),
         g_out.reshape(4, 2, 48, D),
         ffn_sum,

time: 512 us -> 498 us (0.973)
  matrix products: 43.2 us -> 33.2 us
    dot_general x5 -> x4, matrix products: 26.9 us -> 16.9 us  [t_dot(): lax.dot_general(a, b, (((0,), (0,)), ((), ())), preferred_element_type=jn...]
  transfers between devices with their start and end apart: 1 -> 1, of which waited for: 0 -> 0; matrix products, arithmetic and copies ran while one was open for 5% -> 3% of each run, Pallas kernels for 29% -> 29%
where the time goes in v7:
time: 498 us; the launch traced here: 489 us
  Pallas kernels  436 us (88%)
  matrix products  33.2 us (7%)
  other arithmetic  10.1 us (2%)
  local copies, waits for them, and re-layouts  7.2 us (1%)
    pallas_call x1, Pallas kernels, close_layer(): pl.pallas_call(close_kernel, in_specs=[ANY_SPEC] + [V] * 8, out_specs=[V]...  141 us
    pallas_call x1, Pallas kernels, open_layer(): pl.pallas_call(open_kernel, in_specs=[V] * 8 + [ANY_SPEC] * 3, out_specs=...  135 us
    pallas_call x1, Pallas kernels, back_layer(): pl.pallas_call(back_kernel, in_specs=[V] * len(early) + [ANY_SPEC] * (LAT...  91.3 us
    pallas_call x1, Pallas kernels, forward_layer(): pl.pallas_call(forward_kernel, in_specs=[V] * (len(args) - 3) + [ANY_SPEC...  68.8 us
    dot_general x4, matrix products, t_dot(): lax.dot_general(a, b, (((0,), (0,)), ((), ())), preferred_element_type=jn...  16.9 us
  transfers between devices with their start and end apart: 1, of which 0 were waited for; matrix products, arithmetic and copies ran while one was open for 3% of the time, Pallas kernels for 29%

profile of v7, /device:TPU:0, one launch (start us, length us, event | category | flops | bytes accessed | tf_op | source)
XLA Modules:
  0.0 489.5 jit_solution(5237579387605737795)
XLA Ops:
  0.7 0.1 pad.13.clone
  0.7 0.7 pad_convert_fusion
  1.4 0.8 convert_dynamic-update-slice_fusion
  2.3 0.7 reshape.72.bias_ref
  2.9 1.3 add_add_fusion.idx_ref
  4.3 0.2 dynamic_update_slice.6.gain_ref
  4.5 0.0 copy-start.5
  4.5 0.6 copy-done.5
  5.2 135.1 %shard_map.231 = (f32[8,3072]{1,0:T(8,128)}, f32[8,1536]{1,0:T(8,128)}, bf16[4,128,1536]{2,1,0:T(8,128)(2,1)}, s32[4,8,128]{2,1,0:T(8,128)}, bf16[4,2,4,48,1152]...) custom-call(bf16[4,1024]{1,0:T(4,128)(2,1)} %bitcast.41, ...), custom_call_target="tpu_custom_call" | custom-call | flops 10000000000 | bytes 400000000 | tf_op jit(solution)/shard_map/pallas_call | solution.py:940
  140.3 68.8 %shard_map.232 = (bf16[512,384]{1,0:T(8,128)(2,1)}, f32[512,384]{1,0:T(8,128)}, bf16[512,384]{1,0:T(8,128)(2,1)}, bf16[512,384]{1,0:T(8,128)(2,1)}, bf16[1024,38...) custom-call(f32[512,384]{1,0:T(8,128)} %get-tuple-element.58.q_ref.r, ...), custom_call_target="tpu_custom_call" | custom-call | flops 5000000000 | bytes 200000000 | tf_op jit(solution)/shard_map/pallas_call | solution.py:1873
  209.0 0.0 copy-start.8
  209.0 0.0 copy-start.10
  209.1 6.1 %fusion.3 = f32[512,2048]{1,0:T(8,128)S(1)} fusion(bf16[512,1536]{1,0:T(8,128)(2,1)} %bitcast.63, bf16[1536,2048]{1,0:T(8,128)(2,1)} %bitcast.55), kind=kOutput, calls=%fused_computation.18 | convolution fusion | flops 3221225472 | bytes 12058624 | tf_op jit(solution)/shard_map/dot_general | solution.py:143
  215.2 0.0 copy-done.8
  215.2 0.0 copy-done.10
  215.2 2.6 multiply_convert_fusion.2
  217.8 0.0 slice-start
  217.8 3.0 convolution_convert_fusion.3.fo_ref
  220.8 3.5 convolution_convert_fusion.2
  224.3 0.0 slice-done
  224.3 0.0 slice-done.1
  224.3 4.6 convolution_convert_fusion.4.dh2_ref
  228.8 0.0 copy-done.7
  228.8 5.7 %convolution_convert_fusion = bf16[1536,2048]{1,0:T(8,128)(2,1)} fusion(bf16[512,1536]{1,0:T(8,128)(2,1)S(1)} %bitcast.64, bf16[512,1024]{1,0:T(8,128)(2,1)S(1)} %get-tuple-element.107, bf16[512,1024]{1,0:T(8,128)(2,1)S(1)} %get-tuple-element.106), kind=kOutput, calls=%fused_computation | convolution fusion | flops 3228565504 | bytes 9961472 | tf_op jit(solution)/shard_map/dot_general | solution.py:332
  234.6 91.3 %shard_map.233 = (bf16[128,1536]{1,0:T(8,128)(2,1)}, f32[128,1536]{1,0:T(8,128)}, bf16[4,128,1536]{2,1,0:T(8,128)(2,1)}, bf16[512,1152]{1,0:T(8,128)(2,1)}, bf16...) custom-call(bf16[512,1536]{1,0:T(8,128)(2,1)} %convolution_convert_f, ...), custom_call_target="tpu_custom_call" | custom-call | flops 10000000000 | bytes 400000000 | tf_op jit(solution)/shard_map/pallas_call | solution.py:1704
  325.9 1.9 collective-permute-start
  327.8 0.0 copy-start.6
  327.8 0.0 copy-start.9
  327.8 5.9 %convolution_convert_fusion.1 = bf16[1536,1152]{1,0:T(8,128)(2,1)} fusion(bf16[512,1536]{1,0:T(8,128)(2,1)} %bitcast.61, bf16[512,1152]{1,0:T(8,128)(2,1)} %get-tuple-element.92), kind=kOutput, calls=%fused_computation.1 | convolution fusion | flops 1813708800 | bytes 6291456 | tf_op jit(solution)/shard_map/dot_general | solution.py:332
  333.7 0.0 copy-done.6
  333.7 0.0 copy-done.9
  333.7 1.8 convolution_convert_fusion.5
  335.5 140.7 %shard_map.234 = (bf16[2,128,1536]{2,1,0:T(8,128)(2,1)}, bf16[3,48,1536]{2,1,0:T(8,128)(2,1)}, bf16[48,1536]{1,0:T(8,128)(2,1)}, bf16[2,48,4096]{2,1,0:T(8,128)(...) custom-call(bf16[1024,4096]{1,0:T(8,128)(2,1)} %bitcast.36, bf16[1024,768]{1,0:T(8,128)(2,1)} %get-tuple-element.90.dt_ref, ...), custom_call_target="tpu_custom_call" | custom-call | flops 1000000 | bytes 400000000 | tf_op jit(solution)/shard_map/pallas_call | solution.py:1430
  476.2 0.0 copy-start.3
  476.2 0.9 slice.14
  477.1 0.8 slice.15
  477.9 1.7 convert_element_type.59
  479.6 2.0 convert_element_type.58
  481.6 1.3 convert_element_type.60
  483.0 0.0 copy-done.2
  483.0 1.3 convert_element_type.61
  484.3 0.6 dynamic_slice.6
  484.9 0.7 constant_dynamic-slice_fusion
  485.6 0.0 collective-permute-done
  485.6 1.0 convert_element_type.62
  486.5 0.7 copy.31
  487.3 0.9 copy.32
  488.2 0.9 copy.33
  (17 shorter events, 0.1 us)
Async XLA Ops:
  4.5 0.6 copy-start.5
  209.0 6.2 %copy-start.8 = (bf16[4,128,1536]{2,1,0:T(8,128)(2,1)S(1)}, bf16[4,128,1536]{2,1,0:T(8,128)(2,1)}, u32[]{:S(2)}) copy-start(bf16[4,128,1536]{2,1,0:T(8,128)(2,1)} %get-tuple-element.75) | copy-start | bytes 4718596
  209.0 6.2 %copy-start.10 = (bf16[1024,1536]{1,0:T(8,128)(2,1)S(1)}, bf16[1024,1536]{1,0:T(8,128)(2,1)}, u32[]{:S(2)}) copy-start(bf16[1024,1536]{1,0:T(8,128)(2,1)} %get-tuple-element.76) | copy-start | bytes 9437188
  217.8 6.4 %slice-start = ((s8[6291456]{0:T(1024)(128)(4,1)}), s8[4194304]{0:T(1024)(128)(4,1)S(1)}, s32[]{:S(2)}) async-start(s8[6291456]{0:T(1024)(128)(4,1)} %bitcast.56), calls=%async_computation | async-start | bytes 8388608
  220.8 3.5 slice-start.1
  224.3 4.6 copy-start.7
  325.9 159.7 %collective-permute-start = (bf16[128,1536]{1,0:T(8,128)(2,1)}, bf16[128,1536]{1,0:T(8,128)(2,1)S(1)}, u32[]{:S(2)}, u32[]{:S(2)}) collective-permute-start(bf16[128,1536]{1,0:T(8,128)(2,1)} %get-tuple-element.105), channel_id=1, source_target_pairs={{0,0},{1,1},{2,8},{3,9},{4,16},{5,17},{6,24},{7,25},{8,2},{9,3},{1... | collective-permute-start | bytes 1179656 | tf_op jit(solution)/shard_map/ppermute | solution.py:459
  327.8 5.9 %copy-start.6 = (bf16[4,128,1536]{2,1,0:T(8,128)(2,1)S(1)}, bf16[4,128,1536]{2,1,0:T(8,128)(2,1)}, u32[]{:S(2)}) copy-start(bf16[4,128,1536]{2,1,0:T(8,128)(2,1)} %get-tuple-element.94) | copy-start | bytes 4718596
  327.8 5.9 %copy-start.9 = (bf16[512,384]{1,0:T(8,128)(2,1)S(1)}, bf16[512,384]{1,0:T(8,128)(2,1)}, u32[]{:S(2)}) copy-start(bf16[512,384]{1,0:T(8,128)(2,1)} %get-tuple-element.93) | copy-start | bytes 1179652
  476.2 5.4 %copy-start.3 = (bf16[2,128,1536]{2,1,0:T(8,128)(2,1)S(1)}, bf16[2,128,1536]{2,1,0:T(8,128)(2,1)}, u32[]{:S(2)}) copy-start(bf16[2,128,1536]{2,1,0:T(8,128)(2,1)} %get-tuple-element.103) | copy-start | bytes 2359300
  477.9 5.1 %copy-start.2 = (bf16[2,48,4096]{2,1,0:T(8,128)(2,1)S(1)}, bf16[2,48,4096]{2,1,0:T(8,128)(2,1)}, u32[]{:S(2)}) copy-start(bf16[2,48,4096]{2,1,0:T(8,128)(2,1)} %get-tuple-element.104) | copy-start | bytes 2359300
  483.0 3.6 copy-start.4
  483.0 4.3 copy-start
  484.3 3.9 copy-start.1

commit v8 on v7

--- a/solution.py
+++ b/solution.py
@@ -1752,8 +1752,8 @@
 def forward_kernel(
     q_ref, k_ref, v_ref, iq_ref, ik_ref, cos_ref, sin_ref, tk_ref, it_ref, tv_ref, sc_ref, sr_ref,
     gs_ref, mod_ref, seg_ref, gain_ref, tok_ref, cot_ref, w_ref, outw_ref, ffnw_ref, downw_ref,
-    comb_o, cross_o, qr_o, kr_o, tr_o, branch_o, x1_o, h_o, df_o, ow_o, fw_o, dw_o,
-    part_s, buf, far, f_own, d_own, local_sems, line_sems, send_sems, recv_sems,
+    comb_e, cross_e, qr_e, kr_e, tr_e, branch_o, x1_o, h_o, df_e, ow_o, fw_o, dw_o,
+    comb_o, cross_o, qr_o, kr_o, tr_o, df_o, early_sems, part_s, buf, far, f_own, d_own, local_sems, line_sems, send_sems, recv_sems,
 ):
     low = jnp.bfloat16
     full = jnp.float32
@@ -1826,6 +1826,16 @@
         net, lambda j, i: part_s[pl.ds(j * ROW + i * half, half), :], buf, far
     )
     df_far = share4_relay(net, df_o, dx, dy)
+    kept = []
+
+    def keep(src, dst):
+        kept.append(pltpu.make_async_copy(src, dst, early_sems.at[len(kept)]))
+        kept[-1].start()
+
+    for src, dst in (
+        (comb_o, comb_e), (cross_o, cross_e), (qr_o, qr_e), (kr_o, kr_e), (tr_o, tr_e)
+    ):
+        keep(src, dst)
 
     down_here.wait()
     down_out = local(d_own, own(dw_o, down_rows), 4)
@@ -1850,13 +1860,16 @@
 
     lax.fori_loop(0, ROW // block, second, 0)
     hx, hy = share4_start(net, h_o)
+    for c in df_far:
+        c.wait_recv()
+    keep(df_o, df_e)
     ffn_io.finish()
     last = share4_relay(net, h_o, hx, hy)
-    for c in (*df_far, *last, down_core):
+    for c in (*last, down_core):
         c.wait_recv()
     ffn_io.wait()
-    down_out.wait()
-    f_out.wait()
+    for c in (*kept, down_out, f_out):
+        c.wait()
     ffn_io.close()
     net.close()
 
@@ -1873,7 +1886,7 @@
     return pl.pallas_call(
         forward_kernel,
         in_specs=[V] * (len(args) - 3) + [ANY_SPEC] * 3,
-        out_specs=[V] * 10 + [ANY_SPEC] * 2,
+        out_specs=[ANY_SPEC] * 5 + [V] * 3 + [ANY_SPEC, V, ANY_SPEC, ANY_SPEC],
         out_shape=[
             shape((tok, HW), low),
             shape((tok, HW), full),
@@ -1889,6 +1902,13 @@
             shape((2 * down_w.shape[0], D), low),
         ],
         scratch_shapes=[
+            pltpu.VMEM((tok, HW), low),
+            pltpu.VMEM((tok, HW), full),
+            pltpu.VMEM((tok, HW), low),
+            pltpu.VMEM((tok, HW), low),
+            pltpu.VMEM((CHIPS * cap, HW), low),
+            pltpu.VMEM((CHIPS, ROW, D), low),
+            pltpu.SemaphoreType.DMA((6,)),
             pltpu.VMEM((tok, D), full),
             pltpu.VMEM((5, ROW, D), low),
             pltpu.VMEM((2, ROW // 2, D), low),

time: 498 us -> 497 us (level)
  no operation moved by 1% of the time
where the time goes in v8:
time: 497 us; the launch traced here: 488 us
  Pallas kernels  435 us (88%)
  matrix products  33.2 us (7%)
  other arithmetic  10.1 us (2%)
  local copies, waits for them, and re-layouts  7.2 us (1%)
    pallas_call x1, Pallas kernels, close_layer(): pl.pallas_call(close_kernel, in_specs=[ANY_SPEC] + [V] * 8, out_specs=[V]...  141 us
    pallas_call x1, Pallas kernels, open_layer(): pl.pallas_call(open_kernel, in_specs=[V] * 8 + [ANY_SPEC] * 3, out_specs=...  135 us
    pallas_call x1, Pallas kernels, back_layer(): pl.pallas_call(back_kernel, in_specs=[V] * len(early) + [ANY_SPEC] * (LAT...  91.3 us
    pallas_call x1, Pallas kernels, forward_layer(): pl.pallas_call(forward_kernel, in_specs=[V] * (len(args) - 3) + [ANY_SPEC...  67.6 us
    dot_general x4, matrix products, t_dot(): lax.dot_general(a, b, (((0,), (0,)), ((), ())), preferred_element_type=jn...  16.9 us
  transfers between devices with their start and end apart: 1, of which 0 were waited for; matrix products, arithmetic and copies ran while one was open for 3% of the time, Pallas kernels for 29%

profile of v8, /device:TPU:0, one launch (start us, length us, event | category | flops | bytes accessed | tf_op | source)
XLA Modules:
  0.0 488.3 jit_solution(2467183356094873426)
XLA Ops:
  0.7 0.1 pad.13.clone
  0.7 0.7 pad_convert_fusion
  1.4 0.8 convert_dynamic-update-slice_fusion
  2.3 0.7 reshape.72.bias_ref
  2.9 1.3 add_add_fusion.idx_ref
  4.3 0.2 dynamic_update_slice.6.gain_ref
  4.5 0.0 copy-start.5
  4.5 0.6 copy-done.5
  5.2 135.1 %shard_map.231 = (f32[8,3072]{1,0:T(8,128)}, f32[8,1536]{1,0:T(8,128)}, bf16[4,128,1536]{2,1,0:T(8,128)(2,1)}, s32[4,8,128]{2,1,0:T(8,128)}, bf16[4,2,4,48,1152]...) custom-call(bf16[4,1024]{1,0:T(4,128)(2,1)} %bitcast.41, ...), custom_call_target="tpu_custom_call" | custom-call | flops 10000000000 | bytes 400000000 | tf_op jit(solution)/shard_map/pallas_call | solution.py:940
  140.3 67.6 %shard_map.232 = (bf16[512,384]{1,0:T(8,128)(2,1)}, f32[512,384]{1,0:T(8,128)}, bf16[512,384]{1,0:T(8,128)(2,1)}, bf16[512,384]{1,0:T(8,128)(2,1)}, bf16[1024,38...) custom-call(f32[512,384]{1,0:T(8,128)} %get-tuple-element.58.q_ref.r, ...), custom_call_target="tpu_custom_call" | custom-call | flops 5000000000 | bytes 200000000 | tf_op jit(solution)/shard_map/pallas_call | solution.py:1886
  207.8 0.0 copy-start.8
  207.9 0.0 copy-start.10
  207.9 6.1 %fusion.3 = f32[512,2048]{1,0:T(8,128)S(1)} fusion(bf16[512,1536]{1,0:T(8,128)(2,1)} %bitcast.63, bf16[1536,2048]{1,0:T(8,128)(2,1)} %bitcast.55), kind=kOutput, calls=%fused_computation.18 | convolution fusion | flops 3221225472 | bytes 12058624 | tf_op jit(solution)/shard_map/dot_general | solution.py:143
  214.0 0.0 copy-done.8
  214.0 0.0 copy-done.10
  214.0 2.6 multiply_convert_fusion.2
  216.6 0.0 slice-start
  216.6 3.0 convolution_convert_fusion.3.fo_ref
  219.6 3.5 convolution_convert_fusion.2
  223.1 0.0 slice-done
  223.1 0.0 slice-done.1
  223.1 4.6 convolution_convert_fusion.4.dh2_ref
  227.7 0.0 copy-done.7
  227.7 5.7 %convolution_convert_fusion = bf16[1536,2048]{1,0:T(8,128)(2,1)} fusion(bf16[512,1536]{1,0:T(8,128)(2,1)S(1)} %bitcast.64, bf16[512,1024]{1,0:T(8,128)(2,1)S(1)} %get-tuple-element.107, bf16[512,1024]{1,0:T(8,128)(2,1)S(1)} %get-tuple-element.106), kind=kOutput, calls=%fused_computation | convolution fusion | flops 3228565504 | bytes 9961472 | tf_op jit(solution)/shard_map/dot_general | solution.py:332
  233.4 91.3 %shard_map.233 = (bf16[128,1536]{1,0:T(8,128)(2,1)}, f32[128,1536]{1,0:T(8,128)}, bf16[4,128,1536]{2,1,0:T(8,128)(2,1)}, bf16[512,1152]{1,0:T(8,128)(2,1)}, bf16...) custom-call(bf16[512,1536]{1,0:T(8,128)(2,1)} %convolution_convert_f, ...), custom_call_target="tpu_custom_call" | custom-call | flops 10000000000 | bytes 400000000 | tf_op jit(solution)/shard_map/pallas_call | solution.py:1704
  324.7 1.9 collective-permute-start
  326.6 0.0 copy-start.6
  326.6 0.0 copy-start.9
  326.6 5.9 %convolution_convert_fusion.1 = bf16[1536,1152]{1,0:T(8,128)(2,1)} fusion(bf16[512,1536]{1,0:T(8,128)(2,1)} %bitcast.61, bf16[512,1152]{1,0:T(8,128)(2,1)} %get-tuple-element.92), kind=kOutput, calls=%fused_computation.1 | convolution fusion | flops 1813708800 | bytes 6291456 | tf_op jit(solution)/shard_map/dot_general | solution.py:332
  332.5 0.0 copy-done.6
  332.5 0.0 copy-done.9
  332.5 1.8 convolution_convert_fusion.5
  334.3 140.7 %shard_map.234 = (bf16[2,128,1536]{2,1,0:T(8,128)(2,1)}, bf16[3,48,1536]{2,1,0:T(8,128)(2,1)}, bf16[48,1536]{1,0:T(8,128)(2,1)}, bf16[2,48,4096]{2,1,0:T(8,128)(...) custom-call(bf16[1024,4096]{1,0:T(8,128)(2,1)} %bitcast.36, bf16[1024,768]{1,0:T(8,128)(2,1)} %get-tuple-element.90.dt_ref, ...), custom_call_target="tpu_custom_call" | custom-call | flops 1000000 | bytes 400000000 | tf_op jit(solution)/shard_map/pallas_call | solution.py:1430
  475.0 0.0 copy-start.3
  475.0 0.9 slice.14
  475.9 0.8 slice.15
  476.7 1.7 convert_element_type.59
  478.4 2.0 convert_element_type.58
  480.4 1.3 convert_element_type.60
  481.8 1.3 convert_element_type.61
  483.1 0.6 dynamic_slice.6
  483.7 0.7 constant_dynamic-slice_fusion
  484.4 0.0 collective-permute-done
  484.4 1.0 convert_element_type.62
  485.3 0.7 copy.31
  486.1 0.0 copy-done
  486.1 0.9 copy.32
  487.0 0.9 copy.33
  (17 shorter events, 0.1 us)
Async XLA Ops:
  4.5 0.6 copy-start.5
  207.8 6.2 %copy-start.8 = (bf16[4,128,1536]{2,1,0:T(8,128)(2,1)S(1)}, bf16[4,128,1536]{2,1,0:T(8,128)(2,1)}, u32[]{:S(2)}) copy-start(bf16[4,128,1536]{2,1,0:T(8,128)(2,1)} %get-tuple-element.75) | copy-start | bytes 4718596
  207.9 6.2 %copy-start.10 = (bf16[1024,1536]{1,0:T(8,128)(2,1)S(1)}, bf16[1024,1536]{1,0:T(8,128)(2,1)}, u32[]{:S(2)}) copy-start(bf16[1024,1536]{1,0:T(8,128)(2,1)} %get-tuple-element.76) | copy-start | bytes 9437188
  216.6 6.4 %slice-start = ((s8[6291456]{0:T(1024)(128)(4,1)}), s8[4194304]{0:T(1024)(128)(4,1)S(1)}, s32[]{:S(2)}) async-start(s8[6291456]{0:T(1024)(128)(4,1)} %bitcast.56), calls=%async_computation | async-start | bytes 8388608
  219.6 3.5 slice-start.1
  223.1 4.6 copy-start.7
  324.7 159.7 %collective-permute-start = (bf16[128,1536]{1,0:T(8,128)(2,1)}, bf16[128,1536]{1,0:T(8,128)(2,1)S(1)}, u32[]{:S(2)}, u32[]{:S(2)}) collective-permute-start(bf16[128,1536]{1,0:T(8,128)(2,1)} %get-tuple-element.105), channel_id=1, source_target_pairs={{0,0},{1,1},{2,8},{3,9},{4,16},{5,17},{6,24},{7,25},{8,2},{9,3},{1... | collective-permute-start | bytes 1179656 | tf_op jit(solution)/shard_map/ppermute | solution.py:459
  326.6 5.9 %copy-start.6 = (bf16[4,128,1536]{2,1,0:T(8,128)(2,1)S(1)}, bf16[4,128,1536]{2,1,0:T(8,128)(2,1)}, u32[]{:S(2)}) copy-start(bf16[4,128,1536]{2,1,0:T(8,128)(2,1)} %get-tuple-element.94) | copy-start | bytes 4718596
  326.6 5.9 %copy-start.9 = (bf16[512,384]{1,0:T(8,128)(2,1)S(1)}, bf16[512,384]{1,0:T(8,128)(2,1)}, u32[]{:S(2)}) copy-start(bf16[512,384]{1,0:T(8,128)(2,1)} %get-tuple-element.93) | copy-start | bytes 1179652
  475.0 5.4 %copy-start.3 = (bf16[2,128,1536]{2,1,0:T(8,128)(2,1)S(1)}, bf16[2,128,1536]{2,1,0:T(8,128)(2,1)}, u32[]{:S(2)}) copy-start(bf16[2,128,1536]{2,1,0:T(8,128)(2,1)} %get-tuple-element.103) | copy-start | bytes 2359300
  476.7 5.1 %copy-start.2 = (bf16[2,48,4096]{2,1,0:T(8,128)(2,1)S(1)}, bf16[2,48,4096]{2,1,0:T(8,128)(2,1)}, u32[]{:S(2)}) copy-start(bf16[2,48,4096]{2,1,0:T(8,128)(2,1)} %get-tuple-element.104) | copy-start | bytes 2359300
  481.8 3.6 copy-start.4
  481.8 4.3 copy-start
  483.1 3.9 copy-start.1
